TPU v7x, 32 devices: a whole 2x2x4 slice. The times are simulated.
32 devices in a mesh: nodes: 16 (over z, y, x), shard: 2 (over core).
Axes of the slice: x: 2, y: 2, z: 4, core: 2. Of those that a mesh axis runs over, the one named last changes fastest.
Arguments:
- grid_inputs: bfloat16 [32768, 474], P(('nodes', 'shard')), may hold values from -6 to 6
- mesh_static: bfloat16 [32768, 512], P(('nodes', 'shard')), may hold values from -6 to 6
- targets: float32 [32768, 227], P(('nodes', 'shard')), may hold values from -6 to 6
- area_weight: float32 [32768], P(('nodes', 'shard')), may hold values from 0.1 to 1
- valid_rows: int32 [32], P(('nodes', 'shard')), may hold values from 512 to 1024, as said below
- encoder_lists: int32 [32768, 4], P(('nodes', 'shard')), may hold values from 0 to 3071
- mesh_lists: int32 [32768, 4], P(('nodes', 'shard')), may hold values from 0 to 3071
- decoder_lists: int32 [32768, 4], P(('nodes', 'shard')), may hold values from 0 to 3071
- step_count: int32 [1], replicated, may hold values from 1 to 20
- w_in: float32 [474, 512], P(None, ('nodes', 'shard')), may hold values from -0.25 to 0.25
- moment_in: float32 [474, 512], P(None, ('nodes', 'shard')), may hold values from -0.00036621094 to 0.00036621094
- square_in: float32 [474, 512], P(None, ('nodes', 'shard')), may hold values from 5.922408e-10 to 2.3689632e-09
- w_layers: float32 [4, 6, 512, 512], P(None, None, ('nodes', 'shard')), may hold values from -0.25 to 0.25
- moment_layers: float32 [4, 6, 512, 512], P(None, None, ('nodes', 'shard')), may hold values from -0.00036621094 to 0.00036621094
- square_layers: float32 [4, 6, 512, 512], P(None, None, ('nodes', 'shard')), may hold values from 5.922408e-10 to 2.3689632e-09
- norm_gains: float32 [4, 2, 512], P(None, None, ('nodes', 'shard')), may hold values from 0.5 to 1.5
- moment_gains: float32 [4, 2, 512], P(None, None, ('nodes', 'shard')), may hold values from -0.015625 to 0.015625
- square_gains: float32 [4, 2, 512], P(None, None, ('nodes', 'shard')), may hold values from 9.536743e-07 to 3.8146973e-06
- w_out: float32 [512, 227], P(('nodes', 'shard')), may hold values from -0.25 to 0.25
- moment_out: float32 [512, 227], P(('nodes', 'shard')), may hold values from -0.00036621094 to 0.00036621094
- square_out: float32 [512, 227], P(('nodes', 'shard')), may hold values from 5.922408e-10 to 2.3689632e-09
Outputs:
- loss_value: float32 [], replicated
- new_moment_in: float32 [474, 512], P(None, ('nodes', 'shard'))
- new_square_in: float32 [474, 512], P(None, ('nodes', 'shard'))
- new_w_in: float32 [474, 512], P(None, ('nodes', 'shard'))
- new_moment_layers: float32 [4, 6, 512, 512], P(None, None, ('nodes', 'shard'))
- new_square_layers: float32 [4, 6, 512, 512], P(None, None, ('nodes', 'shard'))
- new_w_layers: float32 [4, 6, 512, 512], P(None, None, ('nodes', 'shard'))
- new_moment_gains: float32 [4, 2, 512], P(None, None, ('nodes', 'shard'))
- new_square_gains: float32 [4, 2, 512], P(None, None, ('nodes', 'shard'))
- new_gains: float32 [4, 2, 512], P(None, None, ('nodes', 'shard'))
- new_moment_out: float32 [512, 227], P(('nodes', 'shard'))
- new_square_out: float32 [512, 227], P(('nodes', 'shard'))
- new_w_out: float32 [512, 227], P(('nodes', 'shard'))
Inputs may be any that keep to these rules, and one draw needn't show every extreme that they name: `encoder_lists`: entry e names row e mod 1024 of block (p - 1 + e // 1024) mod 32 for a row of block p. `mesh_lists`: entry e names row e mod 1024 of block (p - 1 + e // 1024) mod 32 for a row of block p. `decoder_lists`: entry e names row e mod 1024 of block (p - 1 + e // 1024) mod 32 for a row of block p. `valid_rows`: some block is full and some holds exactly 512 valid cells.
All inputs are finite; a program needn't handle non-finite values.
Results may differ from a plain program's by a relative error of at most 0.0045.
The roundings to bfloat16 on the way count: a program that leaves them out, or rounds other values in their place, can miss the bound.
Values may be sent and summed in bfloat16 or wider, within the bound.
No kernel may reach another device: no remote copies, remote signals or barrier semaphores. Data moves between devices by JAX's collectives and lax.ppermute only.
A program may use at most 320 MiB of HBM per device.

v0:
```python
import jax
import jax.numpy as jnp
from jax import lax
from jax.sharding import PartitionSpec as P

EPS_NORM = 1e-05
BETA_ONE = 0.5
BETA_TWO = 0.5
ADAM_EPS = 1e-08
LEARN_RATE = 0.04
DECAY_RATE = 0.1


def with_halo(cells, sides, width):
    for axis, dim in sides:
        count = lax.axis_size(axis)
        head = lax.slice_in_dim(cells, 0, width, axis=dim)
        tail = lax.slice_in_dim(cells, cells.shape[dim] - width, cells.shape[dim], axis=dim)
        cells = jnp.concatenate(
            [
                lax.ppermute(tail, axis, [(i, (i + 1) % count) for i in range(count)]),
                cells,
                lax.ppermute(head, axis, [((i + 1) % count, i) for i in range(count)]),
            ],
            axis=dim,
        )
    return cells


def product(left, right):
    return jnp.dot(left, right, preferred_element_type=jnp.float32)


def product_left(left, right):
    return lax.dot_general(
        left, right, (((0,), (0,)), ((), ())), preferred_element_type=jnp.float32
    )


def product_right(left, right):
    return lax.dot_general(
        left, right, (((1,), (1,)), ((), ())), preferred_element_type=jnp.float32
    )


def normalize(tensor):
    centre = tensor - jnp.mean(tensor, axis=-1, keepdims=True)
    inv_scale = lax.rsqrt(jnp.mean(centre * centre, axis=-1, keepdims=True) + EPS_NORM)
    return (centre * inv_scale, inv_scale)


def normal_back(grad_unit, unit_rows, inv_scale):
    centred = grad_unit - jnp.mean(grad_unit, axis=-1, keepdims=True)
    return inv_scale * (
        centred - unit_rows * jnp.mean(grad_unit * unit_rows, axis=-1, keepdims=True)
    )


def silu_slope(tensor):
    sigmoid_v = jax.nn.sigmoid(tensor)
    return sigmoid_v * (1.0 + tensor * (1.0 - sigmoid_v))


def layer_forward(source_low, target, target_low, neighbours, matrices, gain_pair):
    model_width = target.shape[1]
    sent_rows = product(source_low, matrices[0]).astype(jnp.bfloat16)
    window = with_halo(sent_rows, ((("nodes", "shard"), 0),), sent_rows.shape[0])
    own_term = product(target_low, matrices[1])
    pre_edge = window[neighbours].astype(jnp.float32) + own_term[:, None, :]
    edge_hidden = jax.nn.silu(pre_edge).astype(jnp.bfloat16)
    message = product(edge_hidden.reshape(-1, model_width), matrices[2]).reshape(pre_edge.shape)
    unit_rows, inv_scale = normalize(message)
    gain_values = gain_pair.astype(jnp.float32)
    aggregate = jnp.sum(unit_rows * gain_values[0], axis=1).astype(jnp.bfloat16)
    node_mix = product(target_low, matrices[3]) + product(aggregate, matrices[4])
    node_hidden = jax.nn.silu(node_mix).astype(jnp.bfloat16)
    node_out = product(node_hidden, matrices[5])
    out_unit, out_scale = normalize(node_out)
    updated = target + out_unit * gain_values[1]
    return (updated, (pre_edge, message, aggregate, node_mix, node_hidden, node_out))


def return_window(slot_grads):
    block_rows = slot_grads.shape[0] // 3
    rounded = lax.optimization_barrier(slot_grads.astype(jnp.bfloat16))
    rim_pair = jnp.concatenate([rounded[:block_rows], rounded[2 * block_rows :]], axis=0)
    extended = with_halo(rim_pair, ((("nodes", "shard"), 0),), block_rows)
    middle = rounded[block_rows : 2 * block_rows].astype(jnp.float32)
    return (
        middle
        + extended[:block_rows].astype(jnp.float32)
        + extended[3 * block_rows :].astype(jnp.float32)
    )


def layer_backward(grad_new, source_low, target_low, neighbours, matrices, gain_pair, stored):
    pre_edge, message, aggregate, node_mix, node_hidden, node_out = stored
    model_width = grad_new.shape[1]
    gain_values = gain_pair.astype(jnp.float32)
    out_unit, out_scale = normalize(node_out)
    grad_gain_two = jnp.sum(grad_new * out_unit, axis=0)
    grad_out = normal_back(grad_new * gain_values[1], out_unit, out_scale).astype(jnp.bfloat16)
    grad_five = product_left(node_hidden, grad_out)
    grad_mix = (product_right(grad_out, matrices[5]) * silu_slope(node_mix)).astype(jnp.bfloat16)
    grad_three = product_left(target_low, grad_mix)
    grad_four = product_left(aggregate, grad_mix)
    grad_sum = product_right(grad_mix, matrices[4])
    unit_rows, inv_scale = normalize(message)
    grad_gain_one = jnp.sum(grad_sum * jnp.sum(unit_rows, axis=1), axis=0)
    grad_message = normal_back(
        (grad_sum * gain_values[0])[:, None, :], unit_rows, inv_scale
    ).astype(jnp.bfloat16)
    flat_grad = grad_message.reshape(-1, model_width)
    edge_hidden = jax.nn.silu(pre_edge).astype(jnp.bfloat16)
    grad_two = product_left(edge_hidden.reshape(-1, model_width), flat_grad)
    grad_pre = product_right(flat_grad, matrices[2]).reshape(pre_edge.shape) * silu_slope(pre_edge)
    grad_own = jnp.sum(grad_pre, axis=1).astype(jnp.bfloat16)
    grad_one = product_left(target_low, grad_own)
    slot_grads = jnp.zeros((3 * grad_new.shape[0], model_width), jnp.float32)
    slot_grads = slot_grads.at[neighbours.reshape(-1)].add(grad_pre.reshape(-1, model_width))
    grad_sent = return_window(slot_grads).astype(jnp.bfloat16)
    grad_zero = product_left(source_low, grad_sent)
    grad_target_low = product_right(grad_own, matrices[1]) + product_right(grad_mix, matrices[3])
    grad_source_low = product_right(grad_sent, matrices[0])
    grad_matrices = jnp.stack([grad_zero, grad_one, grad_two, grad_three, grad_four, grad_five])
    grad_gains = jnp.stack([grad_gain_one, grad_gain_two])
    return (grad_target_low, grad_source_low, grad_matrices, grad_gains)


def adamw_update(weight, moment_one, moment_two, gradient, step_value, decay_rate):
    new_one = BETA_ONE * moment_one + (1.0 - BETA_ONE) * gradient
    new_two = BETA_TWO * moment_two + (1.0 - BETA_TWO) * gradient * gradient
    correct_one = 1.0 - jnp.power(BETA_ONE, step_value)
    correct_two = 1.0 - jnp.power(BETA_TWO, step_value)
    direction = new_one / correct_one / (jnp.sqrt(new_two / correct_two) + ADAM_EPS)
    return (new_one, new_two, weight - LEARN_RATE * (direction + decay_rate * weight))


def shards(
    grid_inputs,
    mesh_static,
    targets,
    area_weight,
    valid_rows,
    encoder_lists,
    mesh_lists,
    decoder_lists,
    step_count,
    w_in,
    moment_in,
    square_in,
    w_layers,
    moment_layers,
    square_layers,
    norm_gains,
    moment_gains,
    square_gains,
    w_out,
    moment_out,
    square_out,
):
    row_count = grid_inputs.shape[0]
    layer_total = w_layers.shape[0]
    table_in, table_out = (
        lax.all_gather(w_in.astype(jnp.bfloat16), ("nodes", "shard"), axis=1, tiled=True),
        lax.all_gather(w_out.astype(jnp.bfloat16), ("nodes", "shard"), axis=0, tiled=True),
    )
    grid_latent = product(grid_inputs, table_in)
    mesh_latent = mesh_static.astype(jnp.float32)
    stored_list = []
    for layer_id in range(layer_total):
        matrices, gain_pair = (
            lax.all_gather(
                w_layers[layer_id].astype(jnp.bfloat16), ("nodes", "shard"), axis=1, tiled=True
            ),
            lax.all_gather(
                norm_gains[layer_id].astype(jnp.bfloat16), ("nodes", "shard"), axis=1, tiled=True
            ),
        )
        if layer_id == 0:
            neighbours, source, target = (encoder_lists, grid_latent, mesh_latent)
        elif layer_id == layer_total - 1:
            neighbours, source, target = (decoder_lists, mesh_latent, grid_latent)
        else:
            neighbours, source, target = (mesh_lists, mesh_latent, mesh_latent)
        target_low = target.astype(jnp.bfloat16)
        shared_side = 0 < layer_id < layer_total - 1
        source_low = target_low if shared_side else source.astype(jnp.bfloat16)
        updated, stored = layer_forward(
            source_low, target, target_low, neighbours, matrices, gain_pair
        )
        stored_list.append((neighbours, source_low, target_low, stored))
        if layer_id == layer_total - 1:
            grid_latent = updated
        else:
            mesh_latent = updated
    grid_low = grid_latent.astype(jnp.bfloat16)
    prediction = product(grid_low, table_out)
    local_rows = jnp.arange(row_count, dtype=jnp.int32)
    weight_rows = area_weight * (local_rows < valid_rows[0]).astype(jnp.float32)
    error_rows = prediction - targets
    loss_scale = 1.0 / (row_count * lax.axis_size(("nodes", "shard")) * prediction.shape[1])
    loss_local = jnp.sum(weight_rows[:, None] * error_rows * error_rows) * loss_scale
    loss_value = lax.psum(loss_local, ("nodes", "shard"))
    grad_pred = (2.0 * loss_scale * weight_rows[:, None] * error_rows).astype(jnp.bfloat16)
    grad_table_out = product_left(grid_low, grad_pred)
    grad_grid = product_right(grad_pred, table_out)
    grad_mesh = jnp.zeros_like(mesh_latent)
    layer_grads = [None] * layer_total
    gain_grads = [None] * layer_total
    for layer_id in reversed(range(layer_total)):
        neighbours, source_low, target_low, stored = stored_list[layer_id]
        matrices, gain_pair = (
            lax.all_gather(
                w_layers[layer_id].astype(jnp.bfloat16), ("nodes", "shard"), axis=1, tiled=True
            ),
            lax.all_gather(
                norm_gains[layer_id].astype(jnp.bfloat16), ("nodes", "shard"), axis=1, tiled=True
            ),
        )
        last_layer = layer_id == layer_total - 1
        grad_new = grad_grid if last_layer else grad_mesh
        grad_target_low, grad_source_low, grad_matrices, grad_gains = layer_backward(
            grad_new, source_low, target_low, neighbours, matrices, gain_pair, stored
        )
        if last_layer:
            grad_grid = grad_new + grad_target_low
            grad_mesh = grad_source_low
        elif layer_id == 0:
            grad_grid = grad_grid + grad_source_low
        else:
            grad_mesh = grad_new + grad_target_low + grad_source_low
        layer_grads[layer_id], gain_grads[layer_id] = (
            lax.psum_scatter(grad_matrices, ("nodes", "shard"), scatter_dimension=1, tiled=True),
            lax.psum_scatter(grad_gains, ("nodes", "shard"), scatter_dimension=1, tiled=True),
        )
    grad_table_in = product_left(grid_inputs, grad_grid.astype(jnp.bfloat16))
    grad_in, grad_out = (
        lax.psum_scatter(grad_table_in, ("nodes", "shard"), scatter_dimension=1, tiled=True),
        lax.psum_scatter(grad_table_out, ("nodes", "shard"), scatter_dimension=0, tiled=True),
    )
    grad_layers = jnp.stack(layer_grads)
    grad_gain_all = jnp.stack(gain_grads)
    step_value = step_count[0].astype(jnp.float32)
    one_in, two_in, new_in = adamw_update(
        w_in, moment_in, square_in, grad_in, step_value, DECAY_RATE
    )
    one_layers, two_layers, new_layers = adamw_update(
        w_layers, moment_layers, square_layers, grad_layers, step_value, DECAY_RATE
    )
    one_gains, two_gains, new_gains = adamw_update(
        norm_gains, moment_gains, square_gains, grad_gain_all, step_value, 0.0
    )
    one_out, two_out, new_out = adamw_update(
        w_out, moment_out, square_out, grad_out, step_value, DECAY_RATE
    )
    return (
        loss_value,
        one_in,
        two_in,
        new_in,
        one_layers,
        two_layers,
        new_layers,
        one_gains,
        two_gains,
        new_gains,
        one_out,
        two_out,
        new_out,
    )


def solution(mesh):
    in_specs = (
        P(("nodes", "shard"), None),
        P(("nodes", "shard"), None),
        P(("nodes", "shard"), None),
        P(("nodes", "shard")),
        P(("nodes", "shard")),
        P(("nodes", "shard"), None),
        P(("nodes", "shard"), None),
        P(("nodes", "shard"), None),
        P(),
        P(None, ("nodes", "shard")),
        P(None, ("nodes", "shard")),
        P(None, ("nodes", "shard")),
        P(None, None, ("nodes", "shard"), None),
        P(None, None, ("nodes", "shard"), None),
        P(None, None, ("nodes", "shard"), None),
        P(None, None, ("nodes", "shard")),
        P(None, None, ("nodes", "shard")),
        P(None, None, ("nodes", "shard")),
        P(("nodes", "shard"), None),
        P(("nodes", "shard"), None),
        P(("nodes", "shard"), None),
    )
    out_specs = (
        P(),
        P(None, ("nodes", "shard")),
        P(None, ("nodes", "shard")),
        P(None, ("nodes", "shard")),
        P(None, None, ("nodes", "shard"), None),
        P(None, None, ("nodes", "shard"), None),
        P(None, None, ("nodes", "shard"), None),
        P(None, None, ("nodes", "shard")),
        P(None, None, ("nodes", "shard")),
        P(None, None, ("nodes", "shard")),
        P(("nodes", "shard"), None),
        P(("nodes", "shard"), None),
        P(("nodes", "shard"), None),
    )
    return jax.shard_map(shards, mesh=mesh, in_specs=in_specs, out_specs=out_specs, check_vma=False)
```

profile of v0, /device:TPU:0, one launch (start us, length us, event | category | flops | bytes accessed | tf_op | source)
XLA Modules:
  0.0 1993.3 jit_solution(11772579081341894745)
XLA Ops:
  13.0 45.1 %all_gather.38 = bf16[474,512]{0,1:T(8,128)(2,1)S(1)} all-gather(bf16[474,16]{0,1:T(8,128)(2,1)S(1)} %convert_element_type.281), channel_id=1, replica_groups=mesh['nodes'=16,'shard'=2] {'nodes','shard'}, dimensions={1}, use_global_device_ids=true | all-gather | bytes 500544 | tf_op jit(solution)/shard_map/all_gather | solution.py:165
  79.3 57.5 %all-gather.2 = bf16[1,2,512]{1,0,2:T(2,128)(2,1)S(1)} all-gather(bf16[1,2,16]{1,0,2:T(2,128)(2,1)S(1)} %get-tuple-element.130), channel_id=4, replica_groups=mesh['nodes'=16,'shard'=2] {'nodes','shard'}, dimensions={2}, use_global_device_ids=true | all-gather | bytes 2112 | tf_op jit(solution)/shard_map/all_gather | solution.py:176
  152.9 19.7 gather_fusion
  204.3 53.1 %all-gather.4 = bf16[1,2,512]{1,0,2:T(2,128)(2,1)S(1)} all-gather(bf16[1,2,16]{1,0,2:T(2,128)(2,1)S(1)} %get-tuple-element.129), channel_id=6, replica_groups=mesh['nodes'=16,'shard'=2] {'nodes','shard'}, dimensions={2}, use_global_device_ids=true | all-gather | bytes 2112 | tf_op jit(solution)/shard_map/all_gather | solution.py:176
  273.3 19.7 gather_fusion.1
  325.9 52.6 %all-gather.6 = bf16[1,2,512]{1,0,2:T(2,128)(2,1)S(1)} all-gather(bf16[1,2,16]{1,0,2:T(2,128)(2,1)S(1)} %get-tuple-element.128), channel_id=8, replica_groups=mesh['nodes'=16,'shard'=2] {'nodes','shard'}, dimensions={2}, use_global_device_ids=true | all-gather | bytes 2112 | tf_op jit(solution)/shard_map/all_gather | solution.py:176
  389.7 19.7 gather_fusion.2
  443.1 54.0 %all_gather.47 = bf16[512,227]{1,0:T(8,128)(2,1)S(1)} all-gather(bf16[16,227]{1,0:T(8,128)(2,1)S(1)} %convert_element_type.320), channel_id=1, replica_groups=mesh['nodes'=16,'shard'=2] {'nodes','shard'}, dimensions={0}, use_global_device_ids=true | all-gather | bytes 239712 | tf_op jit(solution)/shard_map/all_gather | solution.py:166
  497.3 39.4 %all-gather.7 = bf16[1,2,512]{1,0,2:T(2,128)(2,1)S(1)} all-gather(bf16[1,2,16]{1,0,2:T(2,128)(2,1)S(1)} %get-tuple-element.127), channel_id=9, replica_groups=mesh['nodes'=16,'shard'=2] {'nodes','shard'}, dimensions={2}, use_global_device_ids=true | all-gather | bytes 2112 | tf_op jit(solution)/shard_map/all_gather | solution.py:176
  552.2 19.7 gather_fusion.3
  633.1 15.1 fusion.113
  648.1 12.0 copy.285
  670.2 28.3 %scatter_custom_fusion = f32[3072,512]{1,0:T(8,128)} fusion(s32[4096]{0:T(1024)} %bitcast.384, f32[4096,512]{1,0:T(8,128)} %reshape.431, f32[]{:T(128)} %constant.82.clone.1), kind=kCustom, calls=%fused_computation.58 | custom fusion | flops 2097152 | bytes 6291968 | tf_op jit(solution)/shard_map/scatter-add | solution.py:120
  747.3 14.8 fusion.114
  762.0 12.0 copy.291
  784.4 28.2 %scatter_custom_fusion.1 = f32[3072,512]{1,0:T(8,128)} fusion(s32[4096]{0:T(1024)S(1)} %bitcast.385, f32[4096,512]{1,0:T(8,128)} %reshape.439, f32[]{:T(128)} %constant.82.clone.1), kind=kCustom, calls=%fused_computation.56 | custom fusion | flops 2097152 | bytes 6291968 | tf_op jit(solution)/shard_map/scatter-add | solution.py:120
  863.5 14.9 fusion.115
  878.5 12.0 copy.296
  900.5 28.2 %scatter_custom_fusion.2 = f32[3072,512]{1,0:T(8,128)} fusion(s32[4096]{0:T(1024)S(1)} %bitcast.386, f32[4096,512]{1,0:T(8,128)} %reshape.447, f32[]{:T(128)} %constant.82.clone.1), kind=kCustom, calls=%fused_computation.54 | custom fusion | flops 2097152 | bytes 6291968 | tf_op jit(solution)/shard_map/scatter-add | solution.py:120
  935.2 11.3 collective-permute-start.12
  983.2 14.7 fusion.116
  997.9 12.1 copy.301
  1020.1 28.3 %scatter_custom_fusion.3 = f32[3072,512]{1,0:T(8,128)} fusion(s32[4096]{0:T(1024)} %bitcast.383, f32[4096,512]{1,0:T(8,128)} %reshape.455, f32[]{:T(128)} %constant.82.clone.1), kind=kCustom, calls=%fused_computation.52 | custom fusion | flops 2097152 | bytes 6291968 | tf_op jit(solution)/shard_map/scatter-add | solution.py:120
  1053.1 12.9 collective-permute-start.14
  1162.0 49.9 %psum.7 = f32[]{:T(128)} all-reduce(f32[]{:T(128)S(6)} %mul.746), channel_id=1, replica_groups=mesh['nodes'=16,'shard'=2] {'nodes','shard'}, use_global_device_ids=true, to_apply=%region_21.22 | all-reduce | flops 1 | bytes 8 | tf_op jit(solution)/shard_map/psum | solution.py:204
  1214.7 28.6 %reduce-scatter.35.cloned.1.call-done = f32[16,2]{1,0:T(8,128)} async-done(((f32[512,2]{1,0:T(8,128)}), f32[16,2]{1,0:T(8,128)}) %reduce-scatter.35.cloned.1.call-update) | async-done | bytes 144
  1244.1 130.8 %reduce-scatter.33.cloned.1.call-done = f32[16,2]{1,0:T(8,128)} async-done(((f32[512,2]{1,0:T(8,128)}), f32[16,2]{1,0:T(8,128)}) %reduce-scatter.33.cloned.1.call-update) | async-done | bytes 144
  1376.3 131.5 %reduce-scatter.31.cloned.1.call-done = f32[16,474]{1,0:T(8,128)} async-done(((f32[512,474]{1,0:T(8,128)}), f32[16,474]{1,0:T(8,128)}) %reduce-scatter.31.cloned.1.call-update) | async-done | bytes 30352
  1509.3 114.5 %reduce-scatter.27.cloned.1.call-done = f32[6,16,512]{2,1,0:T(8,128)} async-done(((f32[6,512,512]{2,1,0:T(8,128)}), f32[6,16,512]{2,1,0:T(8,128)}) %reduce-scatter.27.cloned.1.call-update) | async-done | bytes 196624 | tf_op jit(solution)/shard_map/reduce_scatter | solution.py:234
  1623.8 120.1 %reduce-scatter.25.cloned.1.call-done = f32[6,16,512]{2,1,0:T(8,128)} async-done(((f32[6,512,512]{2,1,0:T(8,128)}), f32[6,16,512]{2,1,0:T(8,128)}) %reduce-scatter.25.cloned.1.call-update) | async-done | bytes 196624 | tf_op jit(solution)/shard_map/reduce_scatter | solution.py:234
  1743.9 119.5 %reduce-scatter.23.cloned.1.call-done = f32[6,16,512]{2,1,0:T(8,128)} async-done(((f32[6,512,512]{2,1,0:T(8,128)}), f32[6,16,512]{2,1,0:T(8,128)}) %reduce-scatter.23.cloned.1.call-update) | async-done | bytes 196624 | tf_op jit(solution)/shard_map/reduce_scatter | solution.py:234
  1863.3 119.9 %reduce-scatter.21.cloned.1.call-done = f32[6,16,512]{2,1,0:T(8,128)} async-done(((f32[6,512,512]{2,1,0:T(8,128)}), f32[6,16,512]{2,1,0:T(8,128)}) %reduce-scatter.21.cloned.1.call-update) | async-done | bytes 196624 | tf_op jit(solution)/shard_map/reduce_scatter | solution.py:234
  (633 shorter events, 534.9 us)
Async XLA Ops:
  7.2 66.5 %all-gather.15.cloned.1.call-start = ((), (), s32[]{:S(2)}) async-start(), calls=%async_computation.16 | async-start | bytes 3244032 | tf_op jit(solution)/shard_map/all_gather | solution.py:173
  9.3 190.8 %all-gather.17.cloned.1.call-start = ((), (), s32[]{:S(2)}) async-start(), calls=%async_computation.17 | async-start | bytes 3244032 | tf_op jit(solution)/shard_map/all_gather | solution.py:173
  10.0 311.4 %all-gather.19.cloned.1.call-start = ((), (), s32[]{:S(2)}) async-start(), calls=%async_computation.18 | async-start | bytes 3244032 | tf_op jit(solution)/shard_map/all_gather | solution.py:173
  10.8 428.6 %all-gather.13.cloned.1.call-start = ((), (), s32[]{:S(2)}) async-start(), calls=%async_computation.15 | async-start | bytes 3244032 | tf_op jit(solution)/shard_map/all_gather | solution.py:173
  11.3 1200.5 %reduce-scatter.39.cloned.1.call-start = ((), (), s32[]{:S(2)}) async-start(), calls=%async_computation.23 | async-start | bytes 270336
  76.4 73.3 %collective-permute-start.1 = (bf16[1024,512]{1,0:T(8,128)(2,1)}, bf16[1024,512]{1,0:T(8,128)(2,1)}, u32[]{:S(2)}, u32[]{:S(2)}) collective-permute-start(bf16[1024,512]{1,0:T(8,128)(2,1)} %convolution_convert_fusion.3), channel_id=1, source_target_pairs={{1,0},{2,1},{3,2},{4,3},{5,4},{6,5},{7,6},{8,7},{9,8},{10,9},{11,1... | collective-permute-start | bytes 3145736 | tf_op jit(solution)/shard_map/ppermute | solution.py:23
  79.3 70.4 %collective-permute-start = (bf16[1024,512]{1,0:T(8,128)(2,1)}, bf16[1024,512]{1,0:T(8,128)(2,1)}, u32[]{:S(2)}, u32[]{:S(2)}) collective-permute-start(bf16[1024,512]{1,0:T(8,128)(2,1)} %convolution_convert_fusion.3), channel_id=1, source_target_pairs={{0,1},{1,2},{2,3},{3,4},{4,5},{5,6},{6,7},{7,8},{8,9},{9,10},{10,1... | collective-permute-start | bytes 3145736 | tf_op jit(solution)/shard_map/ppermute | solution.py:21
  203.2 66.6 %collective-permute-start.3 = (bf16[1024,512]{1,0:T(8,128)(2,1)}, bf16[1024,512]{1,0:T(8,128)(2,1)}, u32[]{:S(2)}, u32[]{:S(2)}) collective-permute-start(bf16[1024,512]{1,0:T(8,128)(2,1)} %convolution_convert_fusion.2), channel_id=1, source_target_pairs={{1,0},{2,1},{3,2},{4,3},{5,4},{6,5},{7,6},{8,7},{9,8},{10,9},{11,1... | collective-permute-start | bytes 3145736 | tf_op jit(solution)/shard_map/ppermute | solution.py:23
  203.2 66.6 %collective-permute-start.2 = (bf16[1024,512]{1,0:T(8,128)(2,1)}, bf16[1024,512]{1,0:T(8,128)(2,1)}, u32[]{:S(2)}, u32[]{:S(2)}) collective-permute-start(bf16[1024,512]{1,0:T(8,128)(2,1)} %convolution_convert_fusion.2), channel_id=1, source_target_pairs={{0,1},{1,2},{2,3},{3,4},{4,5},{5,6},{6,7},{7,8},{8,9},{9,10},{10,1... | collective-permute-start | bytes 3145736 | tf_op jit(solution)/shard_map/ppermute | solution.py:21
  323.7 64.2 %collective-permute-start.5 = (bf16[1024,512]{1,0:T(8,128)(2,1)S(1)}, bf16[1024,512]{1,0:T(8,128)(2,1)S(1)}, u32[]{:S(2)}, u32[]{:S(2)}) collective-permute-start(bf16[1024,512]{1,0:T(8,128)(2,1)S(1)} %convolution_convert_fusion.1), channel_id=1, source_target_pairs={{1,0},{2,1},{3,2},{4,3},{5,4},{6,5},{7,6},{8,7},{9,8},{10,9},{11,1... | collective-permute-start | bytes 3145736 | tf_op jit(solution)/shard_map/ppermute | solution.py:23
  325.8 62.0 %collective-permute-start.4 = (bf16[1024,512]{1,0:T(8,128)(2,1)S(1)}, bf16[1024,512]{1,0:T(8,128)(2,1)S(1)}, u32[]{:S(2)}, u32[]{:S(2)}) collective-permute-start(bf16[1024,512]{1,0:T(8,128)(2,1)S(1)} %convolution_convert_fusion.1), channel_id=1, source_target_pairs={{0,1},{1,2},{2,3},{3,4},{4,5},{5,6},{6,7},{7,8},{8,9},{9,10},{10,1... | collective-permute-start | bytes 3145736 | tf_op jit(solution)/shard_map/ppermute | solution.py:21
  442.6 106.1 %collective-permute-start.7 = (bf16[1024,512]{1,0:T(8,128)(2,1)}, bf16[1024,512]{1,0:T(8,128)(2,1)}, u32[]{:S(2)}, u32[]{:S(2)}) collective-permute-start(bf16[1024,512]{1,0:T(8,128)(2,1)} %convolution_convert_fusion), channel_id=1, source_target_pairs={{1,0},{2,1},{3,2},{4,3},{5,4},{6,5},{7,6},{8,7},{9,8},{10,9},{11,1... | collective-permute-start | bytes 3145736 | tf_op jit(solution)/shard_map/ppermute | solution.py:23
  443.0 105.6 %collective-permute-start.6 = (bf16[1024,512]{1,0:T(8,128)(2,1)}, bf16[1024,512]{1,0:T(8,128)(2,1)}, u32[]{:S(2)}, u32[]{:S(2)}) collective-permute-start(bf16[1024,512]{1,0:T(8,128)(2,1)} %convolution_convert_fusion), channel_id=1, source_target_pairs={{0,1},{1,2},{2,3},{3,4},{4,5},{5,6},{6,7},{7,8},{8,9},{9,10},{10,1... | collective-permute-start | bytes 3145736 | tf_op jit(solution)/shard_map/ppermute | solution.py:21
  704.8 18.2 collective-permute-start.8
  705.1 17.9 collective-permute-start.9
  715.8 496.8 %reduce-scatter.29.cloned.1.call-start = ((), (), s32[]{:S(2)}) async-start(), calls=%async_computation.14 | async-start | bytes 540672 | tf_op jit(solution)/shard_map/reduce_scatter | solution.py:240
  718.8 495.2 %reduce-scatter.37.cloned.1.call-start = ((), (), s32[]{:S(2)}) async-start(), calls=%async_computation.22 | async-start | bytes 270336
  817.3 18.4 collective-permute-start.10
  822.8 12.9 collective-permute-start.11
  935.2 18.5 collective-permute-start.12
  946.4 12.8 collective-permute-start.13
  947.3 296.0 %reduce-scatter.35.cloned.1.call-start = ((), (), s32[]{:S(2)}) async-start(), calls=%async_computation.21 | async-start | bytes 270336
  1053.1 27.0 %collective-permute-start.14 = (bf16[1024,512]{1,0:T(8,128)(2,1)}, bf16[1024,512]{1,0:T(8,128)(2,1)}, u32[]{:S(2)}, u32[]{:S(2)}) collective-permute-start(bf16[1024,512]{1,0:T(8,128)(2,1)} %get-tuple-element.115), channel_id=1, source_target_pairs={{0,1},{1,2},{2,3},{3,4},{4,5},{5,6},{6,7},{7,8},{8,9},{9,10},{10,1... | collective-permute-start | bytes 3145736 | tf_op jit(solution)/shard_map/ppermute | solution.py:21
  1066.0 14.1 collective-permute-start.15
  1073.5 301.4 %reduce-scatter.33.cloned.1.call-start = ((), (), s32[]{:S(2)}) async-start(), calls=%async_computation.20 | async-start | bytes 270336
  1080.0 427.8 %reduce-scatter.31.cloned.1.call-start = ((), (), s32[]{:S(2)}) async-start(), calls=%async_computation.19 | async-start | bytes 1081344
  1088.5 535.3 %reduce-scatter.27.cloned.1.call-start = ((), (), s32[]{:S(2)}) async-start(), calls=%async_computation.13 | async-start | bytes 6488064 | tf_op jit(solution)/shard_map/reduce_scatter | solution.py:234
  1102.8 641.1 %reduce-scatter.25.cloned.1.call-start = ((), (), s32[]{:S(2)}) async-start(), calls=%async_computation.12 | async-start | bytes 6488064 | tf_op jit(solution)/shard_map/reduce_scatter | solution.py:234
  1122.1 741.3 %reduce-scatter.23.cloned.1.call-start = ((), (), s32[]{:S(2)}) async-start(), calls=%async_computation.11 | async-start | bytes 6488064 | tf_op jit(solution)/shard_map/reduce_scatter | solution.py:234
  1141.4 841.9 %reduce-scatter.21.cloned.1.call-start = ((), (), s32[]{:S(2)}) async-start(), calls=%async_computation.10 | async-start | bytes 6488064 | tf_op jit(solution)/shard_map/reduce_scatter | solution.py:234
  1160.4 822.9 %copy-start.81 = (f32[4,6,16,512]{3,2,1,0:T(8,128)S(1)}, f32[4,6,16,512]{3,2,1,0:T(8,128)}, u32[]{:S(2)}) copy-start(f32[4,6,16,512]{3,2,1,0:T(8,128)} %param.33) | copy-start | bytes 2359300
  1160.4 822.8 %copy-start.118 = (f32[4,6,16,512]{3,2,1,0:T(8,128)S(1)}, f32[4,6,16,512]{3,2,1,0:T(8,128)}, u32[]{:S(2)}) copy-start(f32[4,6,16,512]{3,2,1,0:T(8,128)} %param.35) | copy-start | bytes 2359300
  (169 other events, 5930.8 us)
Sparse Core Ops, SparseCore 0:
  11.5 62.0 all-gather.14
  77.1 64.0 all-gather.16
  144.7 58.0 all-gather.18
  205.6 61.2 all-gather.12
  715.9 129.6 reduce-scatter.38
  848.4 130.4 reduce-scatter.28
  981.7 129.8 reduce-scatter.36
  1113.9 129.3 reduce-scatter.34
  1245.6 129.3 reduce-scatter.32
  1377.1 130.6 reduce-scatter.30
  1513.5 110.2 reduce-scatter.26
  1630.2 113.6 reduce-scatter.24
  1749.5 113.7 reduce-scatter.22
  1869.8 113.4 reduce-scatter.20
where the time goes:
time: 2010 us; the launch traced here: 1990 us
  waiting for transfers between devices  786 us (39%)
  blocking collectives  352 us (18%)
  local copies, waits for them, and re-layouts  309 us (15%)
  matrix products  245 us (12%)
  other arithmetic  241 us (12%)
  starting transfers between devices  42.3 us (2%)
    reduce_scatter x4, waiting for transfers between devices, shards(): lax.psum_scatter(grad_matrices, ('nodes', 'shard'), scatter_dimension=1,...  474 us
    unnamed x19, waiting for transfers between devices  293 us
    all_gather x4, blocking collectives, shards(): lax.all_gather(norm_gains[layer_id].astype(jnp.bfloat16), ('nodes', 'shar...  203 us
    scatter-add x4, other arithmetic, layer_backward(): slot_grads.at[neighbours.reshape(-1)].add(grad_pre.reshape(-1, model_width))  113 us
    dot_general x22, matrix products, product_right(): lax.dot_general(left, right, (((1,), (1,)), ((), ())), preferred_element_...  105 us
    dot_general x26, matrix products, product_left(): lax.dot_general(left, right, (((0,), (0,)), ((), ())), preferred_element_...  82.5 us
    gather x4, local copies, waits for them, and re-layouts, layer_forward(): pre_edge = window[neighbours].astype(jnp.float32) + own_term[:, None, :]  78.8 us
    dot_general x26, matrix products, product(): return jnp.dot(left, right, preferred_element_type=jnp.float32)  57.3 us
  transfers between devices with their start and end apart: 30, of which 12 were waited for; matrix products, arithmetic and copies ran while one was open for 30% of the time, Pallas kernels for 0%

commit v1 on v0

v1 whole, which is shorter than its diff:
```python
import functools

import jax
import jax.numpy as jnp
from jax import lax
from jax.experimental import pallas as pl
from jax.experimental.pallas import tpu as pltpu
from jax.sharding import PartitionSpec as P

EPS_NORM = 1e-05
BETA_ONE = 0.5
BETA_TWO = 0.5
ADAM_EPS = 1e-08
LEARN_RATE = 0.04
DECAY_RATE = 0.1

AXES = ("nodes", "shard")
LANES = 128
FORWARD_ROWS = 128
BACKWARD_ROWS = 128
WEIGHT_ROWS = 256
UNROLL = 32
VMEM_BYTES = 56 << 20
LOW = jnp.bfloat16
WIDE = jnp.float32


def product(left, right):
    return jnp.dot(left, right, preferred_element_type=WIDE)


def product_left(left, right):
    return lax.dot_general(left, right, (((0,), (0,)), ((), ())), preferred_element_type=WIDE)


def product_right(left, right):
    return lax.dot_general(left, right, (((1,), (1,)), ((), ())), preferred_element_type=WIDE)


def normalize(tensor):
    centre = tensor - jnp.mean(tensor, axis=-1, keepdims=True)
    inv_scale = lax.rsqrt(jnp.mean(centre * centre, axis=-1, keepdims=True) + EPS_NORM)
    return (centre * inv_scale, inv_scale)


def normal_back(grad_unit, unit_rows, inv_scale):
    centred = grad_unit - jnp.mean(grad_unit, axis=-1, keepdims=True)
    return inv_scale * (
        centred - unit_rows * jnp.mean(grad_unit * unit_rows, axis=-1, keepdims=True)
    )


def sigmoid(tensor):
    return 0.5 * jnp.tanh(0.5 * tensor) + 0.5


def fold_rows(store, base, rows, tensor):
    parts = tensor.shape[1] // LANES
    for part in range(parts):
        store[pl.ds(base * parts + part, rows, stride=parts), :] = tensor[
            :, part * LANES : (part + 1) * LANES
        ]


def unfold_rows(store, base, rows, parts):
    return jnp.concatenate(
        [store[pl.ds(base * parts + part, rows, stride=parts), :] for part in range(parts)],
        axis=1,
    )


def forward_kernel(parts, has_next, *refs):
    if has_next:
        (slots, before, middle, after, low, wide, weights, gains, head) = refs[:9]
        (sent, update, update_low, kept, message, aggregate, mix, out) = refs[9:17]
        window, picked = refs[17:]
    else:
        (slots, before, middle, after, low, wide, weights, gains) = refs[:8]
        (update_low, kept, message, aggregate, mix, out) = refs[8:14]
        window, picked = refs[14:]
    step = pl.program_id(0)
    block_rows = before.shape[0]
    rows, width = low.shape
    fan = kept.shape[0]

    @pl.when(step == 0)
    def _():
        for index, block in enumerate((before, middle, after)):
            fold_rows(window, index * block_rows, block_rows, block[...].astype(WIDE))

    for k in range(fan):

        def pick(trip, carry):
            for lane in range(UNROLL):
                row = trip * UNROLL + lane
                slot = slots[k * block_rows + step * rows + row]
                picked[pl.ds(pl.multiple_of((k * rows + row) * parts, parts), parts), :] = window[
                    pl.ds(pl.multiple_of(slot * parts, parts), parts), :
                ]
            return carry

        lax.fori_loop(0, rows // UNROLL, pick, 0)
    target_low = low[...]
    own_term = product(target_low, weights[1])
    total = jnp.zeros((rows, width), WIDE)
    for k in range(fan):
        sender = unfold_rows(picked, k * rows, rows, parts)
        kept[k] = sender.astype(LOW)
        pre_edge = sender + own_term
        hidden = (pre_edge * sigmoid(pre_edge)).astype(LOW)
        spoken = product(hidden, weights[2])
        message[k] = spoken
        total = total + normalize(spoken)[0] * gains[0:1, :]
    total_low = total.astype(LOW)
    aggregate[...] = total_low
    node_mix = product(target_low, weights[3]) + product(total_low, weights[4])
    mix[...] = node_mix
    node_hidden = (node_mix * sigmoid(node_mix)).astype(LOW)
    node_out = product(node_hidden, weights[5])
    out[...] = node_out
    updated = wide[...].astype(WIDE) + normalize(node_out)[0] * gains[1:2, :]
    updated_low = updated.astype(LOW)
    update_low[...] = updated_low
    if has_next:
        update[...] = updated
        sent[...] = product(updated_low, head[0]).astype(LOW)


def whole(shape):
    zeros = (0,) * len(shape)
    return pl.BlockSpec(shape, lambda step: zeros)


def layer_spec(layer_id, count, width):
    return pl.BlockSpec((None, count, width, width), lambda step: (layer_id, 0, 0, 0))


def tiled(rows, width):
    return pl.BlockSpec((rows, width), lambda step: (step, 0))


def fanned(fan, rows, width):
    return pl.BlockSpec((fan, rows, width), lambda step: (0, step, 0))


def forward_layer(layer_id, has_next, slots, blocks, target_low, target, weights, gains):
    block_rows, width = target_low.shape
    fan = slots.shape[0] // block_rows
    parts = width // LANES
    rows = FORWARD_ROWS
    shape = functools.partial(jax.ShapeDtypeStruct, (block_rows, width))
    fan_shape = functools.partial(jax.ShapeDtypeStruct, (fan, block_rows, width))
    tile = tiled(rows, width)
    in_specs = [pl.BlockSpec(memory_space=pltpu.SMEM)]
    in_specs += [whole((block_rows, width))] * 3 + [tile, tile]
    in_specs += [layer_spec(layer_id, 6, width), whole(gains.shape)]
    out_specs = [tile, fanned(fan, rows, width), fanned(fan, rows, width), tile, tile, tile]
    out_shape = [shape(LOW), fan_shape(LOW), fan_shape(WIDE), shape(LOW), shape(WIDE), shape(WIDE)]
    operands = [slots, *blocks, target_low, target, weights, gains]
    if has_next:
        in_specs += [layer_spec(layer_id + 1, 1, width)]
        operands += [weights]
        out_specs = [tile, tile] + out_specs
        out_shape = [shape(LOW), shape(WIDE)] + out_shape
    return pl.pallas_call(
        functools.partial(forward_kernel, parts, has_next),
        grid=(block_rows // rows,),
        in_specs=in_specs,
        out_specs=out_specs,
        out_shape=out_shape,
        scratch_shapes=[
            pltpu.VMEM((3 * block_rows * parts, LANES), WIDE),
            pltpu.VMEM((fan * rows * parts, LANES), WIDE),
        ],
        compiler_params=pltpu.CompilerParams(vmem_limit_bytes=VMEM_BYTES),
        cost_estimate=pl.CostEstimate(
            flops=2 * (fan + 5) * block_rows * width * width,
            transcendentals=(fan + 1) * block_rows * width,
            bytes_accessed=24 * block_rows * width * 2,
        ),
        name="forward_layer",
    )(*operands)


def backward_kernel(parts, mode, *refs):
    refs = list(refs)
    slots = refs.pop(0)
    if mode != "first":
        returned = [refs.pop(0) for _ in range(3)]
        head = refs.pop(0)
    if mode != "second":
        grad_part = refs.pop(0)
    low, kept, message, mix, out, weights, gains = refs[:7]
    refs = refs[7:]
    if mode != "first":
        sent_grad = refs.pop(0)
        grad_full = refs.pop(0)
    (slot_grad, grad_gains, grad_message, edge_hidden, grad_mix, grad_out, grad_own, hidden) = refs[
        :8
    ]
    sum_even, sum_odd, spread = refs[8:]
    step = pl.program_id(0)
    rows, width = low.shape
    fan = kept.shape[0]
    block_rows = slot_grad.shape[1]

    @pl.when(step == 0)
    def _():
        sum_even[...] = jnp.zeros_like(sum_even)
        sum_odd[...] = jnp.zeros_like(sum_odd)
        grad_gains[...] = jnp.zeros_like(grad_gains)

    if mode == "first":
        grad_new = grad_part[...]
    else:
        sent_low = (
            returned[0][...].astype(WIDE)
            + returned[1][...].reshape(rows, width).astype(WIDE)
            + returned[2][...].astype(WIDE)
        ).astype(LOW)
        sent_grad[...] = sent_low
        grad_new = product_right(sent_low, head[0])
        if mode == "third":
            grad_new = grad_part[...] + grad_new
        grad_full[...] = grad_new
    target_low = low[...]
    out_unit, out_scale = normalize(out[...])
    gain_two = jnp.sum(grad_new * out_unit, axis=0, keepdims=True)
    out_low = normal_back(grad_new * gains[1:2, :], out_unit, out_scale).astype(LOW)
    grad_out[...] = out_low
    node_mix = mix[...]
    gate = sigmoid(node_mix)
    hidden[...] = (node_mix * gate).astype(LOW)
    mix_low = (
        product_right(out_low, weights[5]) * (gate * (1.0 + node_mix * (1.0 - gate)))
    ).astype(LOW)
    grad_mix[...] = mix_low
    grad_sum = product_right(mix_low, weights[4])
    own_term = product(target_low, weights[1])
    grad_unit = grad_sum * gains[0:1, :]
    unit_total = jnp.zeros((rows, width), WIDE)
    own_total = jnp.zeros((rows, width), WIDE)
    for k in range(fan):
        unit_rows, inv_scale = normalize(message[k])
        unit_total = unit_total + unit_rows
        message_low = normal_back(grad_unit, unit_rows, inv_scale).astype(LOW)
        grad_message[k] = message_low
        pre_edge = kept[k].astype(WIDE) + own_term
        edge_gate = sigmoid(pre_edge)
        edge_hidden[k] = (pre_edge * edge_gate).astype(LOW)
        grad_pre = product_right(message_low, weights[2]) * (
            edge_gate * (1.0 + pre_edge * (1.0 - edge_gate))
        )
        own_total = own_total + grad_pre
        fold_rows(spread, k * rows, rows, grad_pre)
    gain_one = jnp.sum(grad_sum * unit_total, axis=0, keepdims=True)
    grad_gains[...] += jnp.concatenate([gain_one, gain_two], axis=0)
    grad_own[...] = own_total.astype(LOW)

    for k in range(fan):

        def add(trip, carry):
            for lane in range(UNROLL // 2):
                places, values = [], []
                for store in (sum_even, sum_odd):
                    row = (trip * (UNROLL // 2) + lane) * 2 + len(places)
                    slot = slots[k * block_rows + step * rows + row]
                    place = pl.ds(pl.multiple_of(slot * parts, parts), parts)
                    value = spread[pl.ds(pl.multiple_of((k * rows + row) * parts, parts), parts), :]
                    places.append(place)
                    values.append(store[place, :] + value)
                sum_even[places[0], :] = values[0]
                sum_odd[places[1], :] = values[1]
            return carry

        lax.fori_loop(0, rows // UNROLL, add, 0)

    @pl.when(step == pl.num_programs(0) - 1)
    def _():
        for index in range(3):
            base = index * block_rows
            slot_grad[index] = (
                unfold_rows(sum_even, base, block_rows, parts)
                + unfold_rows(sum_odd, base, block_rows, parts)
            ).astype(LOW)


def backward_layer(layer_id, slots, above, grad_part, stored, weights, gains):
    target_low, kept, message, mix, out = stored
    block_rows, width = target_low.shape
    fan = kept.shape[0]
    parts = width // LANES
    rows = BACKWARD_ROWS
    tile = tiled(rows, width)
    fan_tile = fanned(fan, rows, width)
    in_specs = [pl.BlockSpec(memory_space=pltpu.SMEM)]
    operands = [slots]
    out_specs, out_shape = [], []
    shape = functools.partial(jax.ShapeDtypeStruct, (block_rows, width))
    fan_shape = functools.partial(jax.ShapeDtypeStruct, (fan, block_rows, width))
    mode = "first" if above is None else ("second" if grad_part is None else "third")
    if above is not None:
        from_before, slot_grad, from_after = above
        in_specs += [
            tile,
            pl.BlockSpec((1, rows, width), lambda step: (1, step, 0)),
            tile,
            layer_spec(layer_id + 1, 1, width),
        ]
        operands += [from_before, slot_grad, from_after, weights]
        out_specs += [tile, tile]
        out_shape += [shape(LOW), shape(WIDE)]
    if grad_part is not None:
        in_specs += [tile]
        operands += [grad_part]
    in_specs += [tile, fan_tile, fan_tile, tile, tile]
    in_specs += [layer_spec(layer_id, 6, width), whole(gains.shape)]
    operands += [target_low, kept, message, mix, out, weights, gains]
    out_specs += [
        whole((3, block_rows, width)),
        whole((2, width)),
        fan_tile,
        fan_tile,
        tile,
        tile,
        tile,
        tile,
    ]
    out_shape += [
        jax.ShapeDtypeStruct((3, block_rows, width), LOW),
        jax.ShapeDtypeStruct((2, width), WIDE),
        fan_shape(LOW),
        fan_shape(LOW),
        shape(LOW),
        shape(LOW),
        shape(LOW),
        shape(LOW),
    ]
    results = pl.pallas_call(
        functools.partial(backward_kernel, parts, mode),
        grid=(block_rows // rows,),
        in_specs=in_specs,
        out_specs=out_specs,
        out_shape=out_shape,
        scratch_shapes=[
            pltpu.VMEM((3 * block_rows * parts, LANES), WIDE),
            pltpu.VMEM((3 * block_rows * parts, LANES), WIDE),
            pltpu.VMEM((fan * rows * parts, LANES), WIDE),
        ],
        compiler_params=pltpu.CompilerParams(vmem_limit_bytes=VMEM_BYTES),
        cost_estimate=pl.CostEstimate(
            flops=2 * (fan + 4) * block_rows * width * width,
            transcendentals=(fan + 1) * block_rows * width,
            bytes_accessed=24 * block_rows * width * 2,
        ),
        name="backward_layer",
    )(*operands)
    if above is None:
        return (None, grad_part, *results)
    return tuple(results)


def weight_kernel(has_above, needs_target, *refs):
    refs = list(refs)
    if has_above:
        source, sent_grad = refs[:2]
        refs = refs[2:]
    low, aggregate, edge_hidden, grad_message, grad_mix, grad_out, grad_own, hidden = refs[:8]
    refs = refs[8:]
    if needs_target:
        grad_new, weights = refs[:2]
        refs = refs[2:]
        grad_matrices, grad_part = refs
    else:
        (grad_matrices,) = refs
    step = pl.program_id(0)
    fan = edge_hidden.shape[0]

    @pl.when(step == 0)
    def _():
        grad_matrices[...] = jnp.zeros_like(grad_matrices)

    target_low = low[...]
    mix_low = grad_mix[...]
    own_low = grad_own[...]
    if has_above:
        grad_matrices[0] += product_left(source[...], sent_grad[...])
    grad_matrices[1] += product_left(target_low, own_low)
    for k in range(fan):
        grad_matrices[2] += product_left(edge_hidden[k], grad_message[k])
    grad_matrices[3] += product_left(target_low, mix_low)
    grad_matrices[4] += product_left(aggregate[...], mix_low)
    grad_matrices[5] += product_left(hidden[...], grad_out[...])
    if needs_target:
        grad_part[...] = (
            grad_new[...]
            + product_right(own_low, weights[1])
            + product_right(mix_low, weights[3])
        )


def weight_layer(layer_id, above, low, aggregate, back, grad_new, weights):
    block_rows, width = low.shape
    rows = WEIGHT_ROWS
    fan = back[1].shape[0]
    tile = tiled(rows, width)
    fan_tile = fanned(fan, rows, width)
    in_specs, operands = [], []
    if above is not None:
        in_specs += [tile, tile]
        operands += list(above)
    in_specs += [tile, tile, fan_tile, fan_tile, tile, tile, tile, tile]
    operands += [low, aggregate, *back]
    out_specs = [whole((6, width, width))]
    out_shape = [jax.ShapeDtypeStruct((6, width, width), WIDE)]
    if grad_new is not None:
        in_specs += [tile, layer_spec(layer_id, 6, width)]
        operands += [grad_new, weights]
        out_specs += [tile]
        out_shape += [jax.ShapeDtypeStruct((block_rows, width), WIDE)]
    return pl.pallas_call(
        functools.partial(weight_kernel, above is not None, grad_new is not None),
        grid=(block_rows // rows,),
        in_specs=in_specs,
        out_specs=out_specs,
        out_shape=out_shape,
        compiler_params=pltpu.CompilerParams(vmem_limit_bytes=VMEM_BYTES),
        cost_estimate=pl.CostEstimate(
            flops=2 * (fan + 6) * block_rows * width * width,
            transcendentals=0,
            bytes_accessed=24 * block_rows * width,
        ),
        name="weight_layer",
    )(*operands)


def shift(cells, count, step):
    return lax.ppermute(cells, AXES, [(i, (i + step) % count) for i in range(count)])


def adamw_update(weight, moment_one, moment_two, gradient, step_value, decay_rate):
    new_one = BETA_ONE * moment_one + (1.0 - BETA_ONE) * gradient
    new_two = BETA_TWO * moment_two + (1.0 - BETA_TWO) * gradient * gradient
    correct_one = 1.0 - jnp.power(BETA_ONE, step_value)
    correct_two = 1.0 - jnp.power(BETA_TWO, step_value)
    direction = new_one / correct_one / (jnp.sqrt(new_two / correct_two) + ADAM_EPS)
    return (new_one, new_two, weight - LEARN_RATE * (direction + decay_rate * weight))


def shards(
    grid_inputs,
    mesh_static,
    targets,
    area_weight,
    valid_rows,
    encoder_lists,
    mesh_lists,
    decoder_lists,
    step_count,
    w_in,
    moment_in,
    square_in,
    w_layers,
    moment_layers,
    square_layers,
    norm_gains,
    moment_gains,
    square_gains,
    w_out,
    moment_out,
    square_out,
):
    row_count = grid_inputs.shape[0]
    layer_total = w_layers.shape[0]
    device_count = lax.axis_size(AXES)
    table_in = lax.all_gather(w_in.astype(LOW), AXES, axis=1, tiled=True)
    table_out = lax.all_gather(w_out.astype(LOW), AXES, axis=0, tiled=True)
    matrices = lax.all_gather(w_layers.astype(LOW), AXES, axis=2, tiled=True)
    gains = lax.all_gather(norm_gains.astype(LOW), AXES, axis=2, tiled=True).astype(WIDE)
    slot_lists = [encoder_lists.T.reshape(-1)]
    slot_lists += [mesh_lists.T.reshape(-1)] * (layer_total - 2)
    slot_lists += [decoder_lists.T.reshape(-1)]
    grid_latent = product(grid_inputs, table_in)
    grid_start = grid_latent.astype(LOW)
    sent = product(grid_start, matrices[0, 0]).astype(LOW)
    target, target_low = mesh_static, mesh_static
    stored_list = []
    for layer_id in range(layer_total):
        blocks = (shift(sent, device_count, 1), sent, shift(sent, device_count, -1))
        last_layer = layer_id == layer_total - 1
        if last_layer:
            source_low = target_low
            target, target_low = grid_latent, grid_start
        else:
            source_low = grid_start if layer_id == 0 else target_low
        results = forward_layer(
            layer_id,
            not last_layer,
            slot_lists[layer_id],
            blocks,
            target_low,
            target,
            matrices,
            gains[layer_id],
        )
        if last_layer:
            grid_low, kept, message, aggregate, mix, out = results
        else:
            sent, updated, updated_low, kept, message, aggregate, mix, out = results
        stored_list.append((source_low, (target_low, kept, message, mix, out), aggregate))
        if not last_layer:
            target, target_low = updated, updated_low
    prediction = product(grid_low, table_out)
    local_rows = jnp.arange(row_count, dtype=jnp.int32)
    weight_rows = area_weight * (local_rows < valid_rows[0]).astype(WIDE)
    error_rows = prediction - targets
    loss_scale = 1.0 / (row_count * device_count * prediction.shape[1])
    loss_local = jnp.sum(weight_rows[:, None] * error_rows * error_rows) * loss_scale
    loss_value = lax.psum(loss_local, AXES)
    grad_pred = (2.0 * loss_scale * weight_rows[:, None] * error_rows).astype(LOW)
    grad_table_out = product_left(grid_low, grad_pred)
    grad_part = product_right(grad_pred, table_out)
    grad_grid = None
    above, above_source = None, None
    layer_grads = [None] * layer_total
    gain_grads = [None] * layer_total
    for layer_id in reversed(range(layer_total)):
        source_low, stored, aggregate = stored_list[layer_id]
        sent_grad, grad_new, slot_grad, grad_gain, *back = backward_layer(
            layer_id, slot_lists[layer_id], above, grad_part, stored, matrices, gains[layer_id]
        )
        from_before = shift(slot_grad[2], device_count, 1)
        from_after = shift(slot_grad[0], device_count, -1)
        back = [back[1], back[0], *back[2:]]
        results = weight_layer(
            layer_id,
            None if above is None else (above_source, sent_grad),
            stored[0],
            aggregate,
            back,
            None if layer_id == 0 else grad_new,
            matrices,
        )
        layer_grads[layer_id] = results[0]
        gain_grads[layer_id] = grad_gain
        if layer_id == layer_total - 1:
            grad_grid, grad_part = results[1], None
        elif layer_id > 0:
            grad_part = results[1]
        above = (from_before, slot_grad, from_after)
        above_source = source_low
    sent_grad = (
        from_before.astype(WIDE) + slot_grad[1].astype(WIDE) + from_after.astype(WIDE)
    ).astype(LOW)
    grad_zero = product_left(above_source, sent_grad)
    grad_grid = grad_grid + product_right(sent_grad, matrices[0, 0])
    grad_table_in = product_left(grid_inputs, grad_grid.astype(LOW))
    grad_stack = jnp.concatenate(
        [grad_zero[None]]
        + [
            part
            for layer_id in range(layer_total)
            for part in (
                [layer_grads[layer_id][1:]]
                + ([layer_grads[layer_id][0:1]] if layer_id < layer_total - 1 else [])
            )
        ],
        axis=0,
    ).reshape(layer_total, 6, *grad_zero.shape)
    grad_layers = lax.psum_scatter(grad_stack, AXES, scatter_dimension=2, tiled=True)
    grad_gain_all = lax.psum_scatter(
        jnp.stack(gain_grads), AXES, scatter_dimension=2, tiled=True
    )
    grad_in = lax.psum_scatter(grad_table_in, AXES, scatter_dimension=1, tiled=True)
    grad_out = lax.psum_scatter(grad_table_out, AXES, scatter_dimension=0, tiled=True)
    step_value = step_count[0].astype(WIDE)
    one_in, two_in, new_in = adamw_update(
        w_in, moment_in, square_in, grad_in, step_value, DECAY_RATE
    )
    one_layers, two_layers, new_layers = adamw_update(
        w_layers, moment_layers, square_layers, grad_layers, step_value, DECAY_RATE
    )
    one_gains, two_gains, new_gains = adamw_update(
        norm_gains, moment_gains, square_gains, grad_gain_all, step_value, 0.0
    )
    one_out, two_out, new_out = adamw_update(
        w_out, moment_out, square_out, grad_out, step_value, DECAY_RATE
    )
    return (
        loss_value,
        one_in,
        two_in,
        new_in,
        one_layers,
        two_layers,
        new_layers,
        one_gains,
        two_gains,
        new_gains,
        one_out,
        two_out,
        new_out,
    )


def solution(mesh):
    rows = P(AXES, None)
    layers = P(None, None, AXES, None)
    gains = P(None, None, AXES)
    columns = P(None, AXES)
    in_specs = (rows, rows, rows, P(AXES), P(AXES), rows, rows, rows, P())
    in_specs += (columns,) * 3 + (layers,) * 3 + (gains,) * 3 + (rows,) * 3
    out_specs = (P(),) + (columns,) * 3 + (layers,) * 3 + (gains,) * 3 + (rows,) * 3
    return jax.shard_map(shards, mesh=mesh, in_specs=in_specs, out_specs=out_specs, check_vma=False)
```

time: 2010 us -> 1220 us (0.61)
  Pallas kernels: 0 us -> 297 us
  local copies, waits for them, and re-layouts: 309 us -> 44.4 us
  other arithmetic: 241 us -> 9.16 us
  matrix products: 245 us -> 17.2 us
  waiting for transfers between devices: 786 us -> 582 us
  blocking collectives: 352 us -> 197 us
    pallas_call x0 -> x12, Pallas kernels: none -> 297 us  [the longest x4 139 us: backward_layer(): pl.pallas_call(functools.partial(backward_kernel, parts, mode), grid=(blo...]
    reduce_scatter x5 -> x2, waiting for transfers between devices: 474 us -> 246 us  [the longest x1 246 us: shards(): lax.psum_scatter(grad_stack, AXES, scatter_dimension=2, tiled=True)]
    all_gather x6 -> x3, blocking collectives: 302 us -> 155 us  [the longest x1 55.1 us: shards(): table_out = lax.all_gather(w_out.astype(LOW), AXES, axis=0, tiled=True)]
    scatter-add x4 -> x0, other arithmetic: 113 us -> none  [layer_backward(): slot_grads.at[neighbours.reshape(-1)].add(grad_pre.reshape(-1, model_width))]
    dot_general x22 -> x1, matrix products: 105 us -> 1.85 us  [product_right(): lax.dot_general(left, right, (((1,), (1,)), ((), ())), preferred_element_...]
    gather x4 -> x0, local copies, waits for them, and re-layouts: 78.8 us -> none  [layer_forward(): pre_edge = window[neighbours].astype(jnp.float32) + own_term[:, None, :]]
    dot_general x26 -> x3, matrix products: 82.5 us -> 9.04 us  [product_left(): lax.dot_general(left, right, (((0,), (0,)), ((), ())), preferred_element_...]
    unnamed x19 -> x7, waiting for transfers between devices: 293 us -> 235 us
  transfers between devices with their start and end apart: 30 -> 21, of which waited for: 12 -> 10; matrix products, arithmetic and copies ran while one was open for 30% -> 4% of each run, Pallas kernels for 0% -> 7%
where the time goes in v1:
time: 1220 us; the launch traced here: 1210 us
  waiting for transfers between devices  582 us (48%)
  Pallas kernels  297 us (24%)
  blocking collectives  197 us (16%)
  starting transfers between devices  50 us (4%)
  local copies, waits for them, and re-layouts  44.4 us (4%)
  matrix products  17.2 us (1%)
  between operations  16.6 us (1%)
    reduce_scatter x1, waiting for transfers between devices, shards(): lax.psum_scatter(grad_stack, AXES, scatter_dimension=2, tiled=True)  246 us
    unnamed x7, waiting for transfers between devices  235 us
    pallas_call x4, Pallas kernels, backward_layer(): pl.pallas_call(functools.partial(backward_kernel, parts, mode), grid=(blo...  139 us
    pallas_call x4, Pallas kernels, forward_layer(): pl.pallas_call(functools.partial(forward_kernel, parts, has_next), grid=(...  104 us
    all_gather x1, blocking collectives, shards(): table_out = lax.all_gather(w_out.astype(LOW), AXES, axis=0, tiled=True)  55.1 us
    all_gather x1, waiting for transfers between devices, shards(): matrices = lax.all_gather(w_layers.astype(LOW), AXES, axis=2, tiled=True)  54.6 us
    all_gather x1, blocking collectives, shards(): lax.all_gather(norm_gains.astype(LOW), AXES, axis=2, tiled=True)  54.6 us
    pallas_call x4, Pallas kernels, weight_layer(): pl.pallas_call(functools.partial(weight_kernel, above is not None, grad_n...  53.7 us
  transfers between devices with their start and end apart: 21, of which 10 were waited for; matrix products, arithmetic and copies ran while one was open for 4% of the time, Pallas kernels for 7%

profile of v1, /device:TPU:0, one launch (start us, length us, event | category | flops | bytes accessed | tf_op | source)
XLA Modules:
  0.0 1213.2 jit_solution(9558701586643855403)
XLA Ops:
  10.1 45.5 %all_gather.12 = bf16[474,512]{0,1:T(8,128)(2,1)S(1)} all-gather(bf16[474,16]{0,1:T(8,128)(2,1)S(1)} %convert_element_type.47), channel_id=1, replica_groups=mesh['nodes'=16,'shard'=2] {'nodes','shard'}, dimensions={1}, use_global_device_ids=true | all-gather | bytes 500544 | tf_op jit(solution)/shard_map/all_gather | solution.py:476
  57.7 54.6 %all-gather.2.cloned.1.call-done.refs_6_.refs_8_.refs_7_.refs_9_.refs_4_.refs_10_.refs_11_ = bf16[4,6,512,512]{3,2,1,0:T(8,128)(2,1)} async-done(((bf16[4,6,16,512]{3,2,1,0:T(8,128)(2,1)}), bf16[4,6,512,512]{3,2,1,0:T(8,128)(2,1)}) %all-gather.2.cloned.1.call-update) | async-done | bytes 12582928 | tf_op jit(solution)/shard_map/all_gather | solution.py:478
  118.0 54.6 %all_gather.14 = bf16[4,2,512]{0,1,2:T(2,128)(2,1)S(1)} all-gather(bf16[4,2,16]{0,1,2:T(2,128)(2,1)S(1)} %copy.57), channel_id=1, replica_groups=mesh['nodes'=16,'shard'=2] {'nodes','shard'}, dimensions={2}, use_global_device_ids=true | all-gather | bytes 8448 | tf_op jit(solution)/shard_map/all_gather | solution.py:479
  173.4 26.3 %forward_layer.4 = (bf16[1024,512]{1,0:T(8,128)(2,1)}, f32[1024,512]{1,0:T(8,128)}, bf16[1024,512]{1,0:T(8,128)(2,1)}, bf16[4,1024,512]{2,1,0:T(8,128)(2,1)}, f3...) custom-call(s32[4096]{0:T(1024)} %bitcast.94, ...), custom_call_target="tpu_custom_call" | custom-call | flops 4831838208 | bytes 25165824 | tf_op jit(solution)/shard_map/forward_layer/pallas_call | solution.py:165
  200.9 11.5 collective-permute-done.3.refs_3_
  212.4 5.6 collective-permute-done.2.refs_1_
  218.9 26.2 %forward_layer.5 = (bf16[1024,512]{1,0:T(8,128)(2,1)}, f32[1024,512]{1,0:T(8,128)}, bf16[1024,512]{1,0:T(8,128)(2,1)}, bf16[4,1024,512]{2,1,0:T(8,128)(2,1)}, f3...) custom-call(s32[4096]{0:T(1024)} %bitcast.90, ...), custom_call_target="tpu_custom_call" | custom-call | flops 4831838208 | bytes 25165824 | tf_op jit(solution)/shard_map/forward_layer/pallas_call | solution.py:165
  245.5 5.4 collective-permute-start.4
  250.9 7.2 collective-permute-done.5.refs_3_
  258.1 5.5 collective-permute-done.4.refs_1_
  264.6 26.3 %forward_layer.6 = (bf16[1024,512]{1,0:T(8,128)(2,1)}, f32[1024,512]{1,0:T(8,128)}, bf16[1024,512]{1,0:T(8,128)(2,1)}, bf16[4,1024,512]{2,1,0:T(8,128)(2,1)}, f3...) custom-call(s32[4096]{0:T(1024)} %bitcast.91, ...), custom_call_target="tpu_custom_call" | custom-call | flops 4831838208 | bytes 25165824 | tf_op jit(solution)/shard_map/forward_layer/pallas_call | solution.py:165
  291.4 12.7 %collective-permute-start.6 = (bf16[1024,512]{1,0:T(8,128)(2,1)}, bf16[1024,512]{1,0:T(8,128)(2,1)S(1)}, u32[]{:S(2)}, u32[]{:S(2)}) collective-permute-start(bf16[1024,512]{1,0:T(8,128)(2,1)} %get-tuple-element.91.refs_2_), channel_id=1, source_target_pairs={{0,1},{1,2},{2,3},{3,4},{4,5},{5,6},{6,7},{7,8},{8,9},{9,10},{10,1... | collective-permute-start | bytes 3145736 | tf_op jit(solution)/shard_map/ppermute | solution.py:438
  305.4 55.1 %all_gather.15 = bf16[512,227]{1,0:T(8,128)(2,1)S(1)} all-gather(bf16[16,227]{1,0:T(8,128)(2,1)S(1)} %convert_element_type.53), channel_id=1, replica_groups=mesh['nodes'=16,'shard'=2] {'nodes','shard'}, dimensions={0}, use_global_device_ids=true | all-gather | bytes 239712 | tf_op jit(solution)/shard_map/all_gather | solution.py:477
  362.0 24.9 %forward_layer.7 = (bf16[1024,512]{1,0:T(8,128)(2,1)}, bf16[4,1024,512]{2,1,0:T(8,128)(2,1)}, f32[4,1024,512]{2,1,0:T(8,128)}, bf16[1024,512]{1,0:T(8,128)(2,1)}...) custom-call(s32[4096]{0:T(1024)} %bitcast.96, bf16[1024,512]{1,0:T(8,128)(2,1)} %copy-done.13, ...), custom_call_target="tpu_custom_call" | custom-call | flops 4831838208 | bytes 25165824 | tf_op jit(solution)/shard_map/forward_layer/pallas_call | solution.py:165
  391.1 33.8 %backward_layer.4 = (bf16[3,1024,512]{2,1,0:T(8,128)(2,1)}, f32[2,512]{1,0:T(2,128)}, bf16[4,1024,512]{2,1,0:T(8,128)(2,1)}, bf16[4,1024,512]{2,1,0:T(8,128)(2,1...) custom-call(s32[4096]{0:T(1024)} %bitcast.97, ...), custom_call_target="tpu_custom_call" | custom-call | flops 4294967296 | bytes 25165824 | tf_op jit(solution)/shard_map/backward_layer/pallas_call | solution.py:339
  427.2 11.8 collective-permute-done.9.refs_3_
  439.0 5.7 collective-permute-done.8.refs_1_
  445.6 35.2 %backward_layer.5 = (bf16[1024,512]{1,0:T(8,128)(2,1)}, f32[1024,512]{1,0:T(8,128)}, bf16[3,1024,512]{2,1,0:T(8,128)(2,1)}, f32[2,512]{1,0:T(2,128)}, bf16[4,102...) custom-call(s32[4096]{0:T(1024)} %bitcast.92, ...), custom_call_target="tpu_custom_call" | custom-call | flops 4294967296 | bytes 25165824 | tf_op jit(solution)/shard_map/backward_layer/pallas_call | solution.py:339
  482.8 8.1 collective-permute-start.10
  490.9 14.1 %weight_layer.5 = (f32[6,512,512]{2,1,0:T(8,128)}, f32[1024,512]{1,0:T(8,128)}) custom-call(bf16[1024,512]{1,0:T(8,128)(2,1)} %get-tuple-element.111.refs_0_, bf16[1024,512]{1,0:T(8,128)(2,1)} %get-tuple-element.112.refs_1_, bf16[1024,512]{1,0:T(8,128)(2,1)} %get-tuple-element.89.refs_4_.refs_5_.refs_2_.refs_0_, ...), custom_call_target="tpu_custom_call" | custom-call | flops 5368709120 | bytes 12582912 | tf_op jit(solution)/shard_map/weight_layer/pallas_call | solution.py:421
  506.4 35.2 %backward_layer.6 = (bf16[1024,512]{1,0:T(8,128)(2,1)}, f32[1024,512]{1,0:T(8,128)}, bf16[3,1024,512]{2,1,0:T(8,128)(2,1)}, f32[2,512]{1,0:T(2,128)}, bf16[4,102...) custom-call(s32[4096]{0:T(1024)} %bitcast.93, ...), custom_call_target="tpu_custom_call" | custom-call | flops 4294967296 | bytes 25165824 | tf_op jit(solution)/shard_map/backward_layer/pallas_call | solution.py:339
  544.9 9.5 collective-permute-start.12
  555.9 14.2 %weight_layer.6 = (f32[6,512,512]{2,1,0:T(8,128)}, f32[1024,512]{1,0:T(8,128)}) custom-call(bf16[1024,512]{1,0:T(8,128)(2,1)} %get-tuple-element.89.refs_4_.refs_5_.refs_2_.refs_0_, bf16[1024,512]{1,0:T(8,128)(2,1)} %get-tuple-element.127.refs_1_, bf16[1024,512]{1,0:T(8,128)(2,1)} %get-tuple-element.86.refs_4_.refs_6_.refs_2_.refs_0_, ...), custom_call_target="tpu_custom_call" | custom-call | flops 5368709120 | bytes 12582912 | tf_op jit(solution)/shard_map/weight_layer/pallas_call | solution.py:421
  571.5 35.2 %backward_layer.7 = (bf16[1024,512]{1,0:T(8,128)(2,1)}, f32[1024,512]{1,0:T(8,128)}, bf16[3,1024,512]{2,1,0:T(8,128)(2,1)}, f32[2,512]{1,0:T(2,128)}, bf16[4,102...) custom-call(s32[4096]{0:T(1024)} %bitcast.95, ...), custom_call_target="tpu_custom_call" | custom-call | flops 4294967296 | bytes 25165824 | tf_op jit(solution)/shard_map/backward_layer/pallas_call | solution.py:339
  609.4 8.3 collective-permute-start.14
  617.7 13.5 %weight_layer.4 = (f32[6,512,512]{2,1,0:T(8,128)}, f32[1024,512]{1,0:T(8,128)}) custom-call(bf16[1024,512]{1,0:T(8,128)(2,1)} %copy-done.2, bf16[1024,512]{1,0:T(8,128)(2,1)} %get-tuple-element.93.refs_1_, bf16[4,1024,512]{2,1,0:T(8,128)(2,1)} %get-tuple-element.98.refs_2_, bf16[4,1024,512]{2,1,0:T(8,128)(2,1)} %get-tuple-element.99.refs_3_, ...), custom_call_target="tpu_custom_call" | custom-call | flops 5368709120 | bytes 12582912 | tf_op jit(solution)/shard_map/weight_layer/pallas_call | solution.py:421
  633.1 11.8 weight_layer.7
  659.4 5.9 slice_dynamic-update-slice_fusion.3
  677.3 41.5 %psum.7 = f32[]{:T(128)} all-reduce(f32[]{:T(128)S(6)} %mul.136), channel_id=1, replica_groups=mesh['nodes'=16,'shard'=2] {'nodes','shard'}, use_global_device_ids=true, to_apply=%region_1.0 | all-reduce | flops 1 | bytes 8 | tf_op jit(solution)/shard_map/psum | solution.py:519
  720.2 103.2 %reduce-scatter.15.cloned.1.call-done = f32[16,8]{1,0:T(8,128)} async-done(((f32[512,8]{1,0:T(8,128)}), f32[16,8]{1,0:T(8,128)}) %reduce-scatter.15.cloned.1.call-update) | async-done | bytes 528
  824.9 131.3 %reduce-scatter.13.cloned.1.call-done = f32[16,474]{1,0:T(8,128)} async-done(((f32[512,474]{1,0:T(8,128)}), f32[16,474]{1,0:T(8,128)}) %reduce-scatter.13.cloned.1.call-update) | async-done | bytes 30352
  957.7 245.9 %reduce-scatter.9.cloned.1.call-done = f32[4,6,16,512]{3,2,1,0:T(8,128)} async-done(((f32[4,6,512,512]{3,2,1,0:T(8,128)}), f32[4,6,16,512]{3,2,1,0:T(8,128)}) %reduce-scatter.9.cloned.1.call-update) | async-done | bytes 786448 | tf_op jit(solution)/shard_map/reduce_scatter | solution.py:570
  (159 shorter events, 70.9 us)
Async XLA Ops:
  7.2 105.1 %all-gather.2.cloned.1.call-start = ((), (), s32[]{:S(2)}) async-start(), calls=%async_computation.4 | async-start | bytes 12976128 | tf_op jit(solution)/shard_map/all_gather | solution.py:478
  9.3 108.0 %copy-start.28 = (f32[4,2,16]{2,1,0:T(2,128)S(1)}, f32[4,2,16]{2,1,0:T(2,128)}, u32[]{:S(2)}) copy-start(f32[4,2,16]{2,1,0:T(2,128)} %param.36) | copy-start | bytes 1540
  9.3 108.1 %copy-start.29 = (s32[1024,4]{0,1:T(4,128)S(1)}, s32[1024,4]{0,1:T(4,128)}, u32[]{:S(2)}) copy-start(s32[1024,4]{0,1:T(4,128)} %param.26) | copy-start | bytes 49156
  9.3 709.5 %reduce-scatter.11.cloned.1.call-start = ((), (), s32[]{:S(2)}) async-start(), calls=%async_computation.6 | async-start | bytes 540672 | tf_op jit(solution)/shard_map/reduce_scatter | solution.py:575
  57.7 142.1 %copy-start.2 = (bf16[1024,512]{1,0:T(8,128)(2,1)}, bf16[1024,512]{1,0:T(8,128)(2,1)S(1)}, u32[]{:S(2)}) copy-start(bf16[1024,512]{1,0:T(8,128)(2,1)S(1)} %get-tuple-element.209.refs_4_.refs_2_.refs_0_) | copy-start | bytes 3145732
  114.1 59.3 %collective-permute-start.1 = (bf16[1024,512]{1,0:T(8,128)(2,1)S(1)}, bf16[1024,512]{1,0:T(8,128)(2,1)}, u32[]{:S(2)}, u32[]{:S(2)}) collective-permute-start(bf16[1024,512]{1,0:T(8,128)(2,1)S(1)} %convolution_convert_fusion.refs_2_), channel_id=1, source_target_pairs={{0,31},{1,0},{2,1},{3,2},{4,3},{5,4},{6,5},{7,6},{8,7},{9,8},{10,9... | collective-permute-start | bytes 3145736 | tf_op jit(solution)/shard_map/ppermute | solution.py:438
  117.3 56.1 %collective-permute-start = (bf16[1024,512]{1,0:T(8,128)(2,1)S(1)}, bf16[1024,512]{1,0:T(8,128)(2,1)}, u32[]{:S(2)}, u32[]{:S(2)}) collective-permute-start(bf16[1024,512]{1,0:T(8,128)(2,1)S(1)} %convolution_convert_fusion.refs_2_), channel_id=1, source_target_pairs={{0,1},{1,2},{2,3},{3,4},{4,5},{5,6},{6,7},{7,8},{8,9},{9,10},{10,1... | collective-permute-start | bytes 3145736 | tf_op jit(solution)/shard_map/ppermute | solution.py:438
  199.7 12.7 %collective-permute-start.3 = (bf16[1024,512]{1,0:T(8,128)(2,1)}, bf16[1024,512]{1,0:T(8,128)(2,1)S(1)}, u32[]{:S(2)}, u32[]{:S(2)}) collective-permute-start(bf16[1024,512]{1,0:T(8,128)(2,1)} %get-tuple-element.85.refs_2_), channel_id=1, source_target_pairs={{0,31},{1,0},{2,1},{3,2},{4,3},{5,4},{6,5},{7,6},{8,7},{9,8},{10,9... | collective-permute-start | bytes 3145736 | tf_op jit(solution)/shard_map/ppermute | solution.py:438
  199.8 18.2 %collective-permute-start.2 = (bf16[1024,512]{1,0:T(8,128)(2,1)}, bf16[1024,512]{1,0:T(8,128)(2,1)S(1)}, u32[]{:S(2)}, u32[]{:S(2)}) collective-permute-start(bf16[1024,512]{1,0:T(8,128)(2,1)} %get-tuple-element.85.refs_2_), channel_id=1, source_target_pairs={{0,1},{1,2},{2,3},{3,4},{4,5},{5,6},{6,7},{7,8},{8,9},{9,10},{10,1... | collective-permute-start | bytes 3145736 | tf_op jit(solution)/shard_map/ppermute | solution.py:438
  245.2 12.9 %collective-permute-start.5 = (bf16[1024,512]{1,0:T(8,128)(2,1)}, bf16[1024,512]{1,0:T(8,128)(2,1)S(1)}, u32[]{:S(2)}, u32[]{:S(2)}) collective-permute-start(bf16[1024,512]{1,0:T(8,128)(2,1)} %get-tuple-element.88.refs_2_), channel_id=1, source_target_pairs={{0,31},{1,0},{2,1},{3,2},{4,3},{5,4},{6,5},{7,6},{8,7},{9,8},{10,9... | collective-permute-start | bytes 3145736 | tf_op jit(solution)/shard_map/ppermute | solution.py:438
  245.5 18.1 %collective-permute-start.4 = (bf16[1024,512]{1,0:T(8,128)(2,1)}, bf16[1024,512]{1,0:T(8,128)(2,1)S(1)}, u32[]{:S(2)}, u32[]{:S(2)}) collective-permute-start(bf16[1024,512]{1,0:T(8,128)(2,1)} %get-tuple-element.88.refs_2_), channel_id=1, source_target_pairs={{0,1},{1,2},{2,3},{3,4},{4,5},{5,6},{6,7},{7,8},{8,9},{9,10},{10,1... | collective-permute-start | bytes 3145736 | tf_op jit(solution)/shard_map/ppermute | solution.py:438
  290.9 69.6 %collective-permute-start.7 = (bf16[1024,512]{1,0:T(8,128)(2,1)}, bf16[1024,512]{1,0:T(8,128)(2,1)S(1)}, u32[]{:S(2)}, u32[]{:S(2)}) collective-permute-start(bf16[1024,512]{1,0:T(8,128)(2,1)} %get-tuple-element.91.refs_2_), channel_id=1, source_target_pairs={{0,31},{1,0},{2,1},{3,2},{4,3},{5,4},{6,5},{7,6},{8,7},{9,8},{10,9... | collective-permute-start | bytes 3145736 | tf_op jit(solution)/shard_map/ppermute | solution.py:438
  291.4 69.2 %collective-permute-start.6 = (bf16[1024,512]{1,0:T(8,128)(2,1)}, bf16[1024,512]{1,0:T(8,128)(2,1)S(1)}, u32[]{:S(2)}, u32[]{:S(2)}) collective-permute-start(bf16[1024,512]{1,0:T(8,128)(2,1)} %get-tuple-element.91.refs_2_), channel_id=1, source_target_pairs={{0,1},{1,2},{2,3},{3,4},{4,5},{5,6},{6,7},{7,8},{8,9},{9,10},{10,1... | collective-permute-start | bytes 3145736 | tf_op jit(solution)/shard_map/ppermute | solution.py:438
  426.6 12.4 %collective-permute-start.9 = (bf16[1024,512]{1,0:T(8,128)(2,1)S(1)}, bf16[1024,512]{1,0:T(8,128)(2,1)S(1)}, u32[]{:S(2)}, u32[]{:S(2)}) collective-permute-start(bf16[1024,512]{1,0:T(8,128)(2,1)S(1)} %get-tuple-element.203), channel_id=1, source_target_pairs={{0,31},{1,0},{2,1},{3,2},{4,3},{5,4},{6,5},{7,6},{8,7},{9,8},{10,9... | collective-permute-start | bytes 3145736 | tf_op jit(solution)/shard_map/ppermute | solution.py:438
  426.7 18.0 %collective-permute-start.8 = (bf16[1024,512]{1,0:T(8,128)(2,1)S(1)}, bf16[1024,512]{1,0:T(8,128)(2,1)S(1)}, u32[]{:S(2)}, u32[]{:S(2)}) collective-permute-start(bf16[1024,512]{1,0:T(8,128)(2,1)S(1)} %get-tuple-element.204), channel_id=1, source_target_pairs={{0,1},{1,2},{2,3},{3,4},{4,5},{5,6},{6,7},{7,8},{8,9},{9,10},{10,1... | collective-permute-start | bytes 3145736 | tf_op jit(solution)/shard_map/ppermute | solution.py:438
  482.5 22.5 %collective-permute-start.11 = (bf16[1024,512]{1,0:T(8,128)(2,1)S(1)}, bf16[1024,512]{1,0:T(8,128)(2,1)S(1)}, u32[]{:S(2)}, u32[]{:S(2)}) collective-permute-start(bf16[1024,512]{1,0:T(8,128)(2,1)S(1)} %get-tuple-element.201), channel_id=1, source_target_pairs={{0,31},{1,0},{2,1},{3,2},{4,3},{5,4},{6,5},{7,6},{8,7},{9,8},{10,9... | collective-permute-start | bytes 3145736 | tf_op jit(solution)/shard_map/ppermute | solution.py:438
  482.8 22.3 %collective-permute-start.10 = (bf16[1024,512]{1,0:T(8,128)(2,1)S(1)}, bf16[1024,512]{1,0:T(8,128)(2,1)S(1)}, u32[]{:S(2)}, u32[]{:S(2)}) collective-permute-start(bf16[1024,512]{1,0:T(8,128)(2,1)S(1)} %get-tuple-element.202), channel_id=1, source_target_pairs={{0,1},{1,2},{2,3},{3,4},{4,5},{5,6},{6,7},{7,8},{8,9},{9,10},{10,1... | collective-permute-start | bytes 3145736 | tf_op jit(solution)/shard_map/ppermute | solution.py:438
  544.9 25.2 %collective-permute-start.13 = (bf16[1024,512]{1,0:T(8,128)(2,1)}, bf16[1024,512]{1,0:T(8,128)(2,1)S(1)}, u32[]{:S(2)}, u32[]{:S(2)}) collective-permute-start(bf16[1024,512]{1,0:T(8,128)(2,1)} %get-tuple-element.199), channel_id=1, source_target_pairs={{0,31},{1,0},{2,1},{3,2},{4,3},{5,4},{6,5},{7,6},{8,7},{9,8},{10,9... | collective-permute-start | bytes 3145736 | tf_op jit(solution)/shard_map/ppermute | solution.py:438
  544.9 25.2 %collective-permute-start.12 = (bf16[1024,512]{1,0:T(8,128)(2,1)}, bf16[1024,512]{1,0:T(8,128)(2,1)S(1)}, u32[]{:S(2)}, u32[]{:S(2)}) collective-permute-start(bf16[1024,512]{1,0:T(8,128)(2,1)} %get-tuple-element.200), channel_id=1, source_target_pairs={{0,1},{1,2},{2,3},{3,4},{4,5},{5,6},{6,7},{7,8},{8,9},{9,10},{10,1... | collective-permute-start | bytes 3145736 | tf_op jit(solution)/shard_map/ppermute | solution.py:438
  555.7 267.8 %reduce-scatter.15.cloned.1.call-start = ((), (), s32[]{:S(2)}) async-start(), calls=%async_computation.8 | async-start | bytes 270336
  609.4 35.6 %collective-permute-start.14 = (bf16[1024,512]{1,0:T(8,128)(2,1)}, bf16[1024,512]{1,0:T(8,128)(2,1)}, u32[]{:S(2)}, u32[]{:S(2)}) collective-permute-start(bf16[1024,512]{1,0:T(8,128)(2,1)} %get-tuple-element.197), channel_id=1, source_target_pairs={{0,1},{1,2},{2,3},{3,4},{4,5},{5,6},{6,7},{7,8},{8,9},{9,10},{10,1... | collective-permute-start | bytes 3145736 | tf_op jit(solution)/shard_map/ppermute | solution.py:438
  617.6 27.3 %collective-permute-start.15 = (bf16[1024,512]{1,0:T(8,128)(2,1)S(1)}, bf16[1024,512]{1,0:T(8,128)(2,1)}, u32[]{:S(2)}, u32[]{:S(2)}) collective-permute-start(bf16[1024,512]{1,0:T(8,128)(2,1)S(1)} %get-tuple-element.198), channel_id=1, source_target_pairs={{0,31},{1,0},{2,1},{3,2},{4,3},{5,4},{6,5},{7,6},{8,7},{9,8},{10,9... | collective-permute-start | bytes 3145736 | tf_op jit(solution)/shard_map/ppermute | solution.py:438
  632.8 323.4 %reduce-scatter.13.cloned.1.call-start = ((), (), s32[]{:S(2)}) async-start(), calls=%async_computation.7 | async-start | bytes 1081344
  659.3 544.2 %reduce-scatter.9.cloned.1.call-start = ((), (), s32[]{:S(2)}) async-start(), calls=%async_computation.5 | async-start | bytes 25952256 | tf_op jit(solution)/shard_map/reduce_scatter | solution.py:570
  675.7 148.6 %copy-start.33 = (f32[4,2,16]{2,1,0:T(2,128)S(1)}, f32[4,2,16]{2,1,0:T(2,128)}, u32[]{:S(2)}) copy-start(f32[4,2,16]{2,1,0:T(2,128)} %param.38) | copy-start | bytes 1540
  675.7 148.6 %copy-start.34 = (f32[4,2,16]{2,1,0:T(2,128)S(1)}, f32[4,2,16]{2,1,0:T(2,128)}, u32[]{:S(2)}) copy-start(f32[4,2,16]{2,1,0:T(2,128)} %param.37) | copy-start | bytes 1540
  675.7 280.6 %copy-start.22 = (f32[474,16]{0,1:T(8,128)S(1)}, f32[474,16]{0,1:T(8,128)}, u32[]{:S(2)}) copy-start(f32[474,16]{0,1:T(8,128)} %param.30) | copy-start | bytes 91012
  675.7 280.6 %copy-start.24 = (f32[474,16]{0,1:T(8,128)S(1)}, f32[474,16]{0,1:T(8,128)}, u32[]{:S(2)}) copy-start(f32[474,16]{0,1:T(8,128)} %param.32) | copy-start | bytes 91012
  675.7 280.5 %copy-start.25 = (f32[474,16]{0,1:T(8,128)S(1)}, f32[474,16]{0,1:T(8,128)}, u32[]{:S(2)}) copy-start(f32[474,16]{0,1:T(8,128)} %param.31) | copy-start | bytes 91012
  675.7 527.8 %copy-start.5 = (f32[4,6,16,512]{3,2,1,0:T(8,128)S(1)}, f32[4,6,16,512]{3,2,1,0:T(8,128)}, u32[]{:S(2)}) copy-start(f32[4,6,16,512]{3,2,1,0:T(8,128)} %param.33) | copy-start | bytes 2359300
  675.7 527.8 %copy-start.20 = (f32[4,6,16,512]{3,2,1,0:T(8,128)S(1)}, f32[4,6,16,512]{3,2,1,0:T(8,128)}, u32[]{:S(2)}) copy-start(f32[4,6,16,512]{3,2,1,0:T(8,128)} %param.35) | copy-start | bytes 2359300
  675.7 527.8 %copy-start.21 = (f32[4,6,16,512]{3,2,1,0:T(8,128)S(1)}, f32[4,6,16,512]{3,2,1,0:T(8,128)}, u32[]{:S(2)}) copy-start(f32[4,6,16,512]{3,2,1,0:T(8,128)} %param.34) | copy-start | bytes 2359300
  (32 other events, 557.5 us)
Sparse Core Ops, SparseCore 0:
  11.5 100.7 all-gather.1
  555.8 135.2 reduce-scatter.10
  694.0 129.3 reduce-scatter.14
  825.5 130.6 reduce-scatter.12
  963.7 239.8 reduce-scatter.8

commit v2 on v1

--- a/solution.py
+++ b/solution.py
@@ -23,6 +23,7 @@
 VMEM_BYTES = 56 << 20
 LOW = jnp.bfloat16
 WIDE = jnp.float32
+SEND = jnp.float32
 
 
 def product(left, right):
@@ -131,8 +132,8 @@
     return pl.BlockSpec(shape, lambda step: zeros)
 
 
-def layer_spec(layer_id, count, width):
-    return pl.BlockSpec((None, count, width, width), lambda step: (layer_id, 0, 0, 0))
+def matrix_spec(first, count, width):
+    return pl.BlockSpec((count, width, width), lambda step: (first // count, 0, 0))
 
 
 def tiled(rows, width):
@@ -143,23 +144,24 @@
     return pl.BlockSpec((fan, rows, width), lambda step: (0, step, 0))
 
 
-def forward_layer(layer_id, has_next, slots, blocks, target_low, target, weights, gains):
+def forward_layer(slots, blocks, target_low, target, weights, next_weights, gains):
     block_rows, width = target_low.shape
     fan = slots.shape[0] // block_rows
     parts = width // LANES
     rows = FORWARD_ROWS
+    has_next = next_weights is not None
     shape = functools.partial(jax.ShapeDtypeStruct, (block_rows, width))
     fan_shape = functools.partial(jax.ShapeDtypeStruct, (fan, block_rows, width))
     tile = tiled(rows, width)
     in_specs = [pl.BlockSpec(memory_space=pltpu.SMEM)]
     in_specs += [whole((block_rows, width))] * 3 + [tile, tile]
-    in_specs += [layer_spec(layer_id, 6, width), whole(gains.shape)]
+    in_specs += [matrix_spec(weights[1], 6, width), whole(gains.shape)]
     out_specs = [tile, fanned(fan, rows, width), fanned(fan, rows, width), tile, tile, tile]
     out_shape = [shape(LOW), fan_shape(LOW), fan_shape(WIDE), shape(LOW), shape(WIDE), shape(WIDE)]
-    operands = [slots, *blocks, target_low, target, weights, gains]
+    operands = [slots, *blocks, target_low, target, weights[0], gains]
     if has_next:
-        in_specs += [layer_spec(layer_id + 1, 1, width)]
-        operands += [weights]
+        in_specs += [matrix_spec(next_weights[1], 1, width)]
+        operands += [next_weights[0]]
         out_specs = [tile, tile] + out_specs
         out_shape = [shape(LOW), shape(WIDE)] + out_shape
     return pl.pallas_call(
@@ -285,7 +287,7 @@
             ).astype(LOW)
 
 
-def backward_layer(layer_id, slots, above, grad_part, stored, weights, gains):
+def backward_layer(slots, above, grad_part, stored, weights, gains):
     target_low, kept, message, mix, out = stored
     block_rows, width = target_low.shape
     fan = kept.shape[0]
@@ -300,22 +302,22 @@
     fan_shape = functools.partial(jax.ShapeDtypeStruct, (fan, block_rows, width))
     mode = "first" if above is None else ("second" if grad_part is None else "third")
     if above is not None:
-        from_before, slot_grad, from_after = above
+        from_before, slot_grad, from_after, head = above
         in_specs += [
             tile,
             pl.BlockSpec((1, rows, width), lambda step: (1, step, 0)),
             tile,
-            layer_spec(layer_id + 1, 1, width),
+            matrix_spec(head[1], 1, width),
         ]
-        operands += [from_before, slot_grad, from_after, weights]
+        operands += [from_before, slot_grad, from_after, head[0]]
         out_specs += [tile, tile]
         out_shape += [shape(LOW), shape(WIDE)]
     if grad_part is not None:
         in_specs += [tile]
         operands += [grad_part]
     in_specs += [tile, fan_tile, fan_tile, tile, tile]
-    in_specs += [layer_spec(layer_id, 6, width), whole(gains.shape)]
-    operands += [target_low, kept, message, mix, out, weights, gains]
+    in_specs += [matrix_spec(weights[1], 6, width), whole(gains.shape)]
+    operands += [target_low, kept, message, mix, out, weights[0], gains]
     out_specs += [
         whole((3, block_rows, width)),
         whole((2, width)),
@@ -360,70 +362,117 @@
     return tuple(results)
 
 
-def weight_kernel(has_above, needs_target, *refs):
+def deal(self_id, sums, outs):
+    keep, send = outs
+    share = keep.shape[1] // sums.shape[0]
+
+    def move(node, carry):
+        for core, out in enumerate((keep, send)):
+            place = pl.multiple_of(((2 * node + core) ^ self_id[0]) * share, share)
+            for index in range(sums.shape[0]):
+                out[node, index * share : (index + 1) * share, :] = sums[
+                    index, pl.ds(place, share), :
+                ].astype(out.dtype)
+        return carry
+
+    lax.fori_loop(0, keep.shape[0], move, 0)
+
+
+def weight_kernel(has_above, needs_target, direct, *refs):
     refs = list(refs)
+    if direct:
+        self_id = refs.pop(0)
     if has_above:
         source, sent_grad = refs[:2]
         refs = refs[2:]
+    else:
+        extra = refs.pop(0)
     low, aggregate, edge_hidden, grad_message, grad_mix, grad_out, grad_own, hidden = refs[:8]
     refs = refs[8:]
     if needs_target:
         grad_new, weights = refs[:2]
-        refs = refs[2:]
-        grad_matrices, grad_part = refs
-    else:
-        (grad_matrices,) = refs
+        grad_part = refs[2]
+        refs = refs[3:]
+    outs, sums = (refs[:2], refs[2]) if direct else (None, refs[0])
     step = pl.program_id(0)
     fan = edge_hidden.shape[0]
 
     @pl.when(step == 0)
     def _():
-        grad_matrices[...] = jnp.zeros_like(grad_matrices)
+        sums[...] = jnp.zeros_like(sums)
+        if not has_above:
+            sums[0] = extra[...]
 
     target_low = low[...]
     mix_low = grad_mix[...]
     own_low = grad_own[...]
     if has_above:
-        grad_matrices[0] += product_left(source[...], sent_grad[...])
-    grad_matrices[1] += product_left(target_low, own_low)
+        sums[0] += product_left(source[...], sent_grad[...])
+    sums[1] += product_left(target_low, own_low)
     for k in range(fan):
-        grad_matrices[2] += product_left(edge_hidden[k], grad_message[k])
-    grad_matrices[3] += product_left(target_low, mix_low)
-    grad_matrices[4] += product_left(aggregate[...], mix_low)
-    grad_matrices[5] += product_left(hidden[...], grad_out[...])
+        sums[2] += product_left(edge_hidden[k], grad_message[k])
+    sums[3] += product_left(target_low, mix_low)
+    sums[4] += product_left(aggregate[...], mix_low)
+    sums[5] += product_left(hidden[...], grad_out[...])
     if needs_target:
         grad_part[...] = (
-            grad_new[...]
-            + product_right(own_low, weights[1])
-            + product_right(mix_low, weights[3])
+            grad_new[...] + product_right(own_low, weights[1]) + product_right(mix_low, weights[3])
         )
-
-
-def weight_layer(layer_id, above, low, aggregate, back, grad_new, weights):
+    if direct:
+
+        @pl.when(step == pl.num_programs(0) - 1)
+        def _():
+            deal(self_id, sums, outs)
+
+
+def share_outputs(count, width, device_count):
+    shape = (device_count // 2, count * (width // device_count), width)
+    return (
+        [whole(shape)] * 2,
+        [jax.ShapeDtypeStruct(shape, WIDE), jax.ShapeDtypeStruct(shape, SEND)],
+    )
+
+
+def weight_layer(self_id, device_count, above, extra, low, aggregate, back, grad_new, weights):
     block_rows, width = low.shape
     rows = WEIGHT_ROWS
-    fan = back[1].shape[0]
+    fan = back[0].shape[0]
     tile = tiled(rows, width)
     fan_tile = fanned(fan, rows, width)
     in_specs, operands = [], []
+    direct = self_id is not None
+    if direct:
+        in_specs += [pl.BlockSpec(memory_space=pltpu.SMEM)]
+        operands += [self_id]
     if above is not None:
         in_specs += [tile, tile]
         operands += list(above)
+    else:
+        in_specs += [whole((width, width))]
+        operands += [extra]
     in_specs += [tile, tile, fan_tile, fan_tile, tile, tile, tile, tile]
     operands += [low, aggregate, *back]
-    out_specs = [whole((6, width, width))]
-    out_shape = [jax.ShapeDtypeStruct((6, width, width), WIDE)]
+    out_specs, out_shape, scratch = [], [], []
     if grad_new is not None:
-        in_specs += [tile, layer_spec(layer_id, 6, width)]
-        operands += [grad_new, weights]
+        in_specs += [tile, matrix_spec(weights[1], 6, width)]
+        operands += [grad_new, weights[0]]
         out_specs += [tile]
         out_shape += [jax.ShapeDtypeStruct((block_rows, width), WIDE)]
-    return pl.pallas_call(
-        functools.partial(weight_kernel, above is not None, grad_new is not None),
+    if direct:
+        specs, shapes = share_outputs(6, width, device_count)
+        out_specs += specs
+        out_shape += shapes
+        scratch = [pltpu.VMEM((6, width, width), WIDE)]
+    else:
+        out_specs += [whole((6, width, width))]
+        out_shape += [jax.ShapeDtypeStruct((6, width, width), WIDE)]
+    results = pl.pallas_call(
+        functools.partial(weight_kernel, above is not None, grad_new is not None, direct),
         grid=(block_rows // rows,),
         in_specs=in_specs,
         out_specs=out_specs,
         out_shape=out_shape,
+        scratch_shapes=scratch,
         compiler_params=pltpu.CompilerParams(vmem_limit_bytes=VMEM_BYTES),
         cost_estimate=pl.CostEstimate(
             flops=2 * (fan + 6) * block_rows * width * width,
@@ -432,6 +481,193 @@
         ),
         name="weight_layer",
     )(*operands)
+    if grad_new is None:
+        return (None, results)
+    return (results[0], results[1:])
+
+
+def embed_kernel(pieces_count, *refs):
+    self_id = refs[0]
+    pieces = refs[1 : 1 + pieces_count]
+    before, middle, after = refs[1 + pieces_count : 4 + pieces_count]
+    weights, latent, latent_low, sent_before, sent_middle, sent_after, table = refs[
+        4 + pieces_count :
+    ]
+    count, width = weights.shape[0], weights.shape[1]
+    high = pieces[0].shape[0]
+    share = width // (high * pieces_count)
+
+    @pl.when(pl.program_id(0) == 0)
+    def _():
+        for index, piece in enumerate(pieces):
+            core, low_digit = index // (pieces_count // 2), index % (pieces_count // 2)
+
+            def move(digit, carry, piece=piece, core=core, low_digit=low_digit):
+                relative = digit * pieces_count + low_digit * 2 + core
+                place = pl.multiple_of((relative ^ self_id[0]) * share, share)
+                for j in range(count):
+                    weights[j, pl.ds(place, share), :] = piece[digit, j * share : (j + 1) * share, :]
+                table[pl.ds(place, share), :] = piece[digit, count * share : (count + 1) * share, :]
+                return carry
+
+            lax.fori_loop(0, high, move, 0)
+
+    for block, sent in ((before, sent_before), (middle, sent_middle), (after, sent_after)):
+        wide = product_right(block[...], table[...])
+        low = wide.astype(LOW)
+        sent[...] = product(low, weights[0]).astype(LOW)
+        if block is middle:
+            latent[...] = wide
+            latent_low[...] = low
+
+
+def embed(self_id, pieces, blocks):
+    block_rows, width = blocks[1].shape
+    rows = WEIGHT_ROWS
+    tile = tiled(rows, width)
+    shape = functools.partial(jax.ShapeDtypeStruct, (block_rows, width))
+    return pl.pallas_call(
+        functools.partial(embed_kernel, len(pieces)),
+        grid=(block_rows // rows,),
+        in_specs=[pl.BlockSpec(memory_space=pltpu.SMEM)]
+        + [whole(piece.shape) for piece in pieces]
+        + [tile] * 3,
+        out_specs=[whole((6, width, width))] + [tile] * 5,
+        out_shape=[jax.ShapeDtypeStruct((6, width, width), LOW), shape(WIDE)] + [shape(LOW)] * 4,
+        scratch_shapes=[pltpu.VMEM((width, width), LOW)],
+        compiler_params=pltpu.CompilerParams(vmem_limit_bytes=VMEM_BYTES),
+        cost_estimate=pl.CostEstimate(
+            flops=12 * block_rows * width * width,
+            transcendentals=0,
+            bytes_accessed=24 * block_rows * width,
+        ),
+        name="embed",
+    )(self_id, *pieces, *blocks)
+
+
+def tail_kernel(self_id, before, middle, after, latent_low, inputs, grad_grid, head, misc, *refs):
+    keep, send, sums = refs
+    step = pl.program_id(0)
+    rows, width = inputs.shape
+    share = misc.shape[1]
+
+    @pl.when(step == 0)
+    def _():
+        sums[...] = jnp.zeros_like(sums)
+
+    sent_low = (
+        before[...].astype(WIDE)
+        + middle[...].reshape(rows, width).astype(WIDE)
+        + after[...].astype(WIDE)
+    ).astype(LOW)
+    grad_low = (grad_grid[...] + product_right(sent_low, head[0])).astype(LOW)
+    sums[0] += product_left(latent_low[...], sent_low)
+    sums[1] += product_left(grad_low, inputs[...])
+
+    @pl.when(step == pl.num_programs(0) - 1)
+    def _():
+        size = sums.shape[0] * (width // misc.shape[0])
+        main = [out.at[:, 0:size, :] for out in (keep, send)]
+        deal(self_id, sums, main)
+
+        def move(node, carry):
+            for core, out in enumerate((keep, send)):
+                out[node, size : size + share, :] = misc[(2 * node + core) ^ self_id[0]].astype(
+                    out.dtype
+                )
+            return carry
+
+        lax.fori_loop(0, keep.shape[0], move, 0)
+
+
+def tail_layer(self_id, from_before, slot_grad, from_after, latent_low, inputs, grad_grid, head, misc):
+    block_rows, width = inputs.shape
+    device_count = misc.shape[0]
+    rows = WEIGHT_ROWS
+    tile = tiled(rows, width)
+    shape = (device_count // 2, 2 * (width // device_count) + misc.shape[1], width)
+    return pl.pallas_call(
+        tail_kernel,
+        grid=(block_rows // rows,),
+        in_specs=[
+            pl.BlockSpec(memory_space=pltpu.SMEM),
+            tile,
+            pl.BlockSpec((1, rows, width), lambda step: (1, step, 0)),
+            tile,
+            tile,
+            tile,
+            tile,
+            matrix_spec(head[1], 1, width),
+            whole(misc.shape),
+        ],
+        out_specs=[whole(shape)] * 2,
+        out_shape=[jax.ShapeDtypeStruct(shape, WIDE), jax.ShapeDtypeStruct(shape, SEND)],
+        scratch_shapes=[pltpu.VMEM((2, width, width), WIDE)],
+        compiler_params=pltpu.CompilerParams(vmem_limit_bytes=VMEM_BYTES),
+        cost_estimate=pl.CostEstimate(
+            flops=6 * block_rows * width * width,
+            transcendentals=0,
+            bytes_accessed=24 * block_rows * width,
+        ),
+        name="tail_layer",
+    )(self_id, from_before, slot_grad, from_after, latent_low, inputs, grad_grid, head[0], misc)
+
+
+def combine_kernel(count, *refs):
+    arrived, outs = refs[:count], refs[count:]
+    for digit, out in enumerate(outs):
+        total = arrived[0][0, digit].astype(WIDE)
+        for part in arrived[1:]:
+            total = total + part[0, digit].astype(WIDE)
+        out[0] = total.astype(out.dtype)
+
+
+def combine(arrived, radix):
+    _, rows, width = arrived[0].shape
+    rest = arrived[0].shape[0] // radix
+    arrived = [part.reshape(rest, radix, rows, width) for part in arrived]
+    spec = pl.BlockSpec((1, radix, rows, width), lambda step: (step, 0, 0, 0))
+    shape = (rest, rows, width)
+    return pl.pallas_call(
+        functools.partial(combine_kernel, len(arrived)),
+        grid=(rest,),
+        in_specs=[spec] * len(arrived),
+        out_specs=[pl.BlockSpec((1, rows, width), lambda step: (step, 0, 0))] * radix,
+        out_shape=[jax.ShapeDtypeStruct(shape, WIDE)]
+        + [jax.ShapeDtypeStruct(shape, SEND)] * (radix - 1),
+        compiler_params=pltpu.CompilerParams(vmem_limit_bytes=VMEM_BYTES),
+        cost_estimate=pl.CostEstimate(
+            flops=rest * radix * rows * width * len(arrived),
+            transcendentals=0,
+            bytes_accessed=4 * rest * radix * rows * width * (len(arrived) + 1),
+        ),
+        name="combine",
+    )(*arrived)
+
+
+def swap(cells, count, mask):
+    return lax.ppermute(cells, AXES, [(i, i ^ mask) for i in range(count)])
+
+
+def spread_rows(packed, count):
+    held = [packed]
+    high = 4 * 2
+    held += [swap(packed, count, digit * high) for digit in range(1, count // high)]
+    column = jnp.stack(held)
+    near = [column] + [swap(column, count, digit * 2) for digit in range(1, 4)]
+    return near + [swap(piece, count, 1) for piece in near]
+
+
+def gather_sum(keep, send, count):
+    pieces = combine([keep, swap(send, count, 1)], 4)
+    arrived = [pieces[0]] + [swap(pieces[digit], count, digit * 2) for digit in range(1, 4)]
+    pieces = combine(arrived, count // 8)
+    arrived = [pieces[0]]
+    arrived += [swap(pieces[digit], count, digit * 8) for digit in range(1, count // 8)]
+    total = arrived[0][0]
+    for part in arrived[1:]:
+        total = total + part[0].astype(WIDE)
+    return total
 
 
 def shift(cells, count, step):
@@ -473,20 +709,62 @@
     row_count = grid_inputs.shape[0]
     layer_total = w_layers.shape[0]
     device_count = lax.axis_size(AXES)
-    table_in = lax.all_gather(w_in.astype(LOW), AXES, axis=1, tiled=True)
-    table_out = lax.all_gather(w_out.astype(LOW), AXES, axis=0, tiled=True)
-    matrices = lax.all_gather(w_layers.astype(LOW), AXES, axis=2, tiled=True)
-    gains = lax.all_gather(norm_gains.astype(LOW), AXES, axis=2, tiled=True).astype(WIDE)
+    width = mesh_static.shape[1]
+    share = w_layers.shape[2]
+    channels, outputs = w_in.shape[0], w_out.shape[1]
+    direct = share == 16 and device_count % 8 == 0 and device_count & (device_count - 1) == 0
     slot_lists = [encoder_lists.T.reshape(-1)]
     slot_lists += [mesh_lists.T.reshape(-1)] * (layer_total - 2)
     slot_lists += [decoder_lists.T.reshape(-1)]
-    grid_latent = product(grid_inputs, table_in)
-    grid_start = grid_latent.astype(LOW)
-    sent = product(grid_start, matrices[0, 0]).astype(LOW)
+    if direct:
+        self_id = lax.axis_index(AXES).astype(jnp.int32)
+        order = jnp.arange(device_count, dtype=jnp.int32) ^ self_id
+        self_id = self_id.reshape(1)
+        inputs = jnp.pad(grid_inputs, ((0, 0), (0, width - channels)))
+        flat_gains = norm_gains.astype(LOW).reshape(1, -1)
+        packed = jnp.concatenate(
+            [
+                w_layers[0].astype(LOW).reshape(-1, width),
+                jnp.pad(w_in.astype(LOW).T, ((0, 0), (0, width - channels))),
+                jnp.pad(flat_gains, ((0, 7), (0, width - flat_gains.shape[1]))),
+            ],
+            axis=0,
+        )
+        rest = jnp.concatenate(
+            [
+                w_layers[2:].astype(LOW).reshape(-1, share, width),
+                jnp.pad(w_out.astype(LOW), ((0, 0), (0, width - outputs)))[None],
+            ],
+            axis=0,
+        )
+        input_blocks = (shift(inputs, device_count, 1), inputs, shift(inputs, device_count, -1))
+        pieces = spread_rows(packed, device_count)
+        second = lax.all_gather(w_layers[1].astype(LOW), AXES, axis=1, tiled=True)
+        rest = lax.all_gather(rest, AXES, axis=1, tiled=True)
+        first, grid_latent, grid_start, *blocks = embed(self_id, pieces, input_blocks)
+        weights = [(first, 0), (second, 0)]
+        weights += [(rest, 6 * layer_id) for layer_id in range(layer_total - 2)]
+        table_out = rest[6 * (layer_total - 2), :, :outputs]
+        gain_rows = jnp.stack(pieces)[:, :, packed.shape[0] - 8, : flat_gains.shape[1]]
+        gain_rows = gain_rows.reshape(2, 4, device_count // 8, -1).transpose(2, 1, 0, 3)
+        gain_rows = gain_rows.reshape(device_count, -1)[order]
+        gains = gain_rows.reshape(device_count, layer_total, 2, share).transpose(1, 2, 0, 3)
+        gains = gains.reshape(layer_total, 2, width).astype(WIDE)
+    else:
+        self_id = None
+        table_in = lax.all_gather(w_in.astype(LOW), AXES, axis=1, tiled=True)
+        table_out = lax.all_gather(w_out.astype(LOW), AXES, axis=0, tiled=True)
+        matrices = lax.all_gather(w_layers.astype(LOW), AXES, axis=2, tiled=True)
+        matrices = matrices.reshape(-1, width, width)
+        weights = [(matrices, 6 * layer_id) for layer_id in range(layer_total)]
+        gains = lax.all_gather(norm_gains.astype(LOW), AXES, axis=2, tiled=True).astype(WIDE)
+        grid_latent = product(grid_inputs, table_in)
+        grid_start = grid_latent.astype(LOW)
+        sent = product(grid_start, matrices[0]).astype(LOW)
+        blocks = (shift(sent, device_count, 1), sent, shift(sent, device_count, -1))
     target, target_low = mesh_static, mesh_static
     stored_list = []
     for layer_id in range(layer_total):
-        blocks = (shift(sent, device_count, 1), sent, shift(sent, device_count, -1))
         last_layer = layer_id == layer_total - 1
         if last_layer:
             source_low = target_low
@@ -494,19 +772,19 @@
         else:
             source_low = grid_start if layer_id == 0 else target_low
         results = forward_layer(
-            layer_id,
-            not last_layer,
             slot_lists[layer_id],
             blocks,
             target_low,
             target,
-            matrices,
+            weights[layer_id],
+            None if last_layer else weights[layer_id + 1],
             gains[layer_id],
         )
         if last_layer:
             grid_low, kept, message, aggregate, mix, out = results
         else:
             sent, updated, updated_low, kept, message, aggregate, mix, out = results
+            blocks = (shift(sent, device_count, 1), sent, shift(sent, device_count, -1))
         stored_list.append((source_low, (target_low, kept, message, mix, out), aggregate))
         if not last_layer:
             target, target_low = updated, updated_low
@@ -516,10 +794,10 @@
     error_rows = prediction - targets
     loss_scale = 1.0 / (row_count * device_count * prediction.shape[1])
     loss_local = jnp.sum(weight_rows[:, None] * error_rows * error_rows) * loss_scale
-    loss_value = lax.psum(loss_local, AXES)
     grad_pred = (2.0 * loss_scale * weight_rows[:, None] * error_rows).astype(LOW)
     grad_table_out = product_left(grid_low, grad_pred)
     grad_part = product_right(grad_pred, table_out)
+    extra = jnp.pad(grad_table_out, ((0, 0), (0, width - outputs)))
     grad_grid = None
     above, above_source = None, None
     layer_grads = [None] * layer_total
@@ -527,52 +805,79 @@
     for layer_id in reversed(range(layer_total)):
         source_low, stored, aggregate = stored_list[layer_id]
         sent_grad, grad_new, slot_grad, grad_gain, *back = backward_layer(
-            layer_id, slot_lists[layer_id], above, grad_part, stored, matrices, gains[layer_id]
+            slot_lists[layer_id], above, grad_part, stored, weights[layer_id], gains[layer_id]
         )
         from_before = shift(slot_grad[2], device_count, 1)
         from_after = shift(slot_grad[0], device_count, -1)
         back = [back[1], back[0], *back[2:]]
-        results = weight_layer(
-            layer_id,
+        grad_part, sums = weight_layer(
+            self_id,
+            device_count,
             None if above is None else (above_source, sent_grad),
+            extra,
             stored[0],
             aggregate,
             back,
             None if layer_id == 0 else grad_new,
-            matrices,
+            weights[layer_id],
         )
-        layer_grads[layer_id] = results[0]
+        if direct:
+            total = gather_sum(*sums, device_count)
+            layer_grads[layer_id] = total.reshape(6, share, width)
+        else:
+            layer_grads[layer_id] = sums[0]
         gain_grads[layer_id] = grad_gain
         if layer_id == layer_total - 1:
-            grad_grid, grad_part = results[1], None
-        elif layer_id > 0:
-            grad_part = results[1]
-        above = (from_before, slot_grad, from_after)
+            grad_grid, grad_part = grad_part, None
+        above = (from_before, slot_grad, from_after, weights[layer_id])
         above_source = source_low
-    sent_grad = (
-        from_before.astype(WIDE) + slot_grad[1].astype(WIDE) + from_after.astype(WIDE)
-    ).astype(LOW)
-    grad_zero = product_left(above_source, sent_grad)
-    grad_grid = grad_grid + product_right(sent_grad, matrices[0, 0])
-    grad_table_in = product_left(grid_inputs, grad_grid.astype(LOW))
-    grad_stack = jnp.concatenate(
-        [grad_zero[None]]
-        + [
-            part
-            for layer_id in range(layer_total)
-            for part in (
-                [layer_grads[layer_id][1:]]
-                + ([layer_grads[layer_id][0:1]] if layer_id < layer_total - 1 else [])
-            )
-        ],
-        axis=0,
-    ).reshape(layer_total, 6, *grad_zero.shape)
-    grad_layers = lax.psum_scatter(grad_stack, AXES, scatter_dimension=2, tiled=True)
-    grad_gain_all = lax.psum_scatter(
-        jnp.stack(gain_grads), AXES, scatter_dimension=2, tiled=True
-    )
-    grad_in = lax.psum_scatter(grad_table_in, AXES, scatter_dimension=1, tiled=True)
-    grad_out = lax.psum_scatter(grad_table_out, AXES, scatter_dimension=0, tiled=True)
+    if direct:
+        misc = jnp.stack(gain_grads).reshape(-1, device_count, share).transpose(1, 0, 2)
+        misc = misc.reshape(device_count, -1)
+        misc = jnp.concatenate(
+            [misc, jnp.broadcast_to(loss_local.reshape(1, 1), (device_count, 1))], axis=1
+        )
+        misc = jnp.pad(misc[:, None, :], ((0, 0), (0, 7), (0, width - misc.shape[1])))
+        sums = tail_layer(
+            self_id,
+            from_before,
+            slot_grad,
+            from_after,
+            grid_start,
+            inputs,
+            grad_grid,
+            weights[0],
+            misc,
+        )
+        total = gather_sum(*sums, device_count)
+        grad_zero = total[:share]
+        grad_in = total[share : 2 * share, :channels].T
+        size = layer_total * 2 * share
+        grad_gain_all = total[2 * share, :size].reshape(layer_total, 2, share)
+        loss_value = total[2 * share, size]
+        grad_out = layer_grads[-1][0, :, :outputs]
+    else:
+        loss_value = lax.psum(loss_local, AXES)
+        sent_grad = (
+            from_before.astype(WIDE) + slot_grad[1].astype(WIDE) + from_after.astype(WIDE)
+        ).astype(LOW)
+        grad_zero = product_left(above_source, sent_grad)
+        grad_grid = grad_grid + product_right(sent_grad, matrices[0])
+        grad_table_in = product_left(grid_inputs, grad_grid.astype(LOW))
+        grad_in = lax.psum_scatter(grad_table_in, AXES, scatter_dimension=1, tiled=True)
+        grad_out = lax.psum_scatter(grad_table_out, AXES, scatter_dimension=0, tiled=True)
+        grad_gain_all = lax.psum_scatter(
+            jnp.stack(gain_grads), AXES, scatter_dimension=2, tiled=True
+        )
+    grad_layers = [grad_zero[None]]
+    for layer_id in range(layer_total):
+        grad_layers += [layer_grads[layer_id][1:]]
+        if layer_id < layer_total - 1:
+            grad_layers += [layer_grads[layer_id][0:1]]
+    grad_layers = jnp.concatenate(grad_layers, axis=0)
+    grad_layers = grad_layers.reshape(layer_total, 6, *grad_layers.shape[1:])
+    if not direct:
+        grad_layers = lax.psum_scatter(grad_layers, AXES, scatter_dimension=2, tiled=True)
     step_value = step_count[0].astype(WIDE)
     one_in, two_in, new_in = adamw_update(
         w_in, moment_in, square_in, grad_in, step_value, DECAY_RATE

time: 1220 us -> 829 us (0.68)
  waiting for transfers between devices: 582 us -> 244 us
  blocking collectives: 197 us -> 0 us
  starting transfers between devices: 50 us -> 151 us
  Pallas kernels: 297 us -> 354 us
    reduce_scatter x2 -> x0, waiting for transfers between devices: 246 us -> none  [the longest x1 246 us: shards(): lax.psum_scatter(grad_stack, AXES, scatter_dimension=2, tiled=True)]
    unnamed x7 -> x2, waiting for transfers between devices: 235 us -> 0.03 us
    ppermute x0 -> x45, waiting for transfers between devices: none -> 168 us  [swap(): return lax.ppermute(cells, AXES, [(i, i ^ mask) for i in range(count)])]
    all_gather x3 -> x0, blocking collectives: 155 us -> none  [the longest x1 55.1 us: shards(): table_out = lax.all_gather(w_out.astype(LOW), AXES, axis=0, tiled=True)]
    ppermute x0 -> x45, starting transfers between devices: none -> 89.1 us  [swap(): return lax.ppermute(cells, AXES, [(i, i ^ mask) for i in range(count)])]
    pallas_call x0 -> x12, Pallas kernels: none -> 53.8 us  [the longest x10 36.5 us: combine(): pl.pallas_call(functools.partial(combine_kernel, len(arrived)), grid=(res...]
    psum x1 -> x0, blocking collectives: 41.5 us -> none  [shards(): loss_value = lax.psum(loss_local, AXES)]
    all_gather x1 -> x2, waiting for transfers between devices: 54.6 us -> 13.3 us  [the longest x1 13.3 us: shards(): rest = lax.all_gather(rest, AXES, axis=1, tiled=True)]
  transfers between devices with their start and end apart: 21 -> 63, of which waited for: 10 -> 27; matrix products, arithmetic and copies ran while one was open for 4% -> 3% of each run, Pallas kernels for 7% -> 25%
where the time goes in v2:
time: 829 us; the launch traced here: 821 us
  Pallas kernels  354 us (43%)
  waiting for transfers between devices  244 us (29%)
  starting transfers between devices  151 us (18%)
  local copies, waits for them, and re-layouts  35.6 us (4%)
  between operations  17.2 us (2%)
  other arithmetic  13.5 us (2%)
    ppermute x45, waiting for transfers between devices, swap(): return lax.ppermute(cells, AXES, [(i, i ^ mask) for i in range(count)])  168 us
    pallas_call x4, Pallas kernels, backward_layer(): pl.pallas_call(functools.partial(backward_kernel, parts, mode), grid=(blo...  139 us
    pallas_call x4, Pallas kernels, forward_layer(): pl.pallas_call(functools.partial(forward_kernel, parts, has_next), grid=(...  104 us
    ppermute x45, starting transfers between devices, swap(): return lax.ppermute(cells, AXES, [(i, i ^ mask) for i in range(count)])  89.1 us
    ppermute x16, waiting for transfers between devices, shift(): lax.ppermute(cells, AXES, [(i, (i + step) % count) for i in range(count)])  62.5 us
    ppermute x16, starting transfers between devices, shift(): lax.ppermute(cells, AXES, [(i, (i + step) % count) for i in range(count)])  62 us
    pallas_call x4, Pallas kernels, weight_layer(): pl.pallas_call(functools.partial(weight_kernel, above is not None, grad_n...  56.6 us
    pallas_call x10, Pallas kernels, combine(): pl.pallas_call(functools.partial(combine_kernel, len(arrived)), grid=(res...  36.5 us
  transfers between devices with their start and end apart: 63, of which 27 were waited for; matrix products, arithmetic and copies ran while one was open for 3% of the time, Pallas kernels for 25%

profile of v2, /device:TPU:0, one launch (start us, length us, event | category | flops | bytes accessed | tf_op | source)
XLA Modules:
  0.0 820.8 jit_solution(9627472980270580666)
XLA Ops:
  38.4 18.2 %collective-permute-done.3.refs_2_ = bf16[4,120,512]{2,1,0:T(8,128)(2,1)} collective-permute-done((bf16[4,120,512]{2,1,0:T(8,128)(2,1)}, bf16[4,120,512]{2,1,0:T(8,128)(2,1)}, u32[]{:S(2)}, u32[]{:S(2)}) %collective-permute-start.3) | collective-permute-done | bytes 491552 | tf_op jit(solution)/shard_map/ppermute | solution.py:649
  62.2 21.3 %collective-permute-done.5.refs_4_ = bf16[4,120,512]{2,1,0:T(8,128)(2,1)S(1)} collective-permute-done((bf16[4,120,512]{2,1,0:T(8,128)(2,1)}, bf16[4,120,512]{2,1,0:T(8,128)(2,1)S(1)}, u32[]{:S(2)}, u32[]{:S(2)}) %collective-permute-start.5) | collective-permute-done | bytes 491552 | tf_op jit(solution)/shard_map/ppermute | solution.py:649
  92.0 9.6 %embed.1 = (bf16[6,512,512]{2,1,0:T(8,128)(2,1)}, f32[1024,512]{1,0:T(8,128)}, bf16[1024,512]{1,0:T(8,128)(2,1)}, bf16[1024,512]{1,0:T(8,128)(2,1)}, bf16[1024,5...) custom-call(s32[1]{0:T(128)} %bitcast.refs_0_.self_id, bf16[4,120,512]{2,1,0:T(8,128)(2,1)} %pad_maximum_fusion.refs_1_, ...), custom_call_target="tpu_custom_call" | custom-call | flops 3221225472 | bytes 12582912 | tf_op jit(solution)/shard_map/embed/pallas_call | solution.py:529
  101.6 26.3 %forward_layer.4 = (bf16[1024,512]{1,0:T(8,128)(2,1)}, f32[1024,512]{1,0:T(8,128)}, bf16[1024,512]{1,0:T(8,128)(2,1)}, bf16[4,1024,512]{2,1,0:T(8,128)(2,1)}, f3...) custom-call(s32[4096]{0:T(1024)} %bitcast.203, ...), custom_call_target="tpu_custom_call" | custom-call | flops 4831838208 | bytes 25165824 | tf_op jit(solution)/shard_map/forward_layer/pallas_call | solution.py:167
  134.7 19.9 %collective-permute-done.12.refs_1_ = bf16[1024,512]{1,0:T(8,128)(2,1)S(1)} collective-permute-done((bf16[1024,512]{1,0:T(8,128)(2,1)}, bf16[1024,512]{1,0:T(8,128)(2,1)S(1)}, u32[]{:S(2)}, u32[]{:S(2)}) %collective-permute-start.12) | collective-permute-done | bytes 1048608 | tf_op jit(solution)/shard_map/ppermute | solution.py:674
  159.6 13.3 %all-gather.4.cloned.1.call-done.refs_8_.refs_6_.refs_7_.refs_4_.refs_10_.refs_12_.refs_11_ = bf16[13,512,512]{2,1,0:T(8,128)(2,1)} async-done(((bf16[13,16,512]{2,1,0:T(8,128)(2,1)}), bf16[13,512,512]{2,1,0:T(8,128)(2,1)}) %all-gather.4.cloned.1.call-update) | async-done | bytes 6815760 | tf_op jit(solution)/shard_map/all_gather | solution.py:743
  172.9 26.3 %forward_layer.5 = (bf16[1024,512]{1,0:T(8,128)(2,1)}, f32[1024,512]{1,0:T(8,128)}, bf16[1024,512]{1,0:T(8,128)(2,1)}, bf16[4,1024,512]{2,1,0:T(8,128)(2,1)}, f3...) custom-call(s32[4096]{0:T(1024)} %bitcast.197, ...), custom_call_target="tpu_custom_call" | custom-call | flops 4831838208 | bytes 25165824 | tf_op jit(solution)/shard_map/forward_layer/pallas_call | solution.py:167
  205.4 12.0 %collective-permute-done.14.refs_1_ = bf16[1024,512]{1,0:T(8,128)(2,1)S(1)} collective-permute-done((bf16[1024,512]{1,0:T(8,128)(2,1)}, bf16[1024,512]{1,0:T(8,128)(2,1)S(1)}, u32[]{:S(2)}, u32[]{:S(2)}) %collective-permute-start.14) | collective-permute-done | bytes 1048608 | tf_op jit(solution)/shard_map/ppermute | solution.py:674
  218.8 26.3 %forward_layer.6 = (bf16[1024,512]{1,0:T(8,128)(2,1)}, f32[1024,512]{1,0:T(8,128)}, bf16[1024,512]{1,0:T(8,128)(2,1)}, bf16[4,1024,512]{2,1,0:T(8,128)(2,1)}, f3...) custom-call(s32[4096]{0:T(1024)} %bitcast.198, ...), custom_call_target="tpu_custom_call" | custom-call | flops 4831838208 | bytes 25165824 | tf_op jit(solution)/shard_map/forward_layer/pallas_call | solution.py:167
  254.2 9.1 %collective-permute-done.16.refs_1_ = bf16[1024,512]{1,0:T(8,128)(2,1)S(1)} collective-permute-done((bf16[1024,512]{1,0:T(8,128)(2,1)}, bf16[1024,512]{1,0:T(8,128)(2,1)S(1)}, u32[]{:S(2)}, u32[]{:S(2)}) %collective-permute-start.16) | collective-permute-done | bytes 1048608 | tf_op jit(solution)/shard_map/ppermute | solution.py:674
  264.7 24.9 %forward_layer.7 = (bf16[1024,512]{1,0:T(8,128)(2,1)}, bf16[4,1024,512]{2,1,0:T(8,128)(2,1)}, f32[4,1024,512]{2,1,0:T(8,128)}, bf16[1024,512]{1,0:T(8,128)(2,1)}...) custom-call(s32[4096]{0:T(1024)} %bitcast.205, bf16[1024,512]{1,0:T(8,128)(2,1)} %copy-done.63, ...), custom_call_target="tpu_custom_call" | custom-call | flops 4831838208 | bytes 25165824 | tf_op jit(solution)/shard_map/forward_layer/pallas_call | solution.py:167
  294.9 33.8 %backward_layer.4 = (bf16[3,1024,512]{2,1,0:T(8,128)(2,1)}, f32[2,512]{1,0:T(2,128)}, bf16[4,1024,512]{2,1,0:T(8,128)(2,1)}, bf16[4,1024,512]{2,1,0:T(8,128)(2,1...) custom-call(s32[4096]{0:T(1024)} %bitcast.206, ...), custom_call_target="tpu_custom_call" | custom-call | flops 4294967296 | bytes 25165824 | tf_op jit(solution)/shard_map/backward_layer/pallas_call | solution.py:341
  330.3 13.9 %collective-permute-start.18 = (bf16[1024,512]{1,0:T(8,128)(2,1)S(1)}, bf16[1024,512]{1,0:T(8,128)(2,1)S(1)}, u32[]{:S(2)}, u32[]{:S(2)}) collective-permute-start(bf16[1024,512]{1,0:T(8,128)(2,1)S(1)} %get-tuple-element.284), channel_id=1, source_target_pairs={{0,1},{1,2},{2,3},{3,4},{4,5},{5,6},{6,7},{7,8},{8,9},{9,10},{10,1... | collective-permute-start | bytes 3145736 | tf_op jit(solution)/shard_map/ppermute | solution.py:674
  348.6 8.0 collective-permute-done.19.refs_3_
  357.6 35.2 %backward_layer.5 = (bf16[1024,512]{1,0:T(8,128)(2,1)}, f32[1024,512]{1,0:T(8,128)}, bf16[3,1024,512]{2,1,0:T(8,128)(2,1)}, f32[2,512]{1,0:T(2,128)}, bf16[4,102...) custom-call(s32[4096]{0:T(1024)} %bitcast.199, ...), custom_call_target="tpu_custom_call" | custom-call | flops 4294967296 | bytes 25165824 | tf_op jit(solution)/shard_map/backward_layer/pallas_call | solution.py:341
  394.5 13.4 %collective-permute-start.20 = (bf16[1024,512]{1,0:T(8,128)(2,1)S(1)}, bf16[1024,512]{1,0:T(8,128)(2,1)S(1)}, u32[]{:S(2)}, u32[]{:S(2)}) collective-permute-start(bf16[1024,512]{1,0:T(8,128)(2,1)S(1)} %get-tuple-element.282), channel_id=1, source_target_pairs={{0,1},{1,2},{2,3},{3,4},{4,5},{5,6},{6,7},{7,8},{8,9},{9,10},{10,1... | collective-permute-start | bytes 3145736 | tf_op jit(solution)/shard_map/ppermute | solution.py:674
  409.9 14.4 %weight_layer.6 = (f32[1024,512]{1,0:T(8,128)}, f32[16,96,512]{2,1,0:T(8,128)}, f32[16,96,512]{2,1,0:T(8,128)}) custom-call(s32[1]{0:T(128)} %bitcast.refs_0_.self_id, f32[512,512]{1,0:T(8,128)} %pad.29.refs_1_, bf16[1024,512]{1,0:T(8,128)(2,1)} %get-tuple-element.149.refs_4_.refs_2_.latent_low, bf16[1024,512]{1,0:T(8,128)(2,1)} %get-tuple-element.193.refs_3_, ...), custom_call_target="tpu_custom_call" | custom-call | flops 5368709120 | bytes 12582912 | tf_op jit(solution)/shard_map/weight_layer/pallas_call | solution.py:469
  426.9 14.9 %weight_layer.4 = (f32[1024,512]{1,0:T(8,128)}, f32[16,96,512]{2,1,0:T(8,128)}, f32[16,96,512]{2,1,0:T(8,128)}) custom-call(s32[1]{0:T(128)} %bitcast.refs_0_.self_id, bf16[1024,512]{1,0:T(8,128)(2,1)} %get-tuple-element.162.refs_1_, bf16[1024,512]{1,0:T(8,128)(2,1)} %get-tuple-element.163.refs_2_, ...), custom_call_target="tpu_custom_call" | custom-call | flops 5368709120 | bytes 12582912 | tf_op jit(solution)/shard_map/weight_layer/pallas_call | solution.py:469
  443.1 35.2 %backward_layer.6 = (bf16[1024,512]{1,0:T(8,128)(2,1)}, f32[1024,512]{1,0:T(8,128)}, bf16[3,1024,512]{2,1,0:T(8,128)(2,1)}, f32[2,512]{1,0:T(2,128)}, bf16[4,102...) custom-call(s32[4096]{0:T(1024)} %bitcast.200, ...), custom_call_target="tpu_custom_call" | custom-call | flops 4294967296 | bytes 25165824 | tf_op jit(solution)/shard_map/backward_layer/pallas_call | solution.py:341
  485.5 14.9 %weight_layer.5 = (f32[1024,512]{1,0:T(8,128)}, f32[16,96,512]{2,1,0:T(8,128)}, f32[16,96,512]{2,1,0:T(8,128)}) custom-call(s32[1]{0:T(128)} %bitcast.refs_0_.self_id, bf16[1024,512]{1,0:T(8,128)(2,1)} %get-tuple-element.146.refs_4_.refs_5_.refs_3_.refs_1_, bf16[1024,512]{1,0:T(8,128)(2,1)} %get-tuple-element.178.refs_2_, ...), custom_call_target="tpu_custom_call" | custom-call | flops 5368709120 | bytes 12582912 | tf_op jit(solution)/shard_map/weight_layer/pallas_call | solution.py:469
  501.7 35.2 %backward_layer.7 = (bf16[1024,512]{1,0:T(8,128)(2,1)}, f32[1024,512]{1,0:T(8,128)}, bf16[3,1024,512]{2,1,0:T(8,128)(2,1)}, f32[2,512]{1,0:T(2,128)}, bf16[4,102...) custom-call(s32[4096]{0:T(1024)} %bitcast.204, ...), custom_call_target="tpu_custom_call" | custom-call | flops 4294967296 | bytes 25165824 | tf_op jit(solution)/shard_map/backward_layer/pallas_call | solution.py:341
  556.6 9.3 %collective-permute-start.56 = (f32[4,96,512]{2,1,0:T(8,128)}, f32[4,96,512]{2,1,0:T(8,128)}, u32[]{:S(2)}, u32[]{:S(2)}) collective-permute-start(f32[4,96,512]{2,1,0:T(8,128)} %get-tuple-element.257), channel_id=1, source_target_pairs={{0,4},{1,5},{2,6},{3,7},{4,0},{5,1},{6,2},{7,3},{8,12},{9,13},{10,... | collective-permute-start | bytes 2359304 | tf_op jit(solution)/shard_map/ppermute | solution.py:649
  565.9 12.5 %weight_layer.7 = (f32[16,96,512]{2,1,0:T(8,128)}, f32[16,96,512]{2,1,0:T(8,128)}) custom-call(s32[1]{0:T(128)} %bitcast.refs_0_.self_id, bf16[1024,512]{1,0:T(8,128)(2,1)} %get-tuple-element.143.refs_4_.refs_6_.refs_3_.refs_1_, bf16[1024,512]{1,0:T(8,128)(2,1)} %get-tuple-element.215.refs_2_, bf16[1024,512]{1,0:T(8,128)(2,1)} %refs_3_.1, ...), custom_call_target="tpu_custom_call" | custom-call | flops 5368709120 | bytes 12582912 | tf_op jit(solution)/shard_map/weight_layer/pallas_call | solution.py:469
  579.5 11.0 %collective-permute-start.33 = (f32[16,96,512]{2,1,0:T(8,128)}, f32[16,96,512]{2,1,0:T(8,128)S(1)}, u32[]{:S(2)}, u32[]{:S(2)}) collective-permute-start(f32[16,96,512]{2,1,0:T(8,128)} %get-tuple-element.224), channel_id=1, source_target_pairs={{0,1},{1,0},{2,3},{3,2},{4,5},{5,4},{6,7},{7,6},{8,9},{9,8},{10,11... | collective-permute-start | bytes 9437192 | tf_op jit(solution)/shard_map/ppermute | solution.py:649
  592.4 7.6 tail_layer.1
  604.0 17.8 %collective-permute-done.57 = f32[4,96,512]{2,1,0:T(8,128)S(1)} collective-permute-done((f32[4,96,512]{2,1,0:T(8,128)S(1)}, f32[4,96,512]{2,1,0:T(8,128)S(1)}, u32[]{:S(2)}, u32[]{:S(2)}) %collective-permute-start.57) | collective-permute-done | bytes 786464 | tf_op jit(solution)/shard_map/ppermute | solution.py:649
  656.0 12.6 %collective-permute-done.48 = f32[4,96,512]{2,1,0:T(8,128)S(1)} collective-permute-done((f32[4,96,512]{2,1,0:T(8,128)}, f32[4,96,512]{2,1,0:T(8,128)S(1)}, u32[]{:S(2)}, u32[]{:S(2)}) %collective-permute-start.48) | collective-permute-done | bytes 786464 | tf_op jit(solution)/shard_map/ppermute | solution.py:649
  669.6 15.4 %collective-permute-done.49 = f32[4,96,512]{2,1,0:T(8,128)S(1)} collective-permute-done((f32[4,96,512]{2,1,0:T(8,128)}, f32[4,96,512]{2,1,0:T(8,128)S(1)}, u32[]{:S(2)}, u32[]{:S(2)}) %collective-permute-start.49) | collective-permute-done | bytes 786464 | tf_op jit(solution)/shard_map/ppermute | solution.py:649
  708.9 10.9 %collective-permute-done.52 = f32[1,96,512]{2,1,0:T(8,128)S(1)} collective-permute-done((f32[1,96,512]{2,1,0:T(8,128)}, f32[1,96,512]{2,1,0:T(8,128)S(1)}, u32[]{:S(2)}, u32[]{:S(2)}) %collective-permute-start.52) | collective-permute-done | bytes 196640 | tf_op jit(solution)/shard_map/ppermute | solution.py:649
  738.2 20.8 %collective-permute-done.42 = f32[4,96,512]{2,1,0:T(8,128)} collective-permute-done((f32[4,96,512]{2,1,0:T(8,128)}, f32[4,96,512]{2,1,0:T(8,128)}, u32[]{:S(2)}, u32[]{:S(2)}) %collective-permute-start.42) | collective-permute-done | bytes 786464 | tf_op jit(solution)/shard_map/ppermute | solution.py:649
  762.7 10.5 %collective-permute-start.44 = (f32[1,96,512]{2,1,0:T(8,128)}, f32[1,96,512]{2,1,0:T(8,128)S(1)}, u32[]{:S(2)}, u32[]{:S(2)}) collective-permute-start(f32[1,96,512]{2,1,0:T(8,128)} %get-tuple-element.240), channel_id=1, source_target_pairs={{0,8},{1,9},{2,10},{3,11},{4,12},{5,13},{6,14},{7,15},{8,0},{9,1},... | collective-permute-start | bytes 589832 | tf_op jit(solution)/shard_map/ppermute | solution.py:649
  777.4 11.9 %collective-permute-done.35 = f32[4,96,512]{2,1,0:T(8,128)S(1)} collective-permute-done((f32[4,96,512]{2,1,0:T(8,128)}, f32[4,96,512]{2,1,0:T(8,128)S(1)}, u32[]{:S(2)}, u32[]{:S(2)}) %collective-permute-start.35) | collective-permute-done | bytes 786464 | tf_op jit(solution)/shard_map/ppermute | solution.py:649
  (336 shorter events, 237.2 us)
Async XLA Ops:
  7.2 94.4 %all-gather.6.cloned.1.call-start = ((), (), s32[]{:S(2)}) async-start(), calls=%async_computation.1 | async-start | bytes 3244032 | tf_op jit(solution)/shard_map/all_gather | solution.py:742
  9.2 163.7 %all-gather.4.cloned.1.call-start = ((), (), s32[]{:S(2)}) async-start(), calls=%async_computation | async-start | bytes 7028736 | tf_op jit(solution)/shard_map/all_gather | solution.py:743
  29.3 27.4 %collective-permute-start.3 = (bf16[4,120,512]{2,1,0:T(8,128)(2,1)}, bf16[4,120,512]{2,1,0:T(8,128)(2,1)}, u32[]{:S(2)}, u32[]{:S(2)}) collective-permute-start(bf16[4,120,512]{2,1,0:T(8,128)(2,1)} %pad_maximum_fusion.refs_1_), channel_id=1, source_target_pairs={{0,2},{1,3},{2,0},{3,1},{4,6},{5,7},{6,4},{7,5},{8,10},{9,11},{10,... | collective-permute-start | bytes 1474568 | tf_op jit(solution)/shard_map/ppermute | solution.py:649
  31.5 60.4 %collective-permute-start.10 = (bf16[1024,512]{1,0:T(8,128)(2,1)S(1)}, bf16[1024,512]{1,0:T(8,128)(2,1)}, u32[]{:S(2)}, u32[]{:S(2)}) collective-permute-start(bf16[1024,512]{1,0:T(8,128)(2,1)S(1)} %pad.27.refs_10_.inputs), channel_id=1, source_target_pairs={{0,1},{1,2},{2,3},{3,4},{4,5},{5,6},{6,7},{7,8},{8,9},{9,10},{10,1... | collective-permute-start | bytes 3145736 | tf_op jit(solution)/shard_map/ppermute | solution.py:674
  31.5 60.4 %collective-permute-start.11 = (bf16[1024,512]{1,0:T(8,128)(2,1)S(1)}, bf16[1024,512]{1,0:T(8,128)(2,1)}, u32[]{:S(2)}, u32[]{:S(2)}) collective-permute-start(bf16[1024,512]{1,0:T(8,128)(2,1)S(1)} %pad.27.refs_10_.inputs), channel_id=1, source_target_pairs={{0,31},{1,0},{2,1},{3,2},{4,3},{5,4},{6,5},{7,6},{8,7},{9,8},{10,9... | collective-permute-start | bytes 3145736 | tf_op jit(solution)/shard_map/ppermute | solution.py:674
  36.9 25.3 %collective-permute-start.4 = (bf16[4,120,512]{2,1,0:T(8,128)(2,1)}, bf16[4,120,512]{2,1,0:T(8,128)(2,1)S(1)}, u32[]{:S(2)}, u32[]{:S(2)}) collective-permute-start(bf16[4,120,512]{2,1,0:T(8,128)(2,1)} %pad_maximum_fusion.refs_1_), channel_id=1, source_target_pairs={{0,4},{1,5},{2,6},{3,7},{4,0},{5,1},{6,2},{7,3},{8,12},{9,13},{10,... | collective-permute-start | bytes 1474568 | tf_op jit(solution)/shard_map/ppermute | solution.py:649
  37.5 46.0 %collective-permute-start.5 = (bf16[4,120,512]{2,1,0:T(8,128)(2,1)}, bf16[4,120,512]{2,1,0:T(8,128)(2,1)S(1)}, u32[]{:S(2)}, u32[]{:S(2)}) collective-permute-start(bf16[4,120,512]{2,1,0:T(8,128)(2,1)} %pad_maximum_fusion.refs_1_), channel_id=1, source_target_pairs={{0,6},{1,7},{2,4},{3,5},{4,2},{5,3},{6,0},{7,1},{8,14},{9,15},{10,... | collective-permute-start | bytes 1474568 | tf_op jit(solution)/shard_map/ppermute | solution.py:649
  56.6 26.9 %collective-permute-start.6 = (bf16[4,120,512]{2,1,0:T(8,128)(2,1)}, bf16[4,120,512]{2,1,0:T(8,128)(2,1)S(1)}, u32[]{:S(2)}, u32[]{:S(2)}) collective-permute-start(bf16[4,120,512]{2,1,0:T(8,128)(2,1)} %pad_maximum_fusion.refs_1_), channel_id=1, source_target_pairs={{0,1},{1,0},{2,3},{3,2},{4,5},{5,4},{6,7},{7,6},{8,9},{9,8},{10,11... | collective-permute-start | bytes 1474568 | tf_op jit(solution)/shard_map/ppermute | solution.py:649
  127.9 26.6 %collective-permute-start.12 = (bf16[1024,512]{1,0:T(8,128)(2,1)}, bf16[1024,512]{1,0:T(8,128)(2,1)S(1)}, u32[]{:S(2)}, u32[]{:S(2)}) collective-permute-start(bf16[1024,512]{1,0:T(8,128)(2,1)} %get-tuple-element.142.refs_2_), channel_id=1, source_target_pairs={{0,1},{1,2},{2,3},{3,4},{4,5},{5,6},{6,7},{7,8},{8,9},{9,10},{10,1... | collective-permute-start | bytes 3145736 | tf_op jit(solution)/shard_map/ppermute | solution.py:674
  128.1 31.5 %collective-permute-start.13 = (bf16[1024,512]{1,0:T(8,128)(2,1)}, bf16[1024,512]{1,0:T(8,128)(2,1)S(1)}, u32[]{:S(2)}, u32[]{:S(2)}) collective-permute-start(bf16[1024,512]{1,0:T(8,128)(2,1)} %get-tuple-element.142.refs_2_), channel_id=1, source_target_pairs={{0,31},{1,0},{2,1},{3,2},{4,3},{5,4},{6,5},{7,6},{8,7},{9,8},{10,9... | collective-permute-start | bytes 3145736 | tf_op jit(solution)/shard_map/ppermute | solution.py:674
  394.5 47.2 %collective-permute-start.20 = (bf16[1024,512]{1,0:T(8,128)(2,1)S(1)}, bf16[1024,512]{1,0:T(8,128)(2,1)S(1)}, u32[]{:S(2)}, u32[]{:S(2)}) collective-permute-start(bf16[1024,512]{1,0:T(8,128)(2,1)S(1)} %get-tuple-element.282), channel_id=1, source_target_pairs={{0,1},{1,2},{2,3},{3,4},{4,5},{5,6},{6,7},{7,8},{8,9},{9,10},{10,1... | collective-permute-start | bytes 3145736 | tf_op jit(solution)/shard_map/ppermute | solution.py:674
  407.9 33.8 %collective-permute-start.21 = (bf16[1024,512]{1,0:T(8,128)(2,1)S(1)}, bf16[1024,512]{1,0:T(8,128)(2,1)S(1)}, u32[]{:S(2)}, u32[]{:S(2)}) collective-permute-start(bf16[1024,512]{1,0:T(8,128)(2,1)S(1)} %get-tuple-element.281), channel_id=1, source_target_pairs={{0,31},{1,0},{2,1},{3,2},{4,3},{5,4},{6,5},{7,6},{8,7},{9,8},{10,9... | collective-permute-start | bytes 3145736 | tf_op jit(solution)/shard_map/ppermute | solution.py:674
  424.3 121.5 %collective-permute-start.54 = (f32[16,96,512]{2,1,0:T(8,128)}, f32[16,96,512]{2,1,0:T(8,128)S(1)}, u32[]{:S(2)}, u32[]{:S(2)}) collective-permute-start(f32[16,96,512]{2,1,0:T(8,128)} %get-tuple-element.254), channel_id=1, source_target_pairs={{0,1},{1,0},{2,3},{3,2},{4,5},{5,4},{6,7},{7,6},{8,9},{9,8},{10,11... | collective-permute-start | bytes 9437192 | tf_op jit(solution)/shard_map/ppermute | solution.py:649
  485.5 147.3 %collective-permute-start.47 = (f32[16,96,512]{2,1,0:T(8,128)}, f32[16,96,512]{2,1,0:T(8,128)}, u32[]{:S(2)}, u32[]{:S(2)}) collective-permute-start(f32[16,96,512]{2,1,0:T(8,128)} %get-tuple-element.244), channel_id=1, source_target_pairs={{0,1},{1,0},{2,3},{3,2},{4,5},{5,4},{6,7},{7,6},{8,9},{9,8},{10,11... | collective-permute-start | bytes 9437192 | tf_op jit(solution)/shard_map/ppermute | solution.py:649
  543.2 35.2 %collective-permute-start.25 = (bf16[1024,512]{1,0:T(8,128)(2,1)S(1)}, bf16[1024,512]{1,0:T(8,128)(2,1)S(1)}, u32[]{:S(2)}, u32[]{:S(2)}) collective-permute-start(bf16[1024,512]{1,0:T(8,128)(2,1)S(1)} %get-tuple-element.277), channel_id=1, source_target_pairs={{0,31},{1,0},{2,1},{3,2},{4,3},{5,4},{6,5},{7,6},{8,7},{9,8},{10,9... | collective-permute-start | bytes 3145736 | tf_op jit(solution)/shard_map/ppermute | solution.py:674
  544.2 143.1 %collective-permute-start.40 = (f32[16,96,512]{2,1,0:T(8,128)}, f32[16,96,512]{2,1,0:T(8,128)}, u32[]{:S(2)}, u32[]{:S(2)}) collective-permute-start(f32[16,96,512]{2,1,0:T(8,128)} %get-tuple-element.234), channel_id=1, source_target_pairs={{0,1},{1,0},{2,3},{3,2},{4,5},{5,4},{6,7},{7,6},{8,9},{9,8},{10,11... | collective-permute-start | bytes 9437192 | tf_op jit(solution)/shard_map/ppermute | solution.py:649
  552.4 47.6 %collective-permute-start.55 = (f32[4,96,512]{2,1,0:T(8,128)}, f32[4,96,512]{2,1,0:T(8,128)}, u32[]{:S(2)}, u32[]{:S(2)}) collective-permute-start(f32[4,96,512]{2,1,0:T(8,128)} %get-tuple-element.256), channel_id=1, source_target_pairs={{0,2},{1,3},{2,0},{3,1},{4,6},{5,7},{6,4},{7,5},{8,10},{9,11},{10,... | collective-permute-start | bytes 2359304 | tf_op jit(solution)/shard_map/ppermute | solution.py:649
  556.6 43.5 %collective-permute-start.56 = (f32[4,96,512]{2,1,0:T(8,128)}, f32[4,96,512]{2,1,0:T(8,128)}, u32[]{:S(2)}, u32[]{:S(2)}) collective-permute-start(f32[4,96,512]{2,1,0:T(8,128)} %get-tuple-element.257), channel_id=1, source_target_pairs={{0,4},{1,5},{2,6},{3,7},{4,0},{5,1},{6,2},{7,3},{8,12},{9,13},{10,... | collective-permute-start | bytes 2359304 | tf_op jit(solution)/shard_map/ppermute | solution.py:649
  579.5 141.8 %collective-permute-start.33 = (f32[16,96,512]{2,1,0:T(8,128)}, f32[16,96,512]{2,1,0:T(8,128)S(1)}, u32[]{:S(2)}, u32[]{:S(2)}) collective-permute-start(f32[16,96,512]{2,1,0:T(8,128)} %get-tuple-element.224), channel_id=1, source_target_pairs={{0,1},{1,0},{2,3},{3,2},{4,5},{5,4},{6,7},{7,6},{8,9},{9,8},{10,11... | collective-permute-start | bytes 9437192 | tf_op jit(solution)/shard_map/ppermute | solution.py:649
  600.0 51.2 %collective-permute-start.26 = (f32[16,40,512]{2,1,0:T(8,128)}, f32[16,40,512]{2,1,0:T(8,128)S(1)}, u32[]{:S(2)}, u32[]{:S(2)}) collective-permute-start(f32[16,40,512]{2,1,0:T(8,128)} %get-tuple-element.206), channel_id=1, source_target_pairs={{0,1},{1,0},{2,3},{3,2},{4,5},{5,4},{6,7},{7,6},{8,9},{9,8},{10,11... | collective-permute-start | bytes 3932168 | tf_op jit(solution)/shard_map/ppermute | solution.py:649
  649.6 35.4 %collective-permute-start.49 = (f32[4,96,512]{2,1,0:T(8,128)}, f32[4,96,512]{2,1,0:T(8,128)S(1)}, u32[]{:S(2)}, u32[]{:S(2)}) collective-permute-start(f32[4,96,512]{2,1,0:T(8,128)} %get-tuple-element.247), channel_id=1, source_target_pairs={{0,4},{1,5},{2,6},{3,7},{4,0},{5,1},{6,2},{7,3},{8,12},{9,13},{10,... | collective-permute-start | bytes 2359304 | tf_op jit(solution)/shard_map/ppermute | solution.py:649
  651.2 41.8 %collective-permute-start.50 = (f32[4,96,512]{2,1,0:T(8,128)}, f32[4,96,512]{2,1,0:T(8,128)S(1)}, u32[]{:S(2)}, u32[]{:S(2)}) collective-permute-start(f32[4,96,512]{2,1,0:T(8,128)} %get-tuple-element.248), channel_id=1, source_target_pairs={{0,6},{1,7},{2,4},{3,5},{4,2},{5,3},{6,0},{7,1},{8,14},{9,15},{10,... | collective-permute-start | bytes 2359304 | tf_op jit(solution)/shard_map/ppermute | solution.py:649
  668.7 28.8 %collective-permute-start.27 = (f32[4,40,512]{2,1,0:T(8,128)}, f32[4,40,512]{2,1,0:T(8,128)S(1)}, u32[]{:S(2)}, u32[]{:S(2)}) collective-permute-start(f32[4,40,512]{2,1,0:T(8,128)} %get-tuple-element.208), channel_id=1, source_target_pairs={{0,2},{1,3},{2,0},{3,1},{4,6},{5,7},{6,4},{7,5},{8,10},{9,11},{10,... | collective-permute-start | bytes 983048 | tf_op jit(solution)/shard_map/ppermute | solution.py:649
  693.0 39.9 %collective-permute-start.41 = (f32[4,96,512]{2,1,0:T(8,128)}, f32[4,96,512]{2,1,0:T(8,128)}, u32[]{:S(2)}, u32[]{:S(2)}) collective-permute-start(f32[4,96,512]{2,1,0:T(8,128)} %get-tuple-element.236), channel_id=1, source_target_pairs={{0,2},{1,3},{2,0},{3,1},{4,6},{5,7},{6,4},{7,5},{8,10},{9,11},{10,... | collective-permute-start | bytes 2359304 | tf_op jit(solution)/shard_map/ppermute | solution.py:649
  721.3 37.7 %collective-permute-start.42 = (f32[4,96,512]{2,1,0:T(8,128)}, f32[4,96,512]{2,1,0:T(8,128)}, u32[]{:S(2)}, u32[]{:S(2)}) collective-permute-start(f32[4,96,512]{2,1,0:T(8,128)} %get-tuple-element.237), channel_id=1, source_target_pairs={{0,4},{1,5},{2,6},{3,7},{4,0},{5,1},{6,2},{7,3},{8,12},{9,13},{10,... | collective-permute-start | bytes 2359304 | tf_op jit(solution)/shard_map/ppermute | solution.py:649
  728.0 31.0 %collective-permute-start.43 = (f32[4,96,512]{2,1,0:T(8,128)}, f32[4,96,512]{2,1,0:T(8,128)S(1)}, u32[]{:S(2)}, u32[]{:S(2)}) collective-permute-start(f32[4,96,512]{2,1,0:T(8,128)} %get-tuple-element.238), channel_id=1, source_target_pairs={{0,6},{1,7},{2,4},{3,5},{4,2},{5,3},{6,0},{7,1},{8,14},{9,15},{10,... | collective-permute-start | bytes 2359304 | tf_op jit(solution)/shard_map/ppermute | solution.py:649
  730.6 44.7 %collective-permute-start.34 = (f32[4,96,512]{2,1,0:T(8,128)}, f32[4,96,512]{2,1,0:T(8,128)S(1)}, u32[]{:S(2)}, u32[]{:S(2)}) collective-permute-start(f32[4,96,512]{2,1,0:T(8,128)} %get-tuple-element.226), channel_id=1, source_target_pairs={{0,2},{1,3},{2,0},{3,1},{4,6},{5,7},{6,4},{7,5},{8,10},{9,11},{10,... | collective-permute-start | bytes 2359304 | tf_op jit(solution)/shard_map/ppermute | solution.py:649
  731.5 57.8 %collective-permute-start.35 = (f32[4,96,512]{2,1,0:T(8,128)}, f32[4,96,512]{2,1,0:T(8,128)S(1)}, u32[]{:S(2)}, u32[]{:S(2)}) collective-permute-start(f32[4,96,512]{2,1,0:T(8,128)} %get-tuple-element.227), channel_id=1, source_target_pairs={{0,4},{1,5},{2,6},{3,7},{4,0},{5,1},{6,2},{7,3},{8,12},{9,13},{10,... | collective-permute-start | bytes 2359304 | tf_op jit(solution)/shard_map/ppermute | solution.py:649
  732.9 56.4 %collective-permute-start.36 = (f32[4,96,512]{2,1,0:T(8,128)}, f32[4,96,512]{2,1,0:T(8,128)S(1)}, u32[]{:S(2)}, u32[]{:S(2)}) collective-permute-start(f32[4,96,512]{2,1,0:T(8,128)} %get-tuple-element.228), channel_id=1, source_target_pairs={{0,6},{1,7},{2,4},{3,5},{4,2},{5,3},{6,0},{7,1},{8,14},{9,15},{10,... | collective-permute-start | bytes 2359304 | tf_op jit(solution)/shard_map/ppermute | solution.py:649
  762.7 36.4 %collective-permute-start.44 = (f32[1,96,512]{2,1,0:T(8,128)}, f32[1,96,512]{2,1,0:T(8,128)S(1)}, u32[]{:S(2)}, u32[]{:S(2)}) collective-permute-start(f32[1,96,512]{2,1,0:T(8,128)} %get-tuple-element.240), channel_id=1, source_target_pairs={{0,8},{1,9},{2,10},{3,11},{4,12},{5,13},{6,14},{7,15},{8,0},{9,1},... | collective-permute-start | bytes 589832 | tf_op jit(solution)/shard_map/ppermute | solution.py:649
  773.2 27.4 %collective-permute-start.45 = (f32[1,96,512]{2,1,0:T(8,128)}, f32[1,96,512]{2,1,0:T(8,128)S(1)}, u32[]{:S(2)}, u32[]{:S(2)}) collective-permute-start(f32[1,96,512]{2,1,0:T(8,128)} %get-tuple-element.241), channel_id=1, source_target_pairs={{0,16},{1,17},{2,18},{3,19},{4,20},{5,21},{6,22},{7,23},{8,24},{9,... | collective-permute-start | bytes 589832 | tf_op jit(solution)/shard_map/ppermute | solution.py:649
  775.3 25.3 %collective-permute-start.46 = (f32[1,96,512]{2,1,0:T(8,128)}, f32[1,96,512]{2,1,0:T(8,128)S(1)}, u32[]{:S(2)}, u32[]{:S(2)}) collective-permute-start(f32[1,96,512]{2,1,0:T(8,128)} %get-tuple-element.242), channel_id=1, source_target_pairs={{0,24},{1,25},{2,26},{3,27},{4,28},{5,29},{6,30},{7,31},{8,16},{9,... | collective-permute-start | bytes 589832 | tf_op jit(solution)/shard_map/ppermute | solution.py:649
  (99 other events, 1741.1 us)
Sparse Core Ops, SparseCore 0:
  10.9 77.0 all-gather.5
  90.9 81.9 all-gather.3

commit v3 on v2

--- a/solution.py
+++ b/solution.py
@@ -16,14 +16,14 @@
 
 AXES = ("nodes", "shard")
 LANES = 128
-FORWARD_ROWS = 128
-BACKWARD_ROWS = 128
+FORWARD_ROWS = 256
+BACKWARD_ROWS = 256
 WEIGHT_ROWS = 256
 UNROLL = 32
 VMEM_BYTES = 56 << 20
 LOW = jnp.bfloat16
 WIDE = jnp.float32
-SEND = jnp.float32
+SEND = jnp.bfloat16
 
 
 def product(left, right):
@@ -51,8 +51,14 @@
     )
 
 
-def sigmoid(tensor):
-    return 0.5 * jnp.tanh(0.5 * tensor) + 0.5
+def silu_parts(tensor):
+    half = 0.5 * tensor
+    return half, jnp.tanh(half)
+
+
+def silu(tensor):
+    half, bend = silu_parts(tensor)
+    return half * (1.0 + bend)
 
 
 def fold_rows(store, base, rows, tensor):
@@ -74,11 +80,11 @@
     if has_next:
         (slots, before, middle, after, low, wide, weights, gains, head) = refs[:9]
         (sent, update, update_low, kept, message, aggregate, mix, out) = refs[9:17]
-        window, picked = refs[17:]
+        window, picked, hidden = refs[17:]
     else:
         (slots, before, middle, after, low, wide, weights, gains) = refs[:8]
         (update_low, kept, message, aggregate, mix, out) = refs[8:14]
-        window, picked = refs[14:]
+        window, picked, hidden = refs[14:]
     step = pl.program_id(0)
     block_rows = before.shape[0]
     rows, width = low.shape
@@ -103,21 +109,19 @@
         lax.fori_loop(0, rows // UNROLL, pick, 0)
     target_low = low[...]
     own_term = product(target_low, weights[1])
-    total = jnp.zeros((rows, width), WIDE)
     for k in range(fan):
         sender = unfold_rows(picked, k * rows, rows, parts)
         kept[k] = sender.astype(LOW)
-        pre_edge = sender + own_term
-        hidden = (pre_edge * sigmoid(pre_edge)).astype(LOW)
-        spoken = product(hidden, weights[2])
-        message[k] = spoken
-        total = total + normalize(spoken)[0] * gains[0:1, :]
-    total_low = total.astype(LOW)
+        hidden[k * rows : (k + 1) * rows, :] = silu(sender + own_term).astype(LOW)
+    message[...] = product(hidden[...], weights[2]).reshape(fan, rows, width)
+    total = normalize(message[0])[0]
+    for k in range(1, fan):
+        total = total + normalize(message[k])[0]
+    total_low = (total * gains[0:1, :]).astype(LOW)
     aggregate[...] = total_low
     node_mix = product(target_low, weights[3]) + product(total_low, weights[4])
     mix[...] = node_mix
-    node_hidden = (node_mix * sigmoid(node_mix)).astype(LOW)
-    node_out = product(node_hidden, weights[5])
+    node_out = product(silu(node_mix).astype(LOW), weights[5])
     out[...] = node_out
     updated = wide[...].astype(WIDE) + normalize(node_out)[0] * gains[1:2, :]
     updated_low = updated.astype(LOW)
@@ -173,6 +177,7 @@
         scratch_shapes=[
             pltpu.VMEM((3 * block_rows * parts, LANES), WIDE),
             pltpu.VMEM((fan * rows * parts, LANES), WIDE),
+            pltpu.VMEM((fan * rows, width), LOW),
         ],
         compiler_params=pltpu.CompilerParams(vmem_limit_bytes=VMEM_BYTES),
         cost_estimate=pl.CostEstimate(
@@ -200,7 +205,7 @@
     (slot_grad, grad_gains, grad_message, edge_hidden, grad_mix, grad_out, grad_own, hidden) = refs[
         :8
     ]
-    sum_even, sum_odd, spread = refs[8:]
+    sum_even, sum_odd, spread, grad_hidden = refs[8:]
     step = pl.program_id(0)
     rows, width = low.shape
     fan = kept.shape[0]
@@ -231,29 +236,31 @@
     out_low = normal_back(grad_new * gains[1:2, :], out_unit, out_scale).astype(LOW)
     grad_out[...] = out_low
     node_mix = mix[...]
-    gate = sigmoid(node_mix)
-    hidden[...] = (node_mix * gate).astype(LOW)
+    half, bend = silu_parts(node_mix)
+    hidden[...] = (half * (1.0 + bend)).astype(LOW)
     mix_low = (
-        product_right(out_low, weights[5]) * (gate * (1.0 + node_mix * (1.0 - gate)))
+        product_right(out_low, weights[5]) * ((0.5 + 0.5 * bend) * (1.0 + half * (1.0 - bend)))
     ).astype(LOW)
     grad_mix[...] = mix_low
     grad_sum = product_right(mix_low, weights[4])
     own_term = product(target_low, weights[1])
     grad_unit = grad_sum * gains[0:1, :]
-    unit_total = jnp.zeros((rows, width), WIDE)
-    own_total = jnp.zeros((rows, width), WIDE)
+    unit_total = None
     for k in range(fan):
         unit_rows, inv_scale = normalize(message[k])
-        unit_total = unit_total + unit_rows
-        message_low = normal_back(grad_unit, unit_rows, inv_scale).astype(LOW)
-        grad_message[k] = message_low
-        pre_edge = kept[k].astype(WIDE) + own_term
-        edge_gate = sigmoid(pre_edge)
-        edge_hidden[k] = (pre_edge * edge_gate).astype(LOW)
-        grad_pre = product_right(message_low, weights[2]) * (
-            edge_gate * (1.0 + pre_edge * (1.0 - edge_gate))
+        unit_total = unit_rows if k == 0 else unit_total + unit_rows
+        grad_message[k] = normal_back(grad_unit, unit_rows, inv_scale).astype(LOW)
+    grad_hidden[...] = product_right(
+        grad_message[...].reshape(fan * rows, width), weights[2]
+    )
+    own_total = None
+    for k in range(fan):
+        half, bend = silu_parts(kept[k].astype(WIDE) + own_term)
+        edge_hidden[k] = (half * (1.0 + bend)).astype(LOW)
+        grad_pre = grad_hidden[k * rows : (k + 1) * rows, :] * (
+            (0.5 + 0.5 * bend) * (1.0 + half * (1.0 - bend))
         )
-        own_total = own_total + grad_pre
+        own_total = grad_pre if k == 0 else own_total + grad_pre
         fold_rows(spread, k * rows, rows, grad_pre)
     gain_one = jnp.sum(grad_sum * unit_total, axis=0, keepdims=True)
     grad_gains[...] += jnp.concatenate([gain_one, gain_two], axis=0)
@@ -348,6 +355,7 @@
             pltpu.VMEM((3 * block_rows * parts, LANES), WIDE),
             pltpu.VMEM((3 * block_rows * parts, LANES), WIDE),
             pltpu.VMEM((fan * rows * parts, LANES), WIDE),
+            pltpu.VMEM((fan * rows, width), WIDE),
         ],
         compiler_params=pltpu.CompilerParams(vmem_limit_bytes=VMEM_BYTES),
         cost_estimate=pl.CostEstimate(
@@ -658,20 +666,26 @@
     return near + [swap(piece, count, 1) for piece in near]
 
 
-def gather_sum(keep, send, count):
-    pieces = combine([keep, swap(send, count, 1)], 4)
-    arrived = [pieces[0]] + [swap(pieces[digit], count, digit * 2) for digit in range(1, 4)]
-    pieces = combine(arrived, count // 8)
-    arrived = [pieces[0]]
-    arrived += [swap(pieces[digit], count, digit * 8) for digit in range(1, count // 8)]
+def shift(cells, count, step):
+    return lax.ppermute(cells, AXES, [(i, (i + step) % count) for i in range(count)])
+
+
+def fan_out(pieces, count, unit):
+    return [pieces[0]] + [
+        swap(pieces[digit], count, digit * unit) for digit in range(1, len(pieces))
+    ]
+
+
+def together(first, second):
+    joined = lax.optimization_barrier((tuple(first), tuple(second)))
+    return list(joined[0]), list(joined[1])
+
+
+def add_up(arrived):
     total = arrived[0][0]
     for part in arrived[1:]:
         total = total + part[0].astype(WIDE)
     return total
-
-
-def shift(cells, count, step):
-    return lax.ppermute(cells, AXES, [(i, (i + step) % count) for i in range(count)])
 
 
 def adamw_update(weight, moment_one, moment_two, gradient, step_value, decay_rate):
@@ -802,11 +816,19 @@
     above, above_source = None, None
     layer_grads = [None] * layer_total
     gain_grads = [None] * layer_total
+    in_plane, in_slice = [], []
     for layer_id in reversed(range(layer_total)):
         source_low, stored, aggregate = stored_list[layer_id]
         sent_grad, grad_new, slot_grad, grad_gain, *back = backward_layer(
             slot_lists[layer_id], above, grad_part, stored, weights[layer_id], gains[layer_id]
         )
+        far = []
+        if in_plane:
+            moved = len(in_plane)
+            arrived, (slot_grad,) = together(in_plane + in_slice, [slot_grad])
+            if in_slice:
+                layer_grads[layer_id + 2] = add_up(arrived[moved:]).reshape(6, share, width)
+            far = list(combine(arrived[:moved], device_count // 8))
         from_before = shift(slot_grad[2], device_count, 1)
         from_after = shift(slot_grad[0], device_count, -1)
         back = [back[1], back[0], *back[2:]]
@@ -821,12 +843,19 @@
             None if layer_id == 0 else grad_new,
             weights[layer_id],
         )
+        gain_grads[layer_id] = grad_gain
         if direct:
-            total = gather_sum(*sums, device_count)
-            layer_grads[layer_id] = total.reshape(6, share, width)
+            halo, arrived = together([from_before, from_after], [*sums, *far])
+            keep, send, far = arrived[0], arrived[1], arrived[2:]
+            in_slice = fan_out(far, device_count, 8) if far else []
+            other = swap(send, device_count, 1)
+            if layer_id > 0:
+                near = list(combine([keep, other], 4))
+                halo, near = together(halo, near)
+                in_plane = fan_out(near, device_count, 2)
+            from_before, from_after = halo
         else:
             layer_grads[layer_id] = sums[0]
-        gain_grads[layer_id] = grad_gain
         if layer_id == layer_total - 1:
             grad_grid, grad_part = grad_part, None
         above = (from_before, slot_grad, from_after, weights[layer_id])
@@ -849,7 +878,16 @@
             weights[0],
             misc,
         )
-        total = gather_sum(*sums, device_count)
+        arrived, sums = together([other] + in_slice, sums)
+        other, in_slice = arrived[0], arrived[1:]
+        near = combine([keep, other], 4)
+        layer_grads[1] = add_up(in_slice).reshape(6, share, width)
+        far = combine(fan_out(near, device_count, 2), device_count // 8)
+        layer_grads[0] = add_up(fan_out(far, device_count, 8)).reshape(6, share, width)
+        keep, send = sums
+        pieces = combine([keep, swap(send, device_count, 1)], 4)
+        pieces = combine(fan_out(pieces, device_count, 2), device_count // 8)
+        total = add_up(fan_out(pieces, device_count, 8))
         grad_zero = total[:share]
         grad_in = total[share : 2 * share, :channels].T
         size = layer_total * 2 * share

time: 829 us -> 656 us (0.79)
  waiting for transfers between devices: 244 us -> 143 us
  Pallas kernels: 354 us -> 312 us
  starting transfers between devices: 151 us -> 125 us
    ppermute x45, waiting for transfers between devices: 168 us -> 81.3 us  [swap(): return lax.ppermute(cells, AXES, [(i, i ^ mask) for i in range(count)])]
    ppermute x45, starting transfers between devices: 89.1 us -> 70.5 us  [swap(): return lax.ppermute(cells, AXES, [(i, i ^ mask) for i in range(count)])]
    ppermute x16, waiting for transfers between devices: 62.5 us -> 44.6 us  [shift(): lax.ppermute(cells, AXES, [(i, (i + step) % count) for i in range(count)])]
    pallas_call x4, Pallas kernels: 104 us -> 86.5 us  [forward_layer(): pl.pallas_call(functools.partial(forward_kernel, parts, has_next), grid=(...]
    pallas_call x4, Pallas kernels: 139 us -> 122 us  [backward_layer(): pl.pallas_call(functools.partial(backward_kernel, parts, mode), grid=(blo...]
    unnamed x151 -> x155, local copies, waits for them, and re-layouts: 17.2 us -> 14 us
  transfers between devices with their start and end apart: 63 -> 63, of which waited for: 27 -> 20; matrix products, arithmetic and copies ran while one was open for 3% -> 3% of each run, Pallas kernels for 25% -> 33%
where the time goes in v3:
time: 656 us; the launch traced here: 648 us
  Pallas kernels  312 us (48%)
  waiting for transfers between devices  143 us (22%)
  starting transfers between devices  125 us (19%)
  local copies, waits for them, and re-layouts  32.3 us (5%)
  between operations  17.5 us (3%)
  other arithmetic  12.5 us (2%)
    pallas_call x4, Pallas kernels, backward_layer(): pl.pallas_call(functools.partial(backward_kernel, parts, mode), grid=(blo...  122 us
    pallas_call x4, Pallas kernels, forward_layer(): pl.pallas_call(functools.partial(forward_kernel, parts, has_next), grid=(...  86.5 us
    ppermute x45, waiting for transfers between devices, swap(): return lax.ppermute(cells, AXES, [(i, i ^ mask) for i in range(count)])  81.3 us
    ppermute x45, starting transfers between devices, swap(): return lax.ppermute(cells, AXES, [(i, i ^ mask) for i in range(count)])  70.5 us
    pallas_call x4, Pallas kernels, weight_layer(): pl.pallas_call(functools.partial(weight_kernel, above is not None, grad_n...  54.6 us
    ppermute x16, starting transfers between devices, shift(): lax.ppermute(cells, AXES, [(i, (i + step) % count) for i in range(count)])  54.1 us
    ppermute x16, waiting for transfers between devices, shift(): lax.ppermute(cells, AXES, [(i, (i + step) % count) for i in range(count)])  44.6 us
    pallas_call x10, Pallas kernels, combine(): pl.pallas_call(functools.partial(combine_kernel, len(arrived)), grid=(res...  31.4 us
  transfers between devices with their start and end apart: 63, of which 20 were waited for; matrix products, arithmetic and copies ran while one was open for 3% of the time, Pallas kernels for 33%

profile of v3, /device:TPU:0, one launch (start us, length us, event | category | flops | bytes accessed | tf_op | source)
XLA Modules:
  0.0 647.9 jit_solution(855390366032016703)
XLA Ops:
  31.5 5.3 collective-permute-start.11
  38.4 18.2 %collective-permute-done.3.refs_2_ = bf16[4,120,512]{2,1,0:T(8,128)(2,1)} collective-permute-done((bf16[4,120,512]{2,1,0:T(8,128)(2,1)}, bf16[4,120,512]{2,1,0:T(8,128)(2,1)}, u32[]{:S(2)}, u32[]{:S(2)}) %collective-permute-start.3) | collective-permute-done | bytes 491552 | tf_op jit(solution)/shard_map/ppermute | solution.py:657
  62.2 21.3 %collective-permute-done.5.refs_4_ = bf16[4,120,512]{2,1,0:T(8,128)(2,1)S(1)} collective-permute-done((bf16[4,120,512]{2,1,0:T(8,128)(2,1)}, bf16[4,120,512]{2,1,0:T(8,128)(2,1)S(1)}, u32[]{:S(2)}, u32[]{:S(2)}) %collective-permute-start.5) | collective-permute-done | bytes 491552 | tf_op jit(solution)/shard_map/ppermute | solution.py:657
  92.0 9.6 %embed.1 = (bf16[6,512,512]{2,1,0:T(8,128)(2,1)}, f32[1024,512]{1,0:T(8,128)}, bf16[1024,512]{1,0:T(8,128)(2,1)}, bf16[1024,512]{1,0:T(8,128)(2,1)}, bf16[1024,5...) custom-call(s32[1]{0:T(128)} %bitcast.4.refs_0_.self_id, bf16[4,120,512]{2,1,0:T(8,128)(2,1)} %pad_maximum_fusion.refs_1_, ...), custom_call_target="tpu_custom_call" | custom-call | flops 3221225472 | bytes 12582912 | tf_op jit(solution)/shard_map/embed/pallas_call | solution.py:537
  101.7 21.9 %forward_layer.4 = (bf16[1024,512]{1,0:T(8,128)(2,1)}, f32[1024,512]{1,0:T(8,128)}, bf16[1024,512]{1,0:T(8,128)(2,1)}, bf16[4,1024,512]{2,1,0:T(8,128)(2,1)}, f3...) custom-call(s32[4096]{0:T(1024)} %bitcast.209, ...), custom_call_target="tpu_custom_call" | custom-call | flops 4831838208 | bytes 25165824 | tf_op jit(solution)/shard_map/forward_layer/pallas_call | solution.py:171
  123.8 5.2 collective-permute-start.13
  130.4 16.2 %collective-permute-done.12.refs_1_ = bf16[1024,512]{1,0:T(8,128)(2,1)S(1)} collective-permute-done((bf16[1024,512]{1,0:T(8,128)(2,1)}, bf16[1024,512]{1,0:T(8,128)(2,1)S(1)}, u32[]{:S(2)}, u32[]{:S(2)}) %collective-permute-start.12) | collective-permute-done | bytes 1048608 | tf_op jit(solution)/shard_map/ppermute | solution.py:670
  146.6 5.9 collective-permute-done.13.refs_3_
  152.5 17.4 %all-gather.4.cloned.1.call-done.refs_8_.refs_6_.refs_7_.refs_11_.refs_4_.refs_10_.refs_12_ = bf16[13,512,512]{2,1,0:T(8,128)(2,1)} async-done(((bf16[13,16,512]{2,1,0:T(8,128)(2,1)}), bf16[13,512,512]{2,1,0:T(8,128)(2,1)}) %all-gather.4.cloned.1.call-update) | async-done | bytes 6815760 | tf_op jit(solution)/shard_map/all_gather | solution.py:757
  169.9 21.9 %forward_layer.5 = (bf16[1024,512]{1,0:T(8,128)(2,1)}, f32[1024,512]{1,0:T(8,128)}, bf16[1024,512]{1,0:T(8,128)(2,1)}, bf16[4,1024,512]{2,1,0:T(8,128)(2,1)}, f3...) custom-call(s32[4096]{0:T(1024)} %bitcast.200, ...), custom_call_target="tpu_custom_call" | custom-call | flops 4831838208 | bytes 25165824 | tf_op jit(solution)/shard_map/forward_layer/pallas_call | solution.py:171
  198.1 11.9 %collective-permute-done.14.refs_1_ = bf16[1024,512]{1,0:T(8,128)(2,1)S(1)} collective-permute-done((bf16[1024,512]{1,0:T(8,128)(2,1)}, bf16[1024,512]{1,0:T(8,128)(2,1)S(1)}, u32[]{:S(2)}, u32[]{:S(2)}) %collective-permute-start.14) | collective-permute-done | bytes 1048608 | tf_op jit(solution)/shard_map/ppermute | solution.py:670
  211.4 21.9 %forward_layer.6 = (bf16[1024,512]{1,0:T(8,128)(2,1)}, f32[1024,512]{1,0:T(8,128)}, bf16[1024,512]{1,0:T(8,128)(2,1)}, bf16[4,1024,512]{2,1,0:T(8,128)(2,1)}, f3...) custom-call(s32[4096]{0:T(1024)} %bitcast.201, ...), custom_call_target="tpu_custom_call" | custom-call | flops 4831838208 | bytes 25165824 | tf_op jit(solution)/shard_map/forward_layer/pallas_call | solution.py:171
  233.3 7.1 %collective-permute-start.16 = (bf16[1024,512]{1,0:T(8,128)(2,1)}, bf16[1024,512]{1,0:T(8,128)(2,1)S(1)}, u32[]{:S(2)}, u32[]{:S(2)}) collective-permute-start(bf16[1024,512]{1,0:T(8,128)(2,1)} %get-tuple-element.224.refs_2_), channel_id=1, source_target_pairs={{0,1},{1,2},{2,3},{3,4},{4,5},{5,6},{6,7},{7,8},{8,9},{9,10},{10,1... | collective-permute-start | bytes 3145736 | tf_op jit(solution)/shard_map/ppermute | solution.py:670
  242.4 9.1 %collective-permute-done.16.refs_1_ = bf16[1024,512]{1,0:T(8,128)(2,1)S(1)} collective-permute-done((bf16[1024,512]{1,0:T(8,128)(2,1)}, bf16[1024,512]{1,0:T(8,128)(2,1)S(1)}, u32[]{:S(2)}, u32[]{:S(2)}) %collective-permute-start.16) | collective-permute-done | bytes 1048608 | tf_op jit(solution)/shard_map/ppermute | solution.py:670
  254.0 20.8 %forward_layer.7 = (bf16[1024,512]{1,0:T(8,128)(2,1)}, bf16[4,1024,512]{2,1,0:T(8,128)(2,1)}, f32[4,1024,512]{2,1,0:T(8,128)}, bf16[1024,512]{1,0:T(8,128)(2,1)}...) custom-call(s32[4096]{0:T(1024)} %bitcast.211, bf16[1024,512]{1,0:T(8,128)(2,1)} %copy-done.65, ...), custom_call_target="tpu_custom_call" | custom-call | flops 4831838208 | bytes 25165824 | tf_op jit(solution)/shard_map/forward_layer/pallas_call | solution.py:171
  280.1 30.0 %backward_layer.4 = (bf16[3,1024,512]{2,1,0:T(8,128)(2,1)}, f32[2,512]{1,0:T(2,128)}, bf16[4,1024,512]{2,1,0:T(8,128)(2,1)}, bf16[4,1024,512]{2,1,0:T(8,128)(2,1...) custom-call(s32[4096]{0:T(1024)} %bitcast.212, ...), custom_call_target="tpu_custom_call" | custom-call | flops 4294967296 | bytes 25165824 | tf_op jit(solution)/shard_map/backward_layer/pallas_call | solution.py:348
  311.9 13.6 %collective-permute-start.18 = (bf16[1024,512]{1,0:T(8,128)(2,1)S(1)}, bf16[1024,512]{1,0:T(8,128)(2,1)S(1)}, u32[]{:S(2)}, u32[]{:S(2)}) collective-permute-start(bf16[1024,512]{1,0:T(8,128)(2,1)S(1)} %get-tuple-element.436), channel_id=1, source_target_pairs={{0,1},{1,2},{2,3},{3,4},{4,5},{5,6},{6,7},{7,8},{8,9},{9,10},{10,1... | collective-permute-start | bytes 3145736 | tf_op jit(solution)/shard_map/ppermute | solution.py:670
  327.3 14.0 %weight_layer.4 = (f32[1024,512]{1,0:T(8,128)}, f32[16,96,512]{2,1,0:T(8,128)}, bf16[16,96,512]{2,1,0:T(8,128)(2,1)}) custom-call(s32[1]{0:T(128)} %bitcast.4.refs_0_.self_id, f32[512,512]{1,0:T(8,128)} %pad.29.refs_1_, bf16[1024,512]{1,0:T(8,128)(2,1)} %get-tuple-element.225.refs_4_.refs_2_.latent_low, bf16[1024,512]{1,0:T(8,128)(2,1)} %get-tuple-element.233.refs_3_, ...), custom_call_target="tpu_custom_call" | custom-call | flops 5368709120 | bytes 12582912 | tf_op jit(solution)/shard_map/weight_layer/pallas_call | solution.py:477
  341.3 10.2 %collective-permute-start.20 = (bf16[16,96,512]{2,1,0:T(8,128)(2,1)}, bf16[16,96,512]{2,1,0:T(8,128)(2,1)S(1)}, u32[]{:S(2)}, u32[]{:S(2)}) collective-permute-start(bf16[16,96,512]{2,1,0:T(8,128)(2,1)} %get-tuple-element.245), channel_id=1, source_target_pairs={{0,1},{1,0},{2,3},{3,2},{4,5},{5,4},{6,7},{7,6},{8,9},{9,8},{10,11... | collective-permute-start | bytes 4718600 | tf_op jit(solution)/shard_map/ppermute | solution.py:657
  363.9 30.6 %backward_layer.5 = (bf16[1024,512]{1,0:T(8,128)(2,1)}, f32[1024,512]{1,0:T(8,128)}, bf16[3,1024,512]{2,1,0:T(8,128)(2,1)}, f32[2,512]{1,0:T(2,128)}, bf16[4,102...) custom-call(s32[4096]{0:T(1024)} %bitcast.202, ...), custom_call_target="tpu_custom_call" | custom-call | flops 4294967296 | bytes 25165824 | tf_op jit(solution)/shard_map/backward_layer/pallas_call | solution.py:348
  396.7 5.7 collective-permute-start.25
  402.4 14.4 %weight_layer.5 = (f32[1024,512]{1,0:T(8,128)}, f32[16,96,512]{2,1,0:T(8,128)}, bf16[16,96,512]{2,1,0:T(8,128)(2,1)}) custom-call(s32[1]{0:T(128)} %bitcast.4.refs_0_.self_id, bf16[1024,512]{1,0:T(8,128)(2,1)} %get-tuple-element.262.refs_1_, bf16[1024,512]{1,0:T(8,128)(2,1)} %get-tuple-element.263.refs_2_, ...), custom_call_target="tpu_custom_call" | custom-call | flops 5368709120 | bytes 12582912 | tf_op jit(solution)/shard_map/weight_layer/pallas_call | solution.py:477
  436.2 30.8 %backward_layer.6 = (bf16[1024,512]{1,0:T(8,128)(2,1)}, f32[1024,512]{1,0:T(8,128)}, bf16[3,1024,512]{2,1,0:T(8,128)(2,1)}, f32[2,512]{1,0:T(2,128)}, bf16[4,102...) custom-call(s32[4096]{0:T(1024)} %bitcast.203, ...), custom_call_target="tpu_custom_call" | custom-call | flops 4294967296 | bytes 25165824 | tf_op jit(solution)/shard_map/backward_layer/pallas_call | solution.py:348
  469.3 5.5 collective-permute-start.34
  474.8 14.4 %weight_layer.6 = (f32[1024,512]{1,0:T(8,128)}, f32[16,96,512]{2,1,0:T(8,128)}, bf16[16,96,512]{2,1,0:T(8,128)(2,1)}) custom-call(s32[1]{0:T(128)} %bitcast.4.refs_0_.self_id, bf16[1024,512]{1,0:T(8,128)(2,1)} %get-tuple-element.222.refs_4_.refs_5_.refs_3_.refs_1_, bf16[1024,512]{1,0:T(8,128)(2,1)} %get-tuple-element.307.refs_2_, ...), custom_call_target="tpu_custom_call" | custom-call | flops 5368709120 | bytes 12582912 | tf_op jit(solution)/shard_map/weight_layer/pallas_call | solution.py:477
  508.5 30.8 %backward_layer.7 = (bf16[1024,512]{1,0:T(8,128)(2,1)}, f32[1024,512]{1,0:T(8,128)}, bf16[3,1024,512]{2,1,0:T(8,128)(2,1)}, f32[2,512]{1,0:T(2,128)}, bf16[4,102...) custom-call(s32[4096]{0:T(1024)} %bitcast.210, ...), custom_call_target="tpu_custom_call" | custom-call | flops 4294967296 | bytes 25165824 | tf_op jit(solution)/shard_map/backward_layer/pallas_call | solution.py:348
  541.6 5.5 collective-permute-start.43
  547.1 11.8 %weight_layer.7 = (f32[16,96,512]{2,1,0:T(8,128)}, bf16[16,96,512]{2,1,0:T(8,128)(2,1)}) custom-call(s32[1]{0:T(128)} %bitcast.4.refs_0_.self_id, bf16[1024,512]{1,0:T(8,128)(2,1)} %get-tuple-element.219.refs_4_.refs_6_.refs_3_.refs_1_, bf16[1024,512]{1,0:T(8,128)(2,1)} %get-tuple-element.351.refs_2_, bf16[1024,512]{1,0:T(8,128)(2,1)} %refs_3_.1, ...), custom_call_target="tpu_custom_call" | custom-call | flops 5368709120 | bytes 12582912 | tf_op jit(solution)/shard_map/weight_layer/pallas_call | solution.py:477
  562.3 6.5 %collective-permute-start.44 = (bf16[16,96,512]{2,1,0:T(8,128)(2,1)}, bf16[16,96,512]{2,1,0:T(8,128)(2,1)S(1)}, u32[]{:S(2)}, u32[]{:S(2)}) collective-permute-start(bf16[16,96,512]{2,1,0:T(8,128)(2,1)} %get-tuple-element.369), channel_id=1, source_target_pairs={{0,1},{1,0},{2,3},{3,2},{4,5},{5,4},{6,7},{7,6},{8,9},{9,8},{10,11... | collective-permute-start | bytes 4718600 | tf_op jit(solution)/shard_map/ppermute | solution.py:657
  575.1 7.4 %tail_layer.1 = (f32[16,40,512]{2,1,0:T(8,128)}, bf16[16,40,512]{2,1,0:T(8,128)(2,1)}) custom-call(s32[1]{0:T(128)} %bitcast.4.refs_0_.self_id, bf16[1024,512]{1,0:T(8,128)(2,1)} %copy-done.9, bf16[3,1024,512]{2,1,0:T(8,128)(2,1)} %get-tuple-element.350.middle, bf16[1024,512]{1,0:T(8,128)(2,1)} %copy-done.10, ...), custom_call_target="tpu_custom_call" | custom-call | flops 1610612736 | bytes 12582912 | tf_op jit(solution)/shard_map/tail_layer/pallas_call | solution.py:597
  600.1 7.0 %collective-permute-done.56 = bf16[4,96,512]{2,1,0:T(8,128)(2,1)S(1)} collective-permute-done((bf16[4,96,512]{2,1,0:T(8,128)(2,1)}, bf16[4,96,512]{2,1,0:T(8,128)(2,1)S(1)}, u32[]{:S(2)}, u32[]{:S(2)}) %collective-permute-start.56) | collective-permute-done | bytes 393248 | tf_op jit(solution)/shard_map/ppermute | solution.py:657
  618.9 6.1 collective-permute-done.50
  (339 shorter events, 172.2 us)
Async XLA Ops:
  7.2 94.4 %all-gather.6.cloned.1.call-start = ((), (), s32[]{:S(2)}) async-start(), calls=%async_computation.1 | async-start | bytes 3244032 | tf_op jit(solution)/shard_map/all_gather | solution.py:756
  9.2 160.7 %all-gather.4.cloned.1.call-start = ((), (), s32[]{:S(2)}) async-start(), calls=%async_computation | async-start | bytes 7028736 | tf_op jit(solution)/shard_map/all_gather | solution.py:757
  29.3 27.4 %collective-permute-start.3 = (bf16[4,120,512]{2,1,0:T(8,128)(2,1)}, bf16[4,120,512]{2,1,0:T(8,128)(2,1)}, u32[]{:S(2)}, u32[]{:S(2)}) collective-permute-start(bf16[4,120,512]{2,1,0:T(8,128)(2,1)} %pad_maximum_fusion.refs_1_), channel_id=1, source_target_pairs={{0,2},{1,3},{2,0},{3,1},{4,6},{5,7},{6,4},{7,5},{8,10},{9,11},{10,... | collective-permute-start | bytes 1474568 | tf_op jit(solution)/shard_map/ppermute | solution.py:657
  31.5 60.5 %collective-permute-start.10 = (bf16[1024,512]{1,0:T(8,128)(2,1)S(1)}, bf16[1024,512]{1,0:T(8,128)(2,1)}, u32[]{:S(2)}, u32[]{:S(2)}) collective-permute-start(bf16[1024,512]{1,0:T(8,128)(2,1)S(1)} %pad.27.refs_10_.inputs), channel_id=1, source_target_pairs={{0,1},{1,2},{2,3},{3,4},{4,5},{5,6},{6,7},{7,8},{8,9},{9,10},{10,1... | collective-permute-start | bytes 3145736 | tf_op jit(solution)/shard_map/ppermute | solution.py:670
  31.5 60.4 %collective-permute-start.11 = (bf16[1024,512]{1,0:T(8,128)(2,1)S(1)}, bf16[1024,512]{1,0:T(8,128)(2,1)}, u32[]{:S(2)}, u32[]{:S(2)}) collective-permute-start(bf16[1024,512]{1,0:T(8,128)(2,1)S(1)} %pad.27.refs_10_.inputs), channel_id=1, source_target_pairs={{0,31},{1,0},{2,1},{3,2},{4,3},{5,4},{6,5},{7,6},{8,7},{9,8},{10,9... | collective-permute-start | bytes 3145736 | tf_op jit(solution)/shard_map/ppermute | solution.py:670
  36.9 25.3 %collective-permute-start.4 = (bf16[4,120,512]{2,1,0:T(8,128)(2,1)}, bf16[4,120,512]{2,1,0:T(8,128)(2,1)S(1)}, u32[]{:S(2)}, u32[]{:S(2)}) collective-permute-start(bf16[4,120,512]{2,1,0:T(8,128)(2,1)} %pad_maximum_fusion.refs_1_), channel_id=1, source_target_pairs={{0,4},{1,5},{2,6},{3,7},{4,0},{5,1},{6,2},{7,3},{8,12},{9,13},{10,... | collective-permute-start | bytes 1474568 | tf_op jit(solution)/shard_map/ppermute | solution.py:657
  37.5 46.0 %collective-permute-start.5 = (bf16[4,120,512]{2,1,0:T(8,128)(2,1)}, bf16[4,120,512]{2,1,0:T(8,128)(2,1)S(1)}, u32[]{:S(2)}, u32[]{:S(2)}) collective-permute-start(bf16[4,120,512]{2,1,0:T(8,128)(2,1)} %pad_maximum_fusion.refs_1_), channel_id=1, source_target_pairs={{0,6},{1,7},{2,4},{3,5},{4,2},{5,3},{6,0},{7,1},{8,14},{9,15},{10,... | collective-permute-start | bytes 1474568 | tf_op jit(solution)/shard_map/ppermute | solution.py:657
  56.6 26.9 %collective-permute-start.6 = (bf16[4,120,512]{2,1,0:T(8,128)(2,1)}, bf16[4,120,512]{2,1,0:T(8,128)(2,1)S(1)}, u32[]{:S(2)}, u32[]{:S(2)}) collective-permute-start(bf16[4,120,512]{2,1,0:T(8,128)(2,1)} %pad_maximum_fusion.refs_1_), channel_id=1, source_target_pairs={{0,1},{1,0},{2,3},{3,2},{4,5},{5,4},{6,7},{7,6},{8,9},{9,8},{10,11... | collective-permute-start | bytes 1474568 | tf_op jit(solution)/shard_map/ppermute | solution.py:657
  62.1 22.1 %collective-permute-start.7 = (bf16[4,120,512]{2,1,0:T(8,128)(2,1)}, bf16[4,120,512]{2,1,0:T(8,128)(2,1)S(1)}, u32[]{:S(2)}, u32[]{:S(2)}) collective-permute-start(bf16[4,120,512]{2,1,0:T(8,128)(2,1)} %collective-permute-done.3.refs_2_), channel_id=1, source_target_pairs={{0,1},{1,0},{2,3},{3,2},{4,5},{5,4},{6,7},{7,6},{8,9},{9,8},{10,11... | collective-permute-start | bytes 1474568 | tf_op jit(solution)/shard_map/ppermute | solution.py:657
  123.6 23.0 %collective-permute-start.12 = (bf16[1024,512]{1,0:T(8,128)(2,1)}, bf16[1024,512]{1,0:T(8,128)(2,1)S(1)}, u32[]{:S(2)}, u32[]{:S(2)}) collective-permute-start(bf16[1024,512]{1,0:T(8,128)(2,1)} %get-tuple-element.218.refs_2_), channel_id=1, source_target_pairs={{0,1},{1,2},{2,3},{3,4},{4,5},{5,6},{6,7},{7,8},{8,9},{9,10},{10,1... | collective-permute-start | bytes 3145736 | tf_op jit(solution)/shard_map/ppermute | solution.py:670
  123.8 28.7 %collective-permute-start.13 = (bf16[1024,512]{1,0:T(8,128)(2,1)}, bf16[1024,512]{1,0:T(8,128)(2,1)S(1)}, u32[]{:S(2)}, u32[]{:S(2)}) collective-permute-start(bf16[1024,512]{1,0:T(8,128)(2,1)} %get-tuple-element.218.refs_2_), channel_id=1, source_target_pairs={{0,31},{1,0},{2,1},{3,2},{4,3},{5,4},{6,5},{7,6},{8,7},{9,8},{10,9... | collective-permute-start | bytes 3145736 | tf_op jit(solution)/shard_map/ppermute | solution.py:670
  311.9 29.4 %collective-permute-start.18 = (bf16[1024,512]{1,0:T(8,128)(2,1)S(1)}, bf16[1024,512]{1,0:T(8,128)(2,1)S(1)}, u32[]{:S(2)}, u32[]{:S(2)}) collective-permute-start(bf16[1024,512]{1,0:T(8,128)(2,1)S(1)} %get-tuple-element.436), channel_id=1, source_target_pairs={{0,1},{1,2},{2,3},{3,4},{4,5},{5,6},{6,7},{7,8},{8,9},{9,10},{10,1... | collective-permute-start | bytes 3145736 | tf_op jit(solution)/shard_map/ppermute | solution.py:670
  360.1 34.4 %collective-permute-start.21 = (bf16[4,96,512]{2,1,0:T(8,128)(2,1)}, bf16[4,96,512]{2,1,0:T(8,128)(2,1)S(1)}, u32[]{:S(2)}, u32[]{:S(2)}) collective-permute-start(bf16[4,96,512]{2,1,0:T(8,128)(2,1)} %get-tuple-element.251), channel_id=1, source_target_pairs={{0,2},{1,3},{2,0},{3,1},{4,6},{5,7},{6,4},{7,5},{8,10},{9,11},{10,... | collective-permute-start | bytes 1179656 | tf_op jit(solution)/shard_map/ppermute | solution.py:657
  360.5 34.1 %collective-permute-start.22 = (bf16[4,96,512]{2,1,0:T(8,128)(2,1)}, bf16[4,96,512]{2,1,0:T(8,128)(2,1)S(1)}, u32[]{:S(2)}, u32[]{:S(2)}) collective-permute-start(bf16[4,96,512]{2,1,0:T(8,128)(2,1)} %get-tuple-element.252), channel_id=1, source_target_pairs={{0,4},{1,5},{2,6},{3,7},{4,0},{5,1},{6,2},{7,3},{8,12},{9,13},{10,... | collective-permute-start | bytes 1179656 | tf_op jit(solution)/shard_map/ppermute | solution.py:657
  362.5 32.0 %collective-permute-start.23 = (bf16[4,96,512]{2,1,0:T(8,128)(2,1)}, bf16[4,96,512]{2,1,0:T(8,128)(2,1)S(1)}, u32[]{:S(2)}, u32[]{:S(2)}) collective-permute-start(bf16[4,96,512]{2,1,0:T(8,128)(2,1)} %get-tuple-element.253), channel_id=1, source_target_pairs={{0,6},{1,7},{2,4},{3,5},{4,2},{5,3},{6,0},{7,1},{8,14},{9,15},{10,... | collective-permute-start | bytes 1179656 | tf_op jit(solution)/shard_map/ppermute | solution.py:657
  396.6 22.5 %collective-permute-start.24 = (bf16[1024,512]{1,0:T(8,128)(2,1)S(1)}, bf16[1024,512]{1,0:T(8,128)(2,1)S(1)}, u32[]{:S(2)}, u32[]{:S(2)}) collective-permute-start(bf16[1024,512]{1,0:T(8,128)(2,1)S(1)} %get-tuple-element.434), channel_id=1, source_target_pairs={{0,1},{1,2},{2,3},{3,4},{4,5},{5,6},{6,7},{7,8},{8,9},{9,10},{10,1... | collective-permute-start | bytes 3145736 | tf_op jit(solution)/shard_map/ppermute | solution.py:670
  396.7 22.5 %collective-permute-start.25 = (bf16[1024,512]{1,0:T(8,128)(2,1)S(1)}, bf16[1024,512]{1,0:T(8,128)(2,1)S(1)}, u32[]{:S(2)}, u32[]{:S(2)}) collective-permute-start(bf16[1024,512]{1,0:T(8,128)(2,1)S(1)} %get-tuple-element.433), channel_id=1, source_target_pairs={{0,31},{1,0},{2,1},{3,2},{4,3},{5,4},{6,5},{7,6},{8,7},{9,8},{10,9... | collective-permute-start | bytes 3145736 | tf_op jit(solution)/shard_map/ppermute | solution.py:670
  423.0 44.0 %collective-permute-start.31 = (bf16[1,96,512]{2,1,0:T(8,128)(2,1)}, bf16[1,96,512]{2,1,0:T(8,128)(2,1)S(1)}, u32[]{:S(2)}, u32[]{:S(2)}) collective-permute-start(bf16[1,96,512]{2,1,0:T(8,128)(2,1)} %get-tuple-element.296), channel_id=1, source_target_pairs={{0,16},{1,17},{2,18},{3,19},{4,20},{5,21},{6,22},{7,23},{8,24},{9,... | collective-permute-start | bytes 294920 | tf_op jit(solution)/shard_map/ppermute | solution.py:657
  423.2 43.9 %collective-permute-start.32 = (bf16[1,96,512]{2,1,0:T(8,128)(2,1)}, bf16[1,96,512]{2,1,0:T(8,128)(2,1)S(1)}, u32[]{:S(2)}, u32[]{:S(2)}) collective-permute-start(bf16[1,96,512]{2,1,0:T(8,128)(2,1)} %get-tuple-element.297), channel_id=1, source_target_pairs={{0,24},{1,25},{2,26},{3,27},{4,28},{5,29},{6,30},{7,31},{8,16},{9,... | collective-permute-start | bytes 294920 | tf_op jit(solution)/shard_map/ppermute | solution.py:657
  432.7 34.4 %collective-permute-start.27 = (bf16[4,96,512]{2,1,0:T(8,128)(2,1)}, bf16[4,96,512]{2,1,0:T(8,128)(2,1)S(1)}, u32[]{:S(2)}, u32[]{:S(2)}) collective-permute-start(bf16[4,96,512]{2,1,0:T(8,128)(2,1)} %get-tuple-element.291), channel_id=1, source_target_pairs={{0,2},{1,3},{2,0},{3,1},{4,6},{5,7},{6,4},{7,5},{8,10},{9,11},{10,... | collective-permute-start | bytes 1179656 | tf_op jit(solution)/shard_map/ppermute | solution.py:657
  433.2 33.9 %collective-permute-start.28 = (bf16[4,96,512]{2,1,0:T(8,128)(2,1)}, bf16[4,96,512]{2,1,0:T(8,128)(2,1)S(1)}, u32[]{:S(2)}, u32[]{:S(2)}) collective-permute-start(bf16[4,96,512]{2,1,0:T(8,128)(2,1)} %get-tuple-element.292), channel_id=1, source_target_pairs={{0,4},{1,5},{2,6},{3,7},{4,0},{5,1},{6,2},{7,3},{8,12},{9,13},{10,... | collective-permute-start | bytes 1179656 | tf_op jit(solution)/shard_map/ppermute | solution.py:657
  434.8 32.3 %collective-permute-start.29 = (bf16[4,96,512]{2,1,0:T(8,128)(2,1)}, bf16[4,96,512]{2,1,0:T(8,128)(2,1)S(1)}, u32[]{:S(2)}, u32[]{:S(2)}) collective-permute-start(bf16[4,96,512]{2,1,0:T(8,128)(2,1)} %get-tuple-element.293), channel_id=1, source_target_pairs={{0,6},{1,7},{2,4},{3,5},{4,2},{5,3},{6,0},{7,1},{8,14},{9,15},{10,... | collective-permute-start | bytes 1179656 | tf_op jit(solution)/shard_map/ppermute | solution.py:657
  469.2 22.3 %collective-permute-start.33 = (bf16[1024,512]{1,0:T(8,128)(2,1)S(1)}, bf16[1024,512]{1,0:T(8,128)(2,1)S(1)}, u32[]{:S(2)}, u32[]{:S(2)}) collective-permute-start(bf16[1024,512]{1,0:T(8,128)(2,1)S(1)} %get-tuple-element.432), channel_id=1, source_target_pairs={{0,1},{1,2},{2,3},{3,4},{4,5},{5,6},{6,7},{7,8},{8,9},{9,10},{10,1... | collective-permute-start | bytes 3145736 | tf_op jit(solution)/shard_map/ppermute | solution.py:670
  469.3 22.2 %collective-permute-start.34 = (bf16[1024,512]{1,0:T(8,128)(2,1)S(1)}, bf16[1024,512]{1,0:T(8,128)(2,1)S(1)}, u32[]{:S(2)}, u32[]{:S(2)}) collective-permute-start(bf16[1024,512]{1,0:T(8,128)(2,1)S(1)} %get-tuple-element.431), channel_id=1, source_target_pairs={{0,31},{1,0},{2,1},{3,2},{4,3},{5,4},{6,5},{7,6},{8,7},{9,8},{10,9... | collective-permute-start | bytes 3145736 | tf_op jit(solution)/shard_map/ppermute | solution.py:670
  495.2 44.2 %collective-permute-start.40 = (bf16[1,96,512]{2,1,0:T(8,128)(2,1)}, bf16[1,96,512]{2,1,0:T(8,128)(2,1)S(1)}, u32[]{:S(2)}, u32[]{:S(2)}) collective-permute-start(bf16[1,96,512]{2,1,0:T(8,128)(2,1)} %get-tuple-element.340), channel_id=1, source_target_pairs={{0,16},{1,17},{2,18},{3,19},{4,20},{5,21},{6,22},{7,23},{8,24},{9,... | collective-permute-start | bytes 294920 | tf_op jit(solution)/shard_map/ppermute | solution.py:657
  496.5 42.8 %collective-permute-start.41 = (bf16[1,96,512]{2,1,0:T(8,128)(2,1)}, bf16[1,96,512]{2,1,0:T(8,128)(2,1)S(1)}, u32[]{:S(2)}, u32[]{:S(2)}) collective-permute-start(bf16[1,96,512]{2,1,0:T(8,128)(2,1)} %get-tuple-element.341), channel_id=1, source_target_pairs={{0,24},{1,25},{2,26},{3,27},{4,28},{5,29},{6,30},{7,31},{8,16},{9,... | collective-permute-start | bytes 294920 | tf_op jit(solution)/shard_map/ppermute | solution.py:657
  504.9 34.5 %collective-permute-start.36 = (bf16[4,96,512]{2,1,0:T(8,128)(2,1)}, bf16[4,96,512]{2,1,0:T(8,128)(2,1)S(1)}, u32[]{:S(2)}, u32[]{:S(2)}) collective-permute-start(bf16[4,96,512]{2,1,0:T(8,128)(2,1)} %get-tuple-element.335), channel_id=1, source_target_pairs={{0,2},{1,3},{2,0},{3,1},{4,6},{5,7},{6,4},{7,5},{8,10},{9,11},{10,... | collective-permute-start | bytes 1179656 | tf_op jit(solution)/shard_map/ppermute | solution.py:657
  505.8 33.6 %collective-permute-start.37 = (bf16[4,96,512]{2,1,0:T(8,128)(2,1)}, bf16[4,96,512]{2,1,0:T(8,128)(2,1)S(1)}, u32[]{:S(2)}, u32[]{:S(2)}) collective-permute-start(bf16[4,96,512]{2,1,0:T(8,128)(2,1)} %get-tuple-element.336), channel_id=1, source_target_pairs={{0,4},{1,5},{2,6},{3,7},{4,0},{5,1},{6,2},{7,3},{8,12},{9,13},{10,... | collective-permute-start | bytes 1179656 | tf_op jit(solution)/shard_map/ppermute | solution.py:657
  507.2 32.3 %collective-permute-start.38 = (bf16[4,96,512]{2,1,0:T(8,128)(2,1)}, bf16[4,96,512]{2,1,0:T(8,128)(2,1)S(1)}, u32[]{:S(2)}, u32[]{:S(2)}) collective-permute-start(bf16[4,96,512]{2,1,0:T(8,128)(2,1)} %get-tuple-element.337), channel_id=1, source_target_pairs={{0,6},{1,7},{2,4},{3,5},{4,2},{5,3},{6,0},{7,1},{8,14},{9,15},{10,... | collective-permute-start | bytes 1179656 | tf_op jit(solution)/shard_map/ppermute | solution.py:657
  562.3 20.2 %collective-permute-start.44 = (bf16[16,96,512]{2,1,0:T(8,128)(2,1)}, bf16[16,96,512]{2,1,0:T(8,128)(2,1)S(1)}, u32[]{:S(2)}, u32[]{:S(2)}) collective-permute-start(bf16[16,96,512]{2,1,0:T(8,128)(2,1)} %get-tuple-element.369), channel_id=1, source_target_pairs={{0,1},{1,0},{2,3},{3,2},{4,5},{5,4},{6,7},{7,6},{8,9},{9,8},{10,11... | collective-permute-start | bytes 4718600 | tf_op jit(solution)/shard_map/ppermute | solution.py:657
  589.9 19.9 %collective-permute-start.57 = (bf16[4,96,512]{2,1,0:T(8,128)(2,1)}, bf16[4,96,512]{2,1,0:T(8,128)(2,1)S(1)}, u32[]{:S(2)}, u32[]{:S(2)}) collective-permute-start(bf16[4,96,512]{2,1,0:T(8,128)(2,1)} %get-tuple-element.398), channel_id=1, source_target_pairs={{0,6},{1,7},{2,4},{3,5},{4,2},{5,3},{6,0},{7,1},{8,14},{9,15},{10,... | collective-permute-start | bytes 1179656 | tf_op jit(solution)/shard_map/ppermute | solution.py:657
  596.4 21.1 %collective-permute-start.49 = (bf16[4,40,512]{2,1,0:T(8,128)(2,1)}, bf16[4,40,512]{2,1,0:T(8,128)(2,1)S(1)}, u32[]{:S(2)}, u32[]{:S(2)}) collective-permute-start(bf16[4,40,512]{2,1,0:T(8,128)(2,1)} %get-tuple-element.386), channel_id=1, source_target_pairs={{0,2},{1,3},{2,0},{3,1},{4,6},{5,7},{6,4},{7,5},{8,10},{9,11},{10,... | collective-permute-start | bytes 491528 | tf_op jit(solution)/shard_map/ppermute | solution.py:657
  (100 other events, 1519.2 us)
Sparse Core Ops, SparseCore 0:
  10.9 77.0 all-gather.5
  90.9 78.9 all-gather.3

commit v4 on v3

--- a/solution.py
+++ b/solution.py
@@ -20,7 +20,6 @@
 BACKWARD_ROWS = 256
 WEIGHT_ROWS = 256
 UNROLL = 32
-VMEM_BYTES = 56 << 20
 LOW = jnp.bfloat16
 WIDE = jnp.float32
 SEND = jnp.bfloat16
@@ -79,12 +78,12 @@
 def forward_kernel(parts, has_next, *refs):
     if has_next:
         (slots, before, middle, after, low, wide, weights, gains, head) = refs[:9]
-        (sent, update, update_low, kept, message, aggregate, mix, out) = refs[9:17]
-        window, picked, hidden = refs[17:]
+        (sent, update, update_low, kept, aggregate) = refs[9:14]
+        window, picked, hidden, message = refs[14:]
     else:
         (slots, before, middle, after, low, wide, weights, gains) = refs[:8]
-        (update_low, kept, message, aggregate, mix, out) = refs[8:14]
-        window, picked, hidden = refs[14:]
+        (update_low, kept, aggregate) = refs[8:11]
+        window, picked, hidden, message = refs[11:]
     step = pl.program_id(0)
     block_rows = before.shape[0]
     rows, width = low.shape
@@ -113,16 +112,14 @@
         sender = unfold_rows(picked, k * rows, rows, parts)
         kept[k] = sender.astype(LOW)
         hidden[k * rows : (k + 1) * rows, :] = silu(sender + own_term).astype(LOW)
-    message[...] = product(hidden[...], weights[2]).reshape(fan, rows, width)
-    total = normalize(message[0])[0]
+    message[...] = product(hidden[...], weights[2])
+    total = normalize(message[0:rows, :])[0]
     for k in range(1, fan):
-        total = total + normalize(message[k])[0]
+        total = total + normalize(message[k * rows : (k + 1) * rows, :])[0]
     total_low = (total * gains[0:1, :]).astype(LOW)
     aggregate[...] = total_low
     node_mix = product(target_low, weights[3]) + product(total_low, weights[4])
-    mix[...] = node_mix
     node_out = product(silu(node_mix).astype(LOW), weights[5])
-    out[...] = node_out
     updated = wide[...].astype(WIDE) + normalize(node_out)[0] * gains[1:2, :]
     updated_low = updated.astype(LOW)
     update_low[...] = updated_low
@@ -133,11 +130,13 @@
 
 def whole(shape):
     zeros = (0,) * len(shape)
-    return pl.BlockSpec(shape, lambda step: zeros)
+    return pl.BlockSpec(shape, lambda step: zeros, pipeline_mode=pl.Buffered(1))
 
 
 def matrix_spec(first, count, width):
-    return pl.BlockSpec((count, width, width), lambda step: (first // count, 0, 0))
+    return pl.BlockSpec(
+        (count, width, width), lambda step: (first // count, 0, 0), pipeline_mode=pl.Buffered(1)
+    )
 
 
 def tiled(rows, width):
@@ -160,8 +159,8 @@
     in_specs = [pl.BlockSpec(memory_space=pltpu.SMEM)]
     in_specs += [whole((block_rows, width))] * 3 + [tile, tile]
     in_specs += [matrix_spec(weights[1], 6, width), whole(gains.shape)]
-    out_specs = [tile, fanned(fan, rows, width), fanned(fan, rows, width), tile, tile, tile]
-    out_shape = [shape(LOW), fan_shape(LOW), fan_shape(WIDE), shape(LOW), shape(WIDE), shape(WIDE)]
+    out_specs = [tile, fanned(fan, rows, width), tile]
+    out_shape = [shape(LOW), fan_shape(LOW), shape(LOW)]
     operands = [slots, *blocks, target_low, target, weights[0], gains]
     if has_next:
         in_specs += [matrix_spec(next_weights[1], 1, width)]
@@ -178,8 +177,9 @@
             pltpu.VMEM((3 * block_rows * parts, LANES), WIDE),
             pltpu.VMEM((fan * rows * parts, LANES), WIDE),
             pltpu.VMEM((fan * rows, width), LOW),
+            pltpu.VMEM((fan * rows, width), WIDE),
         ],
-        compiler_params=pltpu.CompilerParams(vmem_limit_bytes=VMEM_BYTES),
+        compiler_params=pltpu.CompilerParams(vmem_limit_bytes=28 << 20),
         cost_estimate=pl.CostEstimate(
             flops=2 * (fan + 5) * block_rows * width * width,
             transcendentals=(fan + 1) * block_rows * width,
@@ -197,19 +197,18 @@
         head = refs.pop(0)
     if mode != "second":
         grad_part = refs.pop(0)
-    low, kept, message, mix, out, weights, gains = refs[:7]
-    refs = refs[7:]
+    low, kept, aggregate, weights, gains = refs[:5]
+    refs = refs[5:]
     if mode != "first":
         sent_grad = refs.pop(0)
         grad_full = refs.pop(0)
-    (slot_grad, grad_gains, grad_message, edge_hidden, grad_mix, grad_out, grad_own, hidden) = refs[
-        :8
-    ]
-    sum_even, sum_odd, spread, grad_hidden = refs[8:]
+    slot_grads = refs[:3]
+    (grad_gains, grad_message, edge_hidden, grad_mix, grad_out, grad_own, hidden) = refs[3:10]
+    sum_even, sum_odd, spread, stage = refs[10:]
     step = pl.program_id(0)
     rows, width = low.shape
     fan = kept.shape[0]
-    block_rows = slot_grad.shape[1]
+    block_rows = slot_grads[0].shape[0]
 
     @pl.when(step == 0)
     def _():
@@ -222,7 +221,7 @@
     else:
         sent_low = (
             returned[0][...].astype(WIDE)
-            + returned[1][...].reshape(rows, width).astype(WIDE)
+            + returned[1][...].astype(WIDE)
             + returned[2][...].astype(WIDE)
         ).astype(LOW)
         sent_grad[...] = sent_low
@@ -231,33 +230,34 @@
             grad_new = grad_part[...] + grad_new
         grad_full[...] = grad_new
     target_low = low[...]
-    out_unit, out_scale = normalize(out[...])
+    own_term = product(target_low, weights[1])
+    node_mix = product(target_low, weights[3]) + product(aggregate[...], weights[4])
+    for k in range(fan):
+        edge_hidden[k] = silu(kept[k].astype(WIDE) + own_term).astype(LOW)
+    stage[...] = product(edge_hidden[...].reshape(fan * rows, width), weights[2])
+    half, bend = silu_parts(node_mix)
+    node_hidden = (half * (1.0 + bend)).astype(LOW)
+    hidden[...] = node_hidden
+    out_unit, out_scale = normalize(product(node_hidden, weights[5]))
     gain_two = jnp.sum(grad_new * out_unit, axis=0, keepdims=True)
     out_low = normal_back(grad_new * gains[1:2, :], out_unit, out_scale).astype(LOW)
     grad_out[...] = out_low
-    node_mix = mix[...]
-    half, bend = silu_parts(node_mix)
-    hidden[...] = (half * (1.0 + bend)).astype(LOW)
     mix_low = (
         product_right(out_low, weights[5]) * ((0.5 + 0.5 * bend) * (1.0 + half * (1.0 - bend)))
     ).astype(LOW)
     grad_mix[...] = mix_low
     grad_sum = product_right(mix_low, weights[4])
-    own_term = product(target_low, weights[1])
     grad_unit = grad_sum * gains[0:1, :]
     unit_total = None
     for k in range(fan):
-        unit_rows, inv_scale = normalize(message[k])
+        unit_rows, inv_scale = normalize(stage[k * rows : (k + 1) * rows, :])
         unit_total = unit_rows if k == 0 else unit_total + unit_rows
         grad_message[k] = normal_back(grad_unit, unit_rows, inv_scale).astype(LOW)
-    grad_hidden[...] = product_right(
-        grad_message[...].reshape(fan * rows, width), weights[2]
-    )
+    stage[...] = product_right(grad_message[...].reshape(fan * rows, width), weights[2])
     own_total = None
     for k in range(fan):
         half, bend = silu_parts(kept[k].astype(WIDE) + own_term)
-        edge_hidden[k] = (half * (1.0 + bend)).astype(LOW)
-        grad_pre = grad_hidden[k * rows : (k + 1) * rows, :] * (
+        grad_pre = stage[k * rows : (k + 1) * rows, :] * (
             (0.5 + 0.5 * bend) * (1.0 + half * (1.0 - bend))
         )
         own_total = grad_pre if k == 0 else own_total + grad_pre
@@ -288,14 +288,14 @@
     def _():
         for index in range(3):
             base = index * block_rows
-            slot_grad[index] = (
+            slot_grads[index][...] = (
                 unfold_rows(sum_even, base, block_rows, parts)
                 + unfold_rows(sum_odd, base, block_rows, parts)
             ).astype(LOW)
 
 
 def backward_layer(slots, above, grad_part, stored, weights, gains):
-    target_low, kept, message, mix, out = stored
+    target_low, kept, aggregate = stored
     block_rows, width = target_low.shape
     fan = kept.shape[0]
     parts = width // LANES
@@ -312,7 +312,7 @@
         from_before, slot_grad, from_after, head = above
         in_specs += [
             tile,
-            pl.BlockSpec((1, rows, width), lambda step: (1, step, 0)),
+            tile,
             tile,
             matrix_spec(head[1], 1, width),
         ]
@@ -322,11 +322,13 @@
     if grad_part is not None:
         in_specs += [tile]
         operands += [grad_part]
-    in_specs += [tile, fan_tile, fan_tile, tile, tile]
+    in_specs += [tile, fan_tile, tile]
     in_specs += [matrix_spec(weights[1], 6, width), whole(gains.shape)]
-    operands += [target_low, kept, message, mix, out, weights[0], gains]
+    operands += [target_low, kept, aggregate, weights[0], gains]
     out_specs += [
-        whole((3, block_rows, width)),
+        whole((block_rows, width)),
+        whole((block_rows, width)),
+        whole((block_rows, width)),
         whole((2, width)),
         fan_tile,
         fan_tile,
@@ -336,7 +338,9 @@
         tile,
     ]
     out_shape += [
-        jax.ShapeDtypeStruct((3, block_rows, width), LOW),
+        shape(LOW),
+        shape(LOW),
+        shape(LOW),
         jax.ShapeDtypeStruct((2, width), WIDE),
         fan_shape(LOW),
         fan_shape(LOW),
@@ -357,7 +361,7 @@
             pltpu.VMEM((fan * rows * parts, LANES), WIDE),
             pltpu.VMEM((fan * rows, width), WIDE),
         ],
-        compiler_params=pltpu.CompilerParams(vmem_limit_bytes=VMEM_BYTES),
+        compiler_params=pltpu.CompilerParams(vmem_limit_bytes=38 << 20),
         cost_estimate=pl.CostEstimate(
             flops=2 * (fan + 4) * block_rows * width * width,
             transcendentals=(fan + 1) * block_rows * width,
@@ -481,7 +485,7 @@
         out_specs=out_specs,
         out_shape=out_shape,
         scratch_shapes=scratch,
-        compiler_params=pltpu.CompilerParams(vmem_limit_bytes=VMEM_BYTES),
+        compiler_params=pltpu.CompilerParams(vmem_limit_bytes=28 << 20),
         cost_estimate=pl.CostEstimate(
             flops=2 * (fan + 6) * block_rows * width * width,
             transcendentals=0,
@@ -540,10 +544,10 @@
         in_specs=[pl.BlockSpec(memory_space=pltpu.SMEM)]
         + [whole(piece.shape) for piece in pieces]
         + [tile] * 3,
-        out_specs=[whole((6, width, width))] + [tile] * 5,
-        out_shape=[jax.ShapeDtypeStruct((6, width, width), LOW), shape(WIDE)] + [shape(LOW)] * 4,
+        out_specs=[whole((7, width, width))] + [tile] * 5,
+        out_shape=[jax.ShapeDtypeStruct((7, width, width), LOW), shape(WIDE)] + [shape(LOW)] * 4,
         scratch_shapes=[pltpu.VMEM((width, width), LOW)],
-        compiler_params=pltpu.CompilerParams(vmem_limit_bytes=VMEM_BYTES),
+        compiler_params=pltpu.CompilerParams(vmem_limit_bytes=20 << 20),
         cost_estimate=pl.CostEstimate(
             flops=12 * block_rows * width * width,
             transcendentals=0,
@@ -565,7 +569,7 @@
 
     sent_low = (
         before[...].astype(WIDE)
-        + middle[...].reshape(rows, width).astype(WIDE)
+        + middle[...].astype(WIDE)
         + after[...].astype(WIDE)
     ).astype(LOW)
     grad_low = (grad_grid[...] + product_right(sent_low, head[0])).astype(LOW)
@@ -600,7 +604,7 @@
         in_specs=[
             pl.BlockSpec(memory_space=pltpu.SMEM),
             tile,
-            pl.BlockSpec((1, rows, width), lambda step: (1, step, 0)),
+            tile,
             tile,
             tile,
             tile,
@@ -611,7 +615,7 @@
         out_specs=[whole(shape)] * 2,
         out_shape=[jax.ShapeDtypeStruct(shape, WIDE), jax.ShapeDtypeStruct(shape, SEND)],
         scratch_shapes=[pltpu.VMEM((2, width, width), WIDE)],
-        compiler_params=pltpu.CompilerParams(vmem_limit_bytes=VMEM_BYTES),
+        compiler_params=pltpu.CompilerParams(vmem_limit_bytes=20 << 20),
         cost_estimate=pl.CostEstimate(
             flops=6 * block_rows * width * width,
             transcendentals=0,
@@ -643,7 +647,7 @@
         out_specs=[pl.BlockSpec((1, rows, width), lambda step: (step, 0, 0))] * radix,
         out_shape=[jax.ShapeDtypeStruct(shape, WIDE)]
         + [jax.ShapeDtypeStruct(shape, SEND)] * (radix - 1),
-        compiler_params=pltpu.CompilerParams(vmem_limit_bytes=VMEM_BYTES),
+        compiler_params=pltpu.CompilerParams(vmem_limit_bytes=12 << 20),
         cost_estimate=pl.CostEstimate(
             flops=rest * radix * rows * width * len(arrived),
             transcendentals=0,
@@ -657,10 +661,12 @@
     return lax.ppermute(cells, AXES, [(i, i ^ mask) for i in range(count)])
 
 
-def spread_rows(packed, count):
-    held = [packed]
+def spread_column(packed, count):
     high = 4 * 2
-    held += [swap(packed, count, digit * high) for digit in range(1, count // high)]
+    return [packed] + [swap(packed, count, digit * high) for digit in range(1, count // high)]
+
+
+def spread_rows(held, count):
     column = jnp.stack(held)
     near = [column] + [swap(column, count, digit * 2) for digit in range(1, 4)]
     return near + [swap(piece, count, 1) for piece in near]
@@ -739,26 +745,36 @@
         packed = jnp.concatenate(
             [
                 w_layers[0].astype(LOW).reshape(-1, width),
+                w_layers[1, 0].astype(LOW),
                 jnp.pad(w_in.astype(LOW).T, ((0, 0), (0, width - channels))),
                 jnp.pad(flat_gains, ((0, 7), (0, width - flat_gains.shape[1]))),
             ],
             axis=0,
         )
+        second = jnp.concatenate([w_layers[2, :1], w_layers[1, 1:]], axis=0).astype(LOW)
         rest = jnp.concatenate(
             [
-                w_layers[2:].astype(LOW).reshape(-1, share, width),
                 jnp.pad(w_out.astype(LOW), ((0, 0), (0, width - outputs)))[None],
+                w_layers[2, 1:].astype(LOW),
+                w_layers[3:].astype(LOW).reshape(-1, share, width),
             ],
             axis=0,
         )
-        input_blocks = (shift(inputs, device_count, 1), inputs, shift(inputs, device_count, -1))
-        pieces = spread_rows(packed, device_count)
-        second = lax.all_gather(w_layers[1].astype(LOW), AXES, axis=1, tiled=True)
+        held = spread_column(packed, device_count)
+        sides = [shift(inputs, device_count, 1), shift(inputs, device_count, -1)]
+        held, sides = together(held, [*sides, second])
+        second = lax.all_gather(sides[2], AXES, axis=1, tiled=True)
+        pieces = spread_rows(held, device_count)
+        pieces, (rest,) = together(pieces, [rest])
         rest = lax.all_gather(rest, AXES, axis=1, tiled=True)
-        first, grid_latent, grid_start, *blocks = embed(self_id, pieces, input_blocks)
+        first, grid_latent, grid_start, *blocks = embed(
+            self_id, pieces, (sides[0], inputs, sides[1])
+        )
         weights = [(first, 0), (second, 0)]
         weights += [(rest, 6 * layer_id) for layer_id in range(layer_total - 2)]
-        table_out = rest[6 * (layer_total - 2), :, :outputs]
+        heads = [(first, 0), (first, 6), (second, 0)]
+        heads += weights[3:]
+        table_out = rest[0, :, :outputs]
         gain_rows = jnp.stack(pieces)[:, :, packed.shape[0] - 8, : flat_gains.shape[1]]
         gain_rows = gain_rows.reshape(2, 4, device_count // 8, -1).transpose(2, 1, 0, 3)
         gain_rows = gain_rows.reshape(device_count, -1)[order]
@@ -771,6 +787,7 @@
         matrices = lax.all_gather(w_layers.astype(LOW), AXES, axis=2, tiled=True)
         matrices = matrices.reshape(-1, width, width)
         weights = [(matrices, 6 * layer_id) for layer_id in range(layer_total)]
+        heads = weights
         gains = lax.all_gather(norm_gains.astype(LOW), AXES, axis=2, tiled=True).astype(WIDE)
         grid_latent = product(grid_inputs, table_in)
         grid_start = grid_latent.astype(LOW)
@@ -791,15 +808,15 @@
             target_low,
             target,
             weights[layer_id],
-            None if last_layer else weights[layer_id + 1],
+            None if last_layer else heads[layer_id + 1],
             gains[layer_id],
         )
         if last_layer:
-            grid_low, kept, message, aggregate, mix, out = results
+            grid_low, kept, aggregate = results
         else:
-            sent, updated, updated_low, kept, message, aggregate, mix, out = results
+            sent, updated, updated_low, kept, aggregate = results
             blocks = (shift(sent, device_count, 1), sent, shift(sent, device_count, -1))
-        stored_list.append((source_low, (target_low, kept, message, mix, out), aggregate))
+        stored_list.append((source_low, (target_low, kept, aggregate), aggregate))
         if not last_layer:
             target, target_low = updated, updated_low
     prediction = product(grid_low, table_out)
@@ -819,19 +836,19 @@
     in_plane, in_slice = [], []
     for layer_id in reversed(range(layer_total)):
         source_low, stored, aggregate = stored_list[layer_id]
-        sent_grad, grad_new, slot_grad, grad_gain, *back = backward_layer(
+        sent_grad, grad_new, *slot_grads, grad_gain, grad_message, edge_hidden, b0, b1, b2, b3 = backward_layer(
             slot_lists[layer_id], above, grad_part, stored, weights[layer_id], gains[layer_id]
         )
         far = []
         if in_plane:
             moved = len(in_plane)
-            arrived, (slot_grad,) = together(in_plane + in_slice, [slot_grad])
+            arrived, slot_grads = together(in_plane + in_slice, slot_grads)
             if in_slice:
                 layer_grads[layer_id + 2] = add_up(arrived[moved:]).reshape(6, share, width)
             far = list(combine(arrived[:moved], device_count // 8))
-        from_before = shift(slot_grad[2], device_count, 1)
-        from_after = shift(slot_grad[0], device_count, -1)
-        back = [back[1], back[0], *back[2:]]
+        from_before = shift(slot_grads[2], device_count, 1)
+        from_after = shift(slot_grads[0], device_count, -1)
+        back = [edge_hidden, grad_message, b0, b1, b2, b3]
         grad_part, sums = weight_layer(
             self_id,
             device_count,
@@ -858,7 +875,7 @@
             layer_grads[layer_id] = sums[0]
         if layer_id == layer_total - 1:
             grad_grid, grad_part = grad_part, None
-        above = (from_before, slot_grad, from_after, weights[layer_id])
+        above = (from_before, slot_grads[1], from_after, heads[layer_id])
         above_source = source_low
     if direct:
         misc = jnp.stack(gain_grads).reshape(-1, device_count, share).transpose(1, 0, 2)
@@ -870,12 +887,12 @@
         sums = tail_layer(
             self_id,
             from_before,
-            slot_grad,
+            slot_grads[1],
             from_after,
             grid_start,
             inputs,
             grad_grid,
-            weights[0],
+            heads[0],
             misc,
         )
         arrived, sums = together([other] + in_slice, sums)
@@ -897,7 +914,7 @@
     else:
         loss_value = lax.psum(loss_local, AXES)
         sent_grad = (
-            from_before.astype(WIDE) + slot_grad[1].astype(WIDE) + from_after.astype(WIDE)
+            from_before.astype(WIDE) + slot_grads[1].astype(WIDE) + from_after.astype(WIDE)
         ).astype(LOW)
         grad_zero = product_left(above_source, sent_grad)
         grad_grid = grad_grid + product_right(sent_grad, matrices[0])

time: 656 us -> 633 us (0.965)
  local copies, waits for them, and re-layouts: 32.3 us -> 89.7 us
  Pallas kernels: 312 us -> 256 us
  waiting for transfers between devices: 143 us -> 121 us
    unnamed x155 -> x258, local copies, waits for them, and re-layouts: 14 us -> 83.3 us
    pallas_call x10, Pallas kernels: 31.4 us -> 4.34 us  [combine(): pl.pallas_call(functools.partial(combine_kernel, len(arrived)), grid=(res...]
    all_gather x1, waiting for transfers between devices: 17.4 us -> 0.01 us  [shards(): rest = lax.all_gather(rest, AXES, axis=1, tiled=True)]
    ppermute x45, waiting for transfers between devices: 81.3 us -> 64.4 us  [swap(): return lax.ppermute(cells, AXES, [(i, i ^ mask) for i in range(count)])]
    pallas_call x4, Pallas kernels: 54.6 us -> 37.9 us  [weight_layer(): pl.pallas_call(functools.partial(weight_kernel, above is not None, grad_n...]
    pallas_call x4, Pallas kernels: 86.5 us -> 72.7 us  [forward_layer(): pl.pallas_call(functools.partial(forward_kernel, parts, has_next), grid=(...]
    ppermute x16, waiting for transfers between devices: 44.6 us -> 56.1 us  [shift(): lax.ppermute(cells, AXES, [(i, (i + step) % count) for i in range(count)])]
    pallas_call x4, Pallas kernels: 122 us -> 131 us  [backward_layer(): pl.pallas_call(functools.partial(backward_kernel, parts, mode), grid=(blo...]
  transfers between devices with their start and end apart: 63 -> 63, of which waited for: 20 -> 15; matrix products, arithmetic and copies ran while one was open for 3% -> 3% of each run, Pallas kernels for 33% -> 30%
where the time goes in v4:
time: 633 us; the launch traced here: 624 us
  Pallas kernels  256 us (40%)
  starting transfers between devices  124 us (20%)
  waiting for transfers between devices  121 us (19%)
  local copies, waits for them, and re-layouts  89.7 us (14%)
  between operations  17.8 us (3%)
  other arithmetic  12.8 us (2%)
    pallas_call x4, Pallas kernels, backward_layer(): pl.pallas_call(functools.partial(backward_kernel, parts, mode), grid=(blo...  131 us
    unnamed x258, local copies, waits for them, and re-layouts  83.3 us
    ppermute x45, starting transfers between devices, swap(): return lax.ppermute(cells, AXES, [(i, i ^ mask) for i in range(count)])  77 us
    pallas_call x4, Pallas kernels, forward_layer(): pl.pallas_call(functools.partial(forward_kernel, parts, has_next), grid=(...  72.7 us
    ppermute x45, waiting for transfers between devices, swap(): return lax.ppermute(cells, AXES, [(i, i ^ mask) for i in range(count)])  64.4 us
    ppermute x16, waiting for transfers between devices, shift(): lax.ppermute(cells, AXES, [(i, (i + step) % count) for i in range(count)])  56.1 us
    ppermute x16, starting transfers between devices, shift(): lax.ppermute(cells, AXES, [(i, (i + step) % count) for i in range(count)])  47.3 us
    pallas_call x4, Pallas kernels, weight_layer(): pl.pallas_call(functools.partial(weight_kernel, above is not None, grad_n...  37.9 us
  transfers between devices with their start and end apart: 63, of which 15 were waited for; matrix products, arithmetic and copies ran while one was open for 3% of the time, Pallas kernels for 30%

profile of v4, /device:TPU:0, one launch (start us, length us, event | category | flops | bytes accessed | tf_op | source)
XLA Modules:
  0.0 623.7 jit_solution(9342370949659594020)
XLA Ops:
  9.4 6.0 collective-permute-start.4
  27.5 6.9 %collective-permute-done = bf16[136,512]{1,0:T(8,128)(2,1)} collective-permute-done((bf16[136,512]{1,0:T(8,128)(2,1)}, bf16[136,512]{1,0:T(8,128)(2,1)}, u32[]{:S(2)}, u32[]{:S(2)}) %collective-permute-start) | collective-permute-done | bytes 139296 | tf_op jit(solution)/shard_map/ppermute | solution.py:661
  34.4 5.5 collective-permute-done.1
  46.6 20.0 %collective-permute-done.6.refs_3_ = bf16[4,136,512]{2,1,0:T(8,128)(2,1)S(1)} collective-permute-done((bf16[4,136,512]{2,1,0:T(8,128)(2,1)S(1)}, bf16[4,136,512]{2,1,0:T(8,128)(2,1)S(1)}, u32[]{:S(2)}, u32[]{:S(2)}) %collective-permute-start.6) | collective-permute-done | bytes 557088 | tf_op jit(solution)/shard_map/ppermute | solution.py:661
  79.1 7.2 %embed.1 = (bf16[7,512,512]{2,1,0:T(8,128)(2,1)S(1)}, f32[1024,512]{1,0:T(8,128)S(1)}, bf16[1024,512]{1,0:T(8,128)(2,1)S(1)}, bf16[1024,512]{1,0:T(8,128)(2,1)S(...) custom-call(s32[1]{0:T(128)} %bitcast.4.refs_0_.self_id, ...), custom_call_target="tpu_custom_call" | custom-call | flops 3221225472 | bytes 12582912 | tf_op jit(solution)/shard_map/embed/pallas_call | solution.py:541
  88.6 17.5 %forward_layer.4 = (bf16[1024,512]{1,0:T(8,128)(2,1)S(1)}, f32[1024,512]{1,0:T(8,128)S(1)}, bf16[1024,512]{1,0:T(8,128)(2,1)S(1)}, bf16[4,1024,512]{2,1,0:T(8,128)(2,1)S(1)}, bf16[1024,512]{1,0:T(8,128)(2,1)S(1)}) custom-call(s32[4096]{0:T(1024)S(1)} %bitcast.172, bf16[1024,512]{1,0:T(8,128)(2,1)S(1)} %get-tuple-element.246.refs_1_, ...), custom_call_target="tpu_custom_call" | custom-call | flops 4831838208 | bytes 25165824 | tf_op jit(solution)/shard_map/forward_layer/pallas_call | solution.py:170
  110.7 5.2 collective-permute-start.13
  117.1 14.6 %collective-permute-done.12.refs_1_ = bf16[1024,512]{1,0:T(8,128)(2,1)S(1)} collective-permute-done((bf16[1024,512]{1,0:T(8,128)(2,1)S(1)}, bf16[1024,512]{1,0:T(8,128)(2,1)S(1)}, u32[]{:S(2)}, u32[]{:S(2)}) %collective-permute-start.12) | collective-permute-done | bytes 1048608 | tf_op jit(solution)/shard_map/ppermute | solution.py:676
  138.6 18.5 %forward_layer.5 = (bf16[1024,512]{1,0:T(8,128)(2,1)}, f32[1024,512]{1,0:T(8,128)S(1)}, bf16[1024,512]{1,0:T(8,128)(2,1)S(1)}, bf16[4,1024,512]{2,1,0:T(8,128)(2,1)S(1)}, bf16[1024,512]{1,0:T(8,128)(2,1)S(1)}) custom-call(s32[4096]{0:T(1024)S(1)} %bitcast.165, bf16[1024,512]{1,0:T(8,128)(2,1)S(1)} %copy-done.94, bf16[1024,512]{1,0:T(8,128)(2,1)S(1)} %copy-done.92, ...), custom_call_target="tpu_custom_call" | custom-call | flops 4831838208 | bytes 25165824 | tf_op jit(solution)/shard_map/forward_layer/pallas_call | solution.py:170
  160.3 6.1 collective-permute-start.14
  166.7 29.4 %collective-permute-done.14.refs_1_ = bf16[1024,512]{1,0:T(8,128)(2,1)} collective-permute-done((bf16[1024,512]{1,0:T(8,128)(2,1)}, bf16[1024,512]{1,0:T(8,128)(2,1)}, u32[]{:S(2)}, u32[]{:S(2)}) %collective-permute-start.14) | collective-permute-done | bytes 1048608 | tf_op jit(solution)/shard_map/ppermute | solution.py:676
  200.5 19.2 %forward_layer.6 = (bf16[1024,512]{1,0:T(8,128)(2,1)}, f32[1024,512]{1,0:T(8,128)}, bf16[1024,512]{1,0:T(8,128)(2,1)S(1)}, bf16[4,1024,512]{2,1,0:T(8,128)(2,1)S(1)}, bf16[1024,512]{1,0:T(8,128)(2,1)S(1)}) custom-call(s32[4096]{0:T(1024)S(1)} %bitcast.166, bf16[1024,512]{1,0:T(8,128)(2,1)} %collective-permute-done.14.refs_1_, ...), custom_call_target="tpu_custom_call" | custom-call | flops 4831838208 | bytes 25165824 | tf_op jit(solution)/shard_map/forward_layer/pallas_call | solution.py:170
  223.6 5.3 collective-permute-start.17
  229.8 12.1 %collective-permute-done.16.refs_1_ = bf16[1024,512]{1,0:T(8,128)(2,1)} collective-permute-done((bf16[1024,512]{1,0:T(8,128)(2,1)}, bf16[1024,512]{1,0:T(8,128)(2,1)}, u32[]{:S(2)}, u32[]{:S(2)}) %collective-permute-start.16) | collective-permute-done | bytes 1048608 | tf_op jit(solution)/shard_map/ppermute | solution.py:676
  247.5 17.6 %forward_layer.7 = (bf16[1024,512]{1,0:T(8,128)(2,1)S(1)}, bf16[4,1024,512]{2,1,0:T(8,128)(2,1)S(1)}, bf16[1024,512]{1,0:T(8,128)(2,1)S(1)}) custom-call(s32[4096]{0:T(1024)S(1)} %bitcast.174, bf16[1024,512]{1,0:T(8,128)(2,1)} %collective-permute-done.16.refs_1_, bf16[1024,512]{1,0:T(8,128)(2,1)} %get-tuple-element.258.refs_2_, ...), custom_call_target="tpu_custom_call" | custom-call | flops 4831838208 | bytes 25165824 | tf_op jit(solution)/shard_map/forward_layer/pallas_call | solution.py:170
  267.2 31.4 %backward_layer.4 = (bf16[1024,512]{1,0:T(8,128)(2,1)}, bf16[1024,512]{1,0:T(8,128)(2,1)S(1)}, bf16[1024,512]{1,0:T(8,128)(2,1)}, f32[2,512]{1,0:T(2,128)S(1)}, ...) custom-call(s32[4096]{0:T(1024)S(1)} %bitcast.175, ...), custom_call_target="tpu_custom_call" | custom-call | flops 4294967296 | bytes 25165824 | tf_op jit(solution)/shard_map/backward_layer/pallas_call | solution.py:352
  300.5 6.8 %collective-permute-start.18 = (bf16[1024,512]{1,0:T(8,128)(2,1)}, bf16[1024,512]{1,0:T(8,128)(2,1)S(1)}, u32[]{:S(2)}, u32[]{:S(2)}) collective-permute-start(bf16[1024,512]{1,0:T(8,128)(2,1)} %get-tuple-element.264), channel_id=1, source_target_pairs={{0,1},{1,2},{2,3},{3,4},{4,5},{5,6},{6,7},{7,8},{8,9},{9,10},{10,1... | collective-permute-start | bytes 3145736 | tf_op jit(solution)/shard_map/ppermute | solution.py:676
  311.7 9.7 %weight_layer.4 = (f32[1024,512]{1,0:T(8,128)S(1)}, f32[16,96,512]{2,1,0:T(8,128)S(1)}, bf16[16,96,512]{2,1,0:T(8,128)(2,1)S(1)}) custom-call(s32[1]{0:T(128)} %bitcast.4.refs_0_.self_id, f32[512,512]{1,0:T(8,128)S(1)} %pad.29.refs_1_, bf16[1024,512]{1,0:T(8,128)(2,1)S(1)} %copy-done.17, bf16[1024,512]{1,0:T(8,128)(2,1)S(1)} %get-tuple-element.263.refs_4_.refs_3_, ...), custom_call_target="tpu_custom_call" | custom-call | flops 5368709120 | bytes 12582912 | tf_op jit(solution)/shard_map/weight_layer/pallas_call | solution.py:481
  321.4 11.4 %collective-permute-start.20 = (bf16[16,96,512]{2,1,0:T(8,128)(2,1)S(1)}, bf16[16,96,512]{2,1,0:T(8,128)(2,1)S(1)}, u32[]{:S(2)}, u32[]{:S(2)}) collective-permute-start(bf16[16,96,512]{2,1,0:T(8,128)(2,1)S(1)} %get-tuple-element.277), channel_id=1, source_target_pairs={{0,1},{1,0},{2,3},{3,2},{4,5},{5,4},{6,7},{7,6},{8,9},{9,8},{10,11... | collective-permute-start | bytes 4718600 | tf_op jit(solution)/shard_map/ppermute | solution.py:661
  341.8 33.2 %backward_layer.5 = (bf16[1024,512]{1,0:T(8,128)(2,1)S(1)}, f32[1024,512]{1,0:T(8,128)S(1)}, bf16[1024,512]{1,0:T(8,128)(2,1)}, bf16[1024,512]{1,0:T(8,128)(2,1)...) custom-call(s32[4096]{0:T(1024)S(1)} %bitcast.167, ...), custom_call_target="tpu_custom_call" | custom-call | flops 4294967296 | bytes 25165824 | tf_op jit(solution)/shard_map/backward_layer/pallas_call | solution.py:352
  376.1 5.7 collective-permute-start.25
  387.4 10.1 %weight_layer.5 = (f32[1024,512]{1,0:T(8,128)S(1)}, f32[16,96,512]{2,1,0:T(8,128)S(1)}, bf16[16,96,512]{2,1,0:T(8,128)(2,1)S(1)}) custom-call(s32[1]{0:T(128)} %bitcast.4.refs_0_.self_id, bf16[1024,512]{1,0:T(8,128)(2,1)S(1)} %copy-done.34, bf16[1024,512]{1,0:T(8,128)(2,1)S(1)} %get-tuple-element.297.refs_2_, ...), custom_call_target="tpu_custom_call" | custom-call | flops 5368709120 | bytes 12582912 | tf_op jit(solution)/shard_map/weight_layer/pallas_call | solution.py:481
  414.3 33.7 %backward_layer.6 = (bf16[1024,512]{1,0:T(8,128)(2,1)S(1)}, f32[1024,512]{1,0:T(8,128)S(1)}, bf16[1024,512]{1,0:T(8,128)(2,1)}, bf16[1024,512]{1,0:T(8,128)(2,1)...) custom-call(s32[4096]{0:T(1024)S(1)} %bitcast.168, ...), custom_call_target="tpu_custom_call" | custom-call | flops 4294967296 | bytes 25165824 | tf_op jit(solution)/shard_map/backward_layer/pallas_call | solution.py:352
  449.2 5.5 collective-permute-start.34
  458.1 9.5 %weight_layer.6 = (f32[1024,512]{1,0:T(8,128)S(1)}, f32[16,96,512]{2,1,0:T(8,128)S(1)}, bf16[16,96,512]{2,1,0:T(8,128)(2,1)S(1)}) custom-call(s32[1]{0:T(128)} %bitcast.4.refs_0_.self_id, bf16[1024,512]{1,0:T(8,128)(2,1)S(1)} %get-tuple-element.255.refs_4_.refs_5_.refs_3_.refs_1_, bf16[1024,512]{1,0:T(8,128)(2,1)S(1)} %copy-done.48, ...), custom_call_target="tpu_custom_call" | custom-call | flops 5368709120 | bytes 12582912 | tf_op jit(solution)/shard_map/weight_layer/pallas_call | solution.py:481
  468.0 7.4 %collective-permute-start.35 = (bf16[16,96,512]{2,1,0:T(8,128)(2,1)S(1)}, bf16[16,96,512]{2,1,0:T(8,128)(2,1)S(1)}, u32[]{:S(2)}, u32[]{:S(2)}) collective-permute-start(bf16[16,96,512]{2,1,0:T(8,128)(2,1)S(1)} %get-tuple-element.363), channel_id=1, source_target_pairs={{0,1},{1,0},{2,3},{3,2},{4,5},{5,4},{6,7},{7,6},{8,9},{9,8},{10,11... | collective-permute-start | bytes 4718600 | tf_op jit(solution)/shard_map/ppermute | solution.py:661
  485.0 32.7 %backward_layer.7 = (bf16[1024,512]{1,0:T(8,128)(2,1)S(1)}, f32[1024,512]{1,0:T(8,128)}, bf16[1024,512]{1,0:T(8,128)(2,1)S(1)}, bf16[1024,512]{1,0:T(8,128)(2,1)...) custom-call(s32[4096]{0:T(1024)S(1)} %bitcast.173, ...), custom_call_target="tpu_custom_call" | custom-call | flops 4294967296 | bytes 25165824 | tf_op jit(solution)/shard_map/backward_layer/pallas_call | solution.py:352
  519.9 5.5 collective-permute-start.43
  531.0 8.5 %weight_layer.7 = (f32[16,96,512]{2,1,0:T(8,128)S(1)}, bf16[16,96,512]{2,1,0:T(8,128)(2,1)}) custom-call(s32[1]{0:T(128)} %bitcast.4.refs_0_.self_id, bf16[1024,512]{1,0:T(8,128)(2,1)S(1)} %get-tuple-element.251.refs_4_.refs_6_.refs_3_.refs_1_, bf16[1024,512]{1,0:T(8,128)(2,1)S(1)} %copy-done.90, bf16[1024,512]{1,0:T(8,128)(2,1)S(1)} %copy-done.30, ...), custom_call_target="tpu_custom_call" | custom-call | flops 5368709120 | bytes 12582912 | tf_op jit(solution)/shard_map/weight_layer/pallas_call | solution.py:481
  573.5 5.8 collective-permute-done.55
  579.3 7.3 %collective-permute-done.56 = bf16[4,96,512]{2,1,0:T(8,128)(2,1)S(1)} collective-permute-done((bf16[4,96,512]{2,1,0:T(8,128)(2,1)S(1)}, bf16[4,96,512]{2,1,0:T(8,128)(2,1)S(1)}, u32[]{:S(2)}, u32[]{:S(2)}) %collective-permute-start.56) | collective-permute-done | bytes 393248 | tf_op jit(solution)/shard_map/ppermute | solution.py:661
  595.3 6.5 %collective-permute-done.50 = bf16[4,40,512]{2,1,0:T(8,128)(2,1)S(1)} collective-permute-done((bf16[4,40,512]{2,1,0:T(8,128)(2,1)S(1)}, bf16[4,40,512]{2,1,0:T(8,128)(2,1)S(1)}, u32[]{:S(2)}, u32[]{:S(2)}) %collective-permute-start.50) | collective-permute-done | bytes 163872 | tf_op jit(solution)/shard_map/ppermute | solution.py:661
  (438 shorter events, 184.2 us)
Async XLA Ops:
  7.2 125.4 %all-gather.3.cloned.1.call-start = ((), (), s32[]{:S(2)}) async-start(), calls=%async_computation | async-start | bytes 3244032 | tf_op jit(solution)/shard_map/all_gather | solution.py:766
  8.9 31.0 %collective-permute-start.3 = (bf16[1024,512]{1,0:T(8,128)(2,1)S(1)}, bf16[1024,512]{1,0:T(8,128)(2,1)S(1)}, u32[]{:S(2)}, u32[]{:S(2)}) collective-permute-start(bf16[1024,512]{1,0:T(8,128)(2,1)S(1)} %pad.27.refs_10_.inputs), channel_id=1, source_target_pairs={{0,1},{1,2},{2,3},{3,4},{4,5},{5,6},{6,7},{7,8},{8,9},{9,10},{10,1... | collective-permute-start | bytes 3145736 | tf_op jit(solution)/shard_map/ppermute | solution.py:676
  9.4 31.5 %collective-permute-start.4 = (bf16[1024,512]{1,0:T(8,128)(2,1)S(1)}, bf16[1024,512]{1,0:T(8,128)(2,1)S(1)}, u32[]{:S(2)}, u32[]{:S(2)}) collective-permute-start(bf16[1024,512]{1,0:T(8,128)(2,1)S(1)} %pad.27.refs_10_.inputs), channel_id=1, source_target_pairs={{0,31},{1,0},{2,1},{3,2},{4,3},{5,4},{6,5},{7,6},{8,7},{9,8},{10,9... | collective-permute-start | bytes 3145736 | tf_op jit(solution)/shard_map/ppermute | solution.py:676
  41.9 154.3 %all-gather.5.cloned.1.call-start = ((), (), s32[]{:S(2)}) async-start(), calls=%async_computation.1 | async-start | bytes 6488064 | tf_op jit(solution)/shard_map/all_gather | solution.py:769
  43.1 23.5 %collective-permute-start.6 = (bf16[4,136,512]{2,1,0:T(8,128)(2,1)S(1)}, bf16[4,136,512]{2,1,0:T(8,128)(2,1)S(1)}, u32[]{:S(2)}, u32[]{:S(2)}) collective-permute-start(bf16[4,136,512]{2,1,0:T(8,128)(2,1)S(1)} %pad_maximum_fusion.refs_1_), channel_id=1, source_target_pairs={{0,4},{1,5},{2,6},{3,7},{4,0},{5,1},{6,2},{7,3},{8,12},{9,13},{10,... | collective-permute-start | bytes 1671176 | tf_op jit(solution)/shard_map/ppermute | solution.py:661
  43.2 23.5 %collective-permute-start.7 = (bf16[4,136,512]{2,1,0:T(8,128)(2,1)S(1)}, bf16[4,136,512]{2,1,0:T(8,128)(2,1)S(1)}, u32[]{:S(2)}, u32[]{:S(2)}) collective-permute-start(bf16[4,136,512]{2,1,0:T(8,128)(2,1)S(1)} %pad_maximum_fusion.refs_1_), channel_id=1, source_target_pairs={{0,6},{1,7},{2,4},{3,5},{4,2},{5,3},{6,0},{7,1},{8,14},{9,15},{10,... | collective-permute-start | bytes 1671176 | tf_op jit(solution)/shard_map/ppermute | solution.py:661
  43.2 24.8 %collective-permute-start.5 = (bf16[4,136,512]{2,1,0:T(8,128)(2,1)S(1)}, bf16[4,136,512]{2,1,0:T(8,128)(2,1)S(1)}, u32[]{:S(2)}, u32[]{:S(2)}) collective-permute-start(bf16[4,136,512]{2,1,0:T(8,128)(2,1)S(1)} %pad_maximum_fusion.refs_1_), channel_id=1, source_target_pairs={{0,2},{1,3},{2,0},{3,1},{4,6},{5,7},{6,4},{7,5},{8,10},{9,11},{10,... | collective-permute-start | bytes 1671176 | tf_op jit(solution)/shard_map/ppermute | solution.py:661
  46.6 23.1 %collective-permute-start.8 = (bf16[4,136,512]{2,1,0:T(8,128)(2,1)S(1)}, bf16[4,136,512]{2,1,0:T(8,128)(2,1)}, u32[]{:S(2)}, u32[]{:S(2)}) collective-permute-start(bf16[4,136,512]{2,1,0:T(8,128)(2,1)S(1)} %pad_maximum_fusion.refs_1_), channel_id=1, source_target_pairs={{0,1},{1,0},{2,3},{3,2},{4,5},{5,4},{6,7},{7,6},{8,9},{9,8},{10,11... | collective-permute-start | bytes 1671176 | tf_op jit(solution)/shard_map/ppermute | solution.py:661
  110.6 21.1 %collective-permute-start.12 = (bf16[1024,512]{1,0:T(8,128)(2,1)S(1)}, bf16[1024,512]{1,0:T(8,128)(2,1)S(1)}, u32[]{:S(2)}, u32[]{:S(2)}) collective-permute-start(bf16[1024,512]{1,0:T(8,128)(2,1)S(1)} %get-tuple-element.250.refs_2_), channel_id=1, source_target_pairs={{0,1},{1,2},{2,3},{3,4},{4,5},{5,6},{6,7},{7,8},{8,9},{9,10},{10,1... | collective-permute-start | bytes 3145736 | tf_op jit(solution)/shard_map/ppermute | solution.py:676
  110.7 21.9 %collective-permute-start.13 = (bf16[1024,512]{1,0:T(8,128)(2,1)S(1)}, bf16[1024,512]{1,0:T(8,128)(2,1)}, u32[]{:S(2)}, u32[]{:S(2)}) collective-permute-start(bf16[1024,512]{1,0:T(8,128)(2,1)S(1)} %get-tuple-element.250.refs_2_), channel_id=1, source_target_pairs={{0,31},{1,0},{2,1},{3,2},{4,3},{5,4},{6,5},{7,6},{8,7},{9,8},{10,9... | collective-permute-start | bytes 3145736 | tf_op jit(solution)/shard_map/ppermute | solution.py:676
  160.3 35.8 %collective-permute-start.14 = (bf16[1024,512]{1,0:T(8,128)(2,1)}, bf16[1024,512]{1,0:T(8,128)(2,1)}, u32[]{:S(2)}, u32[]{:S(2)}) collective-permute-start(bf16[1024,512]{1,0:T(8,128)(2,1)} %get-tuple-element.254.refs_2_), channel_id=1, source_target_pairs={{0,1},{1,2},{2,3},{3,4},{4,5},{5,6},{6,7},{7,8},{8,9},{9,10},{10,1... | collective-permute-start | bytes 3145736 | tf_op jit(solution)/shard_map/ppermute | solution.py:676
  166.4 29.7 %collective-permute-start.15 = (bf16[1024,512]{1,0:T(8,128)(2,1)}, bf16[1024,512]{1,0:T(8,128)(2,1)}, u32[]{:S(2)}, u32[]{:S(2)}) collective-permute-start(bf16[1024,512]{1,0:T(8,128)(2,1)} %get-tuple-element.254.refs_2_), channel_id=1, source_target_pairs={{0,31},{1,0},{2,1},{3,2},{4,3},{5,4},{6,5},{7,6},{8,7},{9,8},{10,9... | collective-permute-start | bytes 3145736 | tf_op jit(solution)/shard_map/ppermute | solution.py:676
  300.5 20.9 %collective-permute-start.18 = (bf16[1024,512]{1,0:T(8,128)(2,1)}, bf16[1024,512]{1,0:T(8,128)(2,1)S(1)}, u32[]{:S(2)}, u32[]{:S(2)}) collective-permute-start(bf16[1024,512]{1,0:T(8,128)(2,1)} %get-tuple-element.264), channel_id=1, source_target_pairs={{0,1},{1,2},{2,3},{3,4},{4,5},{5,6},{6,7},{7,8},{8,9},{9,10},{10,1... | collective-permute-start | bytes 3145736 | tf_op jit(solution)/shard_map/ppermute | solution.py:676
  336.3 39.6 %collective-permute-start.21 = (bf16[4,96,512]{2,1,0:T(8,128)(2,1)S(1)}, bf16[4,96,512]{2,1,0:T(8,128)(2,1)S(1)}, u32[]{:S(2)}, u32[]{:S(2)}) collective-permute-start(bf16[4,96,512]{2,1,0:T(8,128)(2,1)S(1)} %get-tuple-element.283), channel_id=1, source_target_pairs={{0,2},{1,3},{2,0},{3,1},{4,6},{5,7},{6,4},{7,5},{8,10},{9,11},{10,... | collective-permute-start | bytes 1179656 | tf_op jit(solution)/shard_map/ppermute | solution.py:661
  337.5 38.5 %collective-permute-start.22 = (bf16[4,96,512]{2,1,0:T(8,128)(2,1)S(1)}, bf16[4,96,512]{2,1,0:T(8,128)(2,1)S(1)}, u32[]{:S(2)}, u32[]{:S(2)}) collective-permute-start(bf16[4,96,512]{2,1,0:T(8,128)(2,1)S(1)} %get-tuple-element.284), channel_id=1, source_target_pairs={{0,4},{1,5},{2,6},{3,7},{4,0},{5,1},{6,2},{7,3},{8,12},{9,13},{10,... | collective-permute-start | bytes 1179656 | tf_op jit(solution)/shard_map/ppermute | solution.py:661
  339.2 36.8 %collective-permute-start.23 = (bf16[4,96,512]{2,1,0:T(8,128)(2,1)S(1)}, bf16[4,96,512]{2,1,0:T(8,128)(2,1)S(1)}, u32[]{:S(2)}, u32[]{:S(2)}) collective-permute-start(bf16[4,96,512]{2,1,0:T(8,128)(2,1)S(1)} %get-tuple-element.285), channel_id=1, source_target_pairs={{0,6},{1,7},{2,4},{3,5},{4,2},{5,3},{6,0},{7,1},{8,14},{9,15},{10,... | collective-permute-start | bytes 1179656 | tf_op jit(solution)/shard_map/ppermute | solution.py:661
  376.0 21.8 %collective-permute-start.24 = (bf16[1024,512]{1,0:T(8,128)(2,1)}, bf16[1024,512]{1,0:T(8,128)(2,1)S(1)}, u32[]{:S(2)}, u32[]{:S(2)}) collective-permute-start(bf16[1024,512]{1,0:T(8,128)(2,1)} %get-tuple-element.294), channel_id=1, source_target_pairs={{0,1},{1,2},{2,3},{3,4},{4,5},{5,6},{6,7},{7,8},{8,9},{9,10},{10,1... | collective-permute-start | bytes 3145736 | tf_op jit(solution)/shard_map/ppermute | solution.py:676
  376.1 21.7 %collective-permute-start.25 = (bf16[1024,512]{1,0:T(8,128)(2,1)}, bf16[1024,512]{1,0:T(8,128)(2,1)S(1)}, u32[]{:S(2)}, u32[]{:S(2)}) collective-permute-start(bf16[1024,512]{1,0:T(8,128)(2,1)} %get-tuple-element.295), channel_id=1, source_target_pairs={{0,31},{1,0},{2,1},{3,2},{4,3},{5,4},{6,5},{7,6},{8,7},{9,8},{10,9... | collective-permute-start | bytes 3145736 | tf_op jit(solution)/shard_map/ppermute | solution.py:676
  404.3 44.8 %collective-permute-start.31 = (bf16[1,96,512]{2,1,0:T(8,128)(2,1)S(1)}, bf16[1,96,512]{2,1,0:T(8,128)(2,1)S(1)}, u32[]{:S(2)}, u32[]{:S(2)}) collective-permute-start(bf16[1,96,512]{2,1,0:T(8,128)(2,1)S(1)} %get-tuple-element.329), channel_id=1, source_target_pairs={{0,16},{1,17},{2,18},{3,19},{4,20},{5,21},{6,22},{7,23},{8,24},{9,... | collective-permute-start | bytes 294920 | tf_op jit(solution)/shard_map/ppermute | solution.py:661
  406.7 42.4 %collective-permute-start.32 = (bf16[1,96,512]{2,1,0:T(8,128)(2,1)S(1)}, bf16[1,96,512]{2,1,0:T(8,128)(2,1)S(1)}, u32[]{:S(2)}, u32[]{:S(2)}) collective-permute-start(bf16[1,96,512]{2,1,0:T(8,128)(2,1)S(1)} %get-tuple-element.330), channel_id=1, source_target_pairs={{0,24},{1,25},{2,26},{3,27},{4,28},{5,29},{6,30},{7,31},{8,16},{9,... | collective-permute-start | bytes 294920 | tf_op jit(solution)/shard_map/ppermute | solution.py:661
  408.4 40.8 %collective-permute-start.27 = (bf16[4,96,512]{2,1,0:T(8,128)(2,1)S(1)}, bf16[4,96,512]{2,1,0:T(8,128)(2,1)S(1)}, u32[]{:S(2)}, u32[]{:S(2)}) collective-permute-start(bf16[4,96,512]{2,1,0:T(8,128)(2,1)S(1)} %get-tuple-element.324), channel_id=1, source_target_pairs={{0,2},{1,3},{2,0},{3,1},{4,6},{5,7},{6,4},{7,5},{8,10},{9,11},{10,... | collective-permute-start | bytes 1179656 | tf_op jit(solution)/shard_map/ppermute | solution.py:661
  408.9 40.3 %collective-permute-start.28 = (bf16[4,96,512]{2,1,0:T(8,128)(2,1)S(1)}, bf16[4,96,512]{2,1,0:T(8,128)(2,1)S(1)}, u32[]{:S(2)}, u32[]{:S(2)}) collective-permute-start(bf16[4,96,512]{2,1,0:T(8,128)(2,1)S(1)} %get-tuple-element.325), channel_id=1, source_target_pairs={{0,4},{1,5},{2,6},{3,7},{4,0},{5,1},{6,2},{7,3},{8,12},{9,13},{10,... | collective-permute-start | bytes 1179656 | tf_op jit(solution)/shard_map/ppermute | solution.py:661
  410.4 38.8 %collective-permute-start.29 = (bf16[4,96,512]{2,1,0:T(8,128)(2,1)S(1)}, bf16[4,96,512]{2,1,0:T(8,128)(2,1)S(1)}, u32[]{:S(2)}, u32[]{:S(2)}) collective-permute-start(bf16[4,96,512]{2,1,0:T(8,128)(2,1)S(1)} %get-tuple-element.326), channel_id=1, source_target_pairs={{0,6},{1,7},{2,4},{3,5},{4,2},{5,3},{6,0},{7,1},{8,14},{9,15},{10,... | collective-permute-start | bytes 1179656 | tf_op jit(solution)/shard_map/ppermute | solution.py:661
  476.0 43.7 %collective-permute-start.40 = (bf16[1,96,512]{2,1,0:T(8,128)(2,1)S(1)}, bf16[1,96,512]{2,1,0:T(8,128)(2,1)S(1)}, u32[]{:S(2)}, u32[]{:S(2)}) collective-permute-start(bf16[1,96,512]{2,1,0:T(8,128)(2,1)S(1)} %get-tuple-element.374), channel_id=1, source_target_pairs={{0,16},{1,17},{2,18},{3,19},{4,20},{5,21},{6,22},{7,23},{8,24},{9,... | collective-permute-start | bytes 294920 | tf_op jit(solution)/shard_map/ppermute | solution.py:661
  479.3 40.5 %collective-permute-start.41 = (bf16[1,96,512]{2,1,0:T(8,128)(2,1)S(1)}, bf16[1,96,512]{2,1,0:T(8,128)(2,1)S(1)}, u32[]{:S(2)}, u32[]{:S(2)}) collective-permute-start(bf16[1,96,512]{2,1,0:T(8,128)(2,1)S(1)} %get-tuple-element.375), channel_id=1, source_target_pairs={{0,24},{1,25},{2,26},{3,27},{4,28},{5,29},{6,30},{7,31},{8,16},{9,... | collective-permute-start | bytes 294920 | tf_op jit(solution)/shard_map/ppermute | solution.py:661
  480.1 39.7 %collective-permute-start.36 = (bf16[4,96,512]{2,1,0:T(8,128)(2,1)S(1)}, bf16[4,96,512]{2,1,0:T(8,128)(2,1)S(1)}, u32[]{:S(2)}, u32[]{:S(2)}) collective-permute-start(bf16[4,96,512]{2,1,0:T(8,128)(2,1)S(1)} %get-tuple-element.369), channel_id=1, source_target_pairs={{0,2},{1,3},{2,0},{3,1},{4,6},{5,7},{6,4},{7,5},{8,10},{9,11},{10,... | collective-permute-start | bytes 1179656 | tf_op jit(solution)/shard_map/ppermute | solution.py:661
  480.9 38.9 %collective-permute-start.37 = (bf16[4,96,512]{2,1,0:T(8,128)(2,1)S(1)}, bf16[4,96,512]{2,1,0:T(8,128)(2,1)S(1)}, u32[]{:S(2)}, u32[]{:S(2)}) collective-permute-start(bf16[4,96,512]{2,1,0:T(8,128)(2,1)S(1)} %get-tuple-element.370), channel_id=1, source_target_pairs={{0,4},{1,5},{2,6},{3,7},{4,0},{5,1},{6,2},{7,3},{8,12},{9,13},{10,... | collective-permute-start | bytes 1179656 | tf_op jit(solution)/shard_map/ppermute | solution.py:661
  482.3 37.5 %collective-permute-start.38 = (bf16[4,96,512]{2,1,0:T(8,128)(2,1)S(1)}, bf16[4,96,512]{2,1,0:T(8,128)(2,1)S(1)}, u32[]{:S(2)}, u32[]{:S(2)}) collective-permute-start(bf16[4,96,512]{2,1,0:T(8,128)(2,1)S(1)} %get-tuple-element.371), channel_id=1, source_target_pairs={{0,6},{1,7},{2,4},{3,5},{4,2},{5,3},{6,0},{7,1},{8,14},{9,15},{10,... | collective-permute-start | bytes 1179656 | tf_op jit(solution)/shard_map/ppermute | solution.py:661
  519.8 21.6 %collective-permute-start.42 = (bf16[1024,512]{1,0:T(8,128)(2,1)}, bf16[1024,512]{1,0:T(8,128)(2,1)S(1)}, u32[]{:S(2)}, u32[]{:S(2)}) collective-permute-start(bf16[1024,512]{1,0:T(8,128)(2,1)} %get-tuple-element.385), channel_id=1, source_target_pairs={{0,1},{1,2},{2,3},{3,4},{4,5},{5,6},{6,7},{7,8},{8,9},{9,10},{10,1... | collective-permute-start | bytes 3145736 | tf_op jit(solution)/shard_map/ppermute | solution.py:676
  519.9 22.5 %collective-permute-start.43 = (bf16[1024,512]{1,0:T(8,128)(2,1)S(1)}, bf16[1024,512]{1,0:T(8,128)(2,1)S(1)}, u32[]{:S(2)}, u32[]{:S(2)}) collective-permute-start(bf16[1024,512]{1,0:T(8,128)(2,1)S(1)} %get-tuple-element.386), channel_id=1, source_target_pairs={{0,31},{1,0},{2,1},{3,2},{4,3},{5,4},{6,5},{7,6},{8,7},{9,8},{10,9... | collective-permute-start | bytes 3145736 | tf_op jit(solution)/shard_map/ppermute | solution.py:676
  543.5 20.5 %collective-permute-start.44 = (bf16[16,96,512]{2,1,0:T(8,128)(2,1)}, bf16[16,96,512]{2,1,0:T(8,128)(2,1)}, u32[]{:S(2)}, u32[]{:S(2)}) collective-permute-start(bf16[16,96,512]{2,1,0:T(8,128)(2,1)} %get-tuple-element.404), channel_id=1, source_target_pairs={{0,1},{1,0},{2,3},{3,2},{4,5},{5,4},{6,7},{7,6},{8,9},{9,8},{10,11... | collective-permute-start | bytes 4718600 | tf_op jit(solution)/shard_map/ppermute | solution.py:661
  571.7 22.1 %collective-permute-start.49 = (bf16[4,40,512]{2,1,0:T(8,128)(2,1)S(1)}, bf16[4,40,512]{2,1,0:T(8,128)(2,1)S(1)}, u32[]{:S(2)}, u32[]{:S(2)}) collective-permute-start(bf16[4,40,512]{2,1,0:T(8,128)(2,1)S(1)} %get-tuple-element.422), channel_id=1, source_target_pairs={{0,2},{1,3},{2,0},{3,1},{4,6},{5,7},{6,4},{7,5},{8,10},{9,11},{10,... | collective-permute-start | bytes 491528 | tf_op jit(solution)/shard_map/ppermute | solution.py:661
  (151 other events, 1728.9 us)
Sparse Core Ops, SparseCore 0:
  42.0 63.0 all-gather.2
  108.6 78.9 all-gather.4

commit v5 on v4

--- a/solution.py
+++ b/solution.py
@@ -128,6 +128,22 @@
         sent[...] = product(updated_low, head[0]).astype(LOW)
 
 
+def in_hbm(shape, dtype):
+    return pltpu.MemorySpace.HBM(shape, dtype)
+
+
+def on_chip(shape, dtype):
+    return pltpu.MemorySpace.VMEM(shape, dtype)
+
+
+def kept_on_chip(array):
+    return pltpu.with_memory_space_constraint(array, pltpu.MemorySpace.VMEM)
+
+
+def pinned(array):
+    return pltpu.with_memory_space_constraint(array, pltpu.MemorySpace.HBM)
+
+
 def whole(shape):
     zeros = (0,) * len(shape)
     return pl.BlockSpec(shape, lambda step: zeros, pipeline_mode=pl.Buffered(1))
@@ -153,8 +169,8 @@
     parts = width // LANES
     rows = FORWARD_ROWS
     has_next = next_weights is not None
-    shape = functools.partial(jax.ShapeDtypeStruct, (block_rows, width))
-    fan_shape = functools.partial(jax.ShapeDtypeStruct, (fan, block_rows, width))
+    shape = functools.partial(in_hbm, (block_rows, width))
+    fan_shape = functools.partial(in_hbm, (fan, block_rows, width))
     tile = tiled(rows, width)
     in_specs = [pl.BlockSpec(memory_space=pltpu.SMEM)]
     in_specs += [whole((block_rows, width))] * 3 + [tile, tile]
@@ -179,14 +195,20 @@
             pltpu.VMEM((fan * rows, width), LOW),
             pltpu.VMEM((fan * rows, width), WIDE),
         ],
-        compiler_params=pltpu.CompilerParams(vmem_limit_bytes=28 << 20),
+        compiler_params=pltpu.CompilerParams(vmem_limit_bytes=54 << 20),
         cost_estimate=pl.CostEstimate(
             flops=2 * (fan + 5) * block_rows * width * width,
             transcendentals=(fan + 1) * block_rows * width,
             bytes_accessed=24 * block_rows * width * 2,
         ),
         name="forward_layer",
-    )(*operands)
+    )(
+        operands[0],
+        kept_on_chip(operands[1]),
+        pinned(operands[2]),
+        kept_on_chip(operands[3]),
+        *map(pinned, operands[4:]),
+    )
 
 
 def backward_kernel(parts, mode, *refs):
@@ -305,8 +327,8 @@
     in_specs = [pl.BlockSpec(memory_space=pltpu.SMEM)]
     operands = [slots]
     out_specs, out_shape = [], []
-    shape = functools.partial(jax.ShapeDtypeStruct, (block_rows, width))
-    fan_shape = functools.partial(jax.ShapeDtypeStruct, (fan, block_rows, width))
+    shape = functools.partial(on_chip, (block_rows, width))
+    fan_shape = functools.partial(on_chip, (fan, block_rows, width))
     mode = "first" if above is None else ("second" if grad_part is None else "third")
     if above is not None:
         from_before, slot_grad, from_after, head = above
@@ -338,9 +360,9 @@
         tile,
     ]
     out_shape += [
-        shape(LOW),
-        shape(LOW),
-        shape(LOW),
+        in_hbm((block_rows, width), LOW),
+        in_hbm((block_rows, width), LOW),
+        in_hbm((block_rows, width), LOW),
         jax.ShapeDtypeStruct((2, width), WIDE),
         fan_shape(LOW),
         fan_shape(LOW),
@@ -368,7 +390,7 @@
             bytes_accessed=24 * block_rows * width * 2,
         ),
         name="backward_layer",
-    )(*operands)
+    )(operands[0], *map(pinned, operands[1:]))
     if above is None:
         return (None, grad_part, *results)
     return tuple(results)
@@ -441,7 +463,7 @@
     shape = (device_count // 2, count * (width // device_count), width)
     return (
         [whole(shape)] * 2,
-        [jax.ShapeDtypeStruct(shape, WIDE), jax.ShapeDtypeStruct(shape, SEND)],
+        [on_chip(shape, WIDE), on_chip(shape, SEND)],
     )
 
 
@@ -458,18 +480,18 @@
         operands += [self_id]
     if above is not None:
         in_specs += [tile, tile]
-        operands += list(above)
+        operands += [pinned(above[0]), kept_on_chip(above[1])]
     else:
         in_specs += [whole((width, width))]
         operands += [extra]
     in_specs += [tile, tile, fan_tile, fan_tile, tile, tile, tile, tile]
-    operands += [low, aggregate, *back]
+    operands += [pinned(low), pinned(aggregate), *map(kept_on_chip, back)]
     out_specs, out_shape, scratch = [], [], []
     if grad_new is not None:
         in_specs += [tile, matrix_spec(weights[1], 6, width)]
-        operands += [grad_new, weights[0]]
+        operands += [kept_on_chip(grad_new), pinned(weights[0])]
         out_specs += [tile]
-        out_shape += [jax.ShapeDtypeStruct((block_rows, width), WIDE)]
+        out_shape += [in_hbm((block_rows, width), WIDE)]
     if direct:
         specs, shapes = share_outputs(6, width, device_count)
         out_specs += specs
@@ -485,7 +507,7 @@
         out_specs=out_specs,
         out_shape=out_shape,
         scratch_shapes=scratch,
-        compiler_params=pltpu.CompilerParams(vmem_limit_bytes=28 << 20),
+        compiler_params=pltpu.CompilerParams(vmem_limit_bytes=30 << 20),
         cost_estimate=pl.CostEstimate(
             flops=2 * (fan + 6) * block_rows * width * width,
             transcendentals=0,
@@ -537,7 +559,6 @@
     block_rows, width = blocks[1].shape
     rows = WEIGHT_ROWS
     tile = tiled(rows, width)
-    shape = functools.partial(jax.ShapeDtypeStruct, (block_rows, width))
     return pl.pallas_call(
         functools.partial(embed_kernel, len(pieces)),
         grid=(block_rows // rows,),
@@ -545,9 +566,16 @@
         + [whole(piece.shape) for piece in pieces]
         + [tile] * 3,
         out_specs=[whole((7, width, width))] + [tile] * 5,
-        out_shape=[jax.ShapeDtypeStruct((7, width, width), LOW), shape(WIDE)] + [shape(LOW)] * 4,
+        out_shape=[
+            in_hbm((7, width, width), LOW),
+            in_hbm((block_rows, width), WIDE),
+            in_hbm((block_rows, width), LOW),
+            on_chip((block_rows, width), LOW),
+            in_hbm((block_rows, width), LOW),
+            on_chip((block_rows, width), LOW),
+        ],
         scratch_shapes=[pltpu.VMEM((width, width), LOW)],
-        compiler_params=pltpu.CompilerParams(vmem_limit_bytes=20 << 20),
+        compiler_params=pltpu.CompilerParams(vmem_limit_bytes=50 << 20),
         cost_estimate=pl.CostEstimate(
             flops=12 * block_rows * width * width,
             transcendentals=0,
@@ -613,16 +641,20 @@
             whole(misc.shape),
         ],
         out_specs=[whole(shape)] * 2,
-        out_shape=[jax.ShapeDtypeStruct(shape, WIDE), jax.ShapeDtypeStruct(shape, SEND)],
+        out_shape=[on_chip(shape, WIDE), on_chip(shape, SEND)],
         scratch_shapes=[pltpu.VMEM((2, width, width), WIDE)],
-        compiler_params=pltpu.CompilerParams(vmem_limit_bytes=20 << 20),
+        compiler_params=pltpu.CompilerParams(vmem_limit_bytes=56 << 20),
         cost_estimate=pl.CostEstimate(
             flops=6 * block_rows * width * width,
             transcendentals=0,
             bytes_accessed=24 * block_rows * width,
         ),
         name="tail_layer",
-    )(self_id, from_before, slot_grad, from_after, latent_low, inputs, grad_grid, head[0], misc)
+    )(
+        self_id,
+        *map(pinned, (from_before, slot_grad, from_after, latent_low, inputs, grad_grid, head[0])),
+        misc,
+    )
 
 
 def combine_kernel(count, *refs):
@@ -645,16 +677,15 @@
         grid=(rest,),
         in_specs=[spec] * len(arrived),
         out_specs=[pl.BlockSpec((1, rows, width), lambda step: (step, 0, 0))] * radix,
-        out_shape=[jax.ShapeDtypeStruct(shape, WIDE)]
-        + [jax.ShapeDtypeStruct(shape, SEND)] * (radix - 1),
-        compiler_params=pltpu.CompilerParams(vmem_limit_bytes=12 << 20),
+        out_shape=[on_chip(shape, WIDE)] + [on_chip(shape, SEND)] * (radix - 1),
+        compiler_params=pltpu.CompilerParams(vmem_limit_bytes=20 << 20),
         cost_estimate=pl.CostEstimate(
             flops=rest * radix * rows * width * len(arrived),
             transcendentals=0,
             bytes_accessed=4 * rest * radix * rows * width * (len(arrived) + 1),
         ),
         name="combine",
-    )(*arrived)
+    )(*map(kept_on_chip, arrived))
 
 
 def swap(cells, count, mask):

time: 633 us -> 614 us (0.970)
  local copies, waits for them, and re-layouts: 89.7 us -> 27.6 us
  waiting for transfers between devices: 121 us -> 140 us
  Pallas kernels: 256 us -> 273 us
  starting transfers between devices: 124 us -> 134 us
    unnamed x258 -> x130, local copies, waits for them, and re-layouts: 83.3 us -> 13.9 us
    all_gather x1, waiting for transfers between devices: 0.01 us -> 13.4 us  [shards(): rest = lax.all_gather(rest, AXES, axis=1, tiled=True)]
    ppermute x45, waiting for transfers between devices: 64.4 us -> 72 us  [swap(): return lax.ppermute(cells, AXES, [(i, i ^ mask) for i in range(count)])]
    pallas_call x4, Pallas kernels: 72.7 us -> 80.1 us  [forward_layer(): pl.pallas_call(functools.partial(forward_kernel, parts, has_next), grid=(...]
  transfers between devices with their start and end apart: 63 -> 63, of which waited for: 15 -> 22; matrix products, arithmetic and copies ran while one was open for 3% -> 3% of each run, Pallas kernels for 30% -> 33%
where the time goes in v5:
time: 614 us; the launch traced here: 605 us
  Pallas kernels  273 us (44%)
  waiting for transfers between devices  140 us (23%)
  starting transfers between devices  134 us (22%)
  local copies, waits for them, and re-layouts  27.6 us (4%)
  between operations  17.5 us (3%)
  other arithmetic  6.91 us (1%)
    pallas_call x4, Pallas kernels, backward_layer(): pl.pallas_call(functools.partial(backward_kernel, parts, mode), grid=(blo...  132 us
    ppermute x45, starting transfers between devices, swap(): return lax.ppermute(cells, AXES, [(i, i ^ mask) for i in range(count)])  83.2 us
    pallas_call x4, Pallas kernels, forward_layer(): pl.pallas_call(functools.partial(forward_kernel, parts, has_next), grid=(...  80.1 us
    ppermute x45, waiting for transfers between devices, swap(): return lax.ppermute(cells, AXES, [(i, i ^ mask) for i in range(count)])  72 us
    ppermute x16, waiting for transfers between devices, shift(): lax.ppermute(cells, AXES, [(i, (i + step) % count) for i in range(count)])  54.4 us
    ppermute x16, starting transfers between devices, shift(): lax.ppermute(cells, AXES, [(i, (i + step) % count) for i in range(count)])  51.2 us
    pallas_call x4, Pallas kernels, weight_layer(): pl.pallas_call(functools.partial(weight_kernel, above is not None, grad_n...  41.7 us
    unnamed x130, local copies, waits for them, and re-layouts  13.9 us
  transfers between devices with their start and end apart: 63, of which 22 were waited for; matrix products, arithmetic and copies ran while one was open for 3% of the time, Pallas kernels for 33%

profile of v5, /device:TPU:0, one launch (start us, length us, event | category | flops | bytes accessed | tf_op | source)
XLA Modules:
  0.0 604.9 jit_solution(17614932329790660391)
XLA Ops:
  9.5 6.0 collective-permute-start.4
  20.8 12.0 %collective-permute-done = bf16[136,512]{1,0:T(8,128)(2,1)S(1)} collective-permute-done((bf16[136,512]{1,0:T(8,128)(2,1)S(1)}, bf16[136,512]{1,0:T(8,128)(2,1)S(1)}, u32[]{:S(2)}, u32[]{:S(2)}) %collective-permute-start) | collective-permute-done | bytes 139296 | tf_op jit(solution)/shard_map/ppermute | solution.py:692
  32.9 6.1 %collective-permute-done.1 = bf16[136,512]{1,0:T(8,128)(2,1)S(1)} collective-permute-done((bf16[136,512]{1,0:T(8,128)(2,1)S(1)}, bf16[136,512]{1,0:T(8,128)(2,1)S(1)}, u32[]{:S(2)}, u32[]{:S(2)}) %collective-permute-start.1) | collective-permute-done | bytes 139296 | tf_op jit(solution)/shard_map/ppermute | solution.py:692
  42.7 22.1 %collective-permute-done.6.refs_3_ = bf16[4,136,512]{2,1,0:T(8,128)(2,1)S(1)} collective-permute-done((bf16[4,136,512]{2,1,0:T(8,128)(2,1)S(1)}, bf16[4,136,512]{2,1,0:T(8,128)(2,1)S(1)}, u32[]{:S(2)}, u32[]{:S(2)}) %collective-permute-start.6) | collective-permute-done | bytes 557088 | tf_op jit(solution)/shard_map/ppermute | solution.py:692
  75.2 9.3 %embed.1 = (bf16[7,512,512]{2,1,0:T(8,128)(2,1)}, f32[1024,512]{1,0:T(8,128)}, bf16[1024,512]{1,0:T(8,128)(2,1)}, bf16[1024,512]{1,0:T(8,128)(2,1)S(1)}, bf16[10...) custom-call(s32[1]{0:T(128)} %bitcast.4.refs_0_.self_id, bf16[4,136,512]{2,1,0:T(8,128)(2,1)S(1)} %pad_maximum_fusion.refs_1_, ...), custom_call_target="tpu_custom_call" | custom-call | flops 3221225472 | bytes 12582912 | tf_op jit(solution)/shard_map/embed/pallas_call | solution.py:562
  84.5 20.5 %forward_layer.4 = (bf16[1024,512]{1,0:T(8,128)(2,1)}, f32[1024,512]{1,0:T(8,128)}, bf16[1024,512]{1,0:T(8,128)(2,1)}, bf16[4,1024,512]{2,1,0:T(8,128)(2,1)}, bf16[1024,512]{1,0:T(8,128)(2,1)}) custom-call(s32[4096]{0:T(1024)} %bitcast.172, bf16[1024,512]{1,0:T(8,128)(2,1)S(1)} %get-tuple-element.246.refs_1_, bf16[1024,512]{1,0:T(8,128)(2,1)} %get-tuple-element.247.refs_2_, ...), custom_call_target="tpu_custom_call" | custom-call | flops 4831838208 | bytes 25165824 | tf_op jit(solution)/shard_map/forward_layer/pallas_call | solution.py:186
  111.7 14.3 %collective-permute-done.12.refs_1_ = bf16[1024,512]{1,0:T(8,128)(2,1)S(1)} collective-permute-done((bf16[1024,512]{1,0:T(8,128)(2,1)}, bf16[1024,512]{1,0:T(8,128)(2,1)S(1)}, u32[]{:S(2)}, u32[]{:S(2)}) %collective-permute-start.12) | collective-permute-done | bytes 1048608 | tf_op jit(solution)/shard_map/ppermute | solution.py:707
  126.9 20.4 %forward_layer.5 = (bf16[1024,512]{1,0:T(8,128)(2,1)}, f32[1024,512]{1,0:T(8,128)}, bf16[1024,512]{1,0:T(8,128)(2,1)}, bf16[4,1024,512]{2,1,0:T(8,128)(2,1)}, bf16[1024,512]{1,0:T(8,128)(2,1)}) custom-call(s32[4096]{0:T(1024)} %bitcast.165, bf16[1024,512]{1,0:T(8,128)(2,1)S(1)} %collective-permute-done.12.refs_1_, ...), custom_call_target="tpu_custom_call" | custom-call | flops 4831838208 | bytes 25165824 | tf_op jit(solution)/shard_map/forward_layer/pallas_call | solution.py:186
  147.3 6.4 %collective-permute-start.14 = (bf16[1024,512]{1,0:T(8,128)(2,1)}, bf16[1024,512]{1,0:T(8,128)(2,1)S(1)}, u32[]{:S(2)}, u32[]{:S(2)}) collective-permute-start(bf16[1024,512]{1,0:T(8,128)(2,1)} %get-tuple-element.254.refs_2_), channel_id=1, source_target_pairs={{0,1},{1,2},{2,3},{3,4},{4,5},{5,6},{6,7},{7,8},{8,9},{9,10},{10,1... | collective-permute-start | bytes 3145736 | tf_op jit(solution)/shard_map/ppermute | solution.py:707
  154.4 15.8 %collective-permute-done.14.refs_1_ = bf16[1024,512]{1,0:T(8,128)(2,1)S(1)} collective-permute-done((bf16[1024,512]{1,0:T(8,128)(2,1)}, bf16[1024,512]{1,0:T(8,128)(2,1)S(1)}, u32[]{:S(2)}, u32[]{:S(2)}) %collective-permute-start.14) | collective-permute-done | bytes 1048608 | tf_op jit(solution)/shard_map/ppermute | solution.py:707
  170.2 8.3 %collective-permute-done.15.refs_3_ = bf16[1024,512]{1,0:T(8,128)(2,1)S(1)} collective-permute-done((bf16[1024,512]{1,0:T(8,128)(2,1)}, bf16[1024,512]{1,0:T(8,128)(2,1)S(1)}, u32[]{:S(2)}, u32[]{:S(2)}) %collective-permute-start.15) | collective-permute-done | bytes 1048608 | tf_op jit(solution)/shard_map/ppermute | solution.py:707
  178.5 13.4 %all-gather.5.cloned.1.call-done.refs_6_.refs_8_.refs_5_.refs_11_.refs_4_.refs_12_ = bf16[12,512,512]{2,1,0:T(8,128)(2,1)} async-done(((bf16[12,16,512]{2,1,0:T(8,128)(2,1)}), bf16[12,512,512]{2,1,0:T(8,128)(2,1)}) %all-gather.5.cloned.1.call-update) | async-done | bytes 6291472 | tf_op jit(solution)/shard_map/all_gather | solution.py:800
  191.9 20.2 %forward_layer.6 = (bf16[1024,512]{1,0:T(8,128)(2,1)}, f32[1024,512]{1,0:T(8,128)}, bf16[1024,512]{1,0:T(8,128)(2,1)}, bf16[4,1024,512]{2,1,0:T(8,128)(2,1)}, bf16[1024,512]{1,0:T(8,128)(2,1)}) custom-call(s32[4096]{0:T(1024)} %bitcast.166, bf16[1024,512]{1,0:T(8,128)(2,1)S(1)} %collective-permute-done.14.refs_1_, ...), custom_call_target="tpu_custom_call" | custom-call | flops 4831838208 | bytes 25165824 | tf_op jit(solution)/shard_map/forward_layer/pallas_call | solution.py:186
  219.7 10.8 %collective-permute-done.16.refs_1_ = bf16[1024,512]{1,0:T(8,128)(2,1)S(1)} collective-permute-done((bf16[1024,512]{1,0:T(8,128)(2,1)}, bf16[1024,512]{1,0:T(8,128)(2,1)S(1)}, u32[]{:S(2)}, u32[]{:S(2)}) %collective-permute-start.16) | collective-permute-done | bytes 1048608 | tf_op jit(solution)/shard_map/ppermute | solution.py:707
  230.5 19.1 %forward_layer.7 = (bf16[1024,512]{1,0:T(8,128)(2,1)}, bf16[4,1024,512]{2,1,0:T(8,128)(2,1)}, bf16[1024,512]{1,0:T(8,128)(2,1)}) custom-call(s32[4096]{0:T(1024)} %bitcast.174, bf16[1024,512]{1,0:T(8,128)(2,1)S(1)} %collective-permute-done.16.refs_1_, bf16[1024,512]{1,0:T(8,128)(2,1)} %get-tuple-element.258.refs_2_, ...), custom_call_target="tpu_custom_call" | custom-call | flops 4831838208 | bytes 25165824 | tf_op jit(solution)/shard_map/forward_layer/pallas_call | solution.py:186
  254.8 32.1 %backward_layer.4 = (bf16[1024,512]{1,0:T(8,128)(2,1)}, bf16[1024,512]{1,0:T(8,128)(2,1)}, bf16[1024,512]{1,0:T(8,128)(2,1)}, f32[2,512]{1,0:T(2,128)S(1)}, bf16...) custom-call(s32[4096]{0:T(1024)S(1)} %bitcast.175, ...), custom_call_target="tpu_custom_call" | custom-call | flops 4294967296 | bytes 25165824 | tf_op jit(solution)/shard_map/backward_layer/pallas_call | solution.py:374
  286.8 10.3 %collective-permute-start.18 = (bf16[1024,512]{1,0:T(8,128)(2,1)}, bf16[1024,512]{1,0:T(8,128)(2,1)S(1)}, u32[]{:S(2)}, u32[]{:S(2)}) collective-permute-start(bf16[1024,512]{1,0:T(8,128)(2,1)} %get-tuple-element.264), channel_id=1, source_target_pairs={{0,1},{1,2},{2,3},{3,4},{4,5},{5,6},{6,7},{7,8},{8,9},{9,10},{10,1... | collective-permute-start | bytes 3145736 | tf_op jit(solution)/shard_map/ppermute | solution.py:707
  298.1 10.4 %weight_layer.4 = (f32[1024,512]{1,0:T(8,128)}, f32[16,96,512]{2,1,0:T(8,128)S(1)}, bf16[16,96,512]{2,1,0:T(8,128)(2,1)S(1)}) custom-call(s32[1]{0:T(128)} %bitcast.4.refs_0_.self_id, f32[512,512]{1,0:T(8,128)S(1)} %pad.29.refs_1_, bf16[1024,512]{1,0:T(8,128)(2,1)} %get-tuple-element.259.refs_4_.refs_2_.latent_low, ...), custom_call_target="tpu_custom_call" | custom-call | flops 5368709120 | bytes 12582912 | tf_op jit(solution)/shard_map/weight_layer/pallas_call | solution.py:503
  310.1 12.0 %collective-permute-start.20 = (bf16[16,96,512]{2,1,0:T(8,128)(2,1)S(1)}, bf16[16,96,512]{2,1,0:T(8,128)(2,1)S(1)}, u32[]{:S(2)}, u32[]{:S(2)}) collective-permute-start(bf16[16,96,512]{2,1,0:T(8,128)(2,1)S(1)} %get-tuple-element.277), channel_id=1, source_target_pairs={{0,1},{1,0},{2,3},{3,2},{4,5},{5,4},{6,7},{7,6},{8,9},{9,8},{10,11... | collective-permute-start | bytes 4718600 | tf_op jit(solution)/shard_map/ppermute | solution.py:692
  329.8 33.0 %backward_layer.5 = (bf16[1024,512]{1,0:T(8,128)(2,1)S(1)}, f32[1024,512]{1,0:T(8,128)S(1)}, bf16[1024,512]{1,0:T(8,128)(2,1)}, bf16[1024,512]{1,0:T(8,128)(2,1)...) custom-call(s32[4096]{0:T(1024)S(1)} %bitcast.167, ...), custom_call_target="tpu_custom_call" | custom-call | flops 4294967296 | bytes 25165824 | tf_op jit(solution)/shard_map/backward_layer/pallas_call | solution.py:374
  368.3 11.1 %weight_layer.5 = (f32[1024,512]{1,0:T(8,128)}, f32[16,96,512]{2,1,0:T(8,128)S(1)}, bf16[16,96,512]{2,1,0:T(8,128)(2,1)S(1)}) custom-call(s32[1]{0:T(128)} %bitcast.4.refs_0_.self_id, bf16[1024,512]{1,0:T(8,128)(2,1)} %get-tuple-element.296.refs_1_, bf16[1024,512]{1,0:T(8,128)(2,1)S(1)} %get-tuple-element.297.refs_2_, ...), custom_call_target="tpu_custom_call" | custom-call | flops 5368709120 | bytes 12582912 | tf_op jit(solution)/shard_map/weight_layer/pallas_call | solution.py:503
  381.0 7.3 %collective-permute-start.26 = (bf16[16,96,512]{2,1,0:T(8,128)(2,1)S(1)}, bf16[16,96,512]{2,1,0:T(8,128)(2,1)S(1)}, u32[]{:S(2)}, u32[]{:S(2)}) collective-permute-start(bf16[16,96,512]{2,1,0:T(8,128)(2,1)S(1)} %get-tuple-element.318), channel_id=1, source_target_pairs={{0,1},{1,0},{2,3},{3,2},{4,5},{5,4},{6,7},{7,6},{8,9},{9,8},{10,11... | collective-permute-start | bytes 4718600 | tf_op jit(solution)/shard_map/ppermute | solution.py:692
  397.1 33.9 %backward_layer.6 = (bf16[1024,512]{1,0:T(8,128)(2,1)S(1)}, f32[1024,512]{1,0:T(8,128)S(1)}, bf16[1024,512]{1,0:T(8,128)(2,1)}, bf16[1024,512]{1,0:T(8,128)(2,1)...) custom-call(s32[4096]{0:T(1024)S(1)} %bitcast.168, ...), custom_call_target="tpu_custom_call" | custom-call | flops 4294967296 | bytes 25165824 | tf_op jit(solution)/shard_map/backward_layer/pallas_call | solution.py:374
  436.6 11.1 %weight_layer.6 = (f32[1024,512]{1,0:T(8,128)}, f32[16,96,512]{2,1,0:T(8,128)S(1)}, bf16[16,96,512]{2,1,0:T(8,128)(2,1)S(1)}) custom-call(s32[1]{0:T(128)} %bitcast.4.refs_0_.self_id, bf16[1024,512]{1,0:T(8,128)(2,1)} %get-tuple-element.255.refs_4_.refs_5_.refs_3_.refs_1_, bf16[1024,512]{1,0:T(8,128)(2,1)S(1)} %get-tuple-element.342.refs_2_, ...), custom_call_target="tpu_custom_call" | custom-call | flops 5368709120 | bytes 12582912 | tf_op jit(solution)/shard_map/weight_layer/pallas_call | solution.py:503
  449.2 8.7 %collective-permute-start.35 = (bf16[16,96,512]{2,1,0:T(8,128)(2,1)S(1)}, bf16[16,96,512]{2,1,0:T(8,128)(2,1)S(1)}, u32[]{:S(2)}, u32[]{:S(2)}) collective-permute-start(bf16[16,96,512]{2,1,0:T(8,128)(2,1)S(1)} %get-tuple-element.363), channel_id=1, source_target_pairs={{0,1},{1,0},{2,3},{3,2},{4,5},{5,4},{6,7},{7,6},{8,9},{9,8},{10,11... | collective-permute-start | bytes 4718600 | tf_op jit(solution)/shard_map/ppermute | solution.py:692
  466.2 32.7 %backward_layer.7 = (bf16[1024,512]{1,0:T(8,128)(2,1)S(1)}, f32[1024,512]{1,0:T(8,128)}, bf16[1024,512]{1,0:T(8,128)(2,1)}, bf16[1024,512]{1,0:T(8,128)(2,1)}, b...) custom-call(s32[4096]{0:T(1024)S(1)} %bitcast.173, ...), custom_call_target="tpu_custom_call" | custom-call | flops 4294967296 | bytes 25165824 | tf_op jit(solution)/shard_map/backward_layer/pallas_call | solution.py:374
  508.8 9.2 %weight_layer.7 = (f32[16,96,512]{2,1,0:T(8,128)S(1)}, bf16[16,96,512]{2,1,0:T(8,128)(2,1)}) custom-call(s32[1]{0:T(128)} %bitcast.4.refs_0_.self_id, bf16[1024,512]{1,0:T(8,128)(2,1)} %get-tuple-element.251.refs_4_.refs_6_.refs_3_.refs_1_, bf16[1024,512]{1,0:T(8,128)(2,1)S(1)} %get-tuple-element.387.refs_2_, bf16[1024,512]{1,0:T(8,128)(2,1)} %refs_3_.1, ...), custom_call_target="tpu_custom_call" | custom-call | flops 5368709120 | bytes 12582912 | tf_op jit(solution)/shard_map/weight_layer/pallas_call | solution.py:503
  520.7 6.5 %collective-permute-start.44 = (bf16[16,96,512]{2,1,0:T(8,128)(2,1)}, bf16[16,96,512]{2,1,0:T(8,128)(2,1)}, u32[]{:S(2)}, u32[]{:S(2)}) collective-permute-start(bf16[16,96,512]{2,1,0:T(8,128)(2,1)} %get-tuple-element.404), channel_id=1, source_target_pairs={{0,1},{1,0},{2,3},{3,2},{4,5},{5,4},{6,7},{7,6},{8,9},{9,8},{10,11... | collective-permute-start | bytes 4718600 | tf_op jit(solution)/shard_map/ppermute | solution.py:692
  539.1 6.1 %tail_layer.1 = (f32[16,40,512]{2,1,0:T(8,128)S(1)}, bf16[16,40,512]{2,1,0:T(8,128)(2,1)S(1)}) custom-call(s32[1]{0:T(128)} %bitcast.4.refs_0_.self_id, bf16[1024,512]{1,0:T(8,128)(2,1)} %collective-permute-done.42.before, bf16[1024,512]{1,0:T(8,128)(2,1)} %get-tuple-element.410.middle, bf16[1024,512]{1,0:T(8,128)(2,1)} %collective-permute-done.43.after, ...), custom_call_target="tpu_custom_call" | custom-call | flops 1610612736 | bytes 12582912 | tf_op jit(solution)/shard_map/tail_layer/pallas_call | solution.py:629
  554.6 7.0 %collective-permute-done.55 = bf16[4,96,512]{2,1,0:T(8,128)(2,1)S(1)} collective-permute-done((bf16[4,96,512]{2,1,0:T(8,128)(2,1)S(1)}, bf16[4,96,512]{2,1,0:T(8,128)(2,1)S(1)}, u32[]{:S(2)}, u32[]{:S(2)}) %collective-permute-start.55) | collective-permute-done | bytes 393248 | tf_op jit(solution)/shard_map/ppermute | solution.py:692
  561.7 9.0 %collective-permute-done.57 = bf16[4,96,512]{2,1,0:T(8,128)(2,1)S(1)} collective-permute-done((bf16[4,96,512]{2,1,0:T(8,128)(2,1)S(1)}, bf16[4,96,512]{2,1,0:T(8,128)(2,1)S(1)}, u32[]{:S(2)}, u32[]{:S(2)}) %collective-permute-start.57) | collective-permute-done | bytes 393248 | tf_op jit(solution)/shard_map/ppermute | solution.py:692
  577.6 6.0 collective-permute-done.50
  (310 shorter events, 136.8 us)
Async XLA Ops:
  7.2 119.7 %all-gather.3.cloned.1.call-start = ((), (), s32[]{:S(2)}) async-start(), calls=%async_computation | async-start | bytes 3244032 | tf_op jit(solution)/shard_map/all_gather | solution.py:797
  9.0 30.0 %collective-permute-start.3 = (bf16[1024,512]{1,0:T(8,128)(2,1)S(1)}, bf16[1024,512]{1,0:T(8,128)(2,1)}, u32[]{:S(2)}, u32[]{:S(2)}) collective-permute-start(bf16[1024,512]{1,0:T(8,128)(2,1)S(1)} %pad.27.refs_10_.inputs), channel_id=1, source_target_pairs={{0,1},{1,2},{2,3},{3,4},{4,5},{5,6},{6,7},{7,8},{8,9},{9,10},{10,1... | collective-permute-start | bytes 3145736 | tf_op jit(solution)/shard_map/ppermute | solution.py:707
  9.5 29.5 %collective-permute-start.4 = (bf16[1024,512]{1,0:T(8,128)(2,1)S(1)}, bf16[1024,512]{1,0:T(8,128)(2,1)}, u32[]{:S(2)}, u32[]{:S(2)}) collective-permute-start(bf16[1024,512]{1,0:T(8,128)(2,1)S(1)} %pad.27.refs_10_.inputs), channel_id=1, source_target_pairs={{0,31},{1,0},{2,1},{3,2},{4,3},{5,4},{6,5},{7,6},{8,7},{9,8},{10,9... | collective-permute-start | bytes 3145736 | tf_op jit(solution)/shard_map/ppermute | solution.py:707
  15.9 23.0 %collective-permute-start.1 = (bf16[136,512]{1,0:T(8,128)(2,1)S(1)}, bf16[136,512]{1,0:T(8,128)(2,1)S(1)}, u32[]{:S(2)}, u32[]{:S(2)}) collective-permute-start(bf16[136,512]{1,0:T(8,128)(2,1)S(1)} %fusion.8), channel_id=1, source_target_pairs={{0,16},{1,17},{2,18},{3,19},{4,20},{5,21},{6,22},{7,23},{8,24},{9,... | collective-permute-start | bytes 417800 | tf_op jit(solution)/shard_map/ppermute | solution.py:692
  18.5 20.5 %collective-permute-start.2 = (bf16[136,512]{1,0:T(8,128)(2,1)S(1)}, bf16[136,512]{1,0:T(8,128)(2,1)S(1)}, u32[]{:S(2)}, u32[]{:S(2)}) collective-permute-start(bf16[136,512]{1,0:T(8,128)(2,1)S(1)} %fusion.8), channel_id=1, source_target_pairs={{0,24},{1,25},{2,26},{3,27},{4,28},{5,29},{6,30},{7,31},{8,16},{9,... | collective-permute-start | bytes 417800 | tf_op jit(solution)/shard_map/ppermute | solution.py:692
  39.0 152.9 %all-gather.5.cloned.1.call-start = ((), (), s32[]{:S(2)}) async-start(), calls=%async_computation.1 | async-start | bytes 6488064 | tf_op jit(solution)/shard_map/all_gather | solution.py:800
  39.1 25.7 %collective-permute-start.6 = (bf16[4,136,512]{2,1,0:T(8,128)(2,1)S(1)}, bf16[4,136,512]{2,1,0:T(8,128)(2,1)S(1)}, u32[]{:S(2)}, u32[]{:S(2)}) collective-permute-start(bf16[4,136,512]{2,1,0:T(8,128)(2,1)S(1)} %pad_maximum_fusion.refs_1_), channel_id=1, source_target_pairs={{0,4},{1,5},{2,6},{3,7},{4,0},{5,1},{6,2},{7,3},{8,12},{9,13},{10,... | collective-permute-start | bytes 1671176 | tf_op jit(solution)/shard_map/ppermute | solution.py:692
  39.2 25.6 %collective-permute-start.7 = (bf16[4,136,512]{2,1,0:T(8,128)(2,1)S(1)}, bf16[4,136,512]{2,1,0:T(8,128)(2,1)S(1)}, u32[]{:S(2)}, u32[]{:S(2)}) collective-permute-start(bf16[4,136,512]{2,1,0:T(8,128)(2,1)S(1)} %pad_maximum_fusion.refs_1_), channel_id=1, source_target_pairs={{0,6},{1,7},{2,4},{3,5},{4,2},{5,3},{6,0},{7,1},{8,14},{9,15},{10,... | collective-permute-start | bytes 1671176 | tf_op jit(solution)/shard_map/ppermute | solution.py:692
  39.3 26.9 %collective-permute-start.5 = (bf16[4,136,512]{2,1,0:T(8,128)(2,1)S(1)}, bf16[4,136,512]{2,1,0:T(8,128)(2,1)S(1)}, u32[]{:S(2)}, u32[]{:S(2)}) collective-permute-start(bf16[4,136,512]{2,1,0:T(8,128)(2,1)S(1)} %pad_maximum_fusion.refs_1_), channel_id=1, source_target_pairs={{0,2},{1,3},{2,0},{3,1},{4,6},{5,7},{6,4},{7,5},{8,10},{9,11},{10,... | collective-permute-start | bytes 1671176 | tf_op jit(solution)/shard_map/ppermute | solution.py:692
  42.7 24.3 %collective-permute-start.8 = (bf16[4,136,512]{2,1,0:T(8,128)(2,1)S(1)}, bf16[4,136,512]{2,1,0:T(8,128)(2,1)}, u32[]{:S(2)}, u32[]{:S(2)}) collective-permute-start(bf16[4,136,512]{2,1,0:T(8,128)(2,1)S(1)} %pad_maximum_fusion.refs_1_), channel_id=1, source_target_pairs={{0,1},{1,0},{2,3},{3,2},{4,5},{5,4},{6,7},{7,6},{8,9},{9,8},{10,11... | collective-permute-start | bytes 1671176 | tf_op jit(solution)/shard_map/ppermute | solution.py:692
  105.0 21.0 %collective-permute-start.12 = (bf16[1024,512]{1,0:T(8,128)(2,1)}, bf16[1024,512]{1,0:T(8,128)(2,1)S(1)}, u32[]{:S(2)}, u32[]{:S(2)}) collective-permute-start(bf16[1024,512]{1,0:T(8,128)(2,1)} %get-tuple-element.250.refs_2_), channel_id=1, source_target_pairs={{0,1},{1,2},{2,3},{3,4},{4,5},{5,6},{6,7},{7,8},{8,9},{9,10},{10,1... | collective-permute-start | bytes 3145736 | tf_op jit(solution)/shard_map/ppermute | solution.py:707
  105.2 21.7 %collective-permute-start.13 = (bf16[1024,512]{1,0:T(8,128)(2,1)}, bf16[1024,512]{1,0:T(8,128)(2,1)S(1)}, u32[]{:S(2)}, u32[]{:S(2)}) collective-permute-start(bf16[1024,512]{1,0:T(8,128)(2,1)} %get-tuple-element.250.refs_2_), channel_id=1, source_target_pairs={{0,31},{1,0},{2,1},{3,2},{4,3},{5,4},{6,5},{7,6},{8,7},{9,8},{10,9... | collective-permute-start | bytes 3145736 | tf_op jit(solution)/shard_map/ppermute | solution.py:707
  147.3 23.0 %collective-permute-start.14 = (bf16[1024,512]{1,0:T(8,128)(2,1)}, bf16[1024,512]{1,0:T(8,128)(2,1)S(1)}, u32[]{:S(2)}, u32[]{:S(2)}) collective-permute-start(bf16[1024,512]{1,0:T(8,128)(2,1)} %get-tuple-element.254.refs_2_), channel_id=1, source_target_pairs={{0,1},{1,2},{2,3},{3,4},{4,5},{5,6},{6,7},{7,8},{8,9},{9,10},{10,1... | collective-permute-start | bytes 3145736 | tf_op jit(solution)/shard_map/ppermute | solution.py:707
  153.6 24.9 %collective-permute-start.15 = (bf16[1024,512]{1,0:T(8,128)(2,1)}, bf16[1024,512]{1,0:T(8,128)(2,1)S(1)}, u32[]{:S(2)}, u32[]{:S(2)}) collective-permute-start(bf16[1024,512]{1,0:T(8,128)(2,1)} %get-tuple-element.254.refs_2_), channel_id=1, source_target_pairs={{0,31},{1,0},{2,1},{3,2},{4,3},{5,4},{6,5},{7,6},{8,7},{9,8},{10,9... | collective-permute-start | bytes 3145736 | tf_op jit(solution)/shard_map/ppermute | solution.py:707
  286.8 21.7 %collective-permute-start.18 = (bf16[1024,512]{1,0:T(8,128)(2,1)}, bf16[1024,512]{1,0:T(8,128)(2,1)S(1)}, u32[]{:S(2)}, u32[]{:S(2)}) collective-permute-start(bf16[1024,512]{1,0:T(8,128)(2,1)} %get-tuple-element.264), channel_id=1, source_target_pairs={{0,1},{1,2},{2,3},{3,4},{4,5},{5,6},{6,7},{7,8},{8,9},{9,10},{10,1... | collective-permute-start | bytes 3145736 | tf_op jit(solution)/shard_map/ppermute | solution.py:707
  325.5 37.3 %collective-permute-start.21 = (bf16[4,96,512]{2,1,0:T(8,128)(2,1)S(1)}, bf16[4,96,512]{2,1,0:T(8,128)(2,1)S(1)}, u32[]{:S(2)}, u32[]{:S(2)}) collective-permute-start(bf16[4,96,512]{2,1,0:T(8,128)(2,1)S(1)} %get-tuple-element.283), channel_id=1, source_target_pairs={{0,2},{1,3},{2,0},{3,1},{4,6},{5,7},{6,4},{7,5},{8,10},{9,11},{10,... | collective-permute-start | bytes 1179656 | tf_op jit(solution)/shard_map/ppermute | solution.py:692
  328.3 34.5 %collective-permute-start.22 = (bf16[4,96,512]{2,1,0:T(8,128)(2,1)S(1)}, bf16[4,96,512]{2,1,0:T(8,128)(2,1)S(1)}, u32[]{:S(2)}, u32[]{:S(2)}) collective-permute-start(bf16[4,96,512]{2,1,0:T(8,128)(2,1)S(1)} %get-tuple-element.284), channel_id=1, source_target_pairs={{0,4},{1,5},{2,6},{3,7},{4,0},{5,1},{6,2},{7,3},{8,12},{9,13},{10,... | collective-permute-start | bytes 1179656 | tf_op jit(solution)/shard_map/ppermute | solution.py:692
  328.3 34.5 %collective-permute-start.23 = (bf16[4,96,512]{2,1,0:T(8,128)(2,1)S(1)}, bf16[4,96,512]{2,1,0:T(8,128)(2,1)S(1)}, u32[]{:S(2)}, u32[]{:S(2)}) collective-permute-start(bf16[4,96,512]{2,1,0:T(8,128)(2,1)S(1)} %get-tuple-element.285), channel_id=1, source_target_pairs={{0,6},{1,7},{2,4},{3,5},{4,2},{5,3},{6,0},{7,1},{8,14},{9,15},{10,... | collective-permute-start | bytes 1179656 | tf_op jit(solution)/shard_map/ppermute | solution.py:692
  389.1 41.8 %collective-permute-start.31 = (bf16[1,96,512]{2,1,0:T(8,128)(2,1)S(1)}, bf16[1,96,512]{2,1,0:T(8,128)(2,1)S(1)}, u32[]{:S(2)}, u32[]{:S(2)}) collective-permute-start(bf16[1,96,512]{2,1,0:T(8,128)(2,1)S(1)} %get-tuple-element.329), channel_id=1, source_target_pairs={{0,16},{1,17},{2,18},{3,19},{4,20},{5,21},{6,22},{7,23},{8,24},{9,... | collective-permute-start | bytes 294920 | tf_op jit(solution)/shard_map/ppermute | solution.py:692
  391.0 39.9 %collective-permute-start.32 = (bf16[1,96,512]{2,1,0:T(8,128)(2,1)S(1)}, bf16[1,96,512]{2,1,0:T(8,128)(2,1)S(1)}, u32[]{:S(2)}, u32[]{:S(2)}) collective-permute-start(bf16[1,96,512]{2,1,0:T(8,128)(2,1)S(1)} %get-tuple-element.330), channel_id=1, source_target_pairs={{0,24},{1,25},{2,26},{3,27},{4,28},{5,29},{6,30},{7,31},{8,16},{9,... | collective-permute-start | bytes 294920 | tf_op jit(solution)/shard_map/ppermute | solution.py:692
  393.0 38.0 %collective-permute-start.27 = (bf16[4,96,512]{2,1,0:T(8,128)(2,1)S(1)}, bf16[4,96,512]{2,1,0:T(8,128)(2,1)S(1)}, u32[]{:S(2)}, u32[]{:S(2)}) collective-permute-start(bf16[4,96,512]{2,1,0:T(8,128)(2,1)S(1)} %get-tuple-element.324), channel_id=1, source_target_pairs={{0,2},{1,3},{2,0},{3,1},{4,6},{5,7},{6,4},{7,5},{8,10},{9,11},{10,... | collective-permute-start | bytes 1179656 | tf_op jit(solution)/shard_map/ppermute | solution.py:692
  395.4 35.6 %collective-permute-start.28 = (bf16[4,96,512]{2,1,0:T(8,128)(2,1)S(1)}, bf16[4,96,512]{2,1,0:T(8,128)(2,1)S(1)}, u32[]{:S(2)}, u32[]{:S(2)}) collective-permute-start(bf16[4,96,512]{2,1,0:T(8,128)(2,1)S(1)} %get-tuple-element.325), channel_id=1, source_target_pairs={{0,4},{1,5},{2,6},{3,7},{4,0},{5,1},{6,2},{7,3},{8,12},{9,13},{10,... | collective-permute-start | bytes 1179656 | tf_op jit(solution)/shard_map/ppermute | solution.py:692
  395.6 35.4 %collective-permute-start.29 = (bf16[4,96,512]{2,1,0:T(8,128)(2,1)S(1)}, bf16[4,96,512]{2,1,0:T(8,128)(2,1)S(1)}, u32[]{:S(2)}, u32[]{:S(2)}) collective-permute-start(bf16[4,96,512]{2,1,0:T(8,128)(2,1)S(1)} %get-tuple-element.326), channel_id=1, source_target_pairs={{0,6},{1,7},{2,4},{3,5},{4,2},{5,3},{6,0},{7,1},{8,14},{9,15},{10,... | collective-permute-start | bytes 1179656 | tf_op jit(solution)/shard_map/ppermute | solution.py:692
  457.9 43.0 %collective-permute-start.40 = (bf16[1,96,512]{2,1,0:T(8,128)(2,1)S(1)}, bf16[1,96,512]{2,1,0:T(8,128)(2,1)S(1)}, u32[]{:S(2)}, u32[]{:S(2)}) collective-permute-start(bf16[1,96,512]{2,1,0:T(8,128)(2,1)S(1)} %get-tuple-element.374), channel_id=1, source_target_pairs={{0,16},{1,17},{2,18},{3,19},{4,20},{5,21},{6,22},{7,23},{8,24},{9,... | collective-permute-start | bytes 294920 | tf_op jit(solution)/shard_map/ppermute | solution.py:692
  460.6 40.3 %collective-permute-start.41 = (bf16[1,96,512]{2,1,0:T(8,128)(2,1)S(1)}, bf16[1,96,512]{2,1,0:T(8,128)(2,1)S(1)}, u32[]{:S(2)}, u32[]{:S(2)}) collective-permute-start(bf16[1,96,512]{2,1,0:T(8,128)(2,1)S(1)} %get-tuple-element.375), channel_id=1, source_target_pairs={{0,24},{1,25},{2,26},{3,27},{4,28},{5,29},{6,30},{7,31},{8,16},{9,... | collective-permute-start | bytes 294920 | tf_op jit(solution)/shard_map/ppermute | solution.py:692
  462.6 38.3 %collective-permute-start.36 = (bf16[4,96,512]{2,1,0:T(8,128)(2,1)S(1)}, bf16[4,96,512]{2,1,0:T(8,128)(2,1)S(1)}, u32[]{:S(2)}, u32[]{:S(2)}) collective-permute-start(bf16[4,96,512]{2,1,0:T(8,128)(2,1)S(1)} %get-tuple-element.369), channel_id=1, source_target_pairs={{0,2},{1,3},{2,0},{3,1},{4,6},{5,7},{6,4},{7,5},{8,10},{9,11},{10,... | collective-permute-start | bytes 1179656 | tf_op jit(solution)/shard_map/ppermute | solution.py:692
  463.5 37.5 %collective-permute-start.37 = (bf16[4,96,512]{2,1,0:T(8,128)(2,1)S(1)}, bf16[4,96,512]{2,1,0:T(8,128)(2,1)S(1)}, u32[]{:S(2)}, u32[]{:S(2)}) collective-permute-start(bf16[4,96,512]{2,1,0:T(8,128)(2,1)S(1)} %get-tuple-element.370), channel_id=1, source_target_pairs={{0,4},{1,5},{2,6},{3,7},{4,0},{5,1},{6,2},{7,3},{8,12},{9,13},{10,... | collective-permute-start | bytes 1179656 | tf_op jit(solution)/shard_map/ppermute | solution.py:692
  464.0 37.0 %collective-permute-start.38 = (bf16[4,96,512]{2,1,0:T(8,128)(2,1)S(1)}, bf16[4,96,512]{2,1,0:T(8,128)(2,1)S(1)}, u32[]{:S(2)}, u32[]{:S(2)}) collective-permute-start(bf16[4,96,512]{2,1,0:T(8,128)(2,1)S(1)} %get-tuple-element.371), channel_id=1, source_target_pairs={{0,6},{1,7},{2,4},{3,5},{4,2},{5,3},{6,0},{7,1},{8,14},{9,15},{10,... | collective-permute-start | bytes 1179656 | tf_op jit(solution)/shard_map/ppermute | solution.py:692
  501.0 19.7 %collective-permute-start.42 = (bf16[1024,512]{1,0:T(8,128)(2,1)}, bf16[1024,512]{1,0:T(8,128)(2,1)}, u32[]{:S(2)}, u32[]{:S(2)}) collective-permute-start(bf16[1024,512]{1,0:T(8,128)(2,1)} %get-tuple-element.385), channel_id=1, source_target_pairs={{0,1},{1,2},{2,3},{3,4},{4,5},{5,6},{6,7},{7,8},{8,9},{9,10},{10,1... | collective-permute-start | bytes 3145736 | tf_op jit(solution)/shard_map/ppermute | solution.py:707
  520.7 25.0 %collective-permute-start.44 = (bf16[16,96,512]{2,1,0:T(8,128)(2,1)}, bf16[16,96,512]{2,1,0:T(8,128)(2,1)}, u32[]{:S(2)}, u32[]{:S(2)}) collective-permute-start(bf16[16,96,512]{2,1,0:T(8,128)(2,1)} %get-tuple-element.404), channel_id=1, source_target_pairs={{0,1},{1,0},{2,3},{3,2},{4,5},{5,4},{6,7},{7,6},{8,9},{9,8},{10,11... | collective-permute-start | bytes 4718600 | tf_op jit(solution)/shard_map/ppermute | solution.py:692
  551.0 19.7 %collective-permute-start.57 = (bf16[4,96,512]{2,1,0:T(8,128)(2,1)S(1)}, bf16[4,96,512]{2,1,0:T(8,128)(2,1)S(1)}, u32[]{:S(2)}, u32[]{:S(2)}) collective-permute-start(bf16[4,96,512]{2,1,0:T(8,128)(2,1)S(1)} %get-tuple-element.434), channel_id=1, source_target_pairs={{0,6},{1,7},{2,4},{3,5},{4,2},{5,3},{6,0},{7,1},{8,14},{9,15},{10,... | collective-permute-start | bytes 1179656 | tf_op jit(solution)/shard_map/ppermute | solution.py:692
  554.2 22.0 %collective-permute-start.49 = (bf16[4,40,512]{2,1,0:T(8,128)(2,1)S(1)}, bf16[4,40,512]{2,1,0:T(8,128)(2,1)S(1)}, u32[]{:S(2)}, u32[]{:S(2)}) collective-permute-start(bf16[4,40,512]{2,1,0:T(8,128)(2,1)S(1)} %get-tuple-element.422), channel_id=1, source_target_pairs={{0,2},{1,3},{2,0},{3,1},{4,6},{5,7},{6,4},{7,5},{8,10},{9,11},{10,... | collective-permute-start | bytes 491528 | tf_op jit(solution)/shard_map/ppermute | solution.py:692
  (87 other events, 1313.3 us)
Sparse Core Ops, SparseCore 0:
  39.1 62.8 all-gather.2
  105.5 86.3 all-gather.4

commit v6 on v5

--- a/solution.py
+++ b/solution.py
@@ -534,10 +534,10 @@
     @pl.when(pl.program_id(0) == 0)
     def _():
         for index, piece in enumerate(pieces):
-            core, low_digit = index // (pieces_count // 2), index % (pieces_count // 2)
-
-            def move(digit, carry, piece=piece, core=core, low_digit=low_digit):
-                relative = digit * pieces_count + low_digit * 2 + core
+            base = (index // 2) + (index % 2) * 4
+
+            def move(digit, carry, piece=piece, base=base):
+                relative = (digit // 2) * 8 + (digit % 2) * 2 + base
                 place = pl.multiple_of((relative ^ self_id[0]) * share, share)
                 for j in range(count):
                     weights[j, pl.ds(place, share), :] = piece[digit, j * share : (j + 1) * share, :]
@@ -585,11 +585,13 @@
     )(self_id, *pieces, *blocks)
 
 
-def tail_kernel(self_id, before, middle, after, latent_low, inputs, grad_grid, head, misc, *refs):
-    keep, send, sums = refs
+def tail_kernel(self_id, loss, before, middle, after, latent_low, inputs, grad_grid, head, *refs):
+    gains = refs[:-3]
+    keep, send, sums = refs[-3:]
     step = pl.program_id(0)
     rows, width = inputs.shape
-    share = misc.shape[1]
+    share = width // (2 * keep.shape[0])
+    gain_count = 2 * len(gains)
 
     @pl.when(step == 0)
     def _():
@@ -606,40 +608,39 @@
 
     @pl.when(step == pl.num_programs(0) - 1)
     def _():
-        size = sums.shape[0] * (width // misc.shape[0])
+        size = sums.shape[0] * share
         main = [out.at[:, 0:size, :] for out in (keep, send)]
         deal(self_id, sums, main)
+        gain_rows = jnp.concatenate([gain[...] for gain in gains], axis=0)
+        lane = lax.broadcasted_iota(jnp.int32, gain_rows.shape, 1)
 
         def move(node, carry):
             for core, out in enumerate((keep, send)):
-                out[node, size : size + share, :] = misc[(2 * node + core) ^ self_id[0]].astype(
-                    out.dtype
-                )
+                device = (2 * node + core) ^ self_id[0]
+                turned = pltpu.roll(gain_rows, width - device * share, axis=1)
+                out[node, size : size + gain_count, :] = jnp.where(
+                    lane == share, loss[0], turned
+                ).astype(out.dtype)
             return carry
 
         lax.fori_loop(0, keep.shape[0], move, 0)
 
 
-def tail_layer(self_id, from_before, slot_grad, from_after, latent_low, inputs, grad_grid, head, misc):
+def tail_layer(
+    self_id, device_count, loss, from_before, slot_grad, from_after, latent_low, inputs, grad_grid, head, gains
+):
     block_rows, width = inputs.shape
-    device_count = misc.shape[0]
     rows = WEIGHT_ROWS
     tile = tiled(rows, width)
-    shape = (device_count // 2, 2 * (width // device_count) + misc.shape[1], width)
+    gain_count = 2 * len(gains)
+    shape = (device_count // 2, 2 * (width // device_count) + gain_count, width)
     return pl.pallas_call(
         tail_kernel,
         grid=(block_rows // rows,),
-        in_specs=[
-            pl.BlockSpec(memory_space=pltpu.SMEM),
-            tile,
-            tile,
-            tile,
-            tile,
-            tile,
-            tile,
-            matrix_spec(head[1], 1, width),
-            whole(misc.shape),
-        ],
+        in_specs=[pl.BlockSpec(memory_space=pltpu.SMEM)] * 2
+        + [tile] * 6
+        + [matrix_spec(head[1], 1, width)]
+        + [whole((2, width))] * len(gains),
         out_specs=[whole(shape)] * 2,
         out_shape=[on_chip(shape, WIDE), on_chip(shape, SEND)],
         scratch_shapes=[pltpu.VMEM((2, width, width), WIDE)],
@@ -652,8 +653,9 @@
         name="tail_layer",
     )(
         self_id,
+        loss,
         *map(pinned, (from_before, slot_grad, from_after, latent_low, inputs, grad_grid, head[0])),
-        misc,
+        *gains,
     )
 
 
@@ -692,19 +694,27 @@
     return lax.ppermute(cells, AXES, [(i, i ^ mask) for i in range(count)])
 
 
-def spread_column(packed, count):
-    high = 4 * 2
-    return [packed] + [swap(packed, count, digit * high) for digit in range(1, count // high)]
-
-
-def spread_rows(held, count):
-    column = jnp.stack(held)
-    near = [column] + [swap(column, count, digit * 2) for digit in range(1, 4)]
-    return near + [swap(piece, count, 1) for piece in near]
-
-
-def shift(cells, count, step):
-    return lax.ppermute(cells, AXES, [(i, (i + step) % count) for i in range(count)])
+def spread_rows(row_pair, count, first_bulk, second_bulk):
+    pair = jnp.stack(row_pair)
+    column = [pair] + [swap(pair, count, digit * 8) for digit in range(1, count // 8)]
+    column, first_bulk = together(column, first_bulk)
+    plane = jnp.concatenate(column)
+    near = [plane, swap(plane, count, 4)]
+    near, second_bulk = together(near, second_bulk)
+    return near + [swap(piece, count, 1) for piece in near], first_bulk, second_bulk
+
+
+def home(block, direct):
+    return block ^ (((block >> 2) & 1) << 1) if direct else block
+
+
+def bring(cells, count, step, direct):
+    return lax.ppermute(cells, AXES, [(i, home((i + step) % count, direct)) for i in range(count)])
+
+
+def shift(cells, count, step, direct):
+    pairs = [(home(i, direct), home((i + step) % count, direct)) for i in range(count)]
+    return lax.ppermute(cells, AXES, pairs)
 
 
 def fan_out(pieces, count, unit):
@@ -764,9 +774,9 @@
     share = w_layers.shape[2]
     channels, outputs = w_in.shape[0], w_out.shape[1]
     direct = share == 16 and device_count % 8 == 0 and device_count & (device_count - 1) == 0
-    slot_lists = [encoder_lists.T.reshape(-1)]
-    slot_lists += [mesh_lists.T.reshape(-1)] * (layer_total - 2)
-    slot_lists += [decoder_lists.T.reshape(-1)]
+    slot_lists = [encoder_lists.T.reshape(-1), mesh_lists.T.reshape(-1), decoder_lists.T.reshape(-1)]
+    local_rows = jnp.arange(row_count, dtype=jnp.int32)
+    weight_rows = area_weight * (local_rows < valid_rows[0]).astype(WIDE)
     if direct:
         self_id = lax.axis_index(AXES).astype(jnp.int32)
         order = jnp.arange(device_count, dtype=jnp.int32) ^ self_id
@@ -791,23 +801,36 @@
             ],
             axis=0,
         )
-        held = spread_column(packed, device_count)
-        sides = [shift(inputs, device_count, 1), shift(inputs, device_count, -1)]
-        held, sides = together(held, [*sides, second])
-        second = lax.all_gather(sides[2], AXES, axis=1, tiled=True)
-        pieces = spread_rows(held, device_count)
-        pieces, (rest,) = together(pieces, [rest])
+        lists = jnp.concatenate(slot_lists).reshape(-1, LANES)
+        lists = bring(lists, device_count, 0, direct)
+        goals = jnp.concatenate([targets, weight_rows[:, None]], axis=1)
+        goals = jnp.pad(goals, ((0, 0), (0, -goals.shape[1] % LANES)))
+        row_pair = [packed, swap(packed, device_count, 2)]
+        sides = [bring(inputs, device_count, step, direct) for step in (1, 0, -1)]
+        mesh_rows = bring(mesh_static, device_count, 0, direct)
+        second = lax.all_gather(second, AXES, axis=1, tiled=True)
+        pieces, (mesh_rows, before, after, lists), (own,) = spread_rows(
+            row_pair, device_count, [mesh_rows, sides[0], sides[2], lists], [sides[1]]
+        )
+        sides = [before, own, after]
+        pieces, (rest, goals) = together(pieces, [rest, goals])
         rest = lax.all_gather(rest, AXES, axis=1, tiled=True)
+        inputs = own
+        lists = lists.reshape(len(slot_lists), -1)
+        slot_lists = [lists[index] for index in range(len(slot_lists))]
         first, grid_latent, grid_start, *blocks = embed(
-            self_id, pieces, (sides[0], inputs, sides[1])
+            self_id, pieces, sides
         )
+        first, goals = lax.optimization_barrier((first, goals))
+        goals = bring(goals, device_count, 0, direct)
+        targets, weight_rows = goals[:, :outputs], goals[:, outputs]
         weights = [(first, 0), (second, 0)]
         weights += [(rest, 6 * layer_id) for layer_id in range(layer_total - 2)]
         heads = [(first, 0), (first, 6), (second, 0)]
         heads += weights[3:]
         table_out = rest[0, :, :outputs]
         gain_rows = jnp.stack(pieces)[:, :, packed.shape[0] - 8, : flat_gains.shape[1]]
-        gain_rows = gain_rows.reshape(2, 4, device_count // 8, -1).transpose(2, 1, 0, 3)
+        gain_rows = gain_rows.reshape(2, 2, device_count // 8, 2, -1).transpose(2, 1, 3, 0, 4)
         gain_rows = gain_rows.reshape(device_count, -1)[order]
         gains = gain_rows.reshape(device_count, layer_total, 2, share).transpose(1, 2, 0, 3)
         gains = gains.reshape(layer_total, 2, width).astype(WIDE)
@@ -823,8 +846,10 @@
         grid_latent = product(grid_inputs, table_in)
         grid_start = grid_latent.astype(LOW)
         sent = product(grid_start, matrices[0]).astype(LOW)
-        blocks = (shift(sent, device_count, 1), sent, shift(sent, device_count, -1))
-    target, target_low = mesh_static, mesh_static
+        blocks = (shift(sent, device_count, 1, direct), sent, shift(sent, device_count, -1, direct))
+        mesh_rows = mesh_static
+    slot_lists = [slot_lists[0]] + [slot_lists[1]] * (layer_total - 2) + [slot_lists[2]]
+    target, target_low = mesh_rows, mesh_rows
     stored_list = []
     for layer_id in range(layer_total):
         last_layer = layer_id == layer_total - 1
@@ -846,13 +871,11 @@
             grid_low, kept, aggregate = results
         else:
             sent, updated, updated_low, kept, aggregate = results
-            blocks = (shift(sent, device_count, 1), sent, shift(sent, device_count, -1))
+            blocks = (shift(sent, device_count, 1, direct), sent, shift(sent, device_count, -1, direct))
         stored_list.append((source_low, (target_low, kept, aggregate), aggregate))
         if not last_layer:
             target, target_low = updated, updated_low
     prediction = product(grid_low, table_out)
-    local_rows = jnp.arange(row_count, dtype=jnp.int32)
-    weight_rows = area_weight * (local_rows < valid_rows[0]).astype(WIDE)
     error_rows = prediction - targets
     loss_scale = 1.0 / (row_count * device_count * prediction.shape[1])
     loss_local = jnp.sum(weight_rows[:, None] * error_rows * error_rows) * loss_scale
@@ -877,8 +900,8 @@
             if in_slice:
                 layer_grads[layer_id + 2] = add_up(arrived[moved:]).reshape(6, share, width)
             far = list(combine(arrived[:moved], device_count // 8))
-        from_before = shift(slot_grads[2], device_count, 1)
-        from_after = shift(slot_grads[0], device_count, -1)
+        from_before = shift(slot_grads[2], device_count, 1, direct)
+        from_after = shift(slot_grads[0], device_count, -1, direct)
         back = [edge_hidden, grad_message, b0, b1, b2, b3]
         grad_part, sums = weight_layer(
             self_id,
@@ -909,14 +932,10 @@
         above = (from_before, slot_grads[1], from_after, heads[layer_id])
         above_source = source_low
     if direct:
-        misc = jnp.stack(gain_grads).reshape(-1, device_count, share).transpose(1, 0, 2)
-        misc = misc.reshape(device_count, -1)
-        misc = jnp.concatenate(
-            [misc, jnp.broadcast_to(loss_local.reshape(1, 1), (device_count, 1))], axis=1
-        )
-        misc = jnp.pad(misc[:, None, :], ((0, 0), (0, 7), (0, width - misc.shape[1])))
         sums = tail_layer(
             self_id,
+            device_count,
+            loss_local.reshape(1),
             from_before,
             slot_grads[1],
             from_after,
@@ -924,7 +943,7 @@
             inputs,
             grad_grid,
             heads[0],
-            misc,
+            gain_grads,
         )
         arrived, sums = together([other] + in_slice, sums)
         other, in_slice = arrived[0], arrived[1:]
@@ -938,9 +957,8 @@
         total = add_up(fan_out(pieces, device_count, 8))
         grad_zero = total[:share]
         grad_in = total[share : 2 * share, :channels].T
-        size = layer_total * 2 * share
-        grad_gain_all = total[2 * share, :size].reshape(layer_total, 2, share)
-        loss_value = total[2 * share, size]
+        grad_gain_all = total[2 * share :, :share].reshape(layer_total, 2, share)
+        loss_value = total[2 * share, share]
         grad_out = layer_grads[-1][0, :, :outputs]
     else:
         loss_value = lax.psum(loss_local, AXES)

time: 614 us -> 610 us (level)
  starting transfers between devices: 134 us -> 145 us
  waiting for transfers between devices: 140 us -> 129 us
  local copies, waits for them, and re-layouts: 27.6 us -> 18 us
    ppermute x45 -> x42, starting transfers between devices: 83.2 us -> 101 us  [swap(): return lax.ppermute(cells, AXES, [(i, i ^ mask) for i in range(count)])]
    all_gather x1, waiting for transfers between devices: 13.4 us -> 0.01 us  [shards(): rest = lax.all_gather(rest, AXES, axis=1, tiled=True)]
    ppermute x45 -> x42, waiting for transfers between devices: 72 us -> 84.7 us  [swap(): return lax.ppermute(cells, AXES, [(i, i ^ mask) for i in range(count)])]
    ppermute x16 -> x20, waiting for transfers between devices: 54.4 us -> 44.2 us  [the longest x14 44.1 us: shift(): return lax.ppermute(cells, AXES, pairs)]
    ppermute x16 -> x20, starting transfers between devices: 51.2 us -> 44.7 us  [the longest x14 32.3 us: shift(): return lax.ppermute(cells, AXES, pairs)]
    unnamed x130 -> x140, local copies, waits for them, and re-layouts: 13.9 us -> 9.51 us
  transfers between devices with their start and end apart: 63 -> 64, of which waited for: 22 -> 19; matrix products, arithmetic and copies ran while one was open for 3% -> 3% of each run, Pallas kernels for 33% -> 37%
where the time goes in v6:
time: 610 us; the launch traced here: 603 us
  Pallas kernels  275 us (45%)
  starting transfers between devices  145 us (24%)
  waiting for transfers between devices  129 us (21%)
  local copies, waits for them, and re-layouts  18 us (3%)
  between operations  17.4 us (3%)
  other arithmetic  12.1 us (2%)
    pallas_call x4, Pallas kernels, backward_layer(): pl.pallas_call(functools.partial(backward_kernel, parts, mode), grid=(blo...  132 us
    ppermute x42, starting transfers between devices, swap(): return lax.ppermute(cells, AXES, [(i, i ^ mask) for i in range(count)])  101 us
    ppermute x42, waiting for transfers between devices, swap(): return lax.ppermute(cells, AXES, [(i, i ^ mask) for i in range(count)])  84.7 us
    pallas_call x4, Pallas kernels, forward_layer(): pl.pallas_call(functools.partial(forward_kernel, parts, has_next), grid=(...  79.7 us
    ppermute x14, waiting for transfers between devices, shift(): return lax.ppermute(cells, AXES, pairs)  44.1 us
    pallas_call x4, Pallas kernels, weight_layer(): pl.pallas_call(functools.partial(weight_kernel, above is not None, grad_n...  42.4 us
    ppermute x14, starting transfers between devices, shift(): return lax.ppermute(cells, AXES, pairs)  32.3 us
    ppermute x6, starting transfers between devices, bring(): lax.ppermute(cells, AXES, [(i, home((i + step) % count, direct)) for i in...  12.4 us
  transfers between devices with their start and end apart: 64, of which 19 were waited for; matrix products, arithmetic and copies ran while one was open for 3% of the time, Pallas kernels for 37%

profile of v6, /device:TPU:0, one launch (start us, length us, event | category | flops | bytes accessed | tf_op | source)
XLA Modules:
  0.0 602.7 jit_solution(2170876437217737356)
XLA Ops:
  12.1 5.7 collective-permute-start.6
  20.5 12.6 %collective-permute-done = bf16[136,512]{1,0:T(8,128)(2,1)S(1)} collective-permute-done((bf16[136,512]{1,0:T(8,128)(2,1)S(1)}, bf16[136,512]{1,0:T(8,128)(2,1)S(1)}, u32[]{:S(2)}, u32[]{:S(2)}) %collective-permute-start) | collective-permute-done | bytes 139296 | tf_op jit(solution)/shard_map/ppermute | solution.py:694
  39.0 4.5 collective-permute-done.1
  46.9 14.6 %collective-permute-done.2 = bf16[2,136,512]{2,1,0:T(8,128)(2,1)S(1)} collective-permute-done((bf16[2,136,512]{2,1,0:T(8,128)(2,1)S(1)}, bf16[2,136,512]{2,1,0:T(8,128)(2,1)S(1)}, u32[]{:S(2)}, u32[]{:S(2)}) %collective-permute-start.2) | collective-permute-done | bytes 278560 | tf_op jit(solution)/shard_map/ppermute | solution.py:694
  62.8 53.4 %collective-permute-start.8 = (bf16[8,136,512]{2,1,0:T(8,128)(2,1)S(1)}, bf16[8,136,512]{2,1,0:T(8,128)(2,1)S(1)}, u32[]{:S(2)}, u32[]{:S(2)}) collective-permute-start(bf16[8,136,512]{2,1,0:T(8,128)(2,1)S(1)} %constant_dynamic-update-slice_fusion.refs_1_), channel_id=1, source_target_pairs={{0,4},{1,5},{2,6},{3,7},{4,0},{5,1},{6,2},{7,3},{8,12},{9,13},{10,... | collective-permute-start | bytes 3342344 | tf_op jit(solution)/shard_map/ppermute | solution.py:694
  118.1 22.8 %collective-permute-done.8.refs_2_ = bf16[8,136,512]{2,1,0:T(8,128)(2,1)S(1)} collective-permute-done((bf16[8,136,512]{2,1,0:T(8,128)(2,1)S(1)}, bf16[8,136,512]{2,1,0:T(8,128)(2,1)S(1)}, u32[]{:S(2)}, u32[]{:S(2)}) %collective-permute-start.8) | collective-permute-done | bytes 1114144 | tf_op jit(solution)/shard_map/ppermute | solution.py:694
  149.6 9.8 %embed.1 = (bf16[7,512,512]{2,1,0:T(8,128)(2,1)}, f32[1024,512]{1,0:T(8,128)}, bf16[1024,512]{1,0:T(8,128)(2,1)}, bf16[1024,512]{1,0:T(8,128)(2,1)S(1)}, bf16[10...) custom-call(s32[1]{0:T(128)} %bitcast.9.refs_0_.self_id, bf16[8,136,512]{2,1,0:T(8,128)(2,1)} %copy-done.17, ...), custom_call_target="tpu_custom_call" | custom-call | flops 3221225472 | bytes 12582912 | tf_op jit(solution)/shard_map/embed/pallas_call | solution.py:562
  159.4 20.2 %forward_layer.4 = (bf16[1024,512]{1,0:T(8,128)(2,1)}, f32[1024,512]{1,0:T(8,128)}, bf16[1024,512]{1,0:T(8,128)(2,1)}, bf16[4,1024,512]{2,1,0:T(8,128)(2,1)}, bf16[1024,512]{1,0:T(8,128)(2,1)}) custom-call(s32[4096]{0:T(1024)} %get-tuple-element.481.refs_0_, bf16[1024,512]{1,0:T(8,128)(2,1)S(1)} %get-tuple-element.252.refs_1_, ...), custom_call_target="tpu_custom_call" | custom-call | flops 4831838208 | bytes 25165824 | tf_op jit(solution)/shard_map/forward_layer/pallas_call | solution.py:186
  184.8 17.1 %collective-permute-done.13.refs_1_ = bf16[1024,512]{1,0:T(8,128)(2,1)S(1)} collective-permute-done((bf16[1024,512]{1,0:T(8,128)(2,1)}, bf16[1024,512]{1,0:T(8,128)(2,1)S(1)}, u32[]{:S(2)}, u32[]{:S(2)}) %collective-permute-start.13) | collective-permute-done | bytes 1048608 | tf_op jit(solution)/shard_map/ppermute | solution.py:717
  201.9 20.2 %forward_layer.5 = (bf16[1024,512]{1,0:T(8,128)(2,1)}, f32[1024,512]{1,0:T(8,128)}, bf16[1024,512]{1,0:T(8,128)(2,1)}, bf16[4,1024,512]{2,1,0:T(8,128)(2,1)}, bf16[1024,512]{1,0:T(8,128)(2,1)}) custom-call(s32[4096]{0:T(1024)} %get-tuple-element.482.refs_0_, bf16[1024,512]{1,0:T(8,128)(2,1)S(1)} %collective-permute-done.13.refs_1_, ...), custom_call_target="tpu_custom_call" | custom-call | flops 4831838208 | bytes 25165824 | tf_op jit(solution)/shard_map/forward_layer/pallas_call | solution.py:186
  222.2 4.4 collective-permute-start.16
  229.2 12.3 %collective-permute-done.15.refs_1_ = bf16[1024,512]{1,0:T(8,128)(2,1)S(1)} collective-permute-done((bf16[1024,512]{1,0:T(8,128)(2,1)}, bf16[1024,512]{1,0:T(8,128)(2,1)S(1)}, u32[]{:S(2)}, u32[]{:S(2)}) %collective-permute-start.15) | collective-permute-done | bytes 1048608 | tf_op jit(solution)/shard_map/ppermute | solution.py:717
  241.5 20.2 %forward_layer.6 = (bf16[1024,512]{1,0:T(8,128)(2,1)}, f32[1024,512]{1,0:T(8,128)}, bf16[1024,512]{1,0:T(8,128)(2,1)}, bf16[4,1024,512]{2,1,0:T(8,128)(2,1)}, bf16[1024,512]{1,0:T(8,128)(2,1)}) custom-call(s32[4096]{0:T(1024)} %get-tuple-element.482.refs_0_, bf16[1024,512]{1,0:T(8,128)(2,1)S(1)} %collective-permute-done.15.refs_1_, ...), custom_call_target="tpu_custom_call" | custom-call | flops 4831838208 | bytes 25165824 | tf_op jit(solution)/shard_map/forward_layer/pallas_call | solution.py:186
  261.7 4.4 collective-permute-start.18
  267.6 11.2 %collective-permute-done.17.refs_1_ = bf16[1024,512]{1,0:T(8,128)(2,1)S(1)} collective-permute-done((bf16[1024,512]{1,0:T(8,128)(2,1)}, bf16[1024,512]{1,0:T(8,128)(2,1)S(1)}, u32[]{:S(2)}, u32[]{:S(2)}) %collective-permute-start.17) | collective-permute-done | bytes 1048608 | tf_op jit(solution)/shard_map/ppermute | solution.py:717
  278.8 19.0 %forward_layer.7 = (bf16[1024,512]{1,0:T(8,128)(2,1)}, bf16[4,1024,512]{2,1,0:T(8,128)(2,1)}, bf16[1024,512]{1,0:T(8,128)(2,1)}) custom-call(s32[4096]{0:T(1024)} %get-tuple-element.483.refs_0_, bf16[1024,512]{1,0:T(8,128)(2,1)S(1)} %collective-permute-done.17.refs_1_, bf16[1024,512]{1,0:T(8,128)(2,1)} %get-tuple-element.264.refs_2_, ...), custom_call_target="tpu_custom_call" | custom-call | flops 4831838208 | bytes 25165824 | tf_op jit(solution)/shard_map/forward_layer/pallas_call | solution.py:186
  303.4 32.1 %backward_layer.4 = (bf16[1024,512]{1,0:T(8,128)(2,1)}, bf16[1024,512]{1,0:T(8,128)(2,1)}, bf16[1024,512]{1,0:T(8,128)(2,1)}, f32[2,512]{1,0:T(2,128)S(1)}, bf16...) custom-call(s32[4096]{0:T(1024)S(1)} %copy-done.5, ...), custom_call_target="tpu_custom_call" | custom-call | flops 4294967296 | bytes 25165824 | tf_op jit(solution)/shard_map/backward_layer/pallas_call | solution.py:374
  335.5 4.7 collective-permute-start.20
  340.8 10.8 %weight_layer.4 = (f32[1024,512]{1,0:T(8,128)}, f32[16,96,512]{2,1,0:T(8,128)S(1)}, bf16[16,96,512]{2,1,0:T(8,128)(2,1)S(1)}) custom-call(s32[1]{0:T(128)} %bitcast.9.refs_0_.self_id, f32[512,512]{1,0:T(8,128)S(1)} %pad.29.refs_1_, bf16[1024,512]{1,0:T(8,128)(2,1)} %get-tuple-element.265.refs_4_.refs_2_.latent_low, ...), custom_call_target="tpu_custom_call" | custom-call | flops 5368709120 | bytes 12582912 | tf_op jit(solution)/shard_map/weight_layer/pallas_call | solution.py:503
  360.1 33.0 %backward_layer.5 = (bf16[1024,512]{1,0:T(8,128)(2,1)S(1)}, f32[1024,512]{1,0:T(8,128)S(1)}, bf16[1024,512]{1,0:T(8,128)(2,1)}, bf16[1024,512]{1,0:T(8,128)(2,1)...) custom-call(s32[4096]{0:T(1024)S(1)} %copy-done.1, ...), custom_call_target="tpu_custom_call" | custom-call | flops 4294967296 | bytes 25165824 | tf_op jit(solution)/shard_map/backward_layer/pallas_call | solution.py:374
  393.2 4.8 collective-permute-start.26
  398.0 11.1 %weight_layer.5 = (f32[1024,512]{1,0:T(8,128)}, f32[16,96,512]{2,1,0:T(8,128)S(1)}, bf16[16,96,512]{2,1,0:T(8,128)(2,1)S(1)}) custom-call(s32[1]{0:T(128)} %bitcast.9.refs_0_.self_id, bf16[1024,512]{1,0:T(8,128)(2,1)} %get-tuple-element.302.refs_1_, bf16[1024,512]{1,0:T(8,128)(2,1)S(1)} %get-tuple-element.303.refs_2_, ...), custom_call_target="tpu_custom_call" | custom-call | flops 5368709120 | bytes 12582912 | tf_op jit(solution)/shard_map/weight_layer/pallas_call | solution.py:503
  419.0 34.1 %backward_layer.6 = (bf16[1024,512]{1,0:T(8,128)(2,1)S(1)}, f32[1024,512]{1,0:T(8,128)S(1)}, bf16[1024,512]{1,0:T(8,128)(2,1)}, bf16[1024,512]{1,0:T(8,128)(2,1)...) custom-call(s32[4096]{0:T(1024)S(1)} %copy-done.1, ...), custom_call_target="tpu_custom_call" | custom-call | flops 4294967296 | bytes 25165824 | tf_op jit(solution)/shard_map/backward_layer/pallas_call | solution.py:374
  453.2 4.6 collective-permute-start.35
  457.8 11.4 %weight_layer.6 = (f32[1024,512]{1,0:T(8,128)}, f32[16,96,512]{2,1,0:T(8,128)S(1)}, bf16[16,96,512]{2,1,0:T(8,128)(2,1)S(1)}) custom-call(s32[1]{0:T(128)} %bitcast.9.refs_0_.self_id, bf16[1024,512]{1,0:T(8,128)(2,1)} %get-tuple-element.261.refs_4_.refs_5_.refs_3_.refs_1_, bf16[1024,512]{1,0:T(8,128)(2,1)S(1)} %get-tuple-element.348.refs_2_, ...), custom_call_target="tpu_custom_call" | custom-call | flops 5368709120 | bytes 12582912 | tf_op jit(solution)/shard_map/weight_layer/pallas_call | solution.py:503
  478.8 32.7 %backward_layer.7 = (bf16[1024,512]{1,0:T(8,128)(2,1)S(1)}, f32[1024,512]{1,0:T(8,128)}, bf16[1024,512]{1,0:T(8,128)(2,1)}, bf16[1024,512]{1,0:T(8,128)(2,1)}, b...) custom-call(s32[4096]{0:T(1024)S(1)} %copy-done.4, ...), custom_call_target="tpu_custom_call" | custom-call | flops 4294967296 | bytes 25165824 | tf_op jit(solution)/shard_map/backward_layer/pallas_call | solution.py:374
  513.6 4.6 collective-permute-start.44
  520.5 9.2 %weight_layer.7 = (f32[16,96,512]{2,1,0:T(8,128)S(1)}, bf16[16,96,512]{2,1,0:T(8,128)(2,1)}) custom-call(s32[1]{0:T(128)} %bitcast.9.refs_0_.self_id, bf16[1024,512]{1,0:T(8,128)(2,1)} %get-tuple-element.258.refs_4_.refs_6_.refs_3_.refs_1_, bf16[1024,512]{1,0:T(8,128)(2,1)S(1)} %get-tuple-element.393.refs_2_, bf16[1024,512]{1,0:T(8,128)(2,1)} %copy-done.19, ...), custom_call_target="tpu_custom_call" | custom-call | flops 5368709120 | bytes 12582912 | tf_op jit(solution)/shard_map/weight_layer/pallas_call | solution.py:503
  537.5 7.0 %tail_layer.1 = (f32[16,40,512]{2,1,0:T(8,128)S(1)}, bf16[16,40,512]{2,1,0:T(8,128)(2,1)S(1)}) custom-call(s32[1]{0:T(128)} %bitcast.9.refs_0_.self_id, f32[1]{0:T(128)} %bitcast.50.loss, bf16[1024,512]{1,0:T(8,128)(2,1)} %collective-permute-done.43.before, bf16[1024,512]{1,0:T(8,128)(2,1)} %get-tuple-element.416.middle, ...), custom_call_target="tpu_custom_call" | custom-call | flops 1610612736 | bytes 12582912 | tf_op jit(solution)/shard_map/tail_layer/pallas_call | solution.py:637
  553.1 7.3 %collective-permute-done.56 = bf16[4,96,512]{2,1,0:T(8,128)(2,1)S(1)} collective-permute-done((bf16[4,96,512]{2,1,0:T(8,128)(2,1)S(1)}, bf16[4,96,512]{2,1,0:T(8,128)(2,1)S(1)}, u32[]{:S(2)}, u32[]{:S(2)}) %collective-permute-start.56) | collective-permute-done | bytes 393248 | tf_op jit(solution)/shard_map/ppermute | solution.py:694
  560.5 8.9 %collective-permute-done.58 = bf16[4,96,512]{2,1,0:T(8,128)(2,1)S(1)} collective-permute-done((bf16[4,96,512]{2,1,0:T(8,128)(2,1)S(1)}, bf16[4,96,512]{2,1,0:T(8,128)(2,1)S(1)}, u32[]{:S(2)}, u32[]{:S(2)}) %collective-permute-start.58) | collective-permute-done | bytes 393248 | tf_op jit(solution)/shard_map/ppermute | solution.py:694
  576.5 5.8 collective-permute-done.51
  (321 shorter events, 110.9 us)
Async XLA Ops:
  7.2 194.7 %all-gather.3.cloned.1.call-start = ((), (), s32[]{:S(2)}) async-start(), calls=%async_computation | async-start | bytes 3244032 | tf_op jit(solution)/shard_map/all_gather | solution.py:811
  9.8 231.6 %all-gather.5.cloned.1.call-start = ((), (), s32[]{:S(2)}) async-start(), calls=%async_computation.1 | async-start | bytes 6488064 | tf_op jit(solution)/shard_map/all_gather | solution.py:817
  11.6 49.9 %collective-permute-start.5 = (bf16[1024,512]{1,0:T(8,128)(2,1)}, bf16[1024,512]{1,0:T(8,128)(2,1)S(1)}, u32[]{:S(2)}, u32[]{:S(2)}) collective-permute-start(bf16[1024,512]{1,0:T(8,128)(2,1)} %pad.26), channel_id=1, source_target_pairs={{0,1},{1,2},{2,3},{3,6},{4,7},{5,4},{6,5},{7,8},{8,9},{9,10},{10,1... | collective-permute-start | bytes 3145736 | tf_op jit(solution)/shard_map/ppermute | solution.py:712
  12.1 49.4 %collective-permute-start.6 = (bf16[1024,512]{1,0:T(8,128)(2,1)}, bf16[1024,512]{1,0:T(8,128)(2,1)}, u32[]{:S(2)}, u32[]{:S(2)}) collective-permute-start(bf16[1024,512]{1,0:T(8,128)(2,1)} %pad.26), channel_id=1, source_target_pairs={{0,29},{1,0},{2,1},{3,2},{4,3},{5,6},{6,7},{7,4},{8,5},{9,8},{10,9... | collective-permute-start | bytes 3145736 | tf_op jit(solution)/shard_map/ppermute | solution.py:712
  17.7 43.8 %collective-permute-start.4 = (bf16[1024,512]{1,0:T(8,128)(2,1)}, bf16[1024,512]{1,0:T(8,128)(2,1)S(1)}, u32[]{:S(2)}, u32[]{:S(2)}) collective-permute-start(bf16[1024,512]{1,0:T(8,128)(2,1)} %param.22), channel_id=1, source_target_pairs={{0,0},{1,1},{2,2},{3,3},{4,6},{5,7},{6,4},{7,5},{8,8},{9,9},{10,10... | collective-permute-start | bytes 3145736 | tf_op jit(solution)/shard_map/ppermute | solution.py:712
  36.3 25.1 %collective-permute-start.2 = (bf16[2,136,512]{2,1,0:T(8,128)(2,1)S(1)}, bf16[2,136,512]{2,1,0:T(8,128)(2,1)S(1)}, u32[]{:S(2)}, u32[]{:S(2)}) collective-permute-start(bf16[2,136,512]{2,1,0:T(8,128)(2,1)S(1)} %pad_maximum_fusion), channel_id=1, source_target_pairs={{0,16},{1,17},{2,18},{3,19},{4,20},{5,21},{6,22},{7,23},{8,24},{9,... | collective-permute-start | bytes 835592 | tf_op jit(solution)/shard_map/ppermute | solution.py:694
  43.5 18.0 %collective-permute-start.3 = (bf16[2,136,512]{2,1,0:T(8,128)(2,1)S(1)}, bf16[2,136,512]{2,1,0:T(8,128)(2,1)S(1)}, u32[]{:S(2)}, u32[]{:S(2)}) collective-permute-start(bf16[2,136,512]{2,1,0:T(8,128)(2,1)S(1)} %pad_maximum_fusion), channel_id=1, source_target_pairs={{0,24},{1,25},{2,26},{3,27},{4,28},{5,29},{6,30},{7,31},{8,16},{9,... | collective-permute-start | bytes 835592 | tf_op jit(solution)/shard_map/ppermute | solution.py:694
  62.8 78.1 %collective-permute-start.8 = (bf16[8,136,512]{2,1,0:T(8,128)(2,1)S(1)}, bf16[8,136,512]{2,1,0:T(8,128)(2,1)S(1)}, u32[]{:S(2)}, u32[]{:S(2)}) collective-permute-start(bf16[8,136,512]{2,1,0:T(8,128)(2,1)S(1)} %constant_dynamic-update-slice_fusion.refs_1_), channel_id=1, source_target_pairs={{0,4},{1,5},{2,6},{3,7},{4,0},{5,1},{6,2},{7,3},{8,12},{9,13},{10,... | collective-permute-start | bytes 3342344 | tf_op jit(solution)/shard_map/ppermute | solution.py:694
  179.6 22.3 %collective-permute-start.13 = (bf16[1024,512]{1,0:T(8,128)(2,1)}, bf16[1024,512]{1,0:T(8,128)(2,1)S(1)}, u32[]{:S(2)}, u32[]{:S(2)}) collective-permute-start(bf16[1024,512]{1,0:T(8,128)(2,1)} %get-tuple-element.257.refs_2_), channel_id=1, source_target_pairs={{0,1},{1,2},{2,3},{3,6},{6,7},{7,4},{4,5},{5,8},{8,9},{9,10},{10,1... | collective-permute-start | bytes 3145736 | tf_op jit(solution)/shard_map/ppermute | solution.py:717
  179.7 22.2 %collective-permute-start.14 = (bf16[1024,512]{1,0:T(8,128)(2,1)}, bf16[1024,512]{1,0:T(8,128)(2,1)S(1)}, u32[]{:S(2)}, u32[]{:S(2)}) collective-permute-start(bf16[1024,512]{1,0:T(8,128)(2,1)} %get-tuple-element.257.refs_2_), channel_id=1, source_target_pairs={{0,29},{1,0},{2,1},{3,2},{6,3},{7,6},{4,7},{5,4},{8,5},{9,8},{10,9... | collective-permute-start | bytes 3145736 | tf_op jit(solution)/shard_map/ppermute | solution.py:717
  222.2 19.3 %collective-permute-start.15 = (bf16[1024,512]{1,0:T(8,128)(2,1)}, bf16[1024,512]{1,0:T(8,128)(2,1)S(1)}, u32[]{:S(2)}, u32[]{:S(2)}) collective-permute-start(bf16[1024,512]{1,0:T(8,128)(2,1)} %get-tuple-element.260.refs_2_), channel_id=1, source_target_pairs={{0,1},{1,2},{2,3},{3,6},{6,7},{7,4},{4,5},{5,8},{8,9},{9,10},{10,1... | collective-permute-start | bytes 3145736 | tf_op jit(solution)/shard_map/ppermute | solution.py:717
  222.2 19.3 %collective-permute-start.16 = (bf16[1024,512]{1,0:T(8,128)(2,1)}, bf16[1024,512]{1,0:T(8,128)(2,1)S(1)}, u32[]{:S(2)}, u32[]{:S(2)}) collective-permute-start(bf16[1024,512]{1,0:T(8,128)(2,1)} %get-tuple-element.260.refs_2_), channel_id=1, source_target_pairs={{0,29},{1,0},{2,1},{3,2},{6,3},{7,6},{4,7},{5,4},{8,5},{9,8},{10,9... | collective-permute-start | bytes 3145736 | tf_op jit(solution)/shard_map/ppermute | solution.py:717
  227.4 39.5 %collective-permute-start.12 = (f32[1024,256]{0,1:T(8,128)S(1)}, f32[1024,256]{0,1:T(8,128)}, u32[]{:S(2)}, u32[]{:S(2)}) collective-permute-start(f32[1024,256]{0,1:T(8,128)S(1)} %copy-done.24), channel_id=1, source_target_pairs={{0,0},{1,1},{2,2},{3,3},{4,6},{5,7},{6,4},{7,5},{8,8},{9,9},{10,10... | collective-permute-start | bytes 3145736 | tf_op jit(solution)/shard_map/ppermute | solution.py:712
  335.5 17.3 %collective-permute-start.20 = (bf16[1024,512]{1,0:T(8,128)(2,1)}, bf16[1024,512]{1,0:T(8,128)(2,1)S(1)}, u32[]{:S(2)}, u32[]{:S(2)}) collective-permute-start(bf16[1024,512]{1,0:T(8,128)(2,1)} %get-tuple-element.271), channel_id=1, source_target_pairs={{0,29},{1,0},{2,1},{3,2},{6,3},{7,6},{4,7},{5,4},{8,5},{9,8},{10,9... | collective-permute-start | bytes 3145736 | tf_op jit(solution)/shard_map/ppermute | solution.py:717
  356.6 36.5 %collective-permute-start.22 = (bf16[4,96,512]{2,1,0:T(8,128)(2,1)S(1)}, bf16[4,96,512]{2,1,0:T(8,128)(2,1)S(1)}, u32[]{:S(2)}, u32[]{:S(2)}) collective-permute-start(bf16[4,96,512]{2,1,0:T(8,128)(2,1)S(1)} %get-tuple-element.289), channel_id=1, source_target_pairs={{0,2},{1,3},{2,0},{3,1},{4,6},{5,7},{6,4},{7,5},{8,10},{9,11},{10,... | collective-permute-start | bytes 1179656 | tf_op jit(solution)/shard_map/ppermute | solution.py:694
  356.7 36.5 %collective-permute-start.23 = (bf16[4,96,512]{2,1,0:T(8,128)(2,1)S(1)}, bf16[4,96,512]{2,1,0:T(8,128)(2,1)S(1)}, u32[]{:S(2)}, u32[]{:S(2)}) collective-permute-start(bf16[4,96,512]{2,1,0:T(8,128)(2,1)S(1)} %get-tuple-element.290), channel_id=1, source_target_pairs={{0,4},{1,5},{2,6},{3,7},{4,0},{5,1},{6,2},{7,3},{8,12},{9,13},{10,... | collective-permute-start | bytes 1179656 | tf_op jit(solution)/shard_map/ppermute | solution.py:694
  356.9 36.2 %collective-permute-start.24 = (bf16[4,96,512]{2,1,0:T(8,128)(2,1)S(1)}, bf16[4,96,512]{2,1,0:T(8,128)(2,1)S(1)}, u32[]{:S(2)}, u32[]{:S(2)}) collective-permute-start(bf16[4,96,512]{2,1,0:T(8,128)(2,1)S(1)} %get-tuple-element.291), channel_id=1, source_target_pairs={{0,6},{1,7},{2,4},{3,5},{4,2},{5,3},{6,0},{7,1},{8,14},{9,15},{10,... | collective-permute-start | bytes 1179656 | tf_op jit(solution)/shard_map/ppermute | solution.py:694
  393.2 17.4 %collective-permute-start.26 = (bf16[1024,512]{1,0:T(8,128)(2,1)}, bf16[1024,512]{1,0:T(8,128)(2,1)S(1)}, u32[]{:S(2)}, u32[]{:S(2)}) collective-permute-start(bf16[1024,512]{1,0:T(8,128)(2,1)} %get-tuple-element.301), channel_id=1, source_target_pairs={{0,29},{1,0},{2,1},{3,2},{6,3},{7,6},{4,7},{5,4},{8,5},{9,8},{10,9... | collective-permute-start | bytes 3145736 | tf_op jit(solution)/shard_map/ppermute | solution.py:717
  410.7 42.4 %collective-permute-start.32 = (bf16[1,96,512]{2,1,0:T(8,128)(2,1)S(1)}, bf16[1,96,512]{2,1,0:T(8,128)(2,1)S(1)}, u32[]{:S(2)}, u32[]{:S(2)}) collective-permute-start(bf16[1,96,512]{2,1,0:T(8,128)(2,1)S(1)} %get-tuple-element.335), channel_id=1, source_target_pairs={{0,16},{1,17},{2,18},{3,19},{4,20},{5,21},{6,22},{7,23},{8,24},{9,... | collective-permute-start | bytes 294920 | tf_op jit(solution)/shard_map/ppermute | solution.py:694
  412.5 40.6 %collective-permute-start.33 = (bf16[1,96,512]{2,1,0:T(8,128)(2,1)S(1)}, bf16[1,96,512]{2,1,0:T(8,128)(2,1)S(1)}, u32[]{:S(2)}, u32[]{:S(2)}) collective-permute-start(bf16[1,96,512]{2,1,0:T(8,128)(2,1)S(1)} %get-tuple-element.336), channel_id=1, source_target_pairs={{0,24},{1,25},{2,26},{3,27},{4,28},{5,29},{6,30},{7,31},{8,16},{9,... | collective-permute-start | bytes 294920 | tf_op jit(solution)/shard_map/ppermute | solution.py:694
  415.5 37.7 %collective-permute-start.28 = (bf16[4,96,512]{2,1,0:T(8,128)(2,1)S(1)}, bf16[4,96,512]{2,1,0:T(8,128)(2,1)S(1)}, u32[]{:S(2)}, u32[]{:S(2)}) collective-permute-start(bf16[4,96,512]{2,1,0:T(8,128)(2,1)S(1)} %get-tuple-element.330), channel_id=1, source_target_pairs={{0,2},{1,3},{2,0},{3,1},{4,6},{5,7},{6,4},{7,5},{8,10},{9,11},{10,... | collective-permute-start | bytes 1179656 | tf_op jit(solution)/shard_map/ppermute | solution.py:694
  415.6 37.6 %collective-permute-start.29 = (bf16[4,96,512]{2,1,0:T(8,128)(2,1)S(1)}, bf16[4,96,512]{2,1,0:T(8,128)(2,1)S(1)}, u32[]{:S(2)}, u32[]{:S(2)}) collective-permute-start(bf16[4,96,512]{2,1,0:T(8,128)(2,1)S(1)} %get-tuple-element.331), channel_id=1, source_target_pairs={{0,4},{1,5},{2,6},{3,7},{4,0},{5,1},{6,2},{7,3},{8,12},{9,13},{10,... | collective-permute-start | bytes 1179656 | tf_op jit(solution)/shard_map/ppermute | solution.py:694
  417.3 35.9 %collective-permute-start.30 = (bf16[4,96,512]{2,1,0:T(8,128)(2,1)S(1)}, bf16[4,96,512]{2,1,0:T(8,128)(2,1)S(1)}, u32[]{:S(2)}, u32[]{:S(2)}) collective-permute-start(bf16[4,96,512]{2,1,0:T(8,128)(2,1)S(1)} %get-tuple-element.332), channel_id=1, source_target_pairs={{0,6},{1,7},{2,4},{3,5},{4,2},{5,3},{6,0},{7,1},{8,14},{9,15},{10,... | collective-permute-start | bytes 1179656 | tf_op jit(solution)/shard_map/ppermute | solution.py:694
  470.5 43.0 %collective-permute-start.41 = (bf16[1,96,512]{2,1,0:T(8,128)(2,1)S(1)}, bf16[1,96,512]{2,1,0:T(8,128)(2,1)S(1)}, u32[]{:S(2)}, u32[]{:S(2)}) collective-permute-start(bf16[1,96,512]{2,1,0:T(8,128)(2,1)S(1)} %get-tuple-element.380), channel_id=1, source_target_pairs={{0,16},{1,17},{2,18},{3,19},{4,20},{5,21},{6,22},{7,23},{8,24},{9,... | collective-permute-start | bytes 294920 | tf_op jit(solution)/shard_map/ppermute | solution.py:694
  473.1 40.4 %collective-permute-start.42 = (bf16[1,96,512]{2,1,0:T(8,128)(2,1)S(1)}, bf16[1,96,512]{2,1,0:T(8,128)(2,1)S(1)}, u32[]{:S(2)}, u32[]{:S(2)}) collective-permute-start(bf16[1,96,512]{2,1,0:T(8,128)(2,1)S(1)} %get-tuple-element.381), channel_id=1, source_target_pairs={{0,24},{1,25},{2,26},{3,27},{4,28},{5,29},{6,30},{7,31},{8,16},{9,... | collective-permute-start | bytes 294920 | tf_op jit(solution)/shard_map/ppermute | solution.py:694
  475.2 38.3 %collective-permute-start.37 = (bf16[4,96,512]{2,1,0:T(8,128)(2,1)S(1)}, bf16[4,96,512]{2,1,0:T(8,128)(2,1)S(1)}, u32[]{:S(2)}, u32[]{:S(2)}) collective-permute-start(bf16[4,96,512]{2,1,0:T(8,128)(2,1)S(1)} %get-tuple-element.375), channel_id=1, source_target_pairs={{0,2},{1,3},{2,0},{3,1},{4,6},{5,7},{6,4},{7,5},{8,10},{9,11},{10,... | collective-permute-start | bytes 1179656 | tf_op jit(solution)/shard_map/ppermute | solution.py:694
  475.3 38.2 %collective-permute-start.38 = (bf16[4,96,512]{2,1,0:T(8,128)(2,1)S(1)}, bf16[4,96,512]{2,1,0:T(8,128)(2,1)S(1)}, u32[]{:S(2)}, u32[]{:S(2)}) collective-permute-start(bf16[4,96,512]{2,1,0:T(8,128)(2,1)S(1)} %get-tuple-element.376), channel_id=1, source_target_pairs={{0,4},{1,5},{2,6},{3,7},{4,0},{5,1},{6,2},{7,3},{8,12},{9,13},{10,... | collective-permute-start | bytes 1179656 | tf_op jit(solution)/shard_map/ppermute | solution.py:694
  477.0 36.6 %collective-permute-start.39 = (bf16[4,96,512]{2,1,0:T(8,128)(2,1)S(1)}, bf16[4,96,512]{2,1,0:T(8,128)(2,1)S(1)}, u32[]{:S(2)}, u32[]{:S(2)}) collective-permute-start(bf16[4,96,512]{2,1,0:T(8,128)(2,1)S(1)} %get-tuple-element.377), channel_id=1, source_target_pairs={{0,6},{1,7},{2,4},{3,5},{4,2},{5,3},{6,0},{7,1},{8,14},{9,15},{10,... | collective-permute-start | bytes 1179656 | tf_op jit(solution)/shard_map/ppermute | solution.py:694
  513.6 18.8 %collective-permute-start.43 = (bf16[1024,512]{1,0:T(8,128)(2,1)}, bf16[1024,512]{1,0:T(8,128)(2,1)}, u32[]{:S(2)}, u32[]{:S(2)}) collective-permute-start(bf16[1024,512]{1,0:T(8,128)(2,1)} %get-tuple-element.391), channel_id=1, source_target_pairs={{0,1},{1,2},{2,3},{3,6},{6,7},{7,4},{4,5},{5,8},{8,9},{9,10},{10,1... | collective-permute-start | bytes 3145736 | tf_op jit(solution)/shard_map/ppermute | solution.py:717
  513.6 18.8 %collective-permute-start.44 = (bf16[1024,512]{1,0:T(8,128)(2,1)}, bf16[1024,512]{1,0:T(8,128)(2,1)}, u32[]{:S(2)}, u32[]{:S(2)}) collective-permute-start(bf16[1024,512]{1,0:T(8,128)(2,1)} %get-tuple-element.392), channel_id=1, source_target_pairs={{0,29},{1,0},{2,1},{3,2},{6,3},{7,6},{4,7},{5,4},{8,5},{9,8},{10,9... | collective-permute-start | bytes 3145736 | tf_op jit(solution)/shard_map/ppermute | solution.py:717
  549.7 19.7 %collective-permute-start.58 = (bf16[4,96,512]{2,1,0:T(8,128)(2,1)S(1)}, bf16[4,96,512]{2,1,0:T(8,128)(2,1)S(1)}, u32[]{:S(2)}, u32[]{:S(2)}) collective-permute-start(bf16[4,96,512]{2,1,0:T(8,128)(2,1)S(1)} %get-tuple-element.440), channel_id=1, source_target_pairs={{0,6},{1,7},{2,4},{3,5},{4,2},{5,3},{6,0},{7,1},{8,14},{9,15},{10,... | collective-permute-start | bytes 1179656 | tf_op jit(solution)/shard_map/ppermute | solution.py:694
  552.9 22.1 %collective-permute-start.50 = (bf16[4,40,512]{2,1,0:T(8,128)(2,1)S(1)}, bf16[4,40,512]{2,1,0:T(8,128)(2,1)S(1)}, u32[]{:S(2)}, u32[]{:S(2)}) collective-permute-start(bf16[4,40,512]{2,1,0:T(8,128)(2,1)S(1)} %get-tuple-element.428), channel_id=1, source_target_pairs={{0,2},{1,3},{2,0},{3,1},{4,6},{5,7},{6,4},{7,5},{8,10},{9,11},{10,... | collective-permute-start | bytes 491528 | tf_op jit(solution)/shard_map/ppermute | solution.py:694
  (96 other events, 1248.0 us)
Sparse Core Ops, SparseCore 0:
  11.5 72.5 all-gather.2
  146.8 82.8 all-gather.4

commit v7 on v6

--- a/solution.py
+++ b/solution.py
@@ -802,10 +802,12 @@
             axis=0,
         )
         lists = jnp.concatenate(slot_lists).reshape(-1, LANES)
-        lists = bring(lists, device_count, 0, direct)
         goals = jnp.concatenate([targets, weight_rows[:, None]], axis=1)
         goals = jnp.pad(goals, ((0, 0), (0, -goals.shape[1] % LANES)))
         row_pair = [packed, swap(packed, device_count, 2)]
+        row_pair, bulk = together(row_pair, [inputs, mesh_static, lists])
+        inputs, mesh_static, lists = bulk
+        lists = bring(lists, device_count, 0, direct)
         sides = [bring(inputs, device_count, step, direct) for step in (1, 0, -1)]
         mesh_rows = bring(mesh_static, device_count, 0, direct)
         second = lax.all_gather(second, AXES, axis=1, tiled=True)

time: 610 us -> 605 us (level)
  transfers between devices with their start and end apart: 64 -> 64, of which waited for: 19 -> 20; matrix products, arithmetic and copies ran while one was open for 3% -> 2% of each run, Pallas kernels for 37% -> 37%
where the time goes in v7:
time: 605 us; the launch traced here: 597 us
  Pallas kernels  275 us (45%)
  starting transfers between devices  140 us (23%)
  waiting for transfers between devices  132 us (22%)
  between operations  17.5 us (3%)
  local copies, waits for them, and re-layouts  14.7 us (2%)
  other arithmetic  11.9 us (2%)
  matrix products  6.06 us (1%)
    pallas_call x4, Pallas kernels, backward_layer(): pl.pallas_call(functools.partial(backward_kernel, parts, mode), grid=(blo...  132 us
    ppermute x42, starting transfers between devices, swap(): return lax.ppermute(cells, AXES, [(i, i ^ mask) for i in range(count)])  98.4 us
    ppermute x42, waiting for transfers between devices, swap(): return lax.ppermute(cells, AXES, [(i, i ^ mask) for i in range(count)])  87.5 us
    pallas_call x4, Pallas kernels, forward_layer(): pl.pallas_call(functools.partial(forward_kernel, parts, has_next), grid=(...  79.7 us
    ppermute x14, waiting for transfers between devices, shift(): return lax.ppermute(cells, AXES, pairs)  44.4 us
    pallas_call x4, Pallas kernels, weight_layer(): pl.pallas_call(functools.partial(weight_kernel, above is not None, grad_n...  42.4 us
    ppermute x14, starting transfers between devices, shift(): return lax.ppermute(cells, AXES, pairs)  33.1 us
  transfers between devices with their start and end apart: 64, of which 20 were waited for; matrix products, arithmetic and copies ran while one was open for 2% of the time, Pallas kernels for 37%

profile of v7, /device:TPU:0, one launch (start us, length us, event | category | flops | bytes accessed | tf_op | source)
XLA Modules:
  0.0 597.4 jit_solution(4926692673271970050)
XLA Ops:
  17.6 4.9 collective-permute-start.6
  25.0 22.5 %collective-permute-done.1 = bf16[2,136,512]{2,1,0:T(8,128)(2,1)S(1)} collective-permute-done((bf16[2,136,512]{2,1,0:T(8,128)(2,1)S(1)}, bf16[2,136,512]{2,1,0:T(8,128)(2,1)S(1)}, u32[]{:S(2)}, u32[]{:S(2)}) %collective-permute-start.1) | collective-permute-done | bytes 278560 | tf_op jit(solution)/shard_map/ppermute | solution.py:694
  50.0 7.4 %collective-permute-done.3 = bf16[2,136,512]{2,1,0:T(8,128)(2,1)S(1)} collective-permute-done((bf16[2,136,512]{2,1,0:T(8,128)(2,1)S(1)}, bf16[2,136,512]{2,1,0:T(8,128)(2,1)S(1)}, u32[]{:S(2)}, u32[]{:S(2)}) %collective-permute-start.3) | collective-permute-done | bytes 278560 | tf_op jit(solution)/shard_map/ppermute | solution.py:694
  58.4 52.6 %collective-permute-start.8 = (bf16[8,136,512]{2,1,0:T(8,128)(2,1)S(1)}, bf16[8,136,512]{2,1,0:T(8,128)(2,1)S(1)}, u32[]{:S(2)}, u32[]{:S(2)}) collective-permute-start(bf16[8,136,512]{2,1,0:T(8,128)(2,1)S(1)} %constant_dynamic-update-slice_fusion.refs_1_), channel_id=1, source_target_pairs={{0,4},{1,5},{2,6},{3,7},{4,0},{5,1},{6,2},{7,3},{8,12},{9,13},{10,... | collective-permute-start | bytes 3342344 | tf_op jit(solution)/shard_map/ppermute | solution.py:694
  111.8 24.1 %collective-permute-done.8.refs_2_ = bf16[8,136,512]{2,1,0:T(8,128)(2,1)S(1)} collective-permute-done((bf16[8,136,512]{2,1,0:T(8,128)(2,1)S(1)}, bf16[8,136,512]{2,1,0:T(8,128)(2,1)S(1)}, u32[]{:S(2)}, u32[]{:S(2)}) %collective-permute-start.8) | collective-permute-done | bytes 1114144 | tf_op jit(solution)/shard_map/ppermute | solution.py:694
  143.3 9.7 %embed.1 = (bf16[7,512,512]{2,1,0:T(8,128)(2,1)}, f32[1024,512]{1,0:T(8,128)}, bf16[1024,512]{1,0:T(8,128)(2,1)}, bf16[1024,512]{1,0:T(8,128)(2,1)S(1)}, bf16[10...) custom-call(s32[1]{0:T(128)} %bitcast.9.refs_0_.self_id, bf16[8,136,512]{2,1,0:T(8,128)(2,1)} %copy-done.17, ...), custom_call_target="tpu_custom_call" | custom-call | flops 3221225472 | bytes 12582912 | tf_op jit(solution)/shard_map/embed/pallas_call | solution.py:562
  153.0 20.2 %forward_layer.4 = (bf16[1024,512]{1,0:T(8,128)(2,1)}, f32[1024,512]{1,0:T(8,128)}, bf16[1024,512]{1,0:T(8,128)(2,1)}, bf16[4,1024,512]{2,1,0:T(8,128)(2,1)}, bf16[1024,512]{1,0:T(8,128)(2,1)}) custom-call(s32[4096]{0:T(1024)} %get-tuple-element.491.refs_0_, bf16[1024,512]{1,0:T(8,128)(2,1)S(1)} %get-tuple-element.262.refs_1_, ...), custom_call_target="tpu_custom_call" | custom-call | flops 4831838208 | bytes 25165824 | tf_op jit(solution)/shard_map/forward_layer/pallas_call | solution.py:186
  173.4 5.1 collective-permute-start.14
  179.3 17.1 %collective-permute-done.13.refs_1_ = bf16[1024,512]{1,0:T(8,128)(2,1)S(1)} collective-permute-done((bf16[1024,512]{1,0:T(8,128)(2,1)}, bf16[1024,512]{1,0:T(8,128)(2,1)S(1)}, u32[]{:S(2)}, u32[]{:S(2)}) %collective-permute-start.13) | collective-permute-done | bytes 1048608 | tf_op jit(solution)/shard_map/ppermute | solution.py:717
  196.4 20.2 %forward_layer.5 = (bf16[1024,512]{1,0:T(8,128)(2,1)}, f32[1024,512]{1,0:T(8,128)}, bf16[1024,512]{1,0:T(8,128)(2,1)}, bf16[4,1024,512]{2,1,0:T(8,128)(2,1)}, bf16[1024,512]{1,0:T(8,128)(2,1)}) custom-call(s32[4096]{0:T(1024)} %get-tuple-element.492.refs_0_, bf16[1024,512]{1,0:T(8,128)(2,1)S(1)} %collective-permute-done.13.refs_1_, ...), custom_call_target="tpu_custom_call" | custom-call | flops 4831838208 | bytes 25165824 | tf_op jit(solution)/shard_map/forward_layer/pallas_call | solution.py:186
  216.7 4.4 collective-permute-start.16
  223.6 12.5 %collective-permute-done.15.refs_1_ = bf16[1024,512]{1,0:T(8,128)(2,1)S(1)} collective-permute-done((bf16[1024,512]{1,0:T(8,128)(2,1)}, bf16[1024,512]{1,0:T(8,128)(2,1)S(1)}, u32[]{:S(2)}, u32[]{:S(2)}) %collective-permute-start.15) | collective-permute-done | bytes 1048608 | tf_op jit(solution)/shard_map/ppermute | solution.py:717
  236.1 20.2 %forward_layer.6 = (bf16[1024,512]{1,0:T(8,128)(2,1)}, f32[1024,512]{1,0:T(8,128)}, bf16[1024,512]{1,0:T(8,128)(2,1)}, bf16[4,1024,512]{2,1,0:T(8,128)(2,1)}, bf16[1024,512]{1,0:T(8,128)(2,1)}) custom-call(s32[4096]{0:T(1024)} %get-tuple-element.492.refs_0_, bf16[1024,512]{1,0:T(8,128)(2,1)S(1)} %collective-permute-done.15.refs_1_, ...), custom_call_target="tpu_custom_call" | custom-call | flops 4831838208 | bytes 25165824 | tf_op jit(solution)/shard_map/forward_layer/pallas_call | solution.py:186
  256.4 4.4 collective-permute-start.18
  262.3 11.2 %collective-permute-done.17.refs_1_ = bf16[1024,512]{1,0:T(8,128)(2,1)S(1)} collective-permute-done((bf16[1024,512]{1,0:T(8,128)(2,1)}, bf16[1024,512]{1,0:T(8,128)(2,1)S(1)}, u32[]{:S(2)}, u32[]{:S(2)}) %collective-permute-start.17) | collective-permute-done | bytes 1048608 | tf_op jit(solution)/shard_map/ppermute | solution.py:717
  273.5 19.0 %forward_layer.7 = (bf16[1024,512]{1,0:T(8,128)(2,1)}, bf16[4,1024,512]{2,1,0:T(8,128)(2,1)}, bf16[1024,512]{1,0:T(8,128)(2,1)}) custom-call(s32[4096]{0:T(1024)} %get-tuple-element.493.refs_0_, bf16[1024,512]{1,0:T(8,128)(2,1)S(1)} %collective-permute-done.17.refs_1_, bf16[1024,512]{1,0:T(8,128)(2,1)} %get-tuple-element.274.refs_2_, ...), custom_call_target="tpu_custom_call" | custom-call | flops 4831838208 | bytes 25165824 | tf_op jit(solution)/shard_map/forward_layer/pallas_call | solution.py:186
  298.1 32.1 %backward_layer.4 = (bf16[1024,512]{1,0:T(8,128)(2,1)}, bf16[1024,512]{1,0:T(8,128)(2,1)}, bf16[1024,512]{1,0:T(8,128)(2,1)}, f32[2,512]{1,0:T(2,128)S(1)}, bf16...) custom-call(s32[4096]{0:T(1024)S(1)} %copy-done.5, ...), custom_call_target="tpu_custom_call" | custom-call | flops 4294967296 | bytes 25165824 | tf_op jit(solution)/shard_map/backward_layer/pallas_call | solution.py:374
  330.2 4.7 collective-permute-start.20
  335.5 10.8 %weight_layer.4 = (f32[1024,512]{1,0:T(8,128)}, f32[16,96,512]{2,1,0:T(8,128)S(1)}, bf16[16,96,512]{2,1,0:T(8,128)(2,1)S(1)}) custom-call(s32[1]{0:T(128)} %bitcast.9.refs_0_.self_id, f32[512,512]{1,0:T(8,128)S(1)} %pad.29.refs_1_, bf16[1024,512]{1,0:T(8,128)(2,1)} %get-tuple-element.275.refs_4_.refs_2_.latent_low, ...), custom_call_target="tpu_custom_call" | custom-call | flops 5368709120 | bytes 12582912 | tf_op jit(solution)/shard_map/weight_layer/pallas_call | solution.py:503
  354.8 33.0 %backward_layer.5 = (bf16[1024,512]{1,0:T(8,128)(2,1)S(1)}, f32[1024,512]{1,0:T(8,128)S(1)}, bf16[1024,512]{1,0:T(8,128)(2,1)}, bf16[1024,512]{1,0:T(8,128)(2,1)...) custom-call(s32[4096]{0:T(1024)S(1)} %copy-done.1, ...), custom_call_target="tpu_custom_call" | custom-call | flops 4294967296 | bytes 25165824 | tf_op jit(solution)/shard_map/backward_layer/pallas_call | solution.py:374
  387.9 4.8 collective-permute-start.26
  392.7 11.1 %weight_layer.5 = (f32[1024,512]{1,0:T(8,128)}, f32[16,96,512]{2,1,0:T(8,128)S(1)}, bf16[16,96,512]{2,1,0:T(8,128)(2,1)S(1)}) custom-call(s32[1]{0:T(128)} %bitcast.9.refs_0_.self_id, bf16[1024,512]{1,0:T(8,128)(2,1)} %get-tuple-element.312.refs_1_, bf16[1024,512]{1,0:T(8,128)(2,1)S(1)} %get-tuple-element.313.refs_2_, ...), custom_call_target="tpu_custom_call" | custom-call | flops 5368709120 | bytes 12582912 | tf_op jit(solution)/shard_map/weight_layer/pallas_call | solution.py:503
  413.7 34.1 %backward_layer.6 = (bf16[1024,512]{1,0:T(8,128)(2,1)S(1)}, f32[1024,512]{1,0:T(8,128)S(1)}, bf16[1024,512]{1,0:T(8,128)(2,1)}, bf16[1024,512]{1,0:T(8,128)(2,1)...) custom-call(s32[4096]{0:T(1024)S(1)} %copy-done.1, ...), custom_call_target="tpu_custom_call" | custom-call | flops 4294967296 | bytes 25165824 | tf_op jit(solution)/shard_map/backward_layer/pallas_call | solution.py:374
  447.9 4.6 collective-permute-start.35
  452.5 11.4 %weight_layer.6 = (f32[1024,512]{1,0:T(8,128)}, f32[16,96,512]{2,1,0:T(8,128)S(1)}, bf16[16,96,512]{2,1,0:T(8,128)(2,1)S(1)}) custom-call(s32[1]{0:T(128)} %bitcast.9.refs_0_.self_id, bf16[1024,512]{1,0:T(8,128)(2,1)} %get-tuple-element.271.refs_4_.refs_5_.refs_3_.refs_1_, bf16[1024,512]{1,0:T(8,128)(2,1)S(1)} %get-tuple-element.358.refs_2_, ...), custom_call_target="tpu_custom_call" | custom-call | flops 5368709120 | bytes 12582912 | tf_op jit(solution)/shard_map/weight_layer/pallas_call | solution.py:503
  473.5 32.7 %backward_layer.7 = (bf16[1024,512]{1,0:T(8,128)(2,1)S(1)}, f32[1024,512]{1,0:T(8,128)}, bf16[1024,512]{1,0:T(8,128)(2,1)}, bf16[1024,512]{1,0:T(8,128)(2,1)}, b...) custom-call(s32[4096]{0:T(1024)S(1)} %copy-done.4, ...), custom_call_target="tpu_custom_call" | custom-call | flops 4294967296 | bytes 25165824 | tf_op jit(solution)/shard_map/backward_layer/pallas_call | solution.py:374
  508.3 4.6 collective-permute-start.44
  515.2 9.2 %weight_layer.7 = (f32[16,96,512]{2,1,0:T(8,128)S(1)}, bf16[16,96,512]{2,1,0:T(8,128)(2,1)}) custom-call(s32[1]{0:T(128)} %bitcast.9.refs_0_.self_id, bf16[1024,512]{1,0:T(8,128)(2,1)} %get-tuple-element.268.refs_4_.refs_6_.refs_3_.refs_1_, bf16[1024,512]{1,0:T(8,128)(2,1)S(1)} %get-tuple-element.403.refs_2_, bf16[1024,512]{1,0:T(8,128)(2,1)} %copy-done.19, ...), custom_call_target="tpu_custom_call" | custom-call | flops 5368709120 | bytes 12582912 | tf_op jit(solution)/shard_map/weight_layer/pallas_call | solution.py:503
  532.2 7.0 %tail_layer.1 = (f32[16,40,512]{2,1,0:T(8,128)S(1)}, bf16[16,40,512]{2,1,0:T(8,128)(2,1)S(1)}) custom-call(s32[1]{0:T(128)} %bitcast.9.refs_0_.self_id, f32[1]{0:T(128)} %bitcast.50.loss, bf16[1024,512]{1,0:T(8,128)(2,1)} %collective-permute-done.43.before, bf16[1024,512]{1,0:T(8,128)(2,1)} %get-tuple-element.426.middle, ...), custom_call_target="tpu_custom_call" | custom-call | flops 1610612736 | bytes 12582912 | tf_op jit(solution)/shard_map/tail_layer/pallas_call | solution.py:637
  547.8 7.3 %collective-permute-done.56 = bf16[4,96,512]{2,1,0:T(8,128)(2,1)S(1)} collective-permute-done((bf16[4,96,512]{2,1,0:T(8,128)(2,1)S(1)}, bf16[4,96,512]{2,1,0:T(8,128)(2,1)S(1)}, u32[]{:S(2)}, u32[]{:S(2)}) %collective-permute-start.56) | collective-permute-done | bytes 393248 | tf_op jit(solution)/shard_map/ppermute | solution.py:694
  555.2 8.9 %collective-permute-done.58 = bf16[4,96,512]{2,1,0:T(8,128)(2,1)S(1)} collective-permute-done((bf16[4,96,512]{2,1,0:T(8,128)(2,1)S(1)}, bf16[4,96,512]{2,1,0:T(8,128)(2,1)S(1)}, u32[]{:S(2)}, u32[]{:S(2)}) %collective-permute-start.58) | collective-permute-done | bytes 393248 | tf_op jit(solution)/shard_map/ppermute | solution.py:694
  571.2 5.8 collective-permute-done.51
  (320 shorter events, 102.2 us)
Async XLA Ops:
  7.2 189.2 %all-gather.3.cloned.1.call-start = ((), (), s32[]{:S(2)}) async-start(), calls=%async_computation | async-start | bytes 3244032 | tf_op jit(solution)/shard_map/all_gather | solution.py:813
  9.2 226.9 %all-gather.5.cloned.1.call-start = ((), (), s32[]{:S(2)}) async-start(), calls=%async_computation.1 | async-start | bytes 6488064 | tf_op jit(solution)/shard_map/all_gather | solution.py:819
  17.5 39.9 %collective-permute-start.5 = (bf16[1024,512]{1,0:T(8,128)(2,1)S(1)}, bf16[1024,512]{1,0:T(8,128)(2,1)S(1)}, u32[]{:S(2)}, u32[]{:S(2)}) collective-permute-start(bf16[1024,512]{1,0:T(8,128)(2,1)S(1)} %pad.26), channel_id=1, source_target_pairs={{0,1},{1,2},{2,3},{3,6},{4,7},{5,4},{6,5},{7,8},{8,9},{9,10},{10,1... | collective-permute-start | bytes 3145736 | tf_op jit(solution)/shard_map/ppermute | solution.py:712
  17.6 39.9 %collective-permute-start.6 = (bf16[1024,512]{1,0:T(8,128)(2,1)S(1)}, bf16[1024,512]{1,0:T(8,128)(2,1)S(1)}, u32[]{:S(2)}, u32[]{:S(2)}) collective-permute-start(bf16[1024,512]{1,0:T(8,128)(2,1)S(1)} %pad.26), channel_id=1, source_target_pairs={{0,29},{1,0},{2,1},{3,2},{4,3},{5,6},{6,7},{7,4},{8,5},{9,8},{10,9... | collective-permute-start | bytes 3145736 | tf_op jit(solution)/shard_map/ppermute | solution.py:712
  22.5 35.0 %collective-permute-start.4 = (bf16[1024,512]{1,0:T(8,128)(2,1)S(1)}, bf16[1024,512]{1,0:T(8,128)(2,1)S(1)}, u32[]{:S(2)}, u32[]{:S(2)}) collective-permute-start(bf16[1024,512]{1,0:T(8,128)(2,1)S(1)} %copy-done.62), channel_id=1, source_target_pairs={{0,0},{1,1},{2,2},{3,3},{4,6},{5,7},{6,4},{7,5},{8,8},{9,9},{10,10... | collective-permute-start | bytes 3145736 | tf_op jit(solution)/shard_map/ppermute | solution.py:712
  23.2 24.3 %collective-permute-start.1 = (bf16[2,136,512]{2,1,0:T(8,128)(2,1)S(1)}, bf16[2,136,512]{2,1,0:T(8,128)(2,1)S(1)}, u32[]{:S(2)}, u32[]{:S(2)}) collective-permute-start(bf16[2,136,512]{2,1,0:T(8,128)(2,1)S(1)} %pad_maximum_fusion), channel_id=1, source_target_pairs={{0,8},{1,9},{2,10},{3,11},{4,12},{5,13},{6,14},{7,15},{8,0},{9,1},... | collective-permute-start | bytes 835592 | tf_op jit(solution)/shard_map/ppermute | solution.py:694
  24.0 26.0 %collective-permute-start.2 = (bf16[2,136,512]{2,1,0:T(8,128)(2,1)S(1)}, bf16[2,136,512]{2,1,0:T(8,128)(2,1)S(1)}, u32[]{:S(2)}, u32[]{:S(2)}) collective-permute-start(bf16[2,136,512]{2,1,0:T(8,128)(2,1)S(1)} %pad_maximum_fusion), channel_id=1, source_target_pairs={{0,16},{1,17},{2,18},{3,19},{4,20},{5,21},{6,22},{7,23},{8,24},{9,... | collective-permute-start | bytes 835592 | tf_op jit(solution)/shard_map/ppermute | solution.py:694
  58.4 77.4 %collective-permute-start.8 = (bf16[8,136,512]{2,1,0:T(8,128)(2,1)S(1)}, bf16[8,136,512]{2,1,0:T(8,128)(2,1)S(1)}, u32[]{:S(2)}, u32[]{:S(2)}) collective-permute-start(bf16[8,136,512]{2,1,0:T(8,128)(2,1)S(1)} %constant_dynamic-update-slice_fusion.refs_1_), channel_id=1, source_target_pairs={{0,4},{1,5},{2,6},{3,7},{4,0},{5,1},{6,2},{7,3},{8,12},{9,13},{10,... | collective-permute-start | bytes 3342344 | tf_op jit(solution)/shard_map/ppermute | solution.py:694
  173.3 23.1 %collective-permute-start.13 = (bf16[1024,512]{1,0:T(8,128)(2,1)}, bf16[1024,512]{1,0:T(8,128)(2,1)S(1)}, u32[]{:S(2)}, u32[]{:S(2)}) collective-permute-start(bf16[1024,512]{1,0:T(8,128)(2,1)} %get-tuple-element.267.refs_2_), channel_id=1, source_target_pairs={{0,1},{1,2},{2,3},{3,6},{6,7},{7,4},{4,5},{5,8},{8,9},{9,10},{10,1... | collective-permute-start | bytes 3145736 | tf_op jit(solution)/shard_map/ppermute | solution.py:717
  173.4 23.0 %collective-permute-start.14 = (bf16[1024,512]{1,0:T(8,128)(2,1)}, bf16[1024,512]{1,0:T(8,128)(2,1)S(1)}, u32[]{:S(2)}, u32[]{:S(2)}) collective-permute-start(bf16[1024,512]{1,0:T(8,128)(2,1)} %get-tuple-element.267.refs_2_), channel_id=1, source_target_pairs={{0,29},{1,0},{2,1},{3,2},{6,3},{7,6},{4,7},{5,4},{8,5},{9,8},{10,9... | collective-permute-start | bytes 3145736 | tf_op jit(solution)/shard_map/ppermute | solution.py:717
  216.6 19.5 %collective-permute-start.15 = (bf16[1024,512]{1,0:T(8,128)(2,1)}, bf16[1024,512]{1,0:T(8,128)(2,1)S(1)}, u32[]{:S(2)}, u32[]{:S(2)}) collective-permute-start(bf16[1024,512]{1,0:T(8,128)(2,1)} %get-tuple-element.270.refs_2_), channel_id=1, source_target_pairs={{0,1},{1,2},{2,3},{3,6},{6,7},{7,4},{4,5},{5,8},{8,9},{9,10},{10,1... | collective-permute-start | bytes 3145736 | tf_op jit(solution)/shard_map/ppermute | solution.py:717
  216.7 19.5 %collective-permute-start.16 = (bf16[1024,512]{1,0:T(8,128)(2,1)}, bf16[1024,512]{1,0:T(8,128)(2,1)S(1)}, u32[]{:S(2)}, u32[]{:S(2)}) collective-permute-start(bf16[1024,512]{1,0:T(8,128)(2,1)} %get-tuple-element.270.refs_2_), channel_id=1, source_target_pairs={{0,29},{1,0},{2,1},{3,2},{6,3},{7,6},{4,7},{5,4},{8,5},{9,8},{10,9... | collective-permute-start | bytes 3145736 | tf_op jit(solution)/shard_map/ppermute | solution.py:717
  221.9 39.7 %collective-permute-start.12 = (f32[1024,256]{0,1:T(8,128)S(1)}, f32[1024,256]{0,1:T(8,128)}, u32[]{:S(2)}, u32[]{:S(2)}) collective-permute-start(f32[1024,256]{0,1:T(8,128)S(1)} %copy-done.24), channel_id=1, source_target_pairs={{0,0},{1,1},{2,2},{3,3},{4,6},{5,7},{6,4},{7,5},{8,8},{9,9},{10,10... | collective-permute-start | bytes 3145736 | tf_op jit(solution)/shard_map/ppermute | solution.py:712
  330.2 17.3 %collective-permute-start.20 = (bf16[1024,512]{1,0:T(8,128)(2,1)}, bf16[1024,512]{1,0:T(8,128)(2,1)S(1)}, u32[]{:S(2)}, u32[]{:S(2)}) collective-permute-start(bf16[1024,512]{1,0:T(8,128)(2,1)} %get-tuple-element.281), channel_id=1, source_target_pairs={{0,29},{1,0},{2,1},{3,2},{6,3},{7,6},{4,7},{5,4},{8,5},{9,8},{10,9... | collective-permute-start | bytes 3145736 | tf_op jit(solution)/shard_map/ppermute | solution.py:717
  351.3 36.5 %collective-permute-start.22 = (bf16[4,96,512]{2,1,0:T(8,128)(2,1)S(1)}, bf16[4,96,512]{2,1,0:T(8,128)(2,1)S(1)}, u32[]{:S(2)}, u32[]{:S(2)}) collective-permute-start(bf16[4,96,512]{2,1,0:T(8,128)(2,1)S(1)} %get-tuple-element.299), channel_id=1, source_target_pairs={{0,2},{1,3},{2,0},{3,1},{4,6},{5,7},{6,4},{7,5},{8,10},{9,11},{10,... | collective-permute-start | bytes 1179656 | tf_op jit(solution)/shard_map/ppermute | solution.py:694
  351.4 36.5 %collective-permute-start.23 = (bf16[4,96,512]{2,1,0:T(8,128)(2,1)S(1)}, bf16[4,96,512]{2,1,0:T(8,128)(2,1)S(1)}, u32[]{:S(2)}, u32[]{:S(2)}) collective-permute-start(bf16[4,96,512]{2,1,0:T(8,128)(2,1)S(1)} %get-tuple-element.300), channel_id=1, source_target_pairs={{0,4},{1,5},{2,6},{3,7},{4,0},{5,1},{6,2},{7,3},{8,12},{9,13},{10,... | collective-permute-start | bytes 1179656 | tf_op jit(solution)/shard_map/ppermute | solution.py:694
  351.4 36.4 %collective-permute-start.24 = (bf16[4,96,512]{2,1,0:T(8,128)(2,1)S(1)}, bf16[4,96,512]{2,1,0:T(8,128)(2,1)S(1)}, u32[]{:S(2)}, u32[]{:S(2)}) collective-permute-start(bf16[4,96,512]{2,1,0:T(8,128)(2,1)S(1)} %get-tuple-element.301), channel_id=1, source_target_pairs={{0,6},{1,7},{2,4},{3,5},{4,2},{5,3},{6,0},{7,1},{8,14},{9,15},{10,... | collective-permute-start | bytes 1179656 | tf_op jit(solution)/shard_map/ppermute | solution.py:694
  387.9 17.4 %collective-permute-start.26 = (bf16[1024,512]{1,0:T(8,128)(2,1)}, bf16[1024,512]{1,0:T(8,128)(2,1)S(1)}, u32[]{:S(2)}, u32[]{:S(2)}) collective-permute-start(bf16[1024,512]{1,0:T(8,128)(2,1)} %get-tuple-element.311), channel_id=1, source_target_pairs={{0,29},{1,0},{2,1},{3,2},{6,3},{7,6},{4,7},{5,4},{8,5},{9,8},{10,9... | collective-permute-start | bytes 3145736 | tf_op jit(solution)/shard_map/ppermute | solution.py:717
  405.4 42.4 %collective-permute-start.32 = (bf16[1,96,512]{2,1,0:T(8,128)(2,1)S(1)}, bf16[1,96,512]{2,1,0:T(8,128)(2,1)S(1)}, u32[]{:S(2)}, u32[]{:S(2)}) collective-permute-start(bf16[1,96,512]{2,1,0:T(8,128)(2,1)S(1)} %get-tuple-element.345), channel_id=1, source_target_pairs={{0,16},{1,17},{2,18},{3,19},{4,20},{5,21},{6,22},{7,23},{8,24},{9,... | collective-permute-start | bytes 294920 | tf_op jit(solution)/shard_map/ppermute | solution.py:694
  407.2 40.6 %collective-permute-start.33 = (bf16[1,96,512]{2,1,0:T(8,128)(2,1)S(1)}, bf16[1,96,512]{2,1,0:T(8,128)(2,1)S(1)}, u32[]{:S(2)}, u32[]{:S(2)}) collective-permute-start(bf16[1,96,512]{2,1,0:T(8,128)(2,1)S(1)} %get-tuple-element.346), channel_id=1, source_target_pairs={{0,24},{1,25},{2,26},{3,27},{4,28},{5,29},{6,30},{7,31},{8,16},{9,... | collective-permute-start | bytes 294920 | tf_op jit(solution)/shard_map/ppermute | solution.py:694
  410.2 37.7 %collective-permute-start.28 = (bf16[4,96,512]{2,1,0:T(8,128)(2,1)S(1)}, bf16[4,96,512]{2,1,0:T(8,128)(2,1)S(1)}, u32[]{:S(2)}, u32[]{:S(2)}) collective-permute-start(bf16[4,96,512]{2,1,0:T(8,128)(2,1)S(1)} %get-tuple-element.340), channel_id=1, source_target_pairs={{0,2},{1,3},{2,0},{3,1},{4,6},{5,7},{6,4},{7,5},{8,10},{9,11},{10,... | collective-permute-start | bytes 1179656 | tf_op jit(solution)/shard_map/ppermute | solution.py:694
  410.3 37.6 %collective-permute-start.29 = (bf16[4,96,512]{2,1,0:T(8,128)(2,1)S(1)}, bf16[4,96,512]{2,1,0:T(8,128)(2,1)S(1)}, u32[]{:S(2)}, u32[]{:S(2)}) collective-permute-start(bf16[4,96,512]{2,1,0:T(8,128)(2,1)S(1)} %get-tuple-element.341), channel_id=1, source_target_pairs={{0,4},{1,5},{2,6},{3,7},{4,0},{5,1},{6,2},{7,3},{8,12},{9,13},{10,... | collective-permute-start | bytes 1179656 | tf_op jit(solution)/shard_map/ppermute | solution.py:694
  412.0 35.9 %collective-permute-start.30 = (bf16[4,96,512]{2,1,0:T(8,128)(2,1)S(1)}, bf16[4,96,512]{2,1,0:T(8,128)(2,1)S(1)}, u32[]{:S(2)}, u32[]{:S(2)}) collective-permute-start(bf16[4,96,512]{2,1,0:T(8,128)(2,1)S(1)} %get-tuple-element.342), channel_id=1, source_target_pairs={{0,6},{1,7},{2,4},{3,5},{4,2},{5,3},{6,0},{7,1},{8,14},{9,15},{10,... | collective-permute-start | bytes 1179656 | tf_op jit(solution)/shard_map/ppermute | solution.py:694
  465.2 43.0 %collective-permute-start.41 = (bf16[1,96,512]{2,1,0:T(8,128)(2,1)S(1)}, bf16[1,96,512]{2,1,0:T(8,128)(2,1)S(1)}, u32[]{:S(2)}, u32[]{:S(2)}) collective-permute-start(bf16[1,96,512]{2,1,0:T(8,128)(2,1)S(1)} %get-tuple-element.390), channel_id=1, source_target_pairs={{0,16},{1,17},{2,18},{3,19},{4,20},{5,21},{6,22},{7,23},{8,24},{9,... | collective-permute-start | bytes 294920 | tf_op jit(solution)/shard_map/ppermute | solution.py:694
  467.8 40.4 %collective-permute-start.42 = (bf16[1,96,512]{2,1,0:T(8,128)(2,1)S(1)}, bf16[1,96,512]{2,1,0:T(8,128)(2,1)S(1)}, u32[]{:S(2)}, u32[]{:S(2)}) collective-permute-start(bf16[1,96,512]{2,1,0:T(8,128)(2,1)S(1)} %get-tuple-element.391), channel_id=1, source_target_pairs={{0,24},{1,25},{2,26},{3,27},{4,28},{5,29},{6,30},{7,31},{8,16},{9,... | collective-permute-start | bytes 294920 | tf_op jit(solution)/shard_map/ppermute | solution.py:694
  469.9 38.3 %collective-permute-start.37 = (bf16[4,96,512]{2,1,0:T(8,128)(2,1)S(1)}, bf16[4,96,512]{2,1,0:T(8,128)(2,1)S(1)}, u32[]{:S(2)}, u32[]{:S(2)}) collective-permute-start(bf16[4,96,512]{2,1,0:T(8,128)(2,1)S(1)} %get-tuple-element.385), channel_id=1, source_target_pairs={{0,2},{1,3},{2,0},{3,1},{4,6},{5,7},{6,4},{7,5},{8,10},{9,11},{10,... | collective-permute-start | bytes 1179656 | tf_op jit(solution)/shard_map/ppermute | solution.py:694
  470.0 38.2 %collective-permute-start.38 = (bf16[4,96,512]{2,1,0:T(8,128)(2,1)S(1)}, bf16[4,96,512]{2,1,0:T(8,128)(2,1)S(1)}, u32[]{:S(2)}, u32[]{:S(2)}) collective-permute-start(bf16[4,96,512]{2,1,0:T(8,128)(2,1)S(1)} %get-tuple-element.386), channel_id=1, source_target_pairs={{0,4},{1,5},{2,6},{3,7},{4,0},{5,1},{6,2},{7,3},{8,12},{9,13},{10,... | collective-permute-start | bytes 1179656 | tf_op jit(solution)/shard_map/ppermute | solution.py:694
  471.7 36.6 %collective-permute-start.39 = (bf16[4,96,512]{2,1,0:T(8,128)(2,1)S(1)}, bf16[4,96,512]{2,1,0:T(8,128)(2,1)S(1)}, u32[]{:S(2)}, u32[]{:S(2)}) collective-permute-start(bf16[4,96,512]{2,1,0:T(8,128)(2,1)S(1)} %get-tuple-element.387), channel_id=1, source_target_pairs={{0,6},{1,7},{2,4},{3,5},{4,2},{5,3},{6,0},{7,1},{8,14},{9,15},{10,... | collective-permute-start | bytes 1179656 | tf_op jit(solution)/shard_map/ppermute | solution.py:694
  508.3 18.8 %collective-permute-start.43 = (bf16[1024,512]{1,0:T(8,128)(2,1)}, bf16[1024,512]{1,0:T(8,128)(2,1)}, u32[]{:S(2)}, u32[]{:S(2)}) collective-permute-start(bf16[1024,512]{1,0:T(8,128)(2,1)} %get-tuple-element.401), channel_id=1, source_target_pairs={{0,1},{1,2},{2,3},{3,6},{6,7},{7,4},{4,5},{5,8},{8,9},{9,10},{10,1... | collective-permute-start | bytes 3145736 | tf_op jit(solution)/shard_map/ppermute | solution.py:717
  508.3 18.8 %collective-permute-start.44 = (bf16[1024,512]{1,0:T(8,128)(2,1)}, bf16[1024,512]{1,0:T(8,128)(2,1)}, u32[]{:S(2)}, u32[]{:S(2)}) collective-permute-start(bf16[1024,512]{1,0:T(8,128)(2,1)} %get-tuple-element.402), channel_id=1, source_target_pairs={{0,29},{1,0},{2,1},{3,2},{6,3},{7,6},{4,7},{5,4},{8,5},{9,8},{10,9... | collective-permute-start | bytes 3145736 | tf_op jit(solution)/shard_map/ppermute | solution.py:717
  544.4 19.7 %collective-permute-start.58 = (bf16[4,96,512]{2,1,0:T(8,128)(2,1)S(1)}, bf16[4,96,512]{2,1,0:T(8,128)(2,1)S(1)}, u32[]{:S(2)}, u32[]{:S(2)}) collective-permute-start(bf16[4,96,512]{2,1,0:T(8,128)(2,1)S(1)} %get-tuple-element.450), channel_id=1, source_target_pairs={{0,6},{1,7},{2,4},{3,5},{4,2},{5,3},{6,0},{7,1},{8,14},{9,15},{10,... | collective-permute-start | bytes 1179656 | tf_op jit(solution)/shard_map/ppermute | solution.py:694
  547.6 22.1 %collective-permute-start.50 = (bf16[4,40,512]{2,1,0:T(8,128)(2,1)S(1)}, bf16[4,40,512]{2,1,0:T(8,128)(2,1)S(1)}, u32[]{:S(2)}, u32[]{:S(2)}) collective-permute-start(bf16[4,40,512]{2,1,0:T(8,128)(2,1)S(1)} %get-tuple-element.438), channel_id=1, source_target_pairs={{0,2},{1,3},{2,0},{3,1},{4,6},{5,7},{6,4},{7,5},{8,10},{9,11},{10,... | collective-permute-start | bytes 491528 | tf_op jit(solution)/shard_map/ppermute | solution.py:694
  (96 other events, 1268.9 us)
Sparse Core Ops, SparseCore 0:
  11.5 75.8 all-gather.2
  140.5 83.8 all-gather.4

commit v8 on v7

--- a/solution.py
+++ b/solution.py
@@ -316,7 +316,7 @@
             ).astype(LOW)
 
 
-def backward_layer(slots, above, grad_part, stored, weights, gains):
+def backward_layer(slots, above, grad_part, stored, weights, gains, first_layer):
     target_low, kept, aggregate = stored
     block_rows, width = target_low.shape
     fan = kept.shape[0]
@@ -365,7 +365,7 @@
         in_hbm((block_rows, width), LOW),
         jax.ShapeDtypeStruct((2, width), WIDE),
         fan_shape(LOW),
-        fan_shape(LOW),
+        in_hbm((fan, block_rows, width), LOW) if first_layer else fan_shape(LOW),
         shape(LOW),
         shape(LOW),
         shape(LOW),
@@ -485,7 +485,8 @@
         in_specs += [whole((width, width))]
         operands += [extra]
     in_specs += [tile, tile, fan_tile, fan_tile, tile, tile, tile, tile]
-    operands += [pinned(low), pinned(aggregate), *map(kept_on_chip, back)]
+    place = pinned if grad_new is None else kept_on_chip
+    operands += [pinned(low), pinned(aggregate), place(back[0]), *map(kept_on_chip, back[1:])]
     out_specs, out_shape, scratch = [], [], []
     if grad_new is not None:
         in_specs += [tile, matrix_spec(weights[1], 6, width)]
@@ -520,6 +521,44 @@
     return (results[0], results[1:])
 
 
+def place_rows(self_id, pieces, targets, width):
+    share = width // (pieces[0].shape[0] * len(pieces))
+    for index, piece in enumerate(pieces):
+        base = (index // 2) + (index % 2) * 4
+
+        def move(digit, carry, piece=piece, base=base):
+            relative = (digit // 2) * 8 + (digit % 2) * 2 + base
+            place = pl.multiple_of((relative ^ self_id[0]) * share, share)
+            for j, target in enumerate(targets):
+                target[pl.ds(place, share), :] = piece[digit, j * share : (j + 1) * share, :]
+            return carry
+
+        lax.fori_loop(0, piece.shape[0], move, 0)
+
+
+def assemble_kernel(pieces_count, *refs):
+    matrices = refs[-1]
+    targets = [matrices.at[j] for j in range(matrices.shape[0])]
+    place_rows(refs[0], refs[1 : 1 + pieces_count], targets, matrices.shape[1])
+
+
+def assemble(self_id, pieces):
+    digits, rows, width = pieces[0].shape
+    count = rows * digits * len(pieces) // width
+    return pl.pallas_call(
+        functools.partial(assemble_kernel, len(pieces)),
+        grid=(1,),
+        in_specs=[pl.BlockSpec(memory_space=pltpu.SMEM)] + [whole(piece.shape) for piece in pieces],
+        out_specs=whole((count, width, width)),
+        out_shape=in_hbm((count, width, width), LOW),
+        compiler_params=pltpu.CompilerParams(vmem_limit_bytes=20 << 20),
+        cost_estimate=pl.CostEstimate(
+            flops=0, transcendentals=0, bytes_accessed=4 * count * width * width
+        ),
+        name="assemble",
+    )(self_id, *pieces)
+
+
 def embed_kernel(pieces_count, *refs):
     self_id = refs[0]
     pieces = refs[1 : 1 + pieces_count]
@@ -527,24 +566,11 @@
     weights, latent, latent_low, sent_before, sent_middle, sent_after, table = refs[
         4 + pieces_count :
     ]
-    count, width = weights.shape[0], weights.shape[1]
-    high = pieces[0].shape[0]
-    share = width // (high * pieces_count)
 
     @pl.when(pl.program_id(0) == 0)
     def _():
-        for index, piece in enumerate(pieces):
-            base = (index // 2) + (index % 2) * 4
-
-            def move(digit, carry, piece=piece, base=base):
-                relative = (digit // 2) * 8 + (digit % 2) * 2 + base
-                place = pl.multiple_of((relative ^ self_id[0]) * share, share)
-                for j in range(count):
-                    weights[j, pl.ds(place, share), :] = piece[digit, j * share : (j + 1) * share, :]
-                table[pl.ds(place, share), :] = piece[digit, count * share : (count + 1) * share, :]
-                return carry
-
-            lax.fori_loop(0, high, move, 0)
+        targets = [weights.at[j] for j in range(weights.shape[0])] + [table]
+        place_rows(self_id, pieces, targets, weights.shape[1])
 
     for block, sent in ((before, sent_before), (middle, sent_middle), (after, sent_after)):
         wide = product_right(block[...], table[...])
@@ -694,14 +720,8 @@
     return lax.ppermute(cells, AXES, [(i, i ^ mask) for i in range(count)])
 
 
-def spread_rows(row_pair, count, first_bulk, second_bulk):
-    pair = jnp.stack(row_pair)
-    column = [pair] + [swap(pair, count, digit * 8) for digit in range(1, count // 8)]
-    column, first_bulk = together(column, first_bulk)
-    plane = jnp.concatenate(column)
-    near = [plane, swap(plane, count, 4)]
-    near, second_bulk = together(near, second_bulk)
-    return near + [swap(piece, count, 1) for piece in near], first_bulk, second_bulk
+def spread_high(rows, count):
+    return [rows] + [swap(rows, count, digit * 8) for digit in range(1, count // 8)]
 
 
 def home(block, direct):
@@ -792,7 +812,8 @@
             ],
             axis=0,
         )
-        second = jnp.concatenate([w_layers[2, :1], w_layers[1, 1:]], axis=0).astype(LOW)
+        second = jnp.concatenate([w_layers[2, :1], w_layers[1, 1:]], axis=0)
+        second = second.astype(LOW).reshape(-1, width)
         rest = jnp.concatenate(
             [
                 jnp.pad(w_out.astype(LOW), ((0, 0), (0, width - outputs)))[None],
@@ -804,18 +825,24 @@
         lists = jnp.concatenate(slot_lists).reshape(-1, LANES)
         goals = jnp.concatenate([targets, weight_rows[:, None]], axis=1)
         goals = jnp.pad(goals, ((0, 0), (0, -goals.shape[1] % LANES)))
-        row_pair = [packed, swap(packed, device_count, 2)]
-        row_pair, bulk = together(row_pair, [inputs, mesh_static, lists])
-        inputs, mesh_static, lists = bulk
+        barrier = lax.optimization_barrier
+        pairs = ((packed, swap(packed, device_count, 2)), (second, swap(second, device_count, 2)))
         lists = bring(lists, device_count, 0, direct)
-        sides = [bring(inputs, device_count, step, direct) for step in (1, 0, -1)]
+        pairs, lists, inputs, mesh_static = barrier((pairs, lists, inputs, mesh_static))
+        sides = [bring(inputs, device_count, step, direct) for step in (1, -1)]
         mesh_rows = bring(mesh_static, device_count, 0, direct)
-        second = lax.all_gather(second, AXES, axis=1, tiled=True)
-        pieces, (mesh_rows, before, after, lists), (own,) = spread_rows(
-            row_pair, device_count, [mesh_rows, sides[0], sides[2], lists], [sides[1]]
-        )
-        sides = [before, own, after]
-        pieces, (rest, goals) = together(pieces, [rest, goals])
+        pair, second_pair = (jnp.stack(rows) for rows in pairs)
+        column, sides, mesh_rows, inputs, second_pair = barrier(
+            (spread_high(pair, device_count), sides, mesh_rows, inputs, second_pair)
+        )
+        own = bring(inputs, device_count, 0, direct)
+        second_column = spread_high(second_pair, device_count)
+        plane = jnp.concatenate(column)
+        near, own, second_column, rest, goals = barrier(
+            ((plane, swap(plane, device_count, 4)), own, second_column, rest, goals)
+        )
+        pieces = [*near, *(swap(piece, device_count, 1) for piece in near)]
+        sides = [sides[0], own, sides[1]]
         rest = lax.all_gather(rest, AXES, axis=1, tiled=True)
         inputs = own
         lists = lists.reshape(len(slot_lists), -1)
@@ -823,12 +850,14 @@
         first, grid_latent, grid_start, *blocks = embed(
             self_id, pieces, sides
         )
-        first, goals = lax.optimization_barrier((first, goals))
+        first, goals = barrier((first, goals))
+        second_plane = jnp.concatenate(second_column)
+        second_near = (second_plane, swap(second_plane, device_count, 4))
         goals = bring(goals, device_count, 0, direct)
         targets, weight_rows = goals[:, :outputs], goals[:, outputs]
-        weights = [(first, 0), (second, 0)]
+        weights = [(first, 0), None]
         weights += [(rest, 6 * layer_id) for layer_id in range(layer_total - 2)]
-        heads = [(first, 0), (first, 6), (second, 0)]
+        heads = [(first, 0), (first, 6), None]
         heads += weights[3:]
         table_out = rest[0, :, :outputs]
         gain_rows = jnp.stack(pieces)[:, :, packed.shape[0] - 8, : flat_gains.shape[1]]
@@ -854,6 +883,11 @@
     target, target_low = mesh_rows, mesh_rows
     stored_list = []
     for layer_id in range(layer_total):
+        if direct and layer_id == 1:
+            second_near, target = lax.optimization_barrier((second_near, target))
+            second_pieces = [*second_near, *(swap(piece, device_count, 1) for piece in second_near)]
+            second = assemble(self_id, second_pieces)
+            weights[1] = heads[2] = (second, 0)
         last_layer = layer_id == layer_total - 1
         if last_layer:
             source_low = target_low
@@ -893,7 +927,7 @@
     for layer_id in reversed(range(layer_total)):
         source_low, stored, aggregate = stored_list[layer_id]
         sent_grad, grad_new, *slot_grads, grad_gain, grad_message, edge_hidden, b0, b1, b2, b3 = backward_layer(
-            slot_lists[layer_id], above, grad_part, stored, weights[layer_id], gains[layer_id]
+            slot_lists[layer_id], above, grad_part, stored, weights[layer_id], gains[layer_id], layer_id == 0
         )
         far = []
         if in_plane:

time: 605 us -> 592 us (0.979)
  starting transfers between devices: 140 us -> 123 us
  local copies, waits for them, and re-layouts: 14.7 us -> 20.8 us
    ppermute x42 -> x49, starting transfers between devices: 98.4 us -> 79.8 us  [swap(): return lax.ppermute(cells, AXES, [(i, i ^ mask) for i in range(count)])]
    ppermute x42 -> x49, waiting for transfers between devices: 87.5 us -> 78.8 us  [swap(): return lax.ppermute(cells, AXES, [(i, i ^ mask) for i in range(count)])]
    unnamed x140 -> x151, local copies, waits for them, and re-layouts: 9.2 us -> 13 us
  transfers between devices with their start and end apart: 64 -> 70, of which waited for: 20 -> 26; matrix products, arithmetic and copies ran while one was open for 2% -> 3% of each run, Pallas kernels for 37% -> 39%
where the time goes in v8:
time: 592 us; the launch traced here: 584 us
  Pallas kernels  278 us (47%)
  waiting for transfers between devices  126 us (21%)
  starting transfers between devices  123 us (21%)
  local copies, waits for them, and re-layouts  20.8 us (4%)
  between operations  17.5 us (3%)
  other arithmetic  11.7 us (2%)
  matrix products  6.07 us (1%)
    pallas_call x4, Pallas kernels, backward_layer(): pl.pallas_call(functools.partial(backward_kernel, parts, mode), grid=(blo...  132 us
    pallas_call x4, Pallas kernels, forward_layer(): pl.pallas_call(functools.partial(forward_kernel, parts, has_next), grid=(...  80.3 us
    ppermute x49, starting transfers between devices, swap(): return lax.ppermute(cells, AXES, [(i, i ^ mask) for i in range(count)])  79.8 us
    ppermute x49, waiting for transfers between devices, swap(): return lax.ppermute(cells, AXES, [(i, i ^ mask) for i in range(count)])  78.8 us
    ppermute x14, waiting for transfers between devices, shift(): return lax.ppermute(cells, AXES, pairs)  47.5 us
    pallas_call x4, Pallas kernels, weight_layer(): pl.pallas_call(functools.partial(weight_kernel, above is not None, grad_n...  42.6 us
    ppermute x14, starting transfers between devices, shift(): return lax.ppermute(cells, AXES, pairs)  32.4 us
    unnamed x151, local copies, waits for them, and re-layouts  13 us
  transfers between devices with their start and end apart: 70, of which 26 were waited for; matrix products, arithmetic and copies ran while one was open for 3% of the time, Pallas kernels for 39%

profile of v8, /device:TPU:0, one launch (start us, length us, event | category | flops | bytes accessed | tf_op | source)
XLA Modules:
  0.0 583.8 jit_solution(105509864889709391)
XLA Ops:
  18.1 6.0 %collective-permute-start.7 = (bf16[1024,512]{1,0:T(8,128)(2,1)S(1)}, bf16[1024,512]{1,0:T(8,128)(2,1)S(1)}, u32[]{:S(2)}, u32[]{:S(2)}) collective-permute-start(bf16[1024,512]{1,0:T(8,128)(2,1)S(1)} %pad.26), channel_id=1, source_target_pairs={{0,29},{1,0},{2,1},{3,2},{4,3},{5,6},{6,7},{7,4},{8,5},{9,8},{10,9... | collective-permute-start | bytes 3145736 | tf_op jit(solution)/shard_map/ppermute | solution.py:732
  28.0 19.2 %collective-permute-done.3 = bf16[2,136,512]{2,1,0:T(8,128)(2,1)S(1)} collective-permute-done((bf16[2,136,512]{2,1,0:T(8,128)(2,1)S(1)}, bf16[2,136,512]{2,1,0:T(8,128)(2,1)S(1)}, u32[]{:S(2)}, u32[]{:S(2)}) %collective-permute-start.3) | collective-permute-done | bytes 278560 | tf_op jit(solution)/shard_map/ppermute | solution.py:720
  52.3 5.3 collective-permute-done.5
  60.9 22.3 %collective-permute-start.9 = (bf16[8,136,512]{2,1,0:T(8,128)(2,1)}, bf16[8,136,512]{2,1,0:T(8,128)(2,1)}, u32[]{:S(2)}, u32[]{:S(2)}) collective-permute-start(bf16[8,136,512]{2,1,0:T(8,128)(2,1)} %constant_dynamic-update-slice_fusion.refs_1_), channel_id=1, source_target_pairs={{0,4},{1,5},{2,6},{3,7},{4,0},{5,1},{6,2},{7,3},{8,12},{9,13},{10,... | collective-permute-start | bytes 3342344 | tf_op jit(solution)/shard_map/ppermute | solution.py:720
  95.0 8.6 %collective-permute-done.12 = bf16[2,96,512]{2,1,0:T(8,128)(2,1)} collective-permute-done((bf16[2,96,512]{2,1,0:T(8,128)(2,1)S(1)}, bf16[2,96,512]{2,1,0:T(8,128)(2,1)}, u32[]{:S(2)}, u32[]{:S(2)}) %collective-permute-start.12) | collective-permute-done | bytes 196640 | tf_op jit(solution)/shard_map/ppermute | solution.py:720
  103.6 4.8 collective-permute-done.9.refs_2_
  116.1 9.9 %embed.1 = (bf16[7,512,512]{2,1,0:T(8,128)(2,1)}, f32[1024,512]{1,0:T(8,128)}, bf16[1024,512]{1,0:T(8,128)(2,1)}, bf16[1024,512]{1,0:T(8,128)(2,1)S(1)}, bf16[10...) custom-call(s32[1]{0:T(128)} %bitcast.10.refs_0_.self_id, ...), custom_call_target="tpu_custom_call" | custom-call | flops 3221225472 | bytes 12582912 | tf_op jit(solution)/shard_map/embed/pallas_call | solution.py:588
  131.2 20.1 %forward_layer.4 = (bf16[1024,512]{1,0:T(8,128)(2,1)}, f32[1024,512]{1,0:T(8,128)}, bf16[1024,512]{1,0:T(8,128)(2,1)}, bf16[4,1024,512]{2,1,0:T(8,128)(2,1)}, bf16[1024,512]{1,0:T(8,128)(2,1)}) custom-call(s32[4096]{0:T(1024)} %get-tuple-element.503.refs_0_, bf16[1024,512]{1,0:T(8,128)(2,1)S(1)} %copy-done.14, bf16[1024,512]{1,0:T(8,128)(2,1)} %get-tuple-element.268.refs_2_, ...), custom_call_target="tpu_custom_call" | custom-call | flops 4831838208 | bytes 25165824 | tf_op jit(solution)/shard_map/forward_layer/pallas_call | solution.py:186
  151.3 4.4 collective-permute-start.18
  162.1 22.1 %collective-permute-done.17.refs_1_ = bf16[1024,512]{1,0:T(8,128)(2,1)} collective-permute-done((bf16[1024,512]{1,0:T(8,128)(2,1)}, bf16[1024,512]{1,0:T(8,128)(2,1)}, u32[]{:S(2)}, u32[]{:S(2)}) %collective-permute-start.17) | collective-permute-done | bytes 1048608 | tf_op jit(solution)/shard_map/ppermute | solution.py:737
  184.2 21.0 %forward_layer.5 = (bf16[1024,512]{1,0:T(8,128)(2,1)}, f32[1024,512]{1,0:T(8,128)}, bf16[1024,512]{1,0:T(8,128)(2,1)}, bf16[4,1024,512]{2,1,0:T(8,128)(2,1)}, bf16[1024,512]{1,0:T(8,128)(2,1)}) custom-call(s32[4096]{0:T(1024)} %get-tuple-element.504.refs_0_, bf16[1024,512]{1,0:T(8,128)(2,1)} %collective-permute-done.17.refs_1_, ...), custom_call_target="tpu_custom_call" | custom-call | flops 4831838208 | bytes 25165824 | tf_op jit(solution)/shard_map/forward_layer/pallas_call | solution.py:186
  212.2 10.2 %collective-permute-done.22.refs_1_ = bf16[1024,512]{1,0:T(8,128)(2,1)S(1)} collective-permute-done((bf16[1024,512]{1,0:T(8,128)(2,1)}, bf16[1024,512]{1,0:T(8,128)(2,1)S(1)}, u32[]{:S(2)}, u32[]{:S(2)}) %collective-permute-start.22) | collective-permute-done | bytes 1048608 | tf_op jit(solution)/shard_map/ppermute | solution.py:737
  222.4 20.2 %forward_layer.6 = (bf16[1024,512]{1,0:T(8,128)(2,1)}, f32[1024,512]{1,0:T(8,128)}, bf16[1024,512]{1,0:T(8,128)(2,1)}, bf16[4,1024,512]{2,1,0:T(8,128)(2,1)}, bf16[1024,512]{1,0:T(8,128)(2,1)}) custom-call(s32[4096]{0:T(1024)} %get-tuple-element.504.refs_0_, bf16[1024,512]{1,0:T(8,128)(2,1)S(1)} %collective-permute-done.22.refs_1_, ...), custom_call_target="tpu_custom_call" | custom-call | flops 4831838208 | bytes 25165824 | tf_op jit(solution)/shard_map/forward_layer/pallas_call | solution.py:186
  242.6 4.5 collective-permute-start.25
  248.6 11.1 %collective-permute-done.24.refs_1_ = bf16[1024,512]{1,0:T(8,128)(2,1)S(1)} collective-permute-done((bf16[1024,512]{1,0:T(8,128)(2,1)}, bf16[1024,512]{1,0:T(8,128)(2,1)S(1)}, u32[]{:S(2)}, u32[]{:S(2)}) %collective-permute-start.24) | collective-permute-done | bytes 1048608 | tf_op jit(solution)/shard_map/ppermute | solution.py:737
  259.8 19.0 %forward_layer.7 = (bf16[1024,512]{1,0:T(8,128)(2,1)}, bf16[4,1024,512]{2,1,0:T(8,128)(2,1)}, bf16[1024,512]{1,0:T(8,128)(2,1)}) custom-call(s32[4096]{0:T(1024)} %get-tuple-element.505.refs_0_, bf16[1024,512]{1,0:T(8,128)(2,1)S(1)} %collective-permute-done.24.refs_1_, bf16[1024,512]{1,0:T(8,128)(2,1)} %get-tuple-element.286.refs_2_, ...), custom_call_target="tpu_custom_call" | custom-call | flops 4831838208 | bytes 25165824 | tf_op jit(solution)/shard_map/forward_layer/pallas_call | solution.py:186
  284.3 32.1 %backward_layer.4 = (bf16[1024,512]{1,0:T(8,128)(2,1)}, bf16[1024,512]{1,0:T(8,128)(2,1)}, bf16[1024,512]{1,0:T(8,128)(2,1)}, f32[2,512]{1,0:T(2,128)S(1)}, bf16...) custom-call(s32[4096]{0:T(1024)S(1)} %copy-done.5, ...), custom_call_target="tpu_custom_call" | custom-call | flops 4294967296 | bytes 25165824 | tf_op jit(solution)/shard_map/backward_layer/pallas_call | solution.py:374
  316.5 4.7 collective-permute-start.27
  321.9 10.8 %weight_layer.4 = (f32[1024,512]{1,0:T(8,128)}, f32[16,96,512]{2,1,0:T(8,128)S(1)}, bf16[16,96,512]{2,1,0:T(8,128)(2,1)S(1)}) custom-call(s32[1]{0:T(128)} %bitcast.10.refs_0_.self_id, f32[512,512]{1,0:T(8,128)S(1)} %pad.29.refs_1_, bf16[1024,512]{1,0:T(8,128)(2,1)} %get-tuple-element.287.refs_4_.refs_2_.latent_low, ...), custom_call_target="tpu_custom_call" | custom-call | flops 5368709120 | bytes 12582912 | tf_op jit(solution)/shard_map/weight_layer/pallas_call | solution.py:504
  343.2 33.0 %backward_layer.5 = (bf16[1024,512]{1,0:T(8,128)(2,1)S(1)}, f32[1024,512]{1,0:T(8,128)S(1)}, bf16[1024,512]{1,0:T(8,128)(2,1)}, bf16[1024,512]{1,0:T(8,128)(2,1)...) custom-call(s32[4096]{0:T(1024)S(1)} %copy-done.1, ...), custom_call_target="tpu_custom_call" | custom-call | flops 4294967296 | bytes 25165824 | tf_op jit(solution)/shard_map/backward_layer/pallas_call | solution.py:374
  376.3 4.8 collective-permute-start.33
  381.1 11.0 %weight_layer.5 = (f32[1024,512]{1,0:T(8,128)}, f32[16,96,512]{2,1,0:T(8,128)S(1)}, bf16[16,96,512]{2,1,0:T(8,128)(2,1)S(1)}) custom-call(s32[1]{0:T(128)} %bitcast.10.refs_0_.self_id, bf16[1024,512]{1,0:T(8,128)(2,1)} %get-tuple-element.324.refs_1_, bf16[1024,512]{1,0:T(8,128)(2,1)S(1)} %get-tuple-element.325.refs_2_, ...), custom_call_target="tpu_custom_call" | custom-call | flops 5368709120 | bytes 12582912 | tf_op jit(solution)/shard_map/weight_layer/pallas_call | solution.py:504
  402.1 34.0 %backward_layer.6 = (bf16[1024,512]{1,0:T(8,128)(2,1)S(1)}, f32[1024,512]{1,0:T(8,128)S(1)}, bf16[1024,512]{1,0:T(8,128)(2,1)}, bf16[1024,512]{1,0:T(8,128)(2,1)...) custom-call(s32[4096]{0:T(1024)S(1)} %copy-done.1, ...), custom_call_target="tpu_custom_call" | custom-call | flops 4294967296 | bytes 25165824 | tf_op jit(solution)/shard_map/backward_layer/pallas_call | solution.py:374
  436.3 4.6 collective-permute-start.42
  440.9 11.4 %weight_layer.6 = (f32[1024,512]{1,0:T(8,128)}, f32[16,96,512]{2,1,0:T(8,128)S(1)}, bf16[16,96,512]{2,1,0:T(8,128)(2,1)S(1)}) custom-call(s32[1]{0:T(128)} %bitcast.10.refs_0_.self_id, bf16[1024,512]{1,0:T(8,128)(2,1)} %get-tuple-element.283.refs_4_.refs_5_.refs_3_.refs_1_, bf16[1024,512]{1,0:T(8,128)(2,1)S(1)} %get-tuple-element.370.refs_2_, ...), custom_call_target="tpu_custom_call" | custom-call | flops 5368709120 | bytes 12582912 | tf_op jit(solution)/shard_map/weight_layer/pallas_call | solution.py:504
  461.9 32.7 %backward_layer.7 = (bf16[1024,512]{1,0:T(8,128)(2,1)S(1)}, f32[1024,512]{1,0:T(8,128)}, bf16[1024,512]{1,0:T(8,128)(2,1)}, bf16[1024,512]{1,0:T(8,128)(2,1)}, b...) custom-call(s32[4096]{0:T(1024)S(1)} %copy-done.4, ...), custom_call_target="tpu_custom_call" | custom-call | flops 4294967296 | bytes 25165824 | tf_op jit(solution)/shard_map/backward_layer/pallas_call | solution.py:374
  494.8 4.6 collective-permute-start.51
  499.4 9.4 %weight_layer.7 = (f32[16,96,512]{2,1,0:T(8,128)S(1)}, bf16[16,96,512]{2,1,0:T(8,128)(2,1)}) custom-call(s32[1]{0:T(128)} %bitcast.10.refs_0_.self_id, bf16[1024,512]{1,0:T(8,128)(2,1)} %get-tuple-element.273.refs_4_.refs_6_.refs_3_.refs_1_, bf16[1024,512]{1,0:T(8,128)(2,1)S(1)} %get-tuple-element.415.refs_2_, bf16[1024,512]{1,0:T(8,128)(2,1)} %copy-done.19, ...), custom_call_target="tpu_custom_call" | custom-call | flops 5368709120 | bytes 12582912 | tf_op jit(solution)/shard_map/weight_layer/pallas_call | solution.py:504
  517.1 7.0 %tail_layer.1 = (f32[16,40,512]{2,1,0:T(8,128)S(1)}, bf16[16,40,512]{2,1,0:T(8,128)(2,1)S(1)}) custom-call(s32[1]{0:T(128)} %bitcast.10.refs_0_.self_id, f32[1]{0:T(128)} %bitcast.53.loss, bf16[1024,512]{1,0:T(8,128)(2,1)} %collective-permute-done.50.before, bf16[1024,512]{1,0:T(8,128)(2,1)} %get-tuple-element.438.middle, ...), custom_call_target="tpu_custom_call" | custom-call | flops 1610612736 | bytes 12582912 | tf_op jit(solution)/shard_map/tail_layer/pallas_call | solution.py:663
  533.8 6.3 %collective-permute-done.63 = bf16[4,96,512]{2,1,0:T(8,128)(2,1)S(1)} collective-permute-done((bf16[4,96,512]{2,1,0:T(8,128)(2,1)S(1)}, bf16[4,96,512]{2,1,0:T(8,128)(2,1)S(1)}, u32[]{:S(2)}, u32[]{:S(2)}) %collective-permute-start.63) | collective-permute-done | bytes 393248 | tf_op jit(solution)/shard_map/ppermute | solution.py:720
  540.1 8.2 %collective-permute-done.64 = bf16[4,96,512]{2,1,0:T(8,128)(2,1)S(1)} collective-permute-done((bf16[4,96,512]{2,1,0:T(8,128)(2,1)S(1)}, bf16[4,96,512]{2,1,0:T(8,128)(2,1)S(1)}, u32[]{:S(2)}, u32[]{:S(2)}) %collective-permute-start.64) | collective-permute-done | bytes 393248 | tf_op jit(solution)/shard_map/ppermute | solution.py:720
  557.0 6.4 %collective-permute-done.58 = bf16[4,40,512]{2,1,0:T(8,128)(2,1)S(1)} collective-permute-done((bf16[4,40,512]{2,1,0:T(8,128)(2,1)S(1)}, bf16[4,40,512]{2,1,0:T(8,128)(2,1)S(1)}, u32[]{:S(2)}, u32[]{:S(2)}) %collective-permute-start.58) | collective-permute-done | bytes 163872 | tf_op jit(solution)/shard_map/ppermute | solution.py:720
  (345 shorter events, 136.3 us)
Async XLA Ops:
  7.2 215.1 %all-gather.2.cloned.1.call-start = ((), (), s32[]{:S(2)}) async-start(), calls=%async_computation | async-start | bytes 6488064 | tf_op jit(solution)/shard_map/all_gather | solution.py:846
  18.1 39.5 %collective-permute-start.6 = (bf16[1024,512]{1,0:T(8,128)(2,1)S(1)}, bf16[1024,512]{1,0:T(8,128)(2,1)S(1)}, u32[]{:S(2)}, u32[]{:S(2)}) collective-permute-start(bf16[1024,512]{1,0:T(8,128)(2,1)S(1)} %pad.26), channel_id=1, source_target_pairs={{0,1},{1,2},{2,3},{3,6},{4,7},{5,4},{6,5},{7,8},{8,9},{9,10},{10,1... | collective-permute-start | bytes 3145736 | tf_op jit(solution)/shard_map/ppermute | solution.py:732
  18.1 39.5 %collective-permute-start.7 = (bf16[1024,512]{1,0:T(8,128)(2,1)S(1)}, bf16[1024,512]{1,0:T(8,128)(2,1)S(1)}, u32[]{:S(2)}, u32[]{:S(2)}) collective-permute-start(bf16[1024,512]{1,0:T(8,128)(2,1)S(1)} %pad.26), channel_id=1, source_target_pairs={{0,29},{1,0},{2,1},{3,2},{4,3},{5,6},{6,7},{7,4},{8,5},{9,8},{10,9... | collective-permute-start | bytes 3145736 | tf_op jit(solution)/shard_map/ppermute | solution.py:732
  24.1 33.5 %collective-permute-start.8 = (bf16[1024,512]{1,0:T(8,128)(2,1)}, bf16[1024,512]{1,0:T(8,128)(2,1)S(1)}, u32[]{:S(2)}, u32[]{:S(2)}) collective-permute-start(bf16[1024,512]{1,0:T(8,128)(2,1)} %param.22), channel_id=1, source_target_pairs={{0,0},{1,1},{2,2},{3,3},{4,6},{5,7},{6,4},{7,5},{8,8},{9,9},{10,10... | collective-permute-start | bytes 3145736 | tf_op jit(solution)/shard_map/ppermute | solution.py:732
  26.9 20.3 %collective-permute-start.3 = (bf16[2,136,512]{2,1,0:T(8,128)(2,1)S(1)}, bf16[2,136,512]{2,1,0:T(8,128)(2,1)S(1)}, u32[]{:S(2)}, u32[]{:S(2)}) collective-permute-start(bf16[2,136,512]{2,1,0:T(8,128)(2,1)S(1)} %pad_maximum_fusion), channel_id=1, source_target_pairs={{0,8},{1,9},{2,10},{3,11},{4,12},{5,13},{6,14},{7,15},{8,0},{9,1},... | collective-permute-start | bytes 835592 | tf_op jit(solution)/shard_map/ppermute | solution.py:720
  27.0 25.3 %collective-permute-start.4 = (bf16[2,136,512]{2,1,0:T(8,128)(2,1)S(1)}, bf16[2,136,512]{2,1,0:T(8,128)(2,1)S(1)}, u32[]{:S(2)}, u32[]{:S(2)}) collective-permute-start(bf16[2,136,512]{2,1,0:T(8,128)(2,1)S(1)} %pad_maximum_fusion), channel_id=1, source_target_pairs={{0,16},{1,17},{2,18},{3,19},{4,20},{5,21},{6,22},{7,23},{8,24},{9,... | collective-permute-start | bytes 835592 | tf_op jit(solution)/shard_map/ppermute | solution.py:720
  60.9 47.5 %collective-permute-start.9 = (bf16[8,136,512]{2,1,0:T(8,128)(2,1)}, bf16[8,136,512]{2,1,0:T(8,128)(2,1)}, u32[]{:S(2)}, u32[]{:S(2)}) collective-permute-start(bf16[8,136,512]{2,1,0:T(8,128)(2,1)} %constant_dynamic-update-slice_fusion.refs_1_), channel_id=1, source_target_pairs={{0,4},{1,5},{2,6},{3,7},{4,0},{5,1},{6,2},{7,3},{8,12},{9,13},{10,... | collective-permute-start | bytes 3342344 | tf_op jit(solution)/shard_map/ppermute | solution.py:720
  83.3 20.3 %collective-permute-start.10 = (bf16[1024,512]{1,0:T(8,128)(2,1)S(1)}, bf16[1024,512]{1,0:T(8,128)(2,1)S(1)}, u32[]{:S(2)}, u32[]{:S(2)}) collective-permute-start(bf16[1024,512]{1,0:T(8,128)(2,1)S(1)} %pad.26), channel_id=1, source_target_pairs={{0,0},{1,1},{2,2},{3,3},{4,6},{5,7},{6,4},{7,5},{8,8},{9,9},{10,10... | collective-permute-start | bytes 3145736 | tf_op jit(solution)/shard_map/ppermute | solution.py:732
  86.3 17.3 %collective-permute-start.12 = (bf16[2,96,512]{2,1,0:T(8,128)(2,1)S(1)}, bf16[2,96,512]{2,1,0:T(8,128)(2,1)}, u32[]{:S(2)}, u32[]{:S(2)}) collective-permute-start(bf16[2,96,512]{2,1,0:T(8,128)(2,1)S(1)} %pad_maximum_fusion.1), channel_id=1, source_target_pairs={{0,16},{1,17},{2,18},{3,19},{4,20},{5,21},{6,22},{7,23},{8,24},{9,... | collective-permute-start | bytes 589832 | tf_op jit(solution)/shard_map/ppermute | solution.py:720
  112.5 43.2 %collective-permute-start.19 = (bf16[8,96,512]{2,1,0:T(8,128)(2,1)S(1)}, bf16[8,96,512]{2,1,0:T(8,128)(2,1)S(1)}, u32[]{:S(2)}, u32[]{:S(2)}) collective-permute-start(bf16[8,96,512]{2,1,0:T(8,128)(2,1)S(1)} %constant_dynamic-update-slice_fusion.4.refs_1_), channel_id=1, source_target_pairs={{0,4},{1,5},{2,6},{3,7},{4,0},{5,1},{6,2},{7,3},{8,12},{9,13},{10,... | collective-permute-start | bytes 2359304 | tf_op jit(solution)/shard_map/ppermute | solution.py:720
  151.3 32.9 %collective-permute-start.17 = (bf16[1024,512]{1,0:T(8,128)(2,1)}, bf16[1024,512]{1,0:T(8,128)(2,1)}, u32[]{:S(2)}, u32[]{:S(2)}) collective-permute-start(bf16[1024,512]{1,0:T(8,128)(2,1)} %get-tuple-element.272.refs_2_), channel_id=1, source_target_pairs={{0,1},{1,2},{2,3},{3,6},{6,7},{7,4},{4,5},{5,8},{8,9},{9,10},{10,1... | collective-permute-start | bytes 3145736 | tf_op jit(solution)/shard_map/ppermute | solution.py:737
  151.3 32.9 %collective-permute-start.18 = (bf16[1024,512]{1,0:T(8,128)(2,1)}, bf16[1024,512]{1,0:T(8,128)(2,1)}, u32[]{:S(2)}, u32[]{:S(2)}) collective-permute-start(bf16[1024,512]{1,0:T(8,128)(2,1)} %get-tuple-element.272.refs_2_), channel_id=1, source_target_pairs={{0,29},{1,0},{2,1},{3,2},{6,3},{7,6},{4,7},{5,4},{8,5},{9,8},{10,9... | collective-permute-start | bytes 3145736 | tf_op jit(solution)/shard_map/ppermute | solution.py:737
  210.4 37.4 %collective-permute-start.16 = (f32[1024,256]{0,1:T(8,128)S(1)}, f32[1024,256]{0,1:T(8,128)}, u32[]{:S(2)}, u32[]{:S(2)}) collective-permute-start(f32[1024,256]{0,1:T(8,128)S(1)} %copy-done.24), channel_id=1, source_target_pairs={{0,0},{1,1},{2,2},{3,3},{4,6},{5,7},{6,4},{7,5},{8,8},{9,9},{10,10... | collective-permute-start | bytes 3145736 | tf_op jit(solution)/shard_map/ppermute | solution.py:732
  316.5 17.4 %collective-permute-start.27 = (bf16[1024,512]{1,0:T(8,128)(2,1)}, bf16[1024,512]{1,0:T(8,128)(2,1)S(1)}, u32[]{:S(2)}, u32[]{:S(2)}) collective-permute-start(bf16[1024,512]{1,0:T(8,128)(2,1)} %get-tuple-element.293), channel_id=1, source_target_pairs={{0,29},{1,0},{2,1},{3,2},{6,3},{7,6},{4,7},{5,4},{8,5},{9,8},{10,9... | collective-permute-start | bytes 3145736 | tf_op jit(solution)/shard_map/ppermute | solution.py:737
  339.7 36.6 %collective-permute-start.29 = (bf16[4,96,512]{2,1,0:T(8,128)(2,1)S(1)}, bf16[4,96,512]{2,1,0:T(8,128)(2,1)S(1)}, u32[]{:S(2)}, u32[]{:S(2)}) collective-permute-start(bf16[4,96,512]{2,1,0:T(8,128)(2,1)S(1)} %get-tuple-element.311), channel_id=1, source_target_pairs={{0,2},{1,3},{2,0},{3,1},{4,6},{5,7},{6,4},{7,5},{8,10},{9,11},{10,... | collective-permute-start | bytes 1179656 | tf_op jit(solution)/shard_map/ppermute | solution.py:720
  341.5 34.8 %collective-permute-start.30 = (bf16[4,96,512]{2,1,0:T(8,128)(2,1)S(1)}, bf16[4,96,512]{2,1,0:T(8,128)(2,1)S(1)}, u32[]{:S(2)}, u32[]{:S(2)}) collective-permute-start(bf16[4,96,512]{2,1,0:T(8,128)(2,1)S(1)} %get-tuple-element.312), channel_id=1, source_target_pairs={{0,4},{1,5},{2,6},{3,7},{4,0},{5,1},{6,2},{7,3},{8,12},{9,13},{10,... | collective-permute-start | bytes 1179656 | tf_op jit(solution)/shard_map/ppermute | solution.py:720
  343.1 33.1 %collective-permute-start.31 = (bf16[4,96,512]{2,1,0:T(8,128)(2,1)S(1)}, bf16[4,96,512]{2,1,0:T(8,128)(2,1)S(1)}, u32[]{:S(2)}, u32[]{:S(2)}) collective-permute-start(bf16[4,96,512]{2,1,0:T(8,128)(2,1)S(1)} %get-tuple-element.313), channel_id=1, source_target_pairs={{0,6},{1,7},{2,4},{3,5},{4,2},{5,3},{6,0},{7,1},{8,14},{9,15},{10,... | collective-permute-start | bytes 1179656 | tf_op jit(solution)/shard_map/ppermute | solution.py:720
  376.3 17.4 %collective-permute-start.33 = (bf16[1024,512]{1,0:T(8,128)(2,1)}, bf16[1024,512]{1,0:T(8,128)(2,1)S(1)}, u32[]{:S(2)}, u32[]{:S(2)}) collective-permute-start(bf16[1024,512]{1,0:T(8,128)(2,1)} %get-tuple-element.323), channel_id=1, source_target_pairs={{0,29},{1,0},{2,1},{3,2},{6,3},{7,6},{4,7},{5,4},{8,5},{9,8},{10,9... | collective-permute-start | bytes 3145736 | tf_op jit(solution)/shard_map/ppermute | solution.py:737
  394.6 41.6 %collective-permute-start.39 = (bf16[1,96,512]{2,1,0:T(8,128)(2,1)S(1)}, bf16[1,96,512]{2,1,0:T(8,128)(2,1)S(1)}, u32[]{:S(2)}, u32[]{:S(2)}) collective-permute-start(bf16[1,96,512]{2,1,0:T(8,128)(2,1)S(1)} %get-tuple-element.357), channel_id=1, source_target_pairs={{0,16},{1,17},{2,18},{3,19},{4,20},{5,21},{6,22},{7,23},{8,24},{9,... | collective-permute-start | bytes 294920 | tf_op jit(solution)/shard_map/ppermute | solution.py:720
  395.6 40.6 %collective-permute-start.40 = (bf16[1,96,512]{2,1,0:T(8,128)(2,1)S(1)}, bf16[1,96,512]{2,1,0:T(8,128)(2,1)S(1)}, u32[]{:S(2)}, u32[]{:S(2)}) collective-permute-start(bf16[1,96,512]{2,1,0:T(8,128)(2,1)S(1)} %get-tuple-element.358), channel_id=1, source_target_pairs={{0,24},{1,25},{2,26},{3,27},{4,28},{5,29},{6,30},{7,31},{8,16},{9,... | collective-permute-start | bytes 294920 | tf_op jit(solution)/shard_map/ppermute | solution.py:720
  398.6 37.6 %collective-permute-start.35 = (bf16[4,96,512]{2,1,0:T(8,128)(2,1)S(1)}, bf16[4,96,512]{2,1,0:T(8,128)(2,1)S(1)}, u32[]{:S(2)}, u32[]{:S(2)}) collective-permute-start(bf16[4,96,512]{2,1,0:T(8,128)(2,1)S(1)} %get-tuple-element.352), channel_id=1, source_target_pairs={{0,2},{1,3},{2,0},{3,1},{4,6},{5,7},{6,4},{7,5},{8,10},{9,11},{10,... | collective-permute-start | bytes 1179656 | tf_op jit(solution)/shard_map/ppermute | solution.py:720
  399.5 36.7 %collective-permute-start.36 = (bf16[4,96,512]{2,1,0:T(8,128)(2,1)S(1)}, bf16[4,96,512]{2,1,0:T(8,128)(2,1)S(1)}, u32[]{:S(2)}, u32[]{:S(2)}) collective-permute-start(bf16[4,96,512]{2,1,0:T(8,128)(2,1)S(1)} %get-tuple-element.353), channel_id=1, source_target_pairs={{0,4},{1,5},{2,6},{3,7},{4,0},{5,1},{6,2},{7,3},{8,12},{9,13},{10,... | collective-permute-start | bytes 1179656 | tf_op jit(solution)/shard_map/ppermute | solution.py:720
  400.4 35.8 %collective-permute-start.37 = (bf16[4,96,512]{2,1,0:T(8,128)(2,1)S(1)}, bf16[4,96,512]{2,1,0:T(8,128)(2,1)S(1)}, u32[]{:S(2)}, u32[]{:S(2)}) collective-permute-start(bf16[4,96,512]{2,1,0:T(8,128)(2,1)S(1)} %get-tuple-element.354), channel_id=1, source_target_pairs={{0,6},{1,7},{2,4},{3,5},{4,2},{5,3},{6,0},{7,1},{8,14},{9,15},{10,... | collective-permute-start | bytes 1179656 | tf_op jit(solution)/shard_map/ppermute | solution.py:720
  453.6 41.1 %collective-permute-start.48 = (bf16[1,96,512]{2,1,0:T(8,128)(2,1)S(1)}, bf16[1,96,512]{2,1,0:T(8,128)(2,1)S(1)}, u32[]{:S(2)}, u32[]{:S(2)}) collective-permute-start(bf16[1,96,512]{2,1,0:T(8,128)(2,1)S(1)} %get-tuple-element.402), channel_id=1, source_target_pairs={{0,16},{1,17},{2,18},{3,19},{4,20},{5,21},{6,22},{7,23},{8,24},{9,... | collective-permute-start | bytes 294920 | tf_op jit(solution)/shard_map/ppermute | solution.py:720
  456.2 38.5 %collective-permute-start.49 = (bf16[1,96,512]{2,1,0:T(8,128)(2,1)S(1)}, bf16[1,96,512]{2,1,0:T(8,128)(2,1)S(1)}, u32[]{:S(2)}, u32[]{:S(2)}) collective-permute-start(bf16[1,96,512]{2,1,0:T(8,128)(2,1)S(1)} %get-tuple-element.403), channel_id=1, source_target_pairs={{0,24},{1,25},{2,26},{3,27},{4,28},{5,29},{6,30},{7,31},{8,16},{9,... | collective-permute-start | bytes 294920 | tf_op jit(solution)/shard_map/ppermute | solution.py:720
  458.3 36.4 %collective-permute-start.44 = (bf16[4,96,512]{2,1,0:T(8,128)(2,1)S(1)}, bf16[4,96,512]{2,1,0:T(8,128)(2,1)S(1)}, u32[]{:S(2)}, u32[]{:S(2)}) collective-permute-start(bf16[4,96,512]{2,1,0:T(8,128)(2,1)S(1)} %get-tuple-element.397), channel_id=1, source_target_pairs={{0,2},{1,3},{2,0},{3,1},{4,6},{5,7},{6,4},{7,5},{8,10},{9,11},{10,... | collective-permute-start | bytes 1179656 | tf_op jit(solution)/shard_map/ppermute | solution.py:720
  458.4 36.3 %collective-permute-start.45 = (bf16[4,96,512]{2,1,0:T(8,128)(2,1)S(1)}, bf16[4,96,512]{2,1,0:T(8,128)(2,1)S(1)}, u32[]{:S(2)}, u32[]{:S(2)}) collective-permute-start(bf16[4,96,512]{2,1,0:T(8,128)(2,1)S(1)} %get-tuple-element.398), channel_id=1, source_target_pairs={{0,4},{1,5},{2,6},{3,7},{4,0},{5,1},{6,2},{7,3},{8,12},{9,13},{10,... | collective-permute-start | bytes 1179656 | tf_op jit(solution)/shard_map/ppermute | solution.py:720
  460.1 34.6 %collective-permute-start.46 = (bf16[4,96,512]{2,1,0:T(8,128)(2,1)S(1)}, bf16[4,96,512]{2,1,0:T(8,128)(2,1)S(1)}, u32[]{:S(2)}, u32[]{:S(2)}) collective-permute-start(bf16[4,96,512]{2,1,0:T(8,128)(2,1)S(1)} %get-tuple-element.399), channel_id=1, source_target_pairs={{0,6},{1,7},{2,4},{3,5},{4,2},{5,3},{6,0},{7,1},{8,14},{9,15},{10,... | collective-permute-start | bytes 1179656 | tf_op jit(solution)/shard_map/ppermute | solution.py:720
  494.7 17.3 %collective-permute-start.50 = (bf16[1024,512]{1,0:T(8,128)(2,1)}, bf16[1024,512]{1,0:T(8,128)(2,1)}, u32[]{:S(2)}, u32[]{:S(2)}) collective-permute-start(bf16[1024,512]{1,0:T(8,128)(2,1)} %get-tuple-element.413), channel_id=1, source_target_pairs={{0,1},{1,2},{2,3},{3,6},{6,7},{7,4},{4,5},{5,8},{8,9},{9,10},{10,1... | collective-permute-start | bytes 3145736 | tf_op jit(solution)/shard_map/ppermute | solution.py:737
  528.3 20.1 %collective-permute-start.64 = (bf16[4,96,512]{2,1,0:T(8,128)(2,1)S(1)}, bf16[4,96,512]{2,1,0:T(8,128)(2,1)S(1)}, u32[]{:S(2)}, u32[]{:S(2)}) collective-permute-start(bf16[4,96,512]{2,1,0:T(8,128)(2,1)S(1)} %get-tuple-element.461), channel_id=1, source_target_pairs={{0,4},{1,5},{2,6},{3,7},{4,0},{5,1},{6,2},{7,3},{8,12},{9,13},{10,... | collective-permute-start | bytes 1179656 | tf_op jit(solution)/shard_map/ppermute | solution.py:720
  530.8 19.7 %collective-permute-start.65 = (bf16[4,96,512]{2,1,0:T(8,128)(2,1)S(1)}, bf16[4,96,512]{2,1,0:T(8,128)(2,1)S(1)}, u32[]{:S(2)}, u32[]{:S(2)}) collective-permute-start(bf16[4,96,512]{2,1,0:T(8,128)(2,1)S(1)} %get-tuple-element.462), channel_id=1, source_target_pairs={{0,6},{1,7},{2,4},{3,5},{4,2},{5,3},{6,0},{7,1},{8,14},{9,15},{10,... | collective-permute-start | bytes 1179656 | tf_op jit(solution)/shard_map/ppermute | solution.py:720
  533.1 22.3 %collective-permute-start.57 = (bf16[4,40,512]{2,1,0:T(8,128)(2,1)S(1)}, bf16[4,40,512]{2,1,0:T(8,128)(2,1)S(1)}, u32[]{:S(2)}, u32[]{:S(2)}) collective-permute-start(bf16[4,40,512]{2,1,0:T(8,128)(2,1)S(1)} %get-tuple-element.450), channel_id=1, source_target_pairs={{0,2},{1,3},{2,0},{3,1},{4,6},{5,7},{6,4},{7,5},{8,10},{9,11},{10,... | collective-permute-start | bytes 491528 | tf_op jit(solution)/shard_map/ppermute | solution.py:720
  (106 other events, 1272.6 us)
Sparse Core Ops, SparseCore 0:
  108.6 77.8 all-gather.1

commit v9 on v8

--- a/solution.py
+++ b/solution.py
@@ -19,7 +19,7 @@
 FORWARD_ROWS = 256
 BACKWARD_ROWS = 256
 WEIGHT_ROWS = 256
-UNROLL = 32
+UNROLL = 256
 LOW = jnp.bfloat16
 WIDE = jnp.float32
 SEND = jnp.bfloat16
@@ -163,7 +163,7 @@
     return pl.BlockSpec((fan, rows, width), lambda step: (0, step, 0))
 
 
-def forward_layer(slots, blocks, target_low, target, weights, next_weights, gains):
+def forward_layer(slots, blocks, target_low, target, weights, next_weights, gains, halo_place):
     block_rows, width = target_low.shape
     fan = slots.shape[0] // block_rows
     parts = width // LANES
@@ -204,9 +204,9 @@
         name="forward_layer",
     )(
         operands[0],
-        kept_on_chip(operands[1]),
+        halo_place(operands[1]),
         pinned(operands[2]),
-        kept_on_chip(operands[3]),
+        halo_place(operands[3]),
         *map(pinned, operands[4:]),
     )
 
@@ -559,6 +559,29 @@
     )(self_id, *pieces)
 
 
+def join_kernel(*refs):
+    start = 0
+    for part in refs[:-1]:
+        refs[-1][start : start + part.shape[0]] = part[...]
+        start += part.shape[0]
+
+
+def join(parts):
+    shape = (sum(part.shape[0] for part in parts), *parts[0].shape[1:])
+    return pl.pallas_call(
+        join_kernel,
+        grid=(1,),
+        in_specs=[whole(part.shape) for part in parts],
+        out_specs=whole(shape),
+        out_shape=on_chip(shape, parts[0].dtype),
+        compiler_params=pltpu.CompilerParams(vmem_limit_bytes=8 << 20),
+        cost_estimate=pl.CostEstimate(
+            flops=0, transcendentals=0, bytes_accessed=4 * shape[0] * shape[1] * shape[2]
+        ),
+        name="join",
+    )(*map(kept_on_chip, parts))
+
+
 def embed_kernel(pieces_count, *refs):
     self_id = refs[0]
     pieces = refs[1 : 1 + pieces_count]
@@ -596,9 +619,9 @@
             in_hbm((7, width, width), LOW),
             in_hbm((block_rows, width), WIDE),
             in_hbm((block_rows, width), LOW),
-            on_chip((block_rows, width), LOW),
             in_hbm((block_rows, width), LOW),
-            on_chip((block_rows, width), LOW),
+            in_hbm((block_rows, width), LOW),
+            in_hbm((block_rows, width), LOW),
         ],
         scratch_shapes=[pltpu.VMEM((width, width), LOW)],
         compiler_params=pltpu.CompilerParams(vmem_limit_bytes=50 << 20),
@@ -829,29 +852,27 @@
         pairs = ((packed, swap(packed, device_count, 2)), (second, swap(second, device_count, 2)))
         lists = bring(lists, device_count, 0, direct)
         pairs, lists, inputs, mesh_static = barrier((pairs, lists, inputs, mesh_static))
-        sides = [bring(inputs, device_count, step, direct) for step in (1, -1)]
         mesh_rows = bring(mesh_static, device_count, 0, direct)
         pair, second_pair = (jnp.stack(rows) for rows in pairs)
-        column, sides, mesh_rows, inputs, second_pair = barrier(
-            (spread_high(pair, device_count), sides, mesh_rows, inputs, second_pair)
-        )
-        own = bring(inputs, device_count, 0, direct)
+        column, mesh_rows, inputs, second_pair = barrier(
+            (spread_high(pair, device_count), mesh_rows, inputs, second_pair)
+        )
+        sides = [bring(inputs, device_count, step, direct) for step in (1, 0, -1)]
         second_column = spread_high(second_pair, device_count)
-        plane = jnp.concatenate(column)
-        near, own, second_column, rest, goals = barrier(
-            ((plane, swap(plane, device_count, 4)), own, second_column, rest, goals)
+        plane = join(column)
+        near, sides, second_column, rest, goals = barrier(
+            ((plane, swap(plane, device_count, 4)), sides, second_column, rest, goals)
         )
         pieces = [*near, *(swap(piece, device_count, 1) for piece in near)]
-        sides = [sides[0], own, sides[1]]
         rest = lax.all_gather(rest, AXES, axis=1, tiled=True)
-        inputs = own
+        inputs = sides[1]
         lists = lists.reshape(len(slot_lists), -1)
         slot_lists = [lists[index] for index in range(len(slot_lists))]
         first, grid_latent, grid_start, *blocks = embed(
             self_id, pieces, sides
         )
         first, goals = barrier((first, goals))
-        second_plane = jnp.concatenate(second_column)
+        second_plane = join(second_column)
         second_near = (second_plane, swap(second_plane, device_count, 4))
         goals = bring(goals, device_count, 0, direct)
         targets, weight_rows = goals[:, :outputs], goals[:, outputs]
@@ -902,6 +923,7 @@
             weights[layer_id],
             None if last_layer else heads[layer_id + 1],
             gains[layer_id],
+            kept_on_chip if layer_id > 0 else pinned,
         )
         if last_layer:
             grid_low, kept, aggregate = results

time: 592 us -> 566 us (0.956)
  Pallas kernels: 278 us -> 264 us
  local copies, waits for them, and re-layouts: 20.8 us -> 11.6 us
    ppermute x49, waiting for transfers between devices: 78.8 us -> 88.8 us  [swap(): return lax.ppermute(cells, AXES, [(i, i ^ mask) for i in range(count)])]
    ppermute x14, waiting for transfers between devices: 47.5 us -> 38 us  [shift(): return lax.ppermute(cells, AXES, pairs)]
    pallas_call x4, Pallas kernels: 80.3 us -> 72.1 us  [forward_layer(): pl.pallas_call(functools.partial(forward_kernel, parts, has_next), grid=(...]
    unnamed x151 -> x137, local copies, waits for them, and re-layouts: 13 us -> 5.03 us
    pallas_call x4, Pallas kernels: 132 us -> 125 us  [backward_layer(): pl.pallas_call(functools.partial(backward_kernel, parts, mode), grid=(blo...]
  transfers between devices with their start and end apart: 70 -> 70, of which waited for: 26 -> 27; matrix products, arithmetic and copies ran while one was open for 3% -> 2% of each run, Pallas kernels for 39% -> 39%
where the time goes in v9:
time: 566 us; the launch traced here: 558 us
  Pallas kernels  264 us (47%)
  waiting for transfers between devices  127 us (22%)
  starting transfers between devices  121 us (21%)
  between operations  17.4 us (3%)
  local copies, waits for them, and re-layouts  11.6 us (2%)
  other arithmetic  10.5 us (2%)
  matrix products  6.06 us (1%)
    pallas_call x4, Pallas kernels, backward_layer(): pl.pallas_call(functools.partial(backward_kernel, parts, mode), grid=(blo...  125 us
    ppermute x49, waiting for transfers between devices, swap(): return lax.ppermute(cells, AXES, [(i, i ^ mask) for i in range(count)])  88.8 us
    ppermute x49, starting transfers between devices, swap(): return lax.ppermute(cells, AXES, [(i, i ^ mask) for i in range(count)])  82.6 us
    pallas_call x4, Pallas kernels, forward_layer(): pl.pallas_call(functools.partial(forward_kernel, parts, has_next), grid=(...  72.1 us
    pallas_call x4, Pallas kernels, weight_layer(): pl.pallas_call(functools.partial(weight_kernel, above is not None, grad_n...  42.7 us
    ppermute x14, waiting for transfers between devices, shift(): return lax.ppermute(cells, AXES, pairs)  38 us
    ppermute x14, starting transfers between devices, shift(): return lax.ppermute(cells, AXES, pairs)  32.6 us
  transfers between devices with their start and end apart: 70, of which 27 were waited for; matrix products, arithmetic and copies ran while one was open for 2% of the time, Pallas kernels for 39%

profile of v9, /device:TPU:0, one launch (start us, length us, event | category | flops | bytes accessed | tf_op | source)
XLA Modules:
  0.0 557.5 jit_solution(15686995150024423795)
XLA Ops:
  22.8 8.5 %collective-permute-done.3.refs_1_ = bf16[2,136,512]{2,1,0:T(8,128)(2,1)S(1)} collective-permute-done((bf16[2,136,512]{2,1,0:T(8,128)(2,1)S(1)}, bf16[2,136,512]{2,1,0:T(8,128)(2,1)S(1)}, u32[]{:S(2)}, u32[]{:S(2)}) %collective-permute-start.3) | collective-permute-done | bytes 278560 | tf_op jit(solution)/shard_map/ppermute | solution.py:743
  31.3 11.3 %collective-permute-done.4.refs_2_ = bf16[2,136,512]{2,1,0:T(8,128)(2,1)S(1)} collective-permute-done((bf16[2,136,512]{2,1,0:T(8,128)(2,1)S(1)}, bf16[2,136,512]{2,1,0:T(8,128)(2,1)S(1)}, u32[]{:S(2)}, u32[]{:S(2)}) %collective-permute-start.4) | collective-permute-done | bytes 278560 | tf_op jit(solution)/shard_map/ppermute | solution.py:743
  42.7 5.2 collective-permute-start.7
  54.9 16.3 %collective-permute-done.11.refs_1_ = bf16[2,96,512]{2,1,0:T(8,128)(2,1)S(1)} collective-permute-done((bf16[2,96,512]{2,1,0:T(8,128)(2,1)S(1)}, bf16[2,96,512]{2,1,0:T(8,128)(2,1)S(1)}, u32[]{:S(2)}, u32[]{:S(2)}) %collective-permute-start.11) | collective-permute-done | bytes 196640 | tf_op jit(solution)/shard_map/ppermute | solution.py:743
  71.2 11.8 %collective-permute-done.12.refs_2_ = bf16[2,96,512]{2,1,0:T(8,128)(2,1)S(1)} collective-permute-done((bf16[2,96,512]{2,1,0:T(8,128)(2,1)S(1)}, bf16[2,96,512]{2,1,0:T(8,128)(2,1)S(1)}, u32[]{:S(2)}, u32[]{:S(2)}) %collective-permute-start.12) | collective-permute-done | bytes 196640 | tf_op jit(solution)/shard_map/ppermute | solution.py:743
  93.3 16.9 %collective-permute-start.19 = (bf16[8,96,512]{2,1,0:T(8,128)(2,1)S(1)}, bf16[8,96,512]{2,1,0:T(8,128)(2,1)}, u32[]{:S(2)}, u32[]{:S(2)}) collective-permute-start(bf16[8,96,512]{2,1,0:T(8,128)(2,1)S(1)} %join.3.refs_1_), channel_id=1, source_target_pairs={{0,4},{1,5},{2,6},{3,7},{4,0},{5,1},{6,2},{7,3},{8,12},{9,13},{10,... | collective-permute-start | bytes 2359304 | tf_op jit(solution)/shard_map/ppermute | solution.py:743
  111.9 9.3 %embed.1 = (bf16[7,512,512]{2,1,0:T(8,128)(2,1)}, f32[1024,512]{1,0:T(8,128)}, bf16[1024,512]{1,0:T(8,128)(2,1)}, bf16[1024,512]{1,0:T(8,128)(2,1)}, bf16[1024,5...) custom-call(s32[1]{0:T(128)} %bitcast.10.refs_0_.self_id, bf16[8,136,512]{2,1,0:T(8,128)(2,1)} %copy-done.1, ...), custom_call_target="tpu_custom_call" | custom-call | flops 3221225472 | bytes 12582912 | tf_op jit(solution)/shard_map/embed/pallas_call | solution.py:611
  122.0 18.6 %forward_layer.4 = (bf16[1024,512]{1,0:T(8,128)(2,1)}, f32[1024,512]{1,0:T(8,128)}, bf16[1024,512]{1,0:T(8,128)(2,1)}, bf16[4,1024,512]{2,1,0:T(8,128)(2,1)}, bf16[1024,512]{1,0:T(8,128)(2,1)}) custom-call(s32[4096]{0:T(1024)} %get-tuple-element.503.refs_0_, bf16[1024,512]{1,0:T(8,128)(2,1)} %get-tuple-element.267.refs_1_, ...), custom_call_target="tpu_custom_call" | custom-call | flops 4831838208 | bytes 25165824 | tf_op jit(solution)/shard_map/forward_layer/pallas_call | solution.py:186
  152.0 11.9 %collective-permute-done.17.refs_1_ = bf16[1024,512]{1,0:T(8,128)(2,1)} collective-permute-done((bf16[1024,512]{1,0:T(8,128)(2,1)}, bf16[1024,512]{1,0:T(8,128)(2,1)}, u32[]{:S(2)}, u32[]{:S(2)}) %collective-permute-start.17) | collective-permute-done | bytes 1048608 | tf_op jit(solution)/shard_map/ppermute | solution.py:760
  165.0 18.7 %forward_layer.5 = (bf16[1024,512]{1,0:T(8,128)(2,1)}, f32[1024,512]{1,0:T(8,128)}, bf16[1024,512]{1,0:T(8,128)(2,1)}, bf16[4,1024,512]{2,1,0:T(8,128)(2,1)}, bf16[1024,512]{1,0:T(8,128)(2,1)}) custom-call(s32[4096]{0:T(1024)} %get-tuple-element.504.refs_0_, bf16[1024,512]{1,0:T(8,128)(2,1)} %collective-permute-done.17.refs_1_, ...), custom_call_target="tpu_custom_call" | custom-call | flops 4831838208 | bytes 25165824 | tf_op jit(solution)/shard_map/forward_layer/pallas_call | solution.py:186
  183.7 4.6 collective-permute-start.23
  191.2 9.8 %collective-permute-done.22.refs_1_ = bf16[1024,512]{1,0:T(8,128)(2,1)S(1)} collective-permute-done((bf16[1024,512]{1,0:T(8,128)(2,1)}, bf16[1024,512]{1,0:T(8,128)(2,1)S(1)}, u32[]{:S(2)}, u32[]{:S(2)}) %collective-permute-start.22) | collective-permute-done | bytes 1048608 | tf_op jit(solution)/shard_map/ppermute | solution.py:760
  201.0 18.0 %forward_layer.6 = (bf16[1024,512]{1,0:T(8,128)(2,1)}, f32[1024,512]{1,0:T(8,128)}, bf16[1024,512]{1,0:T(8,128)(2,1)}, bf16[4,1024,512]{2,1,0:T(8,128)(2,1)}, bf16[1024,512]{1,0:T(8,128)(2,1)}) custom-call(s32[4096]{0:T(1024)} %get-tuple-element.504.refs_0_, bf16[1024,512]{1,0:T(8,128)(2,1)S(1)} %collective-permute-done.22.refs_1_, ...), custom_call_target="tpu_custom_call" | custom-call | flops 4831838208 | bytes 25165824 | tf_op jit(solution)/shard_map/forward_layer/pallas_call | solution.py:186
  225.1 11.1 %collective-permute-done.24.refs_1_ = bf16[1024,512]{1,0:T(8,128)(2,1)S(1)} collective-permute-done((bf16[1024,512]{1,0:T(8,128)(2,1)}, bf16[1024,512]{1,0:T(8,128)(2,1)S(1)}, u32[]{:S(2)}, u32[]{:S(2)}) %collective-permute-start.24) | collective-permute-done | bytes 1048608 | tf_op jit(solution)/shard_map/ppermute | solution.py:760
  236.2 16.7 %forward_layer.7 = (bf16[1024,512]{1,0:T(8,128)(2,1)}, bf16[4,1024,512]{2,1,0:T(8,128)(2,1)}, bf16[1024,512]{1,0:T(8,128)(2,1)}) custom-call(s32[4096]{0:T(1024)} %get-tuple-element.505.refs_0_, bf16[1024,512]{1,0:T(8,128)(2,1)S(1)} %collective-permute-done.24.refs_1_, bf16[1024,512]{1,0:T(8,128)(2,1)} %get-tuple-element.286.refs_2_, ...), custom_call_target="tpu_custom_call" | custom-call | flops 4831838208 | bytes 25165824 | tf_op jit(solution)/shard_map/forward_layer/pallas_call | solution.py:186
  258.5 29.8 %backward_layer.4 = (bf16[1024,512]{1,0:T(8,128)(2,1)}, bf16[1024,512]{1,0:T(8,128)(2,1)}, bf16[1024,512]{1,0:T(8,128)(2,1)}, f32[2,512]{1,0:T(2,128)S(1)}, bf16...) custom-call(s32[4096]{0:T(1024)S(1)} %copy-done.9, ...), custom_call_target="tpu_custom_call" | custom-call | flops 4294967296 | bytes 25165824 | tf_op jit(solution)/shard_map/backward_layer/pallas_call | solution.py:374
  288.4 4.7 collective-permute-start.27
  293.7 10.8 %weight_layer.4 = (f32[1024,512]{1,0:T(8,128)}, f32[16,96,512]{2,1,0:T(8,128)S(1)}, bf16[16,96,512]{2,1,0:T(8,128)(2,1)S(1)}) custom-call(s32[1]{0:T(128)} %bitcast.10.refs_0_.self_id, f32[512,512]{1,0:T(8,128)S(1)} %pad.29.refs_1_, bf16[1024,512]{1,0:T(8,128)(2,1)} %get-tuple-element.287.refs_4_.refs_2_.latent_low, ...), custom_call_target="tpu_custom_call" | custom-call | flops 5368709120 | bytes 12582912 | tf_op jit(solution)/shard_map/weight_layer/pallas_call | solution.py:504
  305.7 8.6 %collective-permute-start.28 = (bf16[16,96,512]{2,1,0:T(8,128)(2,1)S(1)}, bf16[16,96,512]{2,1,0:T(8,128)(2,1)S(1)}, u32[]{:S(2)}, u32[]{:S(2)}) collective-permute-start(bf16[16,96,512]{2,1,0:T(8,128)(2,1)S(1)} %get-tuple-element.305), channel_id=1, source_target_pairs={{0,1},{1,0},{2,3},{3,2},{4,5},{5,4},{6,7},{7,6},{8,9},{9,8},{10,11... | collective-permute-start | bytes 4718600 | tf_op jit(solution)/shard_map/ppermute | solution.py:743
  321.2 32.0 %backward_layer.5 = (bf16[1024,512]{1,0:T(8,128)(2,1)S(1)}, f32[1024,512]{1,0:T(8,128)S(1)}, bf16[1024,512]{1,0:T(8,128)(2,1)}, bf16[1024,512]{1,0:T(8,128)(2,1)...) custom-call(s32[4096]{0:T(1024)S(1)} %copy-done.3, ...), custom_call_target="tpu_custom_call" | custom-call | flops 4294967296 | bytes 25165824 | tf_op jit(solution)/shard_map/backward_layer/pallas_call | solution.py:374
  353.3 4.6 collective-permute-start.33
  357.9 11.1 %weight_layer.5 = (f32[1024,512]{1,0:T(8,128)}, f32[16,96,512]{2,1,0:T(8,128)S(1)}, bf16[16,96,512]{2,1,0:T(8,128)(2,1)S(1)}) custom-call(s32[1]{0:T(128)} %bitcast.10.refs_0_.self_id, bf16[1024,512]{1,0:T(8,128)(2,1)} %get-tuple-element.324.refs_1_, bf16[1024,512]{1,0:T(8,128)(2,1)S(1)} %get-tuple-element.325.refs_2_, ...), custom_call_target="tpu_custom_call" | custom-call | flops 5368709120 | bytes 12582912 | tf_op jit(solution)/shard_map/weight_layer/pallas_call | solution.py:504
  379.0 31.6 %backward_layer.6 = (bf16[1024,512]{1,0:T(8,128)(2,1)S(1)}, f32[1024,512]{1,0:T(8,128)S(1)}, bf16[1024,512]{1,0:T(8,128)(2,1)}, bf16[1024,512]{1,0:T(8,128)(2,1)...) custom-call(s32[4096]{0:T(1024)S(1)} %copy-done.3, ...), custom_call_target="tpu_custom_call" | custom-call | flops 4294967296 | bytes 25165824 | tf_op jit(solution)/shard_map/backward_layer/pallas_call | solution.py:374
  410.7 4.8 collective-permute-start.42
  415.5 11.4 %weight_layer.6 = (f32[1024,512]{1,0:T(8,128)}, f32[16,96,512]{2,1,0:T(8,128)S(1)}, bf16[16,96,512]{2,1,0:T(8,128)(2,1)S(1)}) custom-call(s32[1]{0:T(128)} %bitcast.10.refs_0_.self_id, bf16[1024,512]{1,0:T(8,128)(2,1)} %get-tuple-element.283.refs_4_.refs_5_.refs_3_.refs_1_, bf16[1024,512]{1,0:T(8,128)(2,1)S(1)} %get-tuple-element.370.refs_2_, ...), custom_call_target="tpu_custom_call" | custom-call | flops 5368709120 | bytes 12582912 | tf_op jit(solution)/shard_map/weight_layer/pallas_call | solution.py:504
  436.5 31.9 %backward_layer.7 = (bf16[1024,512]{1,0:T(8,128)(2,1)S(1)}, f32[1024,512]{1,0:T(8,128)}, bf16[1024,512]{1,0:T(8,128)(2,1)}, bf16[1024,512]{1,0:T(8,128)(2,1)}, b...) custom-call(s32[4096]{0:T(1024)S(1)} %copy-done.8, ...), custom_call_target="tpu_custom_call" | custom-call | flops 4294967296 | bytes 25165824 | tf_op jit(solution)/shard_map/backward_layer/pallas_call | solution.py:374
  468.5 4.6 collective-permute-start.51
  473.1 9.4 %weight_layer.7 = (f32[16,96,512]{2,1,0:T(8,128)S(1)}, bf16[16,96,512]{2,1,0:T(8,128)(2,1)}) custom-call(s32[1]{0:T(128)} %bitcast.10.refs_0_.self_id, bf16[1024,512]{1,0:T(8,128)(2,1)} %get-tuple-element.273.refs_4_.refs_6_.refs_3_.refs_1_, bf16[1024,512]{1,0:T(8,128)(2,1)S(1)} %get-tuple-element.415.refs_2_, bf16[1024,512]{1,0:T(8,128)(2,1)} %copy-done.19, ...), custom_call_target="tpu_custom_call" | custom-call | flops 5368709120 | bytes 12582912 | tf_op jit(solution)/shard_map/weight_layer/pallas_call | solution.py:504
  490.9 7.0 %tail_layer.1 = (f32[16,40,512]{2,1,0:T(8,128)S(1)}, bf16[16,40,512]{2,1,0:T(8,128)(2,1)S(1)}) custom-call(s32[1]{0:T(128)} %bitcast.10.refs_0_.self_id, f32[1]{0:T(128)} %bitcast.53.loss, bf16[1024,512]{1,0:T(8,128)(2,1)} %collective-permute-done.50.before, bf16[1024,512]{1,0:T(8,128)(2,1)} %get-tuple-element.438.middle, ...), custom_call_target="tpu_custom_call" | custom-call | flops 1610612736 | bytes 12582912 | tf_op jit(solution)/shard_map/tail_layer/pallas_call | solution.py:686
  507.5 6.3 %collective-permute-done.63 = bf16[4,96,512]{2,1,0:T(8,128)(2,1)S(1)} collective-permute-done((bf16[4,96,512]{2,1,0:T(8,128)(2,1)S(1)}, bf16[4,96,512]{2,1,0:T(8,128)(2,1)S(1)}, u32[]{:S(2)}, u32[]{:S(2)}) %collective-permute-start.63) | collective-permute-done | bytes 393248 | tf_op jit(solution)/shard_map/ppermute | solution.py:743
  513.8 8.2 %collective-permute-done.64 = bf16[4,96,512]{2,1,0:T(8,128)(2,1)S(1)} collective-permute-done((bf16[4,96,512]{2,1,0:T(8,128)(2,1)S(1)}, bf16[4,96,512]{2,1,0:T(8,128)(2,1)S(1)}, u32[]{:S(2)}, u32[]{:S(2)}) %collective-permute-start.64) | collective-permute-done | bytes 393248 | tf_op jit(solution)/shard_map/ppermute | solution.py:743
  530.7 6.4 %collective-permute-done.58 = bf16[4,40,512]{2,1,0:T(8,128)(2,1)S(1)} collective-permute-done((bf16[4,40,512]{2,1,0:T(8,128)(2,1)S(1)}, bf16[4,40,512]{2,1,0:T(8,128)(2,1)S(1)}, u32[]{:S(2)}, u32[]{:S(2)}) %collective-permute-start.58) | collective-permute-done | bytes 163872 | tf_op jit(solution)/shard_map/ppermute | solution.py:743
  (331 shorter events, 127.9 us)
Async XLA Ops:
  7.2 193.7 %all-gather.2.cloned.1.call-start = ((), (), s32[]{:S(2)}) async-start(), calls=%async_computation | async-start | bytes 6488064 | tf_op jit(solution)/shard_map/all_gather | solution.py:867
  17.4 25.2 %collective-permute-start.6 = (bf16[1024,512]{1,0:T(8,128)(2,1)S(1)}, bf16[1024,512]{1,0:T(8,128)(2,1)S(1)}, u32[]{:S(2)}, u32[]{:S(2)}) collective-permute-start(bf16[1024,512]{1,0:T(8,128)(2,1)S(1)} %copy-done.63), channel_id=1, source_target_pairs={{0,0},{1,1},{2,2},{3,3},{4,6},{5,7},{6,4},{7,5},{8,8},{9,9},{10,10... | collective-permute-start | bytes 3145736 | tf_op jit(solution)/shard_map/ppermute | solution.py:755
  20.1 22.4 %collective-permute-start.4 = (bf16[2,136,512]{2,1,0:T(8,128)(2,1)S(1)}, bf16[2,136,512]{2,1,0:T(8,128)(2,1)S(1)}, u32[]{:S(2)}, u32[]{:S(2)}) collective-permute-start(bf16[2,136,512]{2,1,0:T(8,128)(2,1)S(1)} %pad_maximum_fusion.refs_0_), channel_id=1, source_target_pairs={{0,16},{1,17},{2,18},{3,19},{4,20},{5,21},{6,22},{7,23},{8,24},{9,... | collective-permute-start | bytes 835592 | tf_op jit(solution)/shard_map/ppermute | solution.py:743
  22.7 19.8 %collective-permute-start.5 = (bf16[2,136,512]{2,1,0:T(8,128)(2,1)S(1)}, bf16[2,136,512]{2,1,0:T(8,128)(2,1)S(1)}, u32[]{:S(2)}, u32[]{:S(2)}) collective-permute-start(bf16[2,136,512]{2,1,0:T(8,128)(2,1)S(1)} %pad_maximum_fusion.refs_0_), channel_id=1, source_target_pairs={{0,24},{1,25},{2,26},{3,27},{4,28},{5,29},{6,30},{7,31},{8,16},{9,... | collective-permute-start | bytes 835592 | tf_op jit(solution)/shard_map/ppermute | solution.py:743
  42.7 47.8 %collective-permute-start.7 = (bf16[8,136,512]{2,1,0:T(8,128)(2,1)S(1)}, bf16[8,136,512]{2,1,0:T(8,128)(2,1)}, u32[]{:S(2)}, u32[]{:S(2)}) collective-permute-start(bf16[8,136,512]{2,1,0:T(8,128)(2,1)S(1)} %join.2.refs_1_), channel_id=1, source_target_pairs={{0,4},{1,5},{2,6},{3,7},{4,0},{5,1},{6,2},{7,3},{8,12},{9,13},{10,... | collective-permute-start | bytes 3342344 | tf_op jit(solution)/shard_map/ppermute | solution.py:743
  47.9 42.6 %collective-permute-start.10 = (bf16[1024,512]{1,0:T(8,128)(2,1)}, bf16[1024,512]{1,0:T(8,128)(2,1)}, u32[]{:S(2)}, u32[]{:S(2)}) collective-permute-start(bf16[1024,512]{1,0:T(8,128)(2,1)} %pad.26), channel_id=1, source_target_pairs={{0,29},{1,0},{2,1},{3,2},{4,3},{5,6},{6,7},{7,4},{8,5},{9,8},{10,9... | collective-permute-start | bytes 3145736 | tf_op jit(solution)/shard_map/ppermute | solution.py:755
  48.0 42.5 %collective-permute-start.8 = (bf16[1024,512]{1,0:T(8,128)(2,1)}, bf16[1024,512]{1,0:T(8,128)(2,1)}, u32[]{:S(2)}, u32[]{:S(2)}) collective-permute-start(bf16[1024,512]{1,0:T(8,128)(2,1)} %pad.26), channel_id=1, source_target_pairs={{0,1},{1,2},{2,3},{3,6},{4,7},{5,4},{6,5},{7,8},{8,9},{9,10},{10,1... | collective-permute-start | bytes 3145736 | tf_op jit(solution)/shard_map/ppermute | solution.py:755
  48.4 42.0 %collective-permute-start.9 = (bf16[1024,512]{1,0:T(8,128)(2,1)}, bf16[1024,512]{1,0:T(8,128)(2,1)S(1)}, u32[]{:S(2)}, u32[]{:S(2)}) collective-permute-start(bf16[1024,512]{1,0:T(8,128)(2,1)} %pad.26), channel_id=1, source_target_pairs={{0,0},{1,1},{2,2},{3,3},{4,6},{5,7},{6,4},{7,5},{8,8},{9,9},{10,10... | collective-permute-start | bytes 3145736 | tf_op jit(solution)/shard_map/ppermute | solution.py:755
  50.3 20.9 %collective-permute-start.11 = (bf16[2,96,512]{2,1,0:T(8,128)(2,1)S(1)}, bf16[2,96,512]{2,1,0:T(8,128)(2,1)S(1)}, u32[]{:S(2)}, u32[]{:S(2)}) collective-permute-start(bf16[2,96,512]{2,1,0:T(8,128)(2,1)S(1)} %pad_maximum_fusion.1.refs_0_), channel_id=1, source_target_pairs={{0,8},{1,9},{2,10},{3,11},{4,12},{5,13},{6,14},{7,15},{8,0},{9,1},... | collective-permute-start | bytes 589832 | tf_op jit(solution)/shard_map/ppermute | solution.py:743
  90.5 19.7 %collective-permute-start.14 = (bf16[8,136,512]{2,1,0:T(8,128)(2,1)S(1)}, bf16[8,136,512]{2,1,0:T(8,128)(2,1)}, u32[]{:S(2)}, u32[]{:S(2)}) collective-permute-start(bf16[8,136,512]{2,1,0:T(8,128)(2,1)S(1)} %join.2.refs_1_), channel_id=1, source_target_pairs={{0,1},{1,0},{2,3},{3,2},{4,5},{5,4},{6,7},{7,6},{8,9},{9,8},{10,11... | collective-permute-start | bytes 3342344 | tf_op jit(solution)/shard_map/ppermute | solution.py:743
  90.6 19.6 %collective-permute-start.15 = (bf16[8,136,512]{2,1,0:T(8,128)(2,1)}, bf16[8,136,512]{2,1,0:T(8,128)(2,1)}, u32[]{:S(2)}, u32[]{:S(2)}) collective-permute-start(bf16[8,136,512]{2,1,0:T(8,128)(2,1)} %collective-permute-done.7.refs_2_), channel_id=1, source_target_pairs={{0,1},{1,0},{2,3},{3,2},{4,5},{5,4},{6,7},{7,6},{8,9},{9,8},{10,11... | collective-permute-start | bytes 3342344 | tf_op jit(solution)/shard_map/ppermute | solution.py:743
  93.3 51.7 %collective-permute-start.19 = (bf16[8,96,512]{2,1,0:T(8,128)(2,1)S(1)}, bf16[8,96,512]{2,1,0:T(8,128)(2,1)}, u32[]{:S(2)}, u32[]{:S(2)}) collective-permute-start(bf16[8,96,512]{2,1,0:T(8,128)(2,1)S(1)} %join.3.refs_1_), channel_id=1, source_target_pairs={{0,4},{1,5},{2,6},{3,7},{4,0},{5,1},{6,2},{7,3},{8,12},{9,13},{10,... | collective-permute-start | bytes 2359304 | tf_op jit(solution)/shard_map/ppermute | solution.py:743
  140.6 23.3 %collective-permute-start.17 = (bf16[1024,512]{1,0:T(8,128)(2,1)}, bf16[1024,512]{1,0:T(8,128)(2,1)}, u32[]{:S(2)}, u32[]{:S(2)}) collective-permute-start(bf16[1024,512]{1,0:T(8,128)(2,1)} %get-tuple-element.272.refs_2_), channel_id=1, source_target_pairs={{0,1},{1,2},{2,3},{3,6},{6,7},{7,4},{4,5},{5,8},{8,9},{9,10},{10,1... | collective-permute-start | bytes 3145736 | tf_op jit(solution)/shard_map/ppermute | solution.py:760
  140.6 24.4 %collective-permute-start.18 = (bf16[1024,512]{1,0:T(8,128)(2,1)}, bf16[1024,512]{1,0:T(8,128)(2,1)}, u32[]{:S(2)}, u32[]{:S(2)}) collective-permute-start(bf16[1024,512]{1,0:T(8,128)(2,1)} %get-tuple-element.272.refs_2_), channel_id=1, source_target_pairs={{0,29},{1,0},{2,1},{3,2},{6,3},{7,6},{4,7},{5,4},{8,5},{9,8},{10,9... | collective-permute-start | bytes 3145736 | tf_op jit(solution)/shard_map/ppermute | solution.py:760
  189.1 35.2 %collective-permute-start.16 = (f32[1024,256]{0,1:T(8,128)S(1)}, f32[1024,256]{0,1:T(8,128)}, u32[]{:S(2)}, u32[]{:S(2)}) collective-permute-start(f32[1024,256]{0,1:T(8,128)S(1)} %copy-done.24), channel_id=1, source_target_pairs={{0,0},{1,1},{2,2},{3,3},{4,6},{5,7},{6,4},{7,5},{8,8},{9,9},{10,10... | collective-permute-start | bytes 3145736 | tf_op jit(solution)/shard_map/ppermute | solution.py:755
  317.6 35.6 %collective-permute-start.29 = (bf16[4,96,512]{2,1,0:T(8,128)(2,1)S(1)}, bf16[4,96,512]{2,1,0:T(8,128)(2,1)S(1)}, u32[]{:S(2)}, u32[]{:S(2)}) collective-permute-start(bf16[4,96,512]{2,1,0:T(8,128)(2,1)S(1)} %get-tuple-element.311), channel_id=1, source_target_pairs={{0,2},{1,3},{2,0},{3,1},{4,6},{5,7},{6,4},{7,5},{8,10},{9,11},{10,... | collective-permute-start | bytes 1179656 | tf_op jit(solution)/shard_map/ppermute | solution.py:743
  319.4 33.8 %collective-permute-start.30 = (bf16[4,96,512]{2,1,0:T(8,128)(2,1)S(1)}, bf16[4,96,512]{2,1,0:T(8,128)(2,1)S(1)}, u32[]{:S(2)}, u32[]{:S(2)}) collective-permute-start(bf16[4,96,512]{2,1,0:T(8,128)(2,1)S(1)} %get-tuple-element.312), channel_id=1, source_target_pairs={{0,4},{1,5},{2,6},{3,7},{4,0},{5,1},{6,2},{7,3},{8,12},{9,13},{10,... | collective-permute-start | bytes 1179656 | tf_op jit(solution)/shard_map/ppermute | solution.py:743
  321.1 32.1 %collective-permute-start.31 = (bf16[4,96,512]{2,1,0:T(8,128)(2,1)S(1)}, bf16[4,96,512]{2,1,0:T(8,128)(2,1)S(1)}, u32[]{:S(2)}, u32[]{:S(2)}) collective-permute-start(bf16[4,96,512]{2,1,0:T(8,128)(2,1)S(1)} %get-tuple-element.313), channel_id=1, source_target_pairs={{0,6},{1,7},{2,4},{3,5},{4,2},{5,3},{6,0},{7,1},{8,14},{9,15},{10,... | collective-permute-start | bytes 1179656 | tf_op jit(solution)/shard_map/ppermute | solution.py:743
  371.9 38.7 %collective-permute-start.39 = (bf16[1,96,512]{2,1,0:T(8,128)(2,1)S(1)}, bf16[1,96,512]{2,1,0:T(8,128)(2,1)S(1)}, u32[]{:S(2)}, u32[]{:S(2)}) collective-permute-start(bf16[1,96,512]{2,1,0:T(8,128)(2,1)S(1)} %get-tuple-element.357), channel_id=1, source_target_pairs={{0,16},{1,17},{2,18},{3,19},{4,20},{5,21},{6,22},{7,23},{8,24},{9,... | collective-permute-start | bytes 294920 | tf_op jit(solution)/shard_map/ppermute | solution.py:743
  371.9 38.7 %collective-permute-start.40 = (bf16[1,96,512]{2,1,0:T(8,128)(2,1)S(1)}, bf16[1,96,512]{2,1,0:T(8,128)(2,1)S(1)}, u32[]{:S(2)}, u32[]{:S(2)}) collective-permute-start(bf16[1,96,512]{2,1,0:T(8,128)(2,1)S(1)} %get-tuple-element.358), channel_id=1, source_target_pairs={{0,24},{1,25},{2,26},{3,27},{4,28},{5,29},{6,30},{7,31},{8,16},{9,... | collective-permute-start | bytes 294920 | tf_op jit(solution)/shard_map/ppermute | solution.py:743
  375.4 35.2 %collective-permute-start.35 = (bf16[4,96,512]{2,1,0:T(8,128)(2,1)S(1)}, bf16[4,96,512]{2,1,0:T(8,128)(2,1)S(1)}, u32[]{:S(2)}, u32[]{:S(2)}) collective-permute-start(bf16[4,96,512]{2,1,0:T(8,128)(2,1)S(1)} %get-tuple-element.352), channel_id=1, source_target_pairs={{0,2},{1,3},{2,0},{3,1},{4,6},{5,7},{6,4},{7,5},{8,10},{9,11},{10,... | collective-permute-start | bytes 1179656 | tf_op jit(solution)/shard_map/ppermute | solution.py:743
  376.4 34.2 %collective-permute-start.36 = (bf16[4,96,512]{2,1,0:T(8,128)(2,1)S(1)}, bf16[4,96,512]{2,1,0:T(8,128)(2,1)S(1)}, u32[]{:S(2)}, u32[]{:S(2)}) collective-permute-start(bf16[4,96,512]{2,1,0:T(8,128)(2,1)S(1)} %get-tuple-element.353), channel_id=1, source_target_pairs={{0,4},{1,5},{2,6},{3,7},{4,0},{5,1},{6,2},{7,3},{8,12},{9,13},{10,... | collective-permute-start | bytes 1179656 | tf_op jit(solution)/shard_map/ppermute | solution.py:743
  377.5 33.2 %collective-permute-start.37 = (bf16[4,96,512]{2,1,0:T(8,128)(2,1)S(1)}, bf16[4,96,512]{2,1,0:T(8,128)(2,1)S(1)}, u32[]{:S(2)}, u32[]{:S(2)}) collective-permute-start(bf16[4,96,512]{2,1,0:T(8,128)(2,1)S(1)} %get-tuple-element.354), channel_id=1, source_target_pairs={{0,6},{1,7},{2,4},{3,5},{4,2},{5,3},{6,0},{7,1},{8,14},{9,15},{10,... | collective-permute-start | bytes 1179656 | tf_op jit(solution)/shard_map/ppermute | solution.py:743
  410.7 17.4 %collective-permute-start.42 = (bf16[1024,512]{1,0:T(8,128)(2,1)}, bf16[1024,512]{1,0:T(8,128)(2,1)S(1)}, u32[]{:S(2)}, u32[]{:S(2)}) collective-permute-start(bf16[1024,512]{1,0:T(8,128)(2,1)} %get-tuple-element.369), channel_id=1, source_target_pairs={{0,29},{1,0},{2,1},{3,2},{6,3},{7,6},{4,7},{5,4},{8,5},{9,8},{10,9... | collective-permute-start | bytes 3145736 | tf_op jit(solution)/shard_map/ppermute | solution.py:760
  428.2 40.2 %collective-permute-start.48 = (bf16[1,96,512]{2,1,0:T(8,128)(2,1)S(1)}, bf16[1,96,512]{2,1,0:T(8,128)(2,1)S(1)}, u32[]{:S(2)}, u32[]{:S(2)}) collective-permute-start(bf16[1,96,512]{2,1,0:T(8,128)(2,1)S(1)} %get-tuple-element.402), channel_id=1, source_target_pairs={{0,16},{1,17},{2,18},{3,19},{4,20},{5,21},{6,22},{7,23},{8,24},{9,... | collective-permute-start | bytes 294920 | tf_op jit(solution)/shard_map/ppermute | solution.py:743
  430.9 37.5 %collective-permute-start.49 = (bf16[1,96,512]{2,1,0:T(8,128)(2,1)S(1)}, bf16[1,96,512]{2,1,0:T(8,128)(2,1)S(1)}, u32[]{:S(2)}, u32[]{:S(2)}) collective-permute-start(bf16[1,96,512]{2,1,0:T(8,128)(2,1)S(1)} %get-tuple-element.403), channel_id=1, source_target_pairs={{0,24},{1,25},{2,26},{3,27},{4,28},{5,29},{6,30},{7,31},{8,16},{9,... | collective-permute-start | bytes 294920 | tf_op jit(solution)/shard_map/ppermute | solution.py:743
  432.9 35.5 %collective-permute-start.44 = (bf16[4,96,512]{2,1,0:T(8,128)(2,1)S(1)}, bf16[4,96,512]{2,1,0:T(8,128)(2,1)S(1)}, u32[]{:S(2)}, u32[]{:S(2)}) collective-permute-start(bf16[4,96,512]{2,1,0:T(8,128)(2,1)S(1)} %get-tuple-element.397), channel_id=1, source_target_pairs={{0,2},{1,3},{2,0},{3,1},{4,6},{5,7},{6,4},{7,5},{8,10},{9,11},{10,... | collective-permute-start | bytes 1179656 | tf_op jit(solution)/shard_map/ppermute | solution.py:743
  433.0 35.5 %collective-permute-start.45 = (bf16[4,96,512]{2,1,0:T(8,128)(2,1)S(1)}, bf16[4,96,512]{2,1,0:T(8,128)(2,1)S(1)}, u32[]{:S(2)}, u32[]{:S(2)}) collective-permute-start(bf16[4,96,512]{2,1,0:T(8,128)(2,1)S(1)} %get-tuple-element.398), channel_id=1, source_target_pairs={{0,4},{1,5},{2,6},{3,7},{4,0},{5,1},{6,2},{7,3},{8,12},{9,13},{10,... | collective-permute-start | bytes 1179656 | tf_op jit(solution)/shard_map/ppermute | solution.py:743
  434.7 33.7 %collective-permute-start.46 = (bf16[4,96,512]{2,1,0:T(8,128)(2,1)S(1)}, bf16[4,96,512]{2,1,0:T(8,128)(2,1)S(1)}, u32[]{:S(2)}, u32[]{:S(2)}) collective-permute-start(bf16[4,96,512]{2,1,0:T(8,128)(2,1)S(1)} %get-tuple-element.399), channel_id=1, source_target_pairs={{0,6},{1,7},{2,4},{3,5},{4,2},{5,3},{6,0},{7,1},{8,14},{9,15},{10,... | collective-permute-start | bytes 1179656 | tf_op jit(solution)/shard_map/ppermute | solution.py:743
  502.0 20.0 %collective-permute-start.64 = (bf16[4,96,512]{2,1,0:T(8,128)(2,1)S(1)}, bf16[4,96,512]{2,1,0:T(8,128)(2,1)S(1)}, u32[]{:S(2)}, u32[]{:S(2)}) collective-permute-start(bf16[4,96,512]{2,1,0:T(8,128)(2,1)S(1)} %get-tuple-element.461), channel_id=1, source_target_pairs={{0,4},{1,5},{2,6},{3,7},{4,0},{5,1},{6,2},{7,3},{8,12},{9,13},{10,... | collective-permute-start | bytes 1179656 | tf_op jit(solution)/shard_map/ppermute | solution.py:743
  504.6 19.7 %collective-permute-start.65 = (bf16[4,96,512]{2,1,0:T(8,128)(2,1)S(1)}, bf16[4,96,512]{2,1,0:T(8,128)(2,1)S(1)}, u32[]{:S(2)}, u32[]{:S(2)}) collective-permute-start(bf16[4,96,512]{2,1,0:T(8,128)(2,1)S(1)} %get-tuple-element.462), channel_id=1, source_target_pairs={{0,6},{1,7},{2,4},{3,5},{4,2},{5,3},{6,0},{7,1},{8,14},{9,15},{10,... | collective-permute-start | bytes 1179656 | tf_op jit(solution)/shard_map/ppermute | solution.py:743
  506.8 22.3 %collective-permute-start.57 = (bf16[4,40,512]{2,1,0:T(8,128)(2,1)S(1)}, bf16[4,40,512]{2,1,0:T(8,128)(2,1)S(1)}, u32[]{:S(2)}, u32[]{:S(2)}) collective-permute-start(bf16[4,40,512]{2,1,0:T(8,128)(2,1)S(1)} %get-tuple-element.450), channel_id=1, source_target_pairs={{0,2},{1,3},{2,0},{3,1},{4,6},{5,7},{6,4},{7,5},{8,10},{9,11},{10,... | collective-permute-start | bytes 491528 | tf_op jit(solution)/shard_map/ppermute | solution.py:743
  (102 other events, 1189.9 us)
Sparse Core Ops, SparseCore 0:
  90.7 91.4 all-gather.1

commit v10 on v9

--- a/solution.py
+++ b/solution.py
@@ -708,32 +708,41 @@
     )
 
 
-def combine_kernel(count, *refs):
-    arrived, outs = refs[:count], refs[count:]
-    for digit, out in enumerate(outs):
-        total = arrived[0][0, digit].astype(WIDE)
-        for part in arrived[1:]:
-            total = total + part[0, digit].astype(WIDE)
-        out[0] = total.astype(out.dtype)
-
-
-def combine(arrived, radix):
-    _, rows, width = arrived[0].shape
-    rest = arrived[0].shape[0] // radix
-    arrived = [part.reshape(rest, radix, rows, width) for part in arrived]
-    spec = pl.BlockSpec((1, radix, rows, width), lambda step: (step, 0, 0, 0))
+def combine_kernel(counts, *refs):
+    outs = refs[sum(counts) :]
+    first, base = 0, 0
+    for count in counts:
+        arrived = refs[first : first + count]
+        rows = arrived[0].shape[2]
+        for digit, out in enumerate(outs):
+            total = arrived[0][0, digit].astype(WIDE)
+            for part in arrived[1:]:
+                total = total + part[0, digit].astype(WIDE)
+            out[0, base : base + rows, :] = total.astype(out.dtype)
+        first, base = first + count, base + rows
+
+
+def combine(radix, *groups):
+    width = groups[0][0].shape[2]
+    rest = groups[0][0].shape[0] // radix
+    arrived, specs = [], []
+    for group in groups:
+        rows = group[0].shape[1]
+        arrived += [part.reshape(rest, radix, rows, width) for part in group]
+        specs += [pl.BlockSpec((1, radix, rows, width), lambda step: (step, 0, 0, 0))] * len(group)
+    rows = sum(group[0].shape[1] for group in groups)
     shape = (rest, rows, width)
     return pl.pallas_call(
-        functools.partial(combine_kernel, len(arrived)),
+        functools.partial(combine_kernel, [len(group) for group in groups]),
         grid=(rest,),
-        in_specs=[spec] * len(arrived),
+        in_specs=specs,
         out_specs=[pl.BlockSpec((1, rows, width), lambda step: (step, 0, 0))] * radix,
         out_shape=[on_chip(shape, WIDE)] + [on_chip(shape, SEND)] * (radix - 1),
         compiler_params=pltpu.CompilerParams(vmem_limit_bytes=20 << 20),
         cost_estimate=pl.CostEstimate(
-            flops=rest * radix * rows * width * len(arrived),
+            flops=rest * radix * rows * width * 4,
             transcendentals=0,
-            bytes_accessed=4 * rest * radix * rows * width * (len(arrived) + 1),
+            bytes_accessed=16 * rest * radix * rows * width,
         ),
         name="combine",
     )(*map(kept_on_chip, arrived))
@@ -852,17 +861,19 @@
         pairs = ((packed, swap(packed, device_count, 2)), (second, swap(second, device_count, 2)))
         lists = bring(lists, device_count, 0, direct)
         pairs, lists, inputs, mesh_static = barrier((pairs, lists, inputs, mesh_static))
+        own = bring(inputs, device_count, 0, direct)
+        pair, second_pair = (jnp.stack(rows) for rows in pairs)
+        column, own, mesh_static, second_pair = barrier(
+            (spread_high(pair, device_count), own, mesh_static, second_pair)
+        )
+        sides = [shift(own, device_count, 1, direct), shift(own, device_count, -1, direct)]
         mesh_rows = bring(mesh_static, device_count, 0, direct)
-        pair, second_pair = (jnp.stack(rows) for rows in pairs)
-        column, mesh_rows, inputs, second_pair = barrier(
-            (spread_high(pair, device_count), mesh_rows, inputs, second_pair)
-        )
-        sides = [bring(inputs, device_count, step, direct) for step in (1, 0, -1)]
         second_column = spread_high(second_pair, device_count)
         plane = join(column)
-        near, sides, second_column, rest, goals = barrier(
-            ((plane, swap(plane, device_count, 4)), sides, second_column, rest, goals)
-        )
+        near, sides, mesh_rows, second_column, rest, goals = barrier(
+            ((plane, swap(plane, device_count, 4)), sides, mesh_rows, second_column, rest, goals)
+        )
+        sides = [sides[0], own, sides[1]]
         pieces = [*near, *(swap(piece, device_count, 1) for piece in near)]
         rest = lax.all_gather(rest, AXES, axis=1, tiled=True)
         inputs = sides[1]
@@ -957,7 +968,7 @@
             arrived, slot_grads = together(in_plane + in_slice, slot_grads)
             if in_slice:
                 layer_grads[layer_id + 2] = add_up(arrived[moved:]).reshape(6, share, width)
-            far = list(combine(arrived[:moved], device_count // 8))
+            far = list(combine(device_count // 8, arrived[:moved]))
         from_before = shift(slot_grads[2], device_count, 1, direct)
         from_after = shift(slot_grads[0], device_count, -1, direct)
         back = [edge_hidden, grad_message, b0, b1, b2, b3]
@@ -974,14 +985,15 @@
         )
         gain_grads[layer_id] = grad_gain
         if direct:
-            halo, arrived = together([from_before, from_after], [*sums, *far])
-            keep, send, far = arrived[0], arrived[1], arrived[2:]
+            tied = [*sums, *far] if layer_id > 0 else sums
+            halo, arrived = together([from_before, from_after], tied)
+            keep, send = arrived[:2]
+            far = arrived[2:] if layer_id > 0 else far
             in_slice = fan_out(far, device_count, 8) if far else []
             other = swap(send, device_count, 1)
-            if layer_id > 0:
-                near = list(combine([keep, other], 4))
-                halo, near = together(halo, near)
-                in_plane = fan_out(near, device_count, 2)
+            near = list(combine(4, [keep, other]))
+            halo, near = together(halo, near)
+            in_plane = fan_out(near, device_count, 2)
             from_before, from_after = halo
         else:
             layer_grads[layer_id] = sums[0]
@@ -1003,16 +1015,16 @@
             heads[0],
             gain_grads,
         )
-        arrived, sums = together([other] + in_slice, sums)
-        other, in_slice = arrived[0], arrived[1:]
-        near = combine([keep, other], 4)
+        early, sums = together(in_plane[1:3], sums)
+        in_plane = [in_plane[0], *early, in_plane[3]]
+        keep, send = sums
+        last_plane = combine(4, [keep, swap(send, device_count, 1)])
+        last_plane, in_slice = together(fan_out(last_plane, device_count, 2), in_slice)
         layer_grads[1] = add_up(in_slice).reshape(6, share, width)
-        far = combine(fan_out(near, device_count, 2), device_count // 8)
-        layer_grads[0] = add_up(fan_out(far, device_count, 8)).reshape(6, share, width)
-        keep, send = sums
-        pieces = combine([keep, swap(send, device_count, 1)], 4)
-        pieces = combine(fan_out(pieces, device_count, 2), device_count // 8)
-        total = add_up(fan_out(pieces, device_count, 8))
+        far = combine(device_count // 8, in_plane, last_plane)
+        total = add_up(fan_out(far, device_count, 8))
+        layer_grads[0] = total[: 6 * share].reshape(6, share, width)
+        total = total[6 * share :]
         grad_zero = total[:share]
         grad_in = total[share : 2 * share, :channels].T
         grad_gain_all = total[2 * share :, :share].reshape(layer_total, 2, share)

time: 566 us -> 548 us (0.968)
  waiting for transfers between devices: 127 us -> 114 us
    ppermute x49 -> x46, waiting for transfers between devices: 88.8 us -> 68.1 us  [swap(): return lax.ppermute(cells, AXES, [(i, i ^ mask) for i in range(count)])]
    ppermute x49 -> x46, starting transfers between devices: 82.6 us -> 65.1 us  [swap(): return lax.ppermute(cells, AXES, [(i, i ^ mask) for i in range(count)])]
    ppermute x6 -> x4, starting transfers between devices: 5.81 us -> 13.6 us  [bring(): lax.ppermute(cells, AXES, [(i, home((i + step) % count, direct)) for i in...]
    ppermute x14 -> x16, waiting for transfers between devices: 38 us -> 45.5 us  [shift(): return lax.ppermute(cells, AXES, pairs)]
    ppermute x14 -> x16, starting transfers between devices: 32.6 us -> 37.3 us  [shift(): return lax.ppermute(cells, AXES, pairs)]
  transfers between devices with their start and end apart: 70 -> 67, of which waited for: 27 -> 28; matrix products, arithmetic and copies ran while one was open for 2% -> 3% of each run, Pallas kernels for 39% -> 40%
where the time goes in v10:
time: 548 us; the launch traced here: 539 us
  Pallas kernels  262 us (48%)
  starting transfers between devices  116 us (21%)
  waiting for transfers between devices  114 us (21%)
  between operations  17.4 us (3%)
  other arithmetic  12 us (2%)
  local copies, waits for them, and re-layouts  11.3 us (2%)
  matrix products  6.05 us (1%)
    pallas_call x4, Pallas kernels, backward_layer(): pl.pallas_call(functools.partial(backward_kernel, parts, mode), grid=(blo...  125 us
    pallas_call x4, Pallas kernels, forward_layer(): pl.pallas_call(functools.partial(forward_kernel, parts, has_next), grid=(...  72.1 us
    ppermute x46, waiting for transfers between devices, swap(): return lax.ppermute(cells, AXES, [(i, i ^ mask) for i in range(count)])  68.1 us
    ppermute x46, starting transfers between devices, swap(): return lax.ppermute(cells, AXES, [(i, i ^ mask) for i in range(count)])  65.1 us
    ppermute x16, waiting for transfers between devices, shift(): return lax.ppermute(cells, AXES, pairs)  45.5 us
    pallas_call x4, Pallas kernels, weight_layer(): pl.pallas_call(functools.partial(weight_kernel, above is not None, grad_n...  41.5 us
    ppermute x16, starting transfers between devices, shift(): return lax.ppermute(cells, AXES, pairs)  37.3 us
    ppermute x4, starting transfers between devices, bring(): lax.ppermute(cells, AXES, [(i, home((i + step) % count, direct)) for i in...  13.6 us
  transfers between devices with their start and end apart: 67, of which 28 were waited for; matrix products, arithmetic and copies ran while one was open for 3% of the time, Pallas kernels for 40%

profile of v10, /device:TPU:0, one launch (start us, length us, event | category | flops | bytes accessed | tf_op | source)
XLA Modules:
  0.0 539.0 jit_solution(16649213845541498500)
XLA Ops:
  24.4 6.6 %collective-permute-done.3.refs_1_ = bf16[2,136,512]{2,1,0:T(8,128)(2,1)S(1)} collective-permute-done((bf16[2,136,512]{2,1,0:T(8,128)(2,1)S(1)}, bf16[2,136,512]{2,1,0:T(8,128)(2,1)S(1)}, u32[]{:S(2)}, u32[]{:S(2)}) %collective-permute-start.3) | collective-permute-done | bytes 278560 | tf_op jit(solution)/shard_map/ppermute | solution.py:752
  31.0 12.2 %collective-permute-done.4.refs_2_ = bf16[2,136,512]{2,1,0:T(8,128)(2,1)S(1)} collective-permute-done((bf16[2,136,512]{2,1,0:T(8,128)(2,1)S(1)}, bf16[2,136,512]{2,1,0:T(8,128)(2,1)S(1)}, u32[]{:S(2)}, u32[]{:S(2)}) %collective-permute-start.4) | collective-permute-done | bytes 278560 | tf_op jit(solution)/shard_map/ppermute | solution.py:752
  43.3 6.6 %collective-permute-start.7 = (bf16[8,136,512]{2,1,0:T(8,128)(2,1)S(1)}, bf16[8,136,512]{2,1,0:T(8,128)(2,1)}, u32[]{:S(2)}, u32[]{:S(2)}) collective-permute-start(bf16[8,136,512]{2,1,0:T(8,128)(2,1)S(1)} %join.2.refs_1_), channel_id=1, source_target_pairs={{0,4},{1,5},{2,6},{3,7},{4,0},{5,1},{6,2},{7,3},{8,12},{9,13},{10,... | collective-permute-start | bytes 3342344 | tf_op jit(solution)/shard_map/ppermute | solution.py:752
  54.4 9.4 %collective-permute-start.10 = (bf16[1024,512]{1,0:T(8,128)(2,1)}, bf16[1024,512]{1,0:T(8,128)(2,1)}, u32[]{:S(2)}, u32[]{:S(2)}) collective-permute-start(bf16[1024,512]{1,0:T(8,128)(2,1)} %param.22), channel_id=1, source_target_pairs={{0,0},{1,1},{2,2},{3,3},{4,6},{5,7},{6,4},{7,5},{8,8},{9,9},{10,10... | collective-permute-start | bytes 3145736 | tf_op jit(solution)/shard_map/ppermute | solution.py:764
  66.2 6.9 %collective-permute-done.11.refs_1_ = bf16[2,96,512]{2,1,0:T(8,128)(2,1)S(1)} collective-permute-done((bf16[2,96,512]{2,1,0:T(8,128)(2,1)S(1)}, bf16[2,96,512]{2,1,0:T(8,128)(2,1)S(1)}, u32[]{:S(2)}, u32[]{:S(2)}) %collective-permute-start.11) | collective-permute-done | bytes 196640 | tf_op jit(solution)/shard_map/ppermute | solution.py:752
  73.3 8.6 %collective-permute-done.12.refs_2_ = bf16[2,96,512]{2,1,0:T(8,128)(2,1)S(1)} collective-permute-done((bf16[2,96,512]{2,1,0:T(8,128)(2,1)S(1)}, bf16[2,96,512]{2,1,0:T(8,128)(2,1)S(1)}, u32[]{:S(2)}, u32[]{:S(2)}) %collective-permute-start.12) | collective-permute-done | bytes 196640 | tf_op jit(solution)/shard_map/ppermute | solution.py:752
  97.1 9.4 %embed.1 = (bf16[7,512,512]{2,1,0:T(8,128)(2,1)}, f32[1024,512]{1,0:T(8,128)}, bf16[1024,512]{1,0:T(8,128)(2,1)}, bf16[1024,512]{1,0:T(8,128)(2,1)}, bf16[1024,5...) custom-call(s32[1]{0:T(128)} %bitcast.10.refs_0_.self_id, bf16[8,136,512]{2,1,0:T(8,128)(2,1)} %copy-done.1, ...), custom_call_target="tpu_custom_call" | custom-call | flops 3221225472 | bytes 12582912 | tf_op jit(solution)/shard_map/embed/pallas_call | solution.py:611
  107.3 18.6 %forward_layer.4 = (bf16[1024,512]{1,0:T(8,128)(2,1)}, f32[1024,512]{1,0:T(8,128)}, bf16[1024,512]{1,0:T(8,128)(2,1)}, bf16[4,1024,512]{2,1,0:T(8,128)(2,1)}, bf16[1024,512]{1,0:T(8,128)(2,1)}) custom-call(s32[4096]{0:T(1024)} %get-tuple-element.509.refs_0_, bf16[1024,512]{1,0:T(8,128)(2,1)} %get-tuple-element.270.refs_1_, ...), custom_call_target="tpu_custom_call" | custom-call | flops 4831838208 | bytes 25165824 | tf_op jit(solution)/shard_map/forward_layer/pallas_call | solution.py:186
  137.5 10.5 %collective-permute-done.17.refs_1_ = bf16[1024,512]{1,0:T(8,128)(2,1)} collective-permute-done((bf16[1024,512]{1,0:T(8,128)(2,1)}, bf16[1024,512]{1,0:T(8,128)(2,1)}, u32[]{:S(2)}, u32[]{:S(2)}) %collective-permute-start.17) | collective-permute-done | bytes 1048608 | tf_op jit(solution)/shard_map/ppermute | solution.py:769
  148.1 7.4 %collective-permute-done.18.refs_3_ = bf16[1024,512]{1,0:T(8,128)(2,1)} collective-permute-done((bf16[1024,512]{1,0:T(8,128)(2,1)}, bf16[1024,512]{1,0:T(8,128)(2,1)}, u32[]{:S(2)}, u32[]{:S(2)}) %collective-permute-start.18) | collective-permute-done | bytes 1048608 | tf_op jit(solution)/shard_map/ppermute | solution.py:769
  155.5 18.7 %forward_layer.5 = (bf16[1024,512]{1,0:T(8,128)(2,1)}, f32[1024,512]{1,0:T(8,128)}, bf16[1024,512]{1,0:T(8,128)(2,1)}, bf16[4,1024,512]{2,1,0:T(8,128)(2,1)}, bf16[1024,512]{1,0:T(8,128)(2,1)}) custom-call(s32[4096]{0:T(1024)} %get-tuple-element.510.refs_0_, bf16[1024,512]{1,0:T(8,128)(2,1)} %collective-permute-done.17.refs_1_, ...), custom_call_target="tpu_custom_call" | custom-call | flops 4831838208 | bytes 25165824 | tf_op jit(solution)/shard_map/forward_layer/pallas_call | solution.py:186
  174.2 4.8 collective-permute-start.23
  181.9 9.8 %collective-permute-done.22.refs_1_ = bf16[1024,512]{1,0:T(8,128)(2,1)S(1)} collective-permute-done((bf16[1024,512]{1,0:T(8,128)(2,1)}, bf16[1024,512]{1,0:T(8,128)(2,1)S(1)}, u32[]{:S(2)}, u32[]{:S(2)}) %collective-permute-start.22) | collective-permute-done | bytes 1048608 | tf_op jit(solution)/shard_map/ppermute | solution.py:769
  191.7 18.0 %forward_layer.6 = (bf16[1024,512]{1,0:T(8,128)(2,1)}, f32[1024,512]{1,0:T(8,128)}, bf16[1024,512]{1,0:T(8,128)(2,1)}, bf16[4,1024,512]{2,1,0:T(8,128)(2,1)}, bf16[1024,512]{1,0:T(8,128)(2,1)}) custom-call(s32[4096]{0:T(1024)} %get-tuple-element.510.refs_0_, bf16[1024,512]{1,0:T(8,128)(2,1)S(1)} %collective-permute-done.22.refs_1_, ...), custom_call_target="tpu_custom_call" | custom-call | flops 4831838208 | bytes 25165824 | tf_op jit(solution)/shard_map/forward_layer/pallas_call | solution.py:186
  215.9 11.1 %collective-permute-done.24.refs_1_ = bf16[1024,512]{1,0:T(8,128)(2,1)S(1)} collective-permute-done((bf16[1024,512]{1,0:T(8,128)(2,1)}, bf16[1024,512]{1,0:T(8,128)(2,1)S(1)}, u32[]{:S(2)}, u32[]{:S(2)}) %collective-permute-start.24) | collective-permute-done | bytes 1048608 | tf_op jit(solution)/shard_map/ppermute | solution.py:769
  227.0 16.8 %forward_layer.7 = (bf16[1024,512]{1,0:T(8,128)(2,1)}, bf16[4,1024,512]{2,1,0:T(8,128)(2,1)}, bf16[1024,512]{1,0:T(8,128)(2,1)}) custom-call(s32[4096]{0:T(1024)} %get-tuple-element.511.refs_0_, bf16[1024,512]{1,0:T(8,128)(2,1)S(1)} %collective-permute-done.24.refs_1_, bf16[1024,512]{1,0:T(8,128)(2,1)} %get-tuple-element.289.refs_2_, ...), custom_call_target="tpu_custom_call" | custom-call | flops 4831838208 | bytes 25165824 | tf_op jit(solution)/shard_map/forward_layer/pallas_call | solution.py:186
  249.3 29.8 %backward_layer.4 = (bf16[1024,512]{1,0:T(8,128)(2,1)}, bf16[1024,512]{1,0:T(8,128)(2,1)}, bf16[1024,512]{1,0:T(8,128)(2,1)}, f32[2,512]{1,0:T(2,128)S(1)}, bf16...) custom-call(s32[4096]{0:T(1024)S(1)} %copy-done.11, ...), custom_call_target="tpu_custom_call" | custom-call | flops 4294967296 | bytes 25165824 | tf_op jit(solution)/shard_map/backward_layer/pallas_call | solution.py:374
  279.2 4.7 collective-permute-start.27
  284.5 10.8 %weight_layer.4 = (f32[1024,512]{1,0:T(8,128)}, f32[16,96,512]{2,1,0:T(8,128)S(1)}, bf16[16,96,512]{2,1,0:T(8,128)(2,1)S(1)}) custom-call(s32[1]{0:T(128)} %bitcast.10.refs_0_.self_id, f32[512,512]{1,0:T(8,128)S(1)} %pad.29.refs_1_, bf16[1024,512]{1,0:T(8,128)(2,1)} %get-tuple-element.290.refs_4_.refs_2_.latent_low, ...), custom_call_target="tpu_custom_call" | custom-call | flops 5368709120 | bytes 12582912 | tf_op jit(solution)/shard_map/weight_layer/pallas_call | solution.py:504
  296.5 4.7 collective-permute-start.28
  308.1 31.9 %backward_layer.5 = (bf16[1024,512]{1,0:T(8,128)(2,1)S(1)}, f32[1024,512]{1,0:T(8,128)S(1)}, bf16[1024,512]{1,0:T(8,128)(2,1)}, bf16[1024,512]{1,0:T(8,128)(2,1)...) custom-call(s32[4096]{0:T(1024)S(1)} %copy-done.3, ...), custom_call_target="tpu_custom_call" | custom-call | flops 4294967296 | bytes 25165824 | tf_op jit(solution)/shard_map/backward_layer/pallas_call | solution.py:374
  340.2 4.6 collective-permute-start.33
  344.8 11.1 %weight_layer.5 = (f32[1024,512]{1,0:T(8,128)}, f32[16,96,512]{2,1,0:T(8,128)S(1)}, bf16[16,96,512]{2,1,0:T(8,128)(2,1)S(1)}) custom-call(s32[1]{0:T(128)} %bitcast.10.refs_0_.self_id, bf16[1024,512]{1,0:T(8,128)(2,1)} %get-tuple-element.327.refs_1_, bf16[1024,512]{1,0:T(8,128)(2,1)S(1)} %get-tuple-element.328.refs_2_, ...), custom_call_target="tpu_custom_call" | custom-call | flops 5368709120 | bytes 12582912 | tf_op jit(solution)/shard_map/weight_layer/pallas_call | solution.py:504
  365.7 31.6 %backward_layer.6 = (bf16[1024,512]{1,0:T(8,128)(2,1)S(1)}, f32[1024,512]{1,0:T(8,128)S(1)}, bf16[1024,512]{1,0:T(8,128)(2,1)}, bf16[1024,512]{1,0:T(8,128)(2,1)...) custom-call(s32[4096]{0:T(1024)S(1)} %copy-done.3, ...), custom_call_target="tpu_custom_call" | custom-call | flops 4294967296 | bytes 25165824 | tf_op jit(solution)/shard_map/backward_layer/pallas_call | solution.py:374
  397.5 4.8 collective-permute-start.42
  402.3 11.4 %weight_layer.6 = (f32[1024,512]{1,0:T(8,128)}, f32[16,96,512]{2,1,0:T(8,128)S(1)}, bf16[16,96,512]{2,1,0:T(8,128)(2,1)S(1)}) custom-call(s32[1]{0:T(128)} %bitcast.10.refs_0_.self_id, bf16[1024,512]{1,0:T(8,128)(2,1)} %get-tuple-element.286.refs_4_.refs_5_.refs_3_.refs_1_, bf16[1024,512]{1,0:T(8,128)(2,1)S(1)} %get-tuple-element.373.refs_2_, ...), custom_call_target="tpu_custom_call" | custom-call | flops 5368709120 | bytes 12582912 | tf_op jit(solution)/shard_map/weight_layer/pallas_call | solution.py:504
  423.2 31.9 %backward_layer.7 = (bf16[1024,512]{1,0:T(8,128)(2,1)S(1)}, f32[1024,512]{1,0:T(8,128)}, bf16[1024,512]{1,0:T(8,128)(2,1)}, bf16[1024,512]{1,0:T(8,128)(2,1)}, b...) custom-call(s32[4096]{0:T(1024)S(1)} %copy-done.10, ...), custom_call_target="tpu_custom_call" | custom-call | flops 4294967296 | bytes 25165824 | tf_op jit(solution)/shard_map/backward_layer/pallas_call | solution.py:374
  459.9 8.3 %weight_layer.7 = (f32[16,96,512]{2,1,0:T(8,128)S(1)}, bf16[16,96,512]{2,1,0:T(8,128)(2,1)S(1)}) custom-call(s32[1]{0:T(128)} %bitcast.10.refs_0_.self_id, bf16[1024,512]{1,0:T(8,128)(2,1)} %get-tuple-element.276.refs_4_.refs_6_.refs_3_.refs_1_, bf16[1024,512]{1,0:T(8,128)(2,1)S(1)} %get-tuple-element.418.refs_2_, ...), custom_call_target="tpu_custom_call" | custom-call | flops 5368709120 | bytes 12582912 | tf_op jit(solution)/shard_map/weight_layer/pallas_call | solution.py:504
  479.7 7.1 %tail_layer.1 = (f32[16,40,512]{2,1,0:T(8,128)S(1)}, bf16[16,40,512]{2,1,0:T(8,128)(2,1)S(1)}) custom-call(s32[1]{0:T(128)} %bitcast.10.refs_0_.self_id, f32[1]{0:T(128)} %bitcast.52.loss, bf16[1024,512]{1,0:T(8,128)(2,1)} %copy-done.25, bf16[1024,512]{1,0:T(8,128)(2,1)} %get-tuple-element.439.middle, bf16[1024,512]{1,0:T(8,128)(2,1)} %copy-done.26, ...), custom_call_target="tpu_custom_call" | custom-call | flops 1610612736 | bytes 12582912 | tf_op jit(solution)/shard_map/tail_layer/pallas_call | solution.py:686
  500.1 5.2 collective-permute-start.59
  505.5 6.1 %collective-permute-done.57 = bf16[4,40,512]{2,1,0:T(8,128)(2,1)S(1)} collective-permute-done((bf16[4,40,512]{2,1,0:T(8,128)(2,1)S(1)}, bf16[4,40,512]{2,1,0:T(8,128)(2,1)S(1)}, u32[]{:S(2)}, u32[]{:S(2)}) %collective-permute-start.57) | collective-permute-done | bytes 163872 | tf_op jit(solution)/shard_map/ppermute | solution.py:752
  521.1 6.7 %collective-permute-done.64 = bf16[1,136,512]{2,1,0:T(8,128)(2,1)S(1)} collective-permute-done((bf16[1,136,512]{2,1,0:T(8,128)(2,1)S(1)}, bf16[1,136,512]{2,1,0:T(8,128)(2,1)S(1)}, u32[]{:S(2)}, u32[]{:S(2)}) %collective-permute-start.64) | collective-permute-done | bytes 139296 | tf_op jit(solution)/shard_map/ppermute | solution.py:752
  (321 shorter events, 135.2 us)
Async XLA Ops:
  7.2 184.5 %all-gather.2.cloned.1.call-start = ((), (), s32[]{:S(2)}) async-start(), calls=%async_computation | async-start | bytes 6488064 | tf_op jit(solution)/shard_map/all_gather | solution.py:878
  18.2 25.0 %collective-permute-start.6 = (bf16[1024,512]{1,0:T(8,128)(2,1)S(1)}, bf16[1024,512]{1,0:T(8,128)(2,1)S(1)}, u32[]{:S(2)}, u32[]{:S(2)}) collective-permute-start(bf16[1024,512]{1,0:T(8,128)(2,1)S(1)} %pad.26), channel_id=1, source_target_pairs={{0,0},{1,1},{2,2},{3,3},{4,6},{5,7},{6,4},{7,5},{8,8},{9,9},{10,10... | collective-permute-start | bytes 3145736 | tf_op jit(solution)/shard_map/ppermute | solution.py:764
  20.8 22.4 %collective-permute-start.4 = (bf16[2,136,512]{2,1,0:T(8,128)(2,1)S(1)}, bf16[2,136,512]{2,1,0:T(8,128)(2,1)S(1)}, u32[]{:S(2)}, u32[]{:S(2)}) collective-permute-start(bf16[2,136,512]{2,1,0:T(8,128)(2,1)S(1)} %pad_maximum_fusion.refs_0_), channel_id=1, source_target_pairs={{0,16},{1,17},{2,18},{3,19},{4,20},{5,21},{6,22},{7,23},{8,24},{9,... | collective-permute-start | bytes 835592 | tf_op jit(solution)/shard_map/ppermute | solution.py:752
  23.3 19.8 %collective-permute-start.5 = (bf16[2,136,512]{2,1,0:T(8,128)(2,1)S(1)}, bf16[2,136,512]{2,1,0:T(8,128)(2,1)S(1)}, u32[]{:S(2)}, u32[]{:S(2)}) collective-permute-start(bf16[2,136,512]{2,1,0:T(8,128)(2,1)S(1)} %pad_maximum_fusion.refs_0_), channel_id=1, source_target_pairs={{0,24},{1,25},{2,26},{3,27},{4,28},{5,29},{6,30},{7,31},{8,16},{9,... | collective-permute-start | bytes 835592 | tf_op jit(solution)/shard_map/ppermute | solution.py:752
  43.3 47.4 %collective-permute-start.7 = (bf16[8,136,512]{2,1,0:T(8,128)(2,1)S(1)}, bf16[8,136,512]{2,1,0:T(8,128)(2,1)}, u32[]{:S(2)}, u32[]{:S(2)}) collective-permute-start(bf16[8,136,512]{2,1,0:T(8,128)(2,1)S(1)} %join.2.refs_1_), channel_id=1, source_target_pairs={{0,4},{1,5},{2,6},{3,7},{4,0},{5,1},{6,2},{7,3},{8,12},{9,13},{10,... | collective-permute-start | bytes 3342344 | tf_op jit(solution)/shard_map/ppermute | solution.py:752
  49.9 40.7 %collective-permute-start.8 = (bf16[1024,512]{1,0:T(8,128)(2,1)S(1)}, bf16[1024,512]{1,0:T(8,128)(2,1)}, u32[]{:S(2)}, u32[]{:S(2)}) collective-permute-start(bf16[1024,512]{1,0:T(8,128)(2,1)S(1)} %collective-permute-done.6.refs_6_.inputs), channel_id=1, source_target_pairs={{0,1},{1,2},{2,3},{3,6},{6,7},{7,4},{4,5},{5,8},{8,9},{9,10},{10,1... | collective-permute-start | bytes 3145736 | tf_op jit(solution)/shard_map/ppermute | solution.py:769
  49.9 40.7 %collective-permute-start.9 = (bf16[1024,512]{1,0:T(8,128)(2,1)S(1)}, bf16[1024,512]{1,0:T(8,128)(2,1)}, u32[]{:S(2)}, u32[]{:S(2)}) collective-permute-start(bf16[1024,512]{1,0:T(8,128)(2,1)S(1)} %collective-permute-done.6.refs_6_.inputs), channel_id=1, source_target_pairs={{0,29},{1,0},{2,1},{3,2},{6,3},{7,6},{4,7},{5,4},{8,5},{9,8},{10,9... | collective-permute-start | bytes 3145736 | tf_op jit(solution)/shard_map/ppermute | solution.py:769
  54.4 36.3 %collective-permute-start.10 = (bf16[1024,512]{1,0:T(8,128)(2,1)}, bf16[1024,512]{1,0:T(8,128)(2,1)}, u32[]{:S(2)}, u32[]{:S(2)}) collective-permute-start(bf16[1024,512]{1,0:T(8,128)(2,1)} %param.22), channel_id=1, source_target_pairs={{0,0},{1,1},{2,2},{3,3},{4,6},{5,7},{6,4},{7,5},{8,8},{9,9},{10,10... | collective-permute-start | bytes 3145736 | tf_op jit(solution)/shard_map/ppermute | solution.py:764
  93.5 36.9 %collective-permute-start.19 = (bf16[8,96,512]{2,1,0:T(8,128)(2,1)S(1)}, bf16[8,96,512]{2,1,0:T(8,128)(2,1)}, u32[]{:S(2)}, u32[]{:S(2)}) collective-permute-start(bf16[8,96,512]{2,1,0:T(8,128)(2,1)S(1)} %join.3.refs_1_), channel_id=1, source_target_pairs={{0,4},{1,5},{2,6},{3,7},{4,0},{5,1},{6,2},{7,3},{8,12},{9,13},{10,... | collective-permute-start | bytes 2359304 | tf_op jit(solution)/shard_map/ppermute | solution.py:752
  125.9 22.2 %collective-permute-start.17 = (bf16[1024,512]{1,0:T(8,128)(2,1)}, bf16[1024,512]{1,0:T(8,128)(2,1)}, u32[]{:S(2)}, u32[]{:S(2)}) collective-permute-start(bf16[1024,512]{1,0:T(8,128)(2,1)} %get-tuple-element.275.refs_2_), channel_id=1, source_target_pairs={{0,1},{1,2},{2,3},{3,6},{6,7},{7,4},{4,5},{5,8},{8,9},{9,10},{10,1... | collective-permute-start | bytes 3145736 | tf_op jit(solution)/shard_map/ppermute | solution.py:769
  126.0 29.5 %collective-permute-start.18 = (bf16[1024,512]{1,0:T(8,128)(2,1)}, bf16[1024,512]{1,0:T(8,128)(2,1)}, u32[]{:S(2)}, u32[]{:S(2)}) collective-permute-start(bf16[1024,512]{1,0:T(8,128)(2,1)} %get-tuple-element.275.refs_2_), channel_id=1, source_target_pairs={{0,29},{1,0},{2,1},{3,2},{6,3},{7,6},{4,7},{5,4},{8,5},{9,8},{10,9... | collective-permute-start | bytes 3145736 | tf_op jit(solution)/shard_map/ppermute | solution.py:769
  174.2 17.5 %collective-permute-start.22 = (bf16[1024,512]{1,0:T(8,128)(2,1)}, bf16[1024,512]{1,0:T(8,128)(2,1)S(1)}, u32[]{:S(2)}, u32[]{:S(2)}) collective-permute-start(bf16[1024,512]{1,0:T(8,128)(2,1)} %get-tuple-element.285.refs_2_), channel_id=1, source_target_pairs={{0,1},{1,2},{2,3},{3,6},{6,7},{7,4},{4,5},{5,8},{8,9},{9,10},{10,1... | collective-permute-start | bytes 3145736 | tf_op jit(solution)/shard_map/ppermute | solution.py:769
  174.2 17.5 %collective-permute-start.23 = (bf16[1024,512]{1,0:T(8,128)(2,1)}, bf16[1024,512]{1,0:T(8,128)(2,1)S(1)}, u32[]{:S(2)}, u32[]{:S(2)}) collective-permute-start(bf16[1024,512]{1,0:T(8,128)(2,1)} %get-tuple-element.285.refs_2_), channel_id=1, source_target_pairs={{0,29},{1,0},{2,1},{3,2},{6,3},{7,6},{4,7},{5,4},{8,5},{9,8},{10,9... | collective-permute-start | bytes 3145736 | tf_op jit(solution)/shard_map/ppermute | solution.py:769
  179.8 35.3 %collective-permute-start.16 = (f32[1024,256]{0,1:T(8,128)S(1)}, f32[1024,256]{0,1:T(8,128)}, u32[]{:S(2)}, u32[]{:S(2)}) collective-permute-start(f32[1024,256]{0,1:T(8,128)S(1)} %copy-done.24), channel_id=1, source_target_pairs={{0,0},{1,1},{2,2},{3,3},{4,6},{5,7},{6,4},{7,5},{8,8},{9,9},{10,10... | collective-permute-start | bytes 3145736 | tf_op jit(solution)/shard_map/ppermute | solution.py:764
  279.2 17.3 %collective-permute-start.27 = (bf16[1024,512]{1,0:T(8,128)(2,1)}, bf16[1024,512]{1,0:T(8,128)(2,1)S(1)}, u32[]{:S(2)}, u32[]{:S(2)}) collective-permute-start(bf16[1024,512]{1,0:T(8,128)(2,1)} %get-tuple-element.296), channel_id=1, source_target_pairs={{0,29},{1,0},{2,1},{3,2},{6,3},{7,6},{4,7},{5,4},{8,5},{9,8},{10,9... | collective-permute-start | bytes 3145736 | tf_op jit(solution)/shard_map/ppermute | solution.py:769
  304.5 35.5 %collective-permute-start.29 = (bf16[4,96,512]{2,1,0:T(8,128)(2,1)S(1)}, bf16[4,96,512]{2,1,0:T(8,128)(2,1)S(1)}, u32[]{:S(2)}, u32[]{:S(2)}) collective-permute-start(bf16[4,96,512]{2,1,0:T(8,128)(2,1)S(1)} %get-tuple-element.314), channel_id=1, source_target_pairs={{0,2},{1,3},{2,0},{3,1},{4,6},{5,7},{6,4},{7,5},{8,10},{9,11},{10,... | collective-permute-start | bytes 1179656 | tf_op jit(solution)/shard_map/ppermute | solution.py:752
  306.3 33.7 %collective-permute-start.30 = (bf16[4,96,512]{2,1,0:T(8,128)(2,1)S(1)}, bf16[4,96,512]{2,1,0:T(8,128)(2,1)S(1)}, u32[]{:S(2)}, u32[]{:S(2)}) collective-permute-start(bf16[4,96,512]{2,1,0:T(8,128)(2,1)S(1)} %get-tuple-element.315), channel_id=1, source_target_pairs={{0,4},{1,5},{2,6},{3,7},{4,0},{5,1},{6,2},{7,3},{8,12},{9,13},{10,... | collective-permute-start | bytes 1179656 | tf_op jit(solution)/shard_map/ppermute | solution.py:752
  308.1 32.0 %collective-permute-start.31 = (bf16[4,96,512]{2,1,0:T(8,128)(2,1)S(1)}, bf16[4,96,512]{2,1,0:T(8,128)(2,1)S(1)}, u32[]{:S(2)}, u32[]{:S(2)}) collective-permute-start(bf16[4,96,512]{2,1,0:T(8,128)(2,1)S(1)} %get-tuple-element.316), channel_id=1, source_target_pairs={{0,6},{1,7},{2,4},{3,5},{4,2},{5,3},{6,0},{7,1},{8,14},{9,15},{10,... | collective-permute-start | bytes 1179656 | tf_op jit(solution)/shard_map/ppermute | solution.py:752
  340.2 17.3 %collective-permute-start.33 = (bf16[1024,512]{1,0:T(8,128)(2,1)}, bf16[1024,512]{1,0:T(8,128)(2,1)S(1)}, u32[]{:S(2)}, u32[]{:S(2)}) collective-permute-start(bf16[1024,512]{1,0:T(8,128)(2,1)} %get-tuple-element.326), channel_id=1, source_target_pairs={{0,29},{1,0},{2,1},{3,2},{6,3},{7,6},{4,7},{5,4},{8,5},{9,8},{10,9... | collective-permute-start | bytes 3145736 | tf_op jit(solution)/shard_map/ppermute | solution.py:769
  357.5 39.9 %collective-permute-start.39 = (bf16[1,96,512]{2,1,0:T(8,128)(2,1)S(1)}, bf16[1,96,512]{2,1,0:T(8,128)(2,1)S(1)}, u32[]{:S(2)}, u32[]{:S(2)}) collective-permute-start(bf16[1,96,512]{2,1,0:T(8,128)(2,1)S(1)} %get-tuple-element.360), channel_id=1, source_target_pairs={{0,16},{1,17},{2,18},{3,19},{4,20},{5,21},{6,22},{7,23},{8,24},{9,... | collective-permute-start | bytes 294920 | tf_op jit(solution)/shard_map/ppermute | solution.py:752
  357.5 39.8 %collective-permute-start.40 = (bf16[1,96,512]{2,1,0:T(8,128)(2,1)S(1)}, bf16[1,96,512]{2,1,0:T(8,128)(2,1)S(1)}, u32[]{:S(2)}, u32[]{:S(2)}) collective-permute-start(bf16[1,96,512]{2,1,0:T(8,128)(2,1)S(1)} %get-tuple-element.361), channel_id=1, source_target_pairs={{0,24},{1,25},{2,26},{3,27},{4,28},{5,29},{6,30},{7,31},{8,16},{9,... | collective-permute-start | bytes 294920 | tf_op jit(solution)/shard_map/ppermute | solution.py:752
  362.2 35.2 %collective-permute-start.35 = (bf16[4,96,512]{2,1,0:T(8,128)(2,1)S(1)}, bf16[4,96,512]{2,1,0:T(8,128)(2,1)S(1)}, u32[]{:S(2)}, u32[]{:S(2)}) collective-permute-start(bf16[4,96,512]{2,1,0:T(8,128)(2,1)S(1)} %get-tuple-element.355), channel_id=1, source_target_pairs={{0,2},{1,3},{2,0},{3,1},{4,6},{5,7},{6,4},{7,5},{8,10},{9,11},{10,... | collective-permute-start | bytes 1179656 | tf_op jit(solution)/shard_map/ppermute | solution.py:752
  363.1 34.3 %collective-permute-start.36 = (bf16[4,96,512]{2,1,0:T(8,128)(2,1)S(1)}, bf16[4,96,512]{2,1,0:T(8,128)(2,1)S(1)}, u32[]{:S(2)}, u32[]{:S(2)}) collective-permute-start(bf16[4,96,512]{2,1,0:T(8,128)(2,1)S(1)} %get-tuple-element.356), channel_id=1, source_target_pairs={{0,4},{1,5},{2,6},{3,7},{4,0},{5,1},{6,2},{7,3},{8,12},{9,13},{10,... | collective-permute-start | bytes 1179656 | tf_op jit(solution)/shard_map/ppermute | solution.py:752
  364.1 33.4 %collective-permute-start.37 = (bf16[4,96,512]{2,1,0:T(8,128)(2,1)S(1)}, bf16[4,96,512]{2,1,0:T(8,128)(2,1)S(1)}, u32[]{:S(2)}, u32[]{:S(2)}) collective-permute-start(bf16[4,96,512]{2,1,0:T(8,128)(2,1)S(1)} %get-tuple-element.357), channel_id=1, source_target_pairs={{0,6},{1,7},{2,4},{3,5},{4,2},{5,3},{6,0},{7,1},{8,14},{9,15},{10,... | collective-permute-start | bytes 1179656 | tf_op jit(solution)/shard_map/ppermute | solution.py:752
  397.5 17.4 %collective-permute-start.42 = (bf16[1024,512]{1,0:T(8,128)(2,1)}, bf16[1024,512]{1,0:T(8,128)(2,1)S(1)}, u32[]{:S(2)}, u32[]{:S(2)}) collective-permute-start(bf16[1024,512]{1,0:T(8,128)(2,1)} %get-tuple-element.372), channel_id=1, source_target_pairs={{0,29},{1,0},{2,1},{3,2},{6,3},{7,6},{4,7},{5,4},{8,5},{9,8},{10,9... | collective-permute-start | bytes 3145736 | tf_op jit(solution)/shard_map/ppermute | solution.py:769
  414.9 40.2 %collective-permute-start.48 = (bf16[1,96,512]{2,1,0:T(8,128)(2,1)S(1)}, bf16[1,96,512]{2,1,0:T(8,128)(2,1)S(1)}, u32[]{:S(2)}, u32[]{:S(2)}) collective-permute-start(bf16[1,96,512]{2,1,0:T(8,128)(2,1)S(1)} %get-tuple-element.405), channel_id=1, source_target_pairs={{0,16},{1,17},{2,18},{3,19},{4,20},{5,21},{6,22},{7,23},{8,24},{9,... | collective-permute-start | bytes 294920 | tf_op jit(solution)/shard_map/ppermute | solution.py:752
  417.7 37.5 %collective-permute-start.49 = (bf16[1,96,512]{2,1,0:T(8,128)(2,1)S(1)}, bf16[1,96,512]{2,1,0:T(8,128)(2,1)S(1)}, u32[]{:S(2)}, u32[]{:S(2)}) collective-permute-start(bf16[1,96,512]{2,1,0:T(8,128)(2,1)S(1)} %get-tuple-element.406), channel_id=1, source_target_pairs={{0,24},{1,25},{2,26},{3,27},{4,28},{5,29},{6,30},{7,31},{8,16},{9,... | collective-permute-start | bytes 294920 | tf_op jit(solution)/shard_map/ppermute | solution.py:752
  419.7 35.6 %collective-permute-start.44 = (bf16[4,96,512]{2,1,0:T(8,128)(2,1)S(1)}, bf16[4,96,512]{2,1,0:T(8,128)(2,1)S(1)}, u32[]{:S(2)}, u32[]{:S(2)}) collective-permute-start(bf16[4,96,512]{2,1,0:T(8,128)(2,1)S(1)} %get-tuple-element.400), channel_id=1, source_target_pairs={{0,2},{1,3},{2,0},{3,1},{4,6},{5,7},{6,4},{7,5},{8,10},{9,11},{10,... | collective-permute-start | bytes 1179656 | tf_op jit(solution)/shard_map/ppermute | solution.py:752
  419.8 35.5 %collective-permute-start.45 = (bf16[4,96,512]{2,1,0:T(8,128)(2,1)S(1)}, bf16[4,96,512]{2,1,0:T(8,128)(2,1)S(1)}, u32[]{:S(2)}, u32[]{:S(2)}) collective-permute-start(bf16[4,96,512]{2,1,0:T(8,128)(2,1)S(1)} %get-tuple-element.401), channel_id=1, source_target_pairs={{0,4},{1,5},{2,6},{3,7},{4,0},{5,1},{6,2},{7,3},{8,12},{9,13},{10,... | collective-permute-start | bytes 1179656 | tf_op jit(solution)/shard_map/ppermute | solution.py:752
  421.5 33.8 %collective-permute-start.46 = (bf16[4,96,512]{2,1,0:T(8,128)(2,1)S(1)}, bf16[4,96,512]{2,1,0:T(8,128)(2,1)S(1)}, u32[]{:S(2)}, u32[]{:S(2)}) collective-permute-start(bf16[4,96,512]{2,1,0:T(8,128)(2,1)S(1)} %get-tuple-element.402), channel_id=1, source_target_pairs={{0,6},{1,7},{2,4},{3,5},{4,2},{5,3},{6,0},{7,1},{8,14},{9,15},{10,... | collective-permute-start | bytes 1179656 | tf_op jit(solution)/shard_map/ppermute | solution.py:752
  455.3 17.2 %collective-permute-start.51 = (bf16[1024,512]{1,0:T(8,128)(2,1)}, bf16[1024,512]{1,0:T(8,128)(2,1)S(1)}, u32[]{:S(2)}, u32[]{:S(2)}) collective-permute-start(bf16[1024,512]{1,0:T(8,128)(2,1)} %get-tuple-element.417), channel_id=1, source_target_pairs={{0,29},{1,0},{2,1},{3,2},{6,3},{7,6},{4,7},{5,4},{8,5},{9,8},{10,9... | collective-permute-start | bytes 3145736 | tf_op jit(solution)/shard_map/ppermute | solution.py:769
  494.8 19.2 %collective-permute-start.55 = (bf16[4,96,512]{2,1,0:T(8,128)(2,1)S(1)}, bf16[4,96,512]{2,1,0:T(8,128)(2,1)S(1)}, u32[]{:S(2)}, u32[]{:S(2)}) collective-permute-start(bf16[4,96,512]{2,1,0:T(8,128)(2,1)S(1)} %copy-done.17), channel_id=1, source_target_pairs={{0,6},{1,7},{2,4},{3,5},{4,2},{5,3},{6,0},{7,1},{8,14},{9,15},{10,... | collective-permute-start | bytes 1179656 | tf_op jit(solution)/shard_map/ppermute | solution.py:752
  (98 other events, 1288.5 us)
Sparse Core Ops, SparseCore 0:
  90.8 74.4 all-gather.1

commit v11 on v10

--- a/solution.py
+++ b/solution.py
@@ -870,6 +870,7 @@
         mesh_rows = bring(mesh_static, device_count, 0, direct)
         second_column = spread_high(second_pair, device_count)
         plane = join(column)
+        second_last = second_column.pop()
         near, sides, mesh_rows, second_column, rest, goals = barrier(
             ((plane, swap(plane, device_count, 4)), sides, mesh_rows, second_column, rest, goals)
         )
@@ -882,8 +883,8 @@
         first, grid_latent, grid_start, *blocks = embed(
             self_id, pieces, sides
         )
-        first, goals = barrier((first, goals))
-        second_plane = join(second_column)
+        first, goals, second_last = barrier((first, goals, second_last))
+        second_plane = join([*second_column, second_last])
         second_near = (second_plane, swap(second_plane, device_count, 4))
         goals = bring(goals, device_count, 0, direct)
         targets, weight_rows = goals[:, :outputs], goals[:, outputs]
@@ -956,19 +957,16 @@
     above, above_source = None, None
     layer_grads = [None] * layer_total
     gain_grads = [None] * layer_total
-    in_plane, in_slice = [], []
+    in_plane = []
     for layer_id in reversed(range(layer_total)):
         source_low, stored, aggregate = stored_list[layer_id]
         sent_grad, grad_new, *slot_grads, grad_gain, grad_message, edge_hidden, b0, b1, b2, b3 = backward_layer(
             slot_lists[layer_id], above, grad_part, stored, weights[layer_id], gains[layer_id], layer_id == 0
         )
-        far = []
+        in_slice = []
         if in_plane:
-            moved = len(in_plane)
-            arrived, slot_grads = together(in_plane + in_slice, slot_grads)
-            if in_slice:
-                layer_grads[layer_id + 2] = add_up(arrived[moved:]).reshape(6, share, width)
-            far = list(combine(device_count // 8, arrived[:moved]))
+            arrived, slot_grads = together(in_plane, slot_grads)
+            in_slice = fan_out(combine(device_count // 8, arrived), device_count, 8)
         from_before = shift(slot_grads[2], device_count, 1, direct)
         from_after = shift(slot_grads[0], device_count, -1, direct)
         back = [edge_hidden, grad_message, b0, b1, b2, b3]
@@ -985,11 +983,10 @@
         )
         gain_grads[layer_id] = grad_gain
         if direct:
-            tied = [*sums, *far] if layer_id > 0 else sums
-            halo, arrived = together([from_before, from_after], tied)
+            halo, arrived = together([from_before, from_after], [*sums, *in_slice])
             keep, send = arrived[:2]
-            far = arrived[2:] if layer_id > 0 else far
-            in_slice = fan_out(far, device_count, 8) if far else []
+            if in_slice:
+                layer_grads[layer_id + 1] = add_up(arrived[2:]).reshape(6, share, width)
             other = swap(send, device_count, 1)
             near = list(combine(4, [keep, other]))
             halo, near = together(halo, near)
@@ -1019,8 +1016,7 @@
         in_plane = [in_plane[0], *early, in_plane[3]]
         keep, send = sums
         last_plane = combine(4, [keep, swap(send, device_count, 1)])
-        last_plane, in_slice = together(fan_out(last_plane, device_count, 2), in_slice)
-        layer_grads[1] = add_up(in_slice).reshape(6, share, width)
+        last_plane = fan_out(last_plane, device_count, 2)
         far = combine(device_count // 8, in_plane, last_plane)
         total = add_up(fan_out(far, device_count, 8))
         layer_grads[0] = total[: 6 * share].reshape(6, share, width)

time: 548 us -> 556 us (1.015)
  waiting for transfers between devices: 114 us -> 134 us
    ppermute x46, waiting for transfers between devices: 68.1 us -> 96.7 us  [swap(): return lax.ppermute(cells, AXES, [(i, i ^ mask) for i in range(count)])]
    ppermute x16, waiting for transfers between devices: 45.5 us -> 36.9 us  [shift(): return lax.ppermute(cells, AXES, pairs)]
  transfers between devices with their start and end apart: 67 -> 67, of which waited for: 28 -> 32; matrix products, arithmetic and copies ran while one was open for 3% -> 2% of each run, Pallas kernels for 40% -> 39%
where the time goes in v11:
time: 556 us; the launch traced here: 547 us
  Pallas kernels  262 us (47%)
  waiting for transfers between devices  134 us (24%)
  starting transfers between devices  112 us (20%)
  between operations  17.3 us (3%)
  other arithmetic  9.85 us (2%)
  local copies, waits for them, and re-layouts  6.21 us (1%)
  matrix products  6.09 us (1%)
    pallas_call x4, Pallas kernels, backward_layer(): pl.pallas_call(functools.partial(backward_kernel, parts, mode), grid=(blo...  125 us
    ppermute x46, waiting for transfers between devices, swap(): return lax.ppermute(cells, AXES, [(i, i ^ mask) for i in range(count)])  96.7 us
    pallas_call x4, Pallas kernels, forward_layer(): pl.pallas_call(functools.partial(forward_kernel, parts, has_next), grid=(...  72 us
    ppermute x46, starting transfers between devices, swap(): return lax.ppermute(cells, AXES, [(i, i ^ mask) for i in range(count)])  62.5 us
    pallas_call x4, Pallas kernels, weight_layer(): pl.pallas_call(functools.partial(weight_kernel, above is not None, grad_n...  41.9 us
    ppermute x16, starting transfers between devices, shift(): return lax.ppermute(cells, AXES, pairs)  37.1 us
    ppermute x16, waiting for transfers between devices, shift(): return lax.ppermute(cells, AXES, pairs)  36.9 us
    ppermute x4, starting transfers between devices, bring(): lax.ppermute(cells, AXES, [(i, home((i + step) % count, direct)) for i in...  12.9 us
  transfers between devices with their start and end apart: 67, of which 32 were waited for; matrix products, arithmetic and copies ran while one was open for 2% of the time, Pallas kernels for 39%

profile of v11, /device:TPU:0, one launch (start us, length us, event | category | flops | bytes accessed | tf_op | source)
XLA Modules:
  0.0 546.9 jit_solution(11013633458722831678)
XLA Ops:
  22.7 8.5 %collective-permute-done.3.refs_1_ = bf16[2,136,512]{2,1,0:T(8,128)(2,1)S(1)} collective-permute-done((bf16[2,136,512]{2,1,0:T(8,128)(2,1)S(1)}, bf16[2,136,512]{2,1,0:T(8,128)(2,1)S(1)}, u32[]{:S(2)}, u32[]{:S(2)}) %collective-permute-start.3) | collective-permute-done | bytes 278560 | tf_op jit(solution)/shard_map/ppermute | solution.py:752
  31.3 11.3 %collective-permute-done.4.refs_2_ = bf16[2,136,512]{2,1,0:T(8,128)(2,1)S(1)} collective-permute-done((bf16[2,136,512]{2,1,0:T(8,128)(2,1)S(1)}, bf16[2,136,512]{2,1,0:T(8,128)(2,1)S(1)}, u32[]{:S(2)}, u32[]{:S(2)}) %collective-permute-start.4) | collective-permute-done | bytes 278560 | tf_op jit(solution)/shard_map/ppermute | solution.py:752
  42.7 5.2 collective-permute-start.7
  52.4 9.5 %collective-permute-start.10 = (bf16[1024,512]{1,0:T(8,128)(2,1)}, bf16[1024,512]{1,0:T(8,128)(2,1)}, u32[]{:S(2)}, u32[]{:S(2)}) collective-permute-start(bf16[1024,512]{1,0:T(8,128)(2,1)} %param.22), channel_id=1, source_target_pairs={{0,0},{1,1},{2,2},{3,3},{4,6},{5,7},{6,4},{7,5},{8,8},{9,9},{10,10... | collective-permute-start | bytes 3145736 | tf_op jit(solution)/shard_map/ppermute | solution.py:764
  64.7 6.8 %collective-permute-done.11.refs_1_ = bf16[2,96,512]{2,1,0:T(8,128)(2,1)S(1)} collective-permute-done((bf16[2,96,512]{2,1,0:T(8,128)(2,1)S(1)}, bf16[2,96,512]{2,1,0:T(8,128)(2,1)S(1)}, u32[]{:S(2)}, u32[]{:S(2)}) %collective-permute-start.11) | collective-permute-done | bytes 196640 | tf_op jit(solution)/shard_map/ppermute | solution.py:752
  74.5 5.9 %collective-permute-done.12.refs_2_ = bf16[2,96,512]{2,1,0:T(8,128)(2,1)S(1)} collective-permute-done((bf16[2,96,512]{2,1,0:T(8,128)(2,1)S(1)}, bf16[2,96,512]{2,1,0:T(8,128)(2,1)S(1)}, u32[]{:S(2)}, u32[]{:S(2)}) %collective-permute-start.12) | collective-permute-done | bytes 196640 | tf_op jit(solution)/shard_map/ppermute | solution.py:752
  86.2 9.3 %embed.1 = (bf16[7,512,512]{2,1,0:T(8,128)(2,1)}, f32[1024,512]{1,0:T(8,128)}, bf16[1024,512]{1,0:T(8,128)(2,1)}, bf16[1024,512]{1,0:T(8,128)(2,1)}, bf16[1024,5...) custom-call(s32[1]{0:T(128)} %bitcast.10.refs_0_.self_id, bf16[8,136,512]{2,1,0:T(8,128)(2,1)} %copy-done.1, ...), custom_call_target="tpu_custom_call" | custom-call | flops 3221225472 | bytes 12582912 | tf_op jit(solution)/shard_map/embed/pallas_call | solution.py:611
  101.1 18.6 %forward_layer.4 = (bf16[1024,512]{1,0:T(8,128)(2,1)}, f32[1024,512]{1,0:T(8,128)}, bf16[1024,512]{1,0:T(8,128)(2,1)}, bf16[4,1024,512]{2,1,0:T(8,128)(2,1)}, bf16[1024,512]{1,0:T(8,128)(2,1)}) custom-call(s32[4096]{0:T(1024)} %get-tuple-element.485.refs_0_, bf16[1024,512]{1,0:T(8,128)(2,1)} %get-tuple-element.258.refs_1_, ...), custom_call_target="tpu_custom_call" | custom-call | flops 4831838208 | bytes 25165824 | tf_op jit(solution)/shard_map/forward_layer/pallas_call | solution.py:186
  129.8 12.0 %collective-permute-done.17.refs_1_ = bf16[1024,512]{1,0:T(8,128)(2,1)} collective-permute-done((bf16[1024,512]{1,0:T(8,128)(2,1)}, bf16[1024,512]{1,0:T(8,128)(2,1)}, u32[]{:S(2)}, u32[]{:S(2)}) %collective-permute-start.17) | collective-permute-done | bytes 1048608 | tf_op jit(solution)/shard_map/ppermute | solution.py:769
  144.4 18.7 %forward_layer.5 = (bf16[1024,512]{1,0:T(8,128)(2,1)}, f32[1024,512]{1,0:T(8,128)}, bf16[1024,512]{1,0:T(8,128)(2,1)}, bf16[4,1024,512]{2,1,0:T(8,128)(2,1)}, bf16[1024,512]{1,0:T(8,128)(2,1)}) custom-call(s32[4096]{0:T(1024)} %get-tuple-element.486.refs_0_, bf16[1024,512]{1,0:T(8,128)(2,1)} %collective-permute-done.17.refs_1_, ...), custom_call_target="tpu_custom_call" | custom-call | flops 4831838208 | bytes 25165824 | tf_op jit(solution)/shard_map/forward_layer/pallas_call | solution.py:186
  163.2 4.6 collective-permute-start.23
  170.6 9.8 %collective-permute-done.22.refs_1_ = bf16[1024,512]{1,0:T(8,128)(2,1)S(1)} collective-permute-done((bf16[1024,512]{1,0:T(8,128)(2,1)}, bf16[1024,512]{1,0:T(8,128)(2,1)S(1)}, u32[]{:S(2)}, u32[]{:S(2)}) %collective-permute-start.22) | collective-permute-done | bytes 1048608 | tf_op jit(solution)/shard_map/ppermute | solution.py:769
  180.5 18.0 %forward_layer.6 = (bf16[1024,512]{1,0:T(8,128)(2,1)}, f32[1024,512]{1,0:T(8,128)}, bf16[1024,512]{1,0:T(8,128)(2,1)}, bf16[4,1024,512]{2,1,0:T(8,128)(2,1)}, bf16[1024,512]{1,0:T(8,128)(2,1)}) custom-call(s32[4096]{0:T(1024)} %get-tuple-element.486.refs_0_, bf16[1024,512]{1,0:T(8,128)(2,1)S(1)} %collective-permute-done.22.refs_1_, ...), custom_call_target="tpu_custom_call" | custom-call | flops 4831838208 | bytes 25165824 | tf_op jit(solution)/shard_map/forward_layer/pallas_call | solution.py:186
  198.5 4.5 collective-permute-start.25
  204.5 11.1 %collective-permute-done.24.refs_1_ = bf16[1024,512]{1,0:T(8,128)(2,1)S(1)} collective-permute-done((bf16[1024,512]{1,0:T(8,128)(2,1)}, bf16[1024,512]{1,0:T(8,128)(2,1)S(1)}, u32[]{:S(2)}, u32[]{:S(2)}) %collective-permute-start.24) | collective-permute-done | bytes 1048608 | tf_op jit(solution)/shard_map/ppermute | solution.py:769
  215.6 16.8 %forward_layer.7 = (bf16[1024,512]{1,0:T(8,128)(2,1)}, bf16[4,1024,512]{2,1,0:T(8,128)(2,1)}, bf16[1024,512]{1,0:T(8,128)(2,1)}) custom-call(s32[4096]{0:T(1024)} %get-tuple-element.487.refs_0_, bf16[1024,512]{1,0:T(8,128)(2,1)S(1)} %collective-permute-done.24.refs_1_, bf16[1024,512]{1,0:T(8,128)(2,1)} %get-tuple-element.277.refs_2_, ...), custom_call_target="tpu_custom_call" | custom-call | flops 4831838208 | bytes 25165824 | tf_op jit(solution)/shard_map/forward_layer/pallas_call | solution.py:186
  238.0 29.8 %backward_layer.4 = (bf16[1024,512]{1,0:T(8,128)(2,1)}, bf16[1024,512]{1,0:T(8,128)(2,1)}, bf16[1024,512]{1,0:T(8,128)(2,1)}, f32[2,512]{1,0:T(2,128)S(1)}, bf16...) custom-call(s32[4096]{0:T(1024)S(1)} %copy-done.6, ...), custom_call_target="tpu_custom_call" | custom-call | flops 4294967296 | bytes 25165824 | tf_op jit(solution)/shard_map/backward_layer/pallas_call | solution.py:374
  267.9 4.7 collective-permute-start.27
  273.2 10.8 %weight_layer.4 = (f32[1024,512]{1,0:T(8,128)}, f32[16,96,512]{2,1,0:T(8,128)S(1)}, bf16[16,96,512]{2,1,0:T(8,128)(2,1)S(1)}) custom-call(s32[1]{0:T(128)} %bitcast.10.refs_0_.self_id, f32[512,512]{1,0:T(8,128)S(1)} %pad.29.refs_1_, bf16[1024,512]{1,0:T(8,128)(2,1)} %get-tuple-element.278.refs_4_.refs_2_.latent_low, ...), custom_call_target="tpu_custom_call" | custom-call | flops 5368709120 | bytes 12582912 | tf_op jit(solution)/shard_map/weight_layer/pallas_call | solution.py:504
  285.2 5.4 collective-permute-start.28
  297.6 32.1 %backward_layer.5 = (bf16[1024,512]{1,0:T(8,128)(2,1)S(1)}, f32[1024,512]{1,0:T(8,128)S(1)}, bf16[1024,512]{1,0:T(8,128)(2,1)}, bf16[1024,512]{1,0:T(8,128)(2,1)...) custom-call(s32[4096]{0:T(1024)S(1)} %copy-done.4, ...), custom_call_target="tpu_custom_call" | custom-call | flops 4294967296 | bytes 25165824 | tf_op jit(solution)/shard_map/backward_layer/pallas_call | solution.py:374
  329.8 4.6 collective-permute-start.33
  339.1 11.4 %weight_layer.5 = (f32[1024,512]{1,0:T(8,128)}, f32[16,96,512]{2,1,0:T(8,128)S(1)}, bf16[16,96,512]{2,1,0:T(8,128)(2,1)S(1)}) custom-call(s32[1]{0:T(128)} %bitcast.10.refs_0_.self_id, bf16[1024,512]{1,0:T(8,128)(2,1)} %get-tuple-element.315.refs_1_, bf16[1024,512]{1,0:T(8,128)(2,1)S(1)} %get-tuple-element.316.refs_2_, ...), custom_call_target="tpu_custom_call" | custom-call | flops 5368709120 | bytes 12582912 | tf_op jit(solution)/shard_map/weight_layer/pallas_call | solution.py:504
  363.4 31.6 %backward_layer.6 = (bf16[1024,512]{1,0:T(8,128)(2,1)S(1)}, f32[1024,512]{1,0:T(8,128)S(1)}, bf16[1024,512]{1,0:T(8,128)(2,1)}, bf16[1024,512]{1,0:T(8,128)(2,1)...) custom-call(s32[4096]{0:T(1024)S(1)} %copy-done.4, ...), custom_call_target="tpu_custom_call" | custom-call | flops 4294967296 | bytes 25165824 | tf_op jit(solution)/shard_map/backward_layer/pallas_call | solution.py:374
  395.2 4.8 collective-permute-start.42
  404.6 11.4 %weight_layer.6 = (f32[1024,512]{1,0:T(8,128)}, f32[16,96,512]{2,1,0:T(8,128)S(1)}, bf16[16,96,512]{2,1,0:T(8,128)(2,1)S(1)}) custom-call(s32[1]{0:T(128)} %bitcast.10.refs_0_.self_id, bf16[1024,512]{1,0:T(8,128)(2,1)} %get-tuple-element.274.refs_4_.refs_5_.refs_3_.refs_1_, bf16[1024,512]{1,0:T(8,128)(2,1)S(1)} %get-tuple-element.357.refs_2_, ...), custom_call_target="tpu_custom_call" | custom-call | flops 5368709120 | bytes 12582912 | tf_op jit(solution)/shard_map/weight_layer/pallas_call | solution.py:504
  427.2 31.9 %backward_layer.7 = (bf16[1024,512]{1,0:T(8,128)(2,1)S(1)}, f32[1024,512]{1,0:T(8,128)}, bf16[1024,512]{1,0:T(8,128)(2,1)}, bf16[1024,512]{1,0:T(8,128)(2,1)}, b...) custom-call(s32[4096]{0:T(1024)S(1)} %copy-done.5, ...), custom_call_target="tpu_custom_call" | custom-call | flops 4294967296 | bytes 25165824 | tf_op jit(solution)/shard_map/backward_layer/pallas_call | solution.py:374
  459.3 4.6 collective-permute-start.51
  468.5 8.3 %weight_layer.7 = (f32[16,96,512]{2,1,0:T(8,128)S(1)}, bf16[16,96,512]{2,1,0:T(8,128)(2,1)S(1)}) custom-call(s32[1]{0:T(128)} %bitcast.10.refs_0_.self_id, bf16[1024,512]{1,0:T(8,128)(2,1)} %get-tuple-element.264.refs_4_.refs_6_.refs_3_.refs_1_, bf16[1024,512]{1,0:T(8,128)(2,1)S(1)} %get-tuple-element.398.refs_2_, ...), custom_call_target="tpu_custom_call" | custom-call | flops 5368709120 | bytes 12582912 | tf_op jit(solution)/shard_map/weight_layer/pallas_call | solution.py:504
  489.7 7.1 %tail_layer.1 = (f32[16,40,512]{2,1,0:T(8,128)S(1)}, bf16[16,40,512]{2,1,0:T(8,128)(2,1)S(1)}) custom-call(s32[1]{0:T(128)} %bitcast.10.refs_0_.self_id, f32[1]{0:T(128)} %bitcast.56.loss, bf16[1024,512]{1,0:T(8,128)(2,1)} %copy-done.18, bf16[1024,512]{1,0:T(8,128)(2,1)} %get-tuple-element.427.middle, bf16[1024,512]{1,0:T(8,128)(2,1)} %copy-done.19, ...), custom_call_target="tpu_custom_call" | custom-call | flops 1610612736 | bytes 12582912 | tf_op jit(solution)/shard_map/tail_layer/pallas_call | solution.py:686
  506.9 7.0 %collective-permute-done.58 = bf16[4,96,512]{2,1,0:T(8,128)(2,1)S(1)} collective-permute-done((bf16[4,96,512]{2,1,0:T(8,128)(2,1)S(1)}, bf16[4,96,512]{2,1,0:T(8,128)(2,1)S(1)}, u32[]{:S(2)}, u32[]{:S(2)}) %collective-permute-start.58) | collective-permute-done | bytes 393248 | tf_op jit(solution)/shard_map/ppermute | solution.py:752
  527.9 8.0 %collective-permute-done.64 = bf16[1,136,512]{2,1,0:T(8,128)(2,1)S(1)} collective-permute-done((bf16[1,136,512]{2,1,0:T(8,128)(2,1)S(1)}, bf16[1,136,512]{2,1,0:T(8,128)(2,1)S(1)}, u32[]{:S(2)}, u32[]{:S(2)}) %collective-permute-start.64) | collective-permute-done | bytes 139296 | tf_op jit(solution)/shard_map/ppermute | solution.py:752
  (271 shorter events, 145.5 us)
Async XLA Ops:
  7.2 173.2 %all-gather.2.cloned.1.call-start = ((), (), s32[]{:S(2)}) async-start(), calls=%async_computation | async-start | bytes 6488064 | tf_op jit(solution)/shard_map/all_gather | solution.py:879
  17.4 25.2 %collective-permute-start.6 = (bf16[1024,512]{1,0:T(8,128)(2,1)S(1)}, bf16[1024,512]{1,0:T(8,128)(2,1)S(1)}, u32[]{:S(2)}, u32[]{:S(2)}) collective-permute-start(bf16[1024,512]{1,0:T(8,128)(2,1)S(1)} %pad.26), channel_id=1, source_target_pairs={{0,0},{1,1},{2,2},{3,3},{4,6},{5,7},{6,4},{7,5},{8,8},{9,9},{10,10... | collective-permute-start | bytes 3145736 | tf_op jit(solution)/shard_map/ppermute | solution.py:764
  20.1 22.4 %collective-permute-start.4 = (bf16[2,136,512]{2,1,0:T(8,128)(2,1)S(1)}, bf16[2,136,512]{2,1,0:T(8,128)(2,1)S(1)}, u32[]{:S(2)}, u32[]{:S(2)}) collective-permute-start(bf16[2,136,512]{2,1,0:T(8,128)(2,1)S(1)} %pad_maximum_fusion.refs_0_), channel_id=1, source_target_pairs={{0,16},{1,17},{2,18},{3,19},{4,20},{5,21},{6,22},{7,23},{8,24},{9,... | collective-permute-start | bytes 835592 | tf_op jit(solution)/shard_map/ppermute | solution.py:752
  22.7 19.8 %collective-permute-start.5 = (bf16[2,136,512]{2,1,0:T(8,128)(2,1)S(1)}, bf16[2,136,512]{2,1,0:T(8,128)(2,1)S(1)}, u32[]{:S(2)}, u32[]{:S(2)}) collective-permute-start(bf16[2,136,512]{2,1,0:T(8,128)(2,1)S(1)} %pad_maximum_fusion.refs_0_), channel_id=1, source_target_pairs={{0,24},{1,25},{2,26},{3,27},{4,28},{5,29},{6,30},{7,31},{8,16},{9,... | collective-permute-start | bytes 835592 | tf_op jit(solution)/shard_map/ppermute | solution.py:752
  42.7 38.6 %collective-permute-start.7 = (bf16[8,136,512]{2,1,0:T(8,128)(2,1)S(1)}, bf16[8,136,512]{2,1,0:T(8,128)(2,1)}, u32[]{:S(2)}, u32[]{:S(2)}) collective-permute-start(bf16[8,136,512]{2,1,0:T(8,128)(2,1)S(1)} %join.2.refs_1_), channel_id=1, source_target_pairs={{0,4},{1,5},{2,6},{3,7},{4,0},{5,1},{6,2},{7,3},{8,12},{9,13},{10,... | collective-permute-start | bytes 3342344 | tf_op jit(solution)/shard_map/ppermute | solution.py:752
  47.9 32.6 %collective-permute-start.8 = (bf16[1024,512]{1,0:T(8,128)(2,1)S(1)}, bf16[1024,512]{1,0:T(8,128)(2,1)}, u32[]{:S(2)}, u32[]{:S(2)}) collective-permute-start(bf16[1024,512]{1,0:T(8,128)(2,1)S(1)} %collective-permute-done.6.refs_6_.inputs), channel_id=1, source_target_pairs={{0,1},{1,2},{2,3},{3,6},{6,7},{7,4},{4,5},{5,8},{8,9},{9,10},{10,1... | collective-permute-start | bytes 3145736 | tf_op jit(solution)/shard_map/ppermute | solution.py:769
  47.9 32.6 %collective-permute-start.9 = (bf16[1024,512]{1,0:T(8,128)(2,1)S(1)}, bf16[1024,512]{1,0:T(8,128)(2,1)}, u32[]{:S(2)}, u32[]{:S(2)}) collective-permute-start(bf16[1024,512]{1,0:T(8,128)(2,1)S(1)} %collective-permute-done.6.refs_6_.inputs), channel_id=1, source_target_pairs={{0,29},{1,0},{2,1},{3,2},{6,3},{7,6},{4,7},{5,4},{8,5},{9,8},{10,9... | collective-permute-start | bytes 3145736 | tf_op jit(solution)/shard_map/ppermute | solution.py:769
  52.4 28.1 %collective-permute-start.10 = (bf16[1024,512]{1,0:T(8,128)(2,1)}, bf16[1024,512]{1,0:T(8,128)(2,1)}, u32[]{:S(2)}, u32[]{:S(2)}) collective-permute-start(bf16[1024,512]{1,0:T(8,128)(2,1)} %param.22), channel_id=1, source_target_pairs={{0,0},{1,1},{2,2},{3,3},{4,6},{5,7},{6,4},{7,5},{8,8},{9,9},{10,10... | collective-permute-start | bytes 3145736 | tf_op jit(solution)/shard_map/ppermute | solution.py:764
  95.6 28.6 %collective-permute-start.19 = (bf16[8,96,512]{2,1,0:T(8,128)(2,1)S(1)}, bf16[8,96,512]{2,1,0:T(8,128)(2,1)S(1)}, u32[]{:S(2)}, u32[]{:S(2)}) collective-permute-start(bf16[8,96,512]{2,1,0:T(8,128)(2,1)S(1)} %join.3.refs_1_), channel_id=1, source_target_pairs={{0,4},{1,5},{2,6},{3,7},{4,0},{5,1},{6,2},{7,3},{8,12},{9,13},{10,... | collective-permute-start | bytes 2359304 | tf_op jit(solution)/shard_map/ppermute | solution.py:752
  119.7 22.1 %collective-permute-start.17 = (bf16[1024,512]{1,0:T(8,128)(2,1)}, bf16[1024,512]{1,0:T(8,128)(2,1)}, u32[]{:S(2)}, u32[]{:S(2)}) collective-permute-start(bf16[1024,512]{1,0:T(8,128)(2,1)} %get-tuple-element.263.refs_2_), channel_id=1, source_target_pairs={{0,1},{1,2},{2,3},{3,6},{6,7},{7,4},{4,5},{5,8},{8,9},{9,10},{10,1... | collective-permute-start | bytes 3145736 | tf_op jit(solution)/shard_map/ppermute | solution.py:769
  119.7 24.7 %collective-permute-start.18 = (bf16[1024,512]{1,0:T(8,128)(2,1)}, bf16[1024,512]{1,0:T(8,128)(2,1)}, u32[]{:S(2)}, u32[]{:S(2)}) collective-permute-start(bf16[1024,512]{1,0:T(8,128)(2,1)} %get-tuple-element.263.refs_2_), channel_id=1, source_target_pairs={{0,29},{1,0},{2,1},{3,2},{6,3},{7,6},{4,7},{5,4},{8,5},{9,8},{10,9... | collective-permute-start | bytes 3145736 | tf_op jit(solution)/shard_map/ppermute | solution.py:769
  168.6 35.2 %collective-permute-start.16 = (f32[1024,256]{0,1:T(8,128)S(1)}, f32[1024,256]{0,1:T(8,128)}, u32[]{:S(2)}, u32[]{:S(2)}) collective-permute-start(f32[1024,256]{0,1:T(8,128)S(1)} %copy-done.17), channel_id=1, source_target_pairs={{0,0},{1,1},{2,2},{3,3},{4,6},{5,7},{6,4},{7,5},{8,8},{9,9},{10,10... | collective-permute-start | bytes 3145736 | tf_op jit(solution)/shard_map/ppermute | solution.py:764
  294.0 35.7 %collective-permute-start.29 = (bf16[4,96,512]{2,1,0:T(8,128)(2,1)S(1)}, bf16[4,96,512]{2,1,0:T(8,128)(2,1)S(1)}, u32[]{:S(2)}, u32[]{:S(2)}) collective-permute-start(bf16[4,96,512]{2,1,0:T(8,128)(2,1)S(1)} %get-tuple-element.302), channel_id=1, source_target_pairs={{0,2},{1,3},{2,0},{3,1},{4,6},{5,7},{6,4},{7,5},{8,10},{9,11},{10,... | collective-permute-start | bytes 1179656 | tf_op jit(solution)/shard_map/ppermute | solution.py:752
  295.8 33.9 %collective-permute-start.30 = (bf16[4,96,512]{2,1,0:T(8,128)(2,1)S(1)}, bf16[4,96,512]{2,1,0:T(8,128)(2,1)S(1)}, u32[]{:S(2)}, u32[]{:S(2)}) collective-permute-start(bf16[4,96,512]{2,1,0:T(8,128)(2,1)S(1)} %get-tuple-element.303), channel_id=1, source_target_pairs={{0,4},{1,5},{2,6},{3,7},{4,0},{5,1},{6,2},{7,3},{8,12},{9,13},{10,... | collective-permute-start | bytes 1179656 | tf_op jit(solution)/shard_map/ppermute | solution.py:752
  297.5 32.2 %collective-permute-start.31 = (bf16[4,96,512]{2,1,0:T(8,128)(2,1)S(1)}, bf16[4,96,512]{2,1,0:T(8,128)(2,1)S(1)}, u32[]{:S(2)}, u32[]{:S(2)}) collective-permute-start(bf16[4,96,512]{2,1,0:T(8,128)(2,1)S(1)} %get-tuple-element.304), channel_id=1, source_target_pairs={{0,6},{1,7},{2,4},{3,5},{4,2},{5,3},{6,0},{7,1},{8,14},{9,15},{10,... | collective-permute-start | bytes 1179656 | tf_op jit(solution)/shard_map/ppermute | solution.py:752
  329.7 26.3 %collective-permute-start.32 = (bf16[1024,512]{1,0:T(8,128)(2,1)}, bf16[1024,512]{1,0:T(8,128)(2,1)S(1)}, u32[]{:S(2)}, u32[]{:S(2)}) collective-permute-start(bf16[1024,512]{1,0:T(8,128)(2,1)} %get-tuple-element.313), channel_id=1, source_target_pairs={{0,1},{1,2},{2,3},{3,6},{6,7},{7,4},{4,5},{5,8},{8,9},{9,10},{10,1... | collective-permute-start | bytes 3145736 | tf_op jit(solution)/shard_map/ppermute | solution.py:769
  329.8 26.2 %collective-permute-start.33 = (bf16[1024,512]{1,0:T(8,128)(2,1)}, bf16[1024,512]{1,0:T(8,128)(2,1)S(1)}, u32[]{:S(2)}, u32[]{:S(2)}) collective-permute-start(bf16[1024,512]{1,0:T(8,128)(2,1)} %get-tuple-element.314), channel_id=1, source_target_pairs={{0,29},{1,0},{2,1},{3,2},{6,3},{7,6},{4,7},{5,4},{8,5},{9,8},{10,9... | collective-permute-start | bytes 3145736 | tf_op jit(solution)/shard_map/ppermute | solution.py:769
  334.6 19.1 %collective-permute-start.34 = (bf16[1,96,512]{2,1,0:T(8,128)(2,1)S(1)}, bf16[1,96,512]{2,1,0:T(8,128)(2,1)S(1)}, u32[]{:S(2)}, u32[]{:S(2)}) collective-permute-start(bf16[1,96,512]{2,1,0:T(8,128)(2,1)S(1)} %get-tuple-element.331), channel_id=1, source_target_pairs={{0,8},{1,9},{2,10},{3,11},{4,12},{5,13},{6,14},{7,15},{8,0},{9,1},... | collective-permute-start | bytes 294920 | tf_op jit(solution)/shard_map/ppermute | solution.py:752
  336.7 19.3 %collective-permute-start.35 = (bf16[1,96,512]{2,1,0:T(8,128)(2,1)S(1)}, bf16[1,96,512]{2,1,0:T(8,128)(2,1)S(1)}, u32[]{:S(2)}, u32[]{:S(2)}) collective-permute-start(bf16[1,96,512]{2,1,0:T(8,128)(2,1)S(1)} %get-tuple-element.332), channel_id=1, source_target_pairs={{0,16},{1,17},{2,18},{3,19},{4,20},{5,21},{6,22},{7,23},{8,24},{9,... | collective-permute-start | bytes 294920 | tf_op jit(solution)/shard_map/ppermute | solution.py:752
  336.7 19.3 %collective-permute-start.36 = (bf16[1,96,512]{2,1,0:T(8,128)(2,1)S(1)}, bf16[1,96,512]{2,1,0:T(8,128)(2,1)S(1)}, u32[]{:S(2)}, u32[]{:S(2)}) collective-permute-start(bf16[1,96,512]{2,1,0:T(8,128)(2,1)S(1)} %get-tuple-element.333), channel_id=1, source_target_pairs={{0,24},{1,25},{2,26},{3,27},{4,28},{5,29},{6,30},{7,31},{8,16},{9,... | collective-permute-start | bytes 294920 | tf_op jit(solution)/shard_map/ppermute | solution.py:752
  359.9 35.2 %collective-permute-start.38 = (bf16[4,96,512]{2,1,0:T(8,128)(2,1)S(1)}, bf16[4,96,512]{2,1,0:T(8,128)(2,1)S(1)}, u32[]{:S(2)}, u32[]{:S(2)}) collective-permute-start(bf16[4,96,512]{2,1,0:T(8,128)(2,1)S(1)} %get-tuple-element.343), channel_id=1, source_target_pairs={{0,2},{1,3},{2,0},{3,1},{4,6},{5,7},{6,4},{7,5},{8,10},{9,11},{10,... | collective-permute-start | bytes 1179656 | tf_op jit(solution)/shard_map/ppermute | solution.py:752
  360.0 35.1 %collective-permute-start.39 = (bf16[4,96,512]{2,1,0:T(8,128)(2,1)S(1)}, bf16[4,96,512]{2,1,0:T(8,128)(2,1)S(1)}, u32[]{:S(2)}, u32[]{:S(2)}) collective-permute-start(bf16[4,96,512]{2,1,0:T(8,128)(2,1)S(1)} %get-tuple-element.344), channel_id=1, source_target_pairs={{0,4},{1,5},{2,6},{3,7},{4,0},{5,1},{6,2},{7,3},{8,12},{9,13},{10,... | collective-permute-start | bytes 1179656 | tf_op jit(solution)/shard_map/ppermute | solution.py:752
  360.0 35.1 %collective-permute-start.40 = (bf16[4,96,512]{2,1,0:T(8,128)(2,1)S(1)}, bf16[4,96,512]{2,1,0:T(8,128)(2,1)S(1)}, u32[]{:S(2)}, u32[]{:S(2)}) collective-permute-start(bf16[4,96,512]{2,1,0:T(8,128)(2,1)S(1)} %get-tuple-element.345), channel_id=1, source_target_pairs={{0,6},{1,7},{2,4},{3,5},{4,2},{5,3},{6,0},{7,1},{8,14},{9,15},{10,... | collective-permute-start | bytes 1179656 | tf_op jit(solution)/shard_map/ppermute | solution.py:752
  395.1 24.7 %collective-permute-start.41 = (bf16[1024,512]{1,0:T(8,128)(2,1)}, bf16[1024,512]{1,0:T(8,128)(2,1)S(1)}, u32[]{:S(2)}, u32[]{:S(2)}) collective-permute-start(bf16[1024,512]{1,0:T(8,128)(2,1)} %get-tuple-element.355), channel_id=1, source_target_pairs={{0,1},{1,2},{2,3},{3,6},{6,7},{7,4},{4,5},{5,8},{8,9},{9,10},{10,1... | collective-permute-start | bytes 3145736 | tf_op jit(solution)/shard_map/ppermute | solution.py:769
  395.2 24.7 %collective-permute-start.42 = (bf16[1024,512]{1,0:T(8,128)(2,1)}, bf16[1024,512]{1,0:T(8,128)(2,1)S(1)}, u32[]{:S(2)}, u32[]{:S(2)}) collective-permute-start(bf16[1024,512]{1,0:T(8,128)(2,1)} %get-tuple-element.356), channel_id=1, source_target_pairs={{0,29},{1,0},{2,1},{3,2},{6,3},{7,6},{4,7},{5,4},{8,5},{9,8},{10,9... | collective-permute-start | bytes 3145736 | tf_op jit(solution)/shard_map/ppermute | solution.py:769
  400.2 19.6 %collective-permute-start.44 = (bf16[1,96,512]{2,1,0:T(8,128)(2,1)S(1)}, bf16[1,96,512]{2,1,0:T(8,128)(2,1)S(1)}, u32[]{:S(2)}, u32[]{:S(2)}) collective-permute-start(bf16[1,96,512]{2,1,0:T(8,128)(2,1)S(1)} %get-tuple-element.373), channel_id=1, source_target_pairs={{0,16},{1,17},{2,18},{3,19},{4,20},{5,21},{6,22},{7,23},{8,24},{9,... | collective-permute-start | bytes 294920 | tf_op jit(solution)/shard_map/ppermute | solution.py:752
  423.7 35.5 %collective-permute-start.47 = (bf16[4,96,512]{2,1,0:T(8,128)(2,1)S(1)}, bf16[4,96,512]{2,1,0:T(8,128)(2,1)S(1)}, u32[]{:S(2)}, u32[]{:S(2)}) collective-permute-start(bf16[4,96,512]{2,1,0:T(8,128)(2,1)S(1)} %get-tuple-element.384), channel_id=1, source_target_pairs={{0,2},{1,3},{2,0},{3,1},{4,6},{5,7},{6,4},{7,5},{8,10},{9,11},{10,... | collective-permute-start | bytes 1179656 | tf_op jit(solution)/shard_map/ppermute | solution.py:752
  423.8 35.4 %collective-permute-start.48 = (bf16[4,96,512]{2,1,0:T(8,128)(2,1)S(1)}, bf16[4,96,512]{2,1,0:T(8,128)(2,1)S(1)}, u32[]{:S(2)}, u32[]{:S(2)}) collective-permute-start(bf16[4,96,512]{2,1,0:T(8,128)(2,1)S(1)} %get-tuple-element.385), channel_id=1, source_target_pairs={{0,4},{1,5},{2,6},{3,7},{4,0},{5,1},{6,2},{7,3},{8,12},{9,13},{10,... | collective-permute-start | bytes 1179656 | tf_op jit(solution)/shard_map/ppermute | solution.py:752
  423.8 35.4 %collective-permute-start.49 = (bf16[4,96,512]{2,1,0:T(8,128)(2,1)S(1)}, bf16[4,96,512]{2,1,0:T(8,128)(2,1)S(1)}, u32[]{:S(2)}, u32[]{:S(2)}) collective-permute-start(bf16[4,96,512]{2,1,0:T(8,128)(2,1)S(1)} %get-tuple-element.386), channel_id=1, source_target_pairs={{0,6},{1,7},{2,4},{3,5},{4,2},{5,3},{6,0},{7,1},{8,14},{9,15},{10,... | collective-permute-start | bytes 1179656 | tf_op jit(solution)/shard_map/ppermute | solution.py:752
  459.2 24.5 %collective-permute-start.50 = (bf16[1024,512]{1,0:T(8,128)(2,1)}, bf16[1024,512]{1,0:T(8,128)(2,1)S(1)}, u32[]{:S(2)}, u32[]{:S(2)}) collective-permute-start(bf16[1024,512]{1,0:T(8,128)(2,1)} %get-tuple-element.396), channel_id=1, source_target_pairs={{0,1},{1,2},{2,3},{3,6},{6,7},{7,4},{4,5},{5,8},{8,9},{9,10},{10,1... | collective-permute-start | bytes 3145736 | tf_op jit(solution)/shard_map/ppermute | solution.py:769
  459.3 24.4 %collective-permute-start.51 = (bf16[1024,512]{1,0:T(8,128)(2,1)}, bf16[1024,512]{1,0:T(8,128)(2,1)S(1)}, u32[]{:S(2)}, u32[]{:S(2)}) collective-permute-start(bf16[1024,512]{1,0:T(8,128)(2,1)} %get-tuple-element.397), channel_id=1, source_target_pairs={{0,29},{1,0},{2,1},{3,2},{6,3},{7,6},{4,7},{5,4},{8,5},{9,8},{10,9... | collective-permute-start | bytes 3145736 | tf_op jit(solution)/shard_map/ppermute | solution.py:769
  464.1 19.6 %collective-permute-start.53 = (bf16[1,96,512]{2,1,0:T(8,128)(2,1)S(1)}, bf16[1,96,512]{2,1,0:T(8,128)(2,1)S(1)}, u32[]{:S(2)}, u32[]{:S(2)}) collective-permute-start(bf16[1,96,512]{2,1,0:T(8,128)(2,1)S(1)} %get-tuple-element.413), channel_id=1, source_target_pairs={{0,16},{1,17},{2,18},{3,19},{4,20},{5,21},{6,22},{7,23},{8,24},{9,... | collective-permute-start | bytes 294920 | tf_op jit(solution)/shard_map/ppermute | solution.py:752
  (73 other events, 890.6 us)
Sparse Core Ops, SparseCore 0:
  81.4 79.7 all-gather.1

commit v12 on v10

--- a/solution.py
+++ b/solution.py
@@ -870,6 +870,7 @@
         mesh_rows = bring(mesh_static, device_count, 0, direct)
         second_column = spread_high(second_pair, device_count)
         plane = join(column)
+        second_last = second_column.pop()
         near, sides, mesh_rows, second_column, rest, goals = barrier(
             ((plane, swap(plane, device_count, 4)), sides, mesh_rows, second_column, rest, goals)
         )
@@ -882,8 +883,8 @@
         first, grid_latent, grid_start, *blocks = embed(
             self_id, pieces, sides
         )
-        first, goals = barrier((first, goals))
-        second_plane = join(second_column)
+        first, goals, second_last = barrier((first, goals, second_last))
+        second_plane = join([*second_column, second_last])
         second_near = (second_plane, swap(second_plane, device_count, 4))
         goals = bring(goals, device_count, 0, direct)
         targets, weight_rows = goals[:, :outputs], goals[:, outputs]
@@ -1015,12 +1016,12 @@
             heads[0],
             gain_grads,
         )
-        early, sums = together(in_plane[1:3], sums)
-        in_plane = [in_plane[0], *early, in_plane[3]]
+        early, sums = together(in_plane[1:3] + in_slice, sums)
+        in_plane = [in_plane[0], *early[:2], in_plane[3]]
+        layer_grads[1] = add_up(early[2:]).reshape(6, share, width)
         keep, send = sums
         last_plane = combine(4, [keep, swap(send, device_count, 1)])
-        last_plane, in_slice = together(fan_out(last_plane, device_count, 2), in_slice)
-        layer_grads[1] = add_up(in_slice).reshape(6, share, width)
+        last_plane = fan_out(last_plane, device_count, 2)
         far = combine(device_count // 8, in_plane, last_plane)
         total = add_up(fan_out(far, device_count, 8))
         layer_grads[0] = total[: 6 * share].reshape(6, share, width)

time: 548 us -> 540 us (0.985)
  transfers between devices with their start and end apart: 67 -> 67, of which waited for: 28 -> 29; matrix products, arithmetic and copies ran while one was open for 3% -> 2% of each run, Pallas kernels for 40% -> 40%
where the time goes in v12:
time: 540 us; the launch traced here: 531 us
  Pallas kernels  261 us (48%)
  starting transfers between devices  115 us (21%)
  waiting for transfers between devices  113 us (21%)
  between operations  17.4 us (3%)
  other arithmetic  9.88 us (2%)
  local copies, waits for them, and re-layouts  8.36 us (2%)
  matrix products  6.07 us (1%)
    pallas_call x4, Pallas kernels, backward_layer(): pl.pallas_call(functools.partial(backward_kernel, parts, mode), grid=(blo...  125 us
    pallas_call x4, Pallas kernels, forward_layer(): pl.pallas_call(functools.partial(forward_kernel, parts, has_next), grid=(...  72.2 us
    ppermute x46, waiting for transfers between devices, swap(): return lax.ppermute(cells, AXES, [(i, i ^ mask) for i in range(count)])  70.7 us
    ppermute x46, starting transfers between devices, swap(): return lax.ppermute(cells, AXES, [(i, i ^ mask) for i in range(count)])  65.1 us
    ppermute x16, waiting for transfers between devices, shift(): return lax.ppermute(cells, AXES, pairs)  42.3 us
    pallas_call x4, Pallas kernels, weight_layer(): pl.pallas_call(functools.partial(weight_kernel, above is not None, grad_n...  41.5 us
    ppermute x16, starting transfers between devices, shift(): return lax.ppermute(cells, AXES, pairs)  37.1 us
    ppermute x4, starting transfers between devices, bring(): lax.ppermute(cells, AXES, [(i, home((i + step) % count, direct)) for i in...  12.9 us
  transfers between devices with their start and end apart: 67, of which 29 were waited for; matrix products, arithmetic and copies ran while one was open for 2% of the time, Pallas kernels for 40%

profile of v12, /device:TPU:0, one launch (start us, length us, event | category | flops | bytes accessed | tf_op | source)
XLA Modules:
  0.0 531.0 jit_solution(2437648587374107176)
XLA Ops:
  22.8 8.5 %collective-permute-done.3.refs_1_ = bf16[2,136,512]{2,1,0:T(8,128)(2,1)S(1)} collective-permute-done((bf16[2,136,512]{2,1,0:T(8,128)(2,1)S(1)}, bf16[2,136,512]{2,1,0:T(8,128)(2,1)S(1)}, u32[]{:S(2)}, u32[]{:S(2)}) %collective-permute-start.3) | collective-permute-done | bytes 278560 | tf_op jit(solution)/shard_map/ppermute | solution.py:752
  31.3 11.3 %collective-permute-done.4.refs_2_ = bf16[2,136,512]{2,1,0:T(8,128)(2,1)S(1)} collective-permute-done((bf16[2,136,512]{2,1,0:T(8,128)(2,1)S(1)}, bf16[2,136,512]{2,1,0:T(8,128)(2,1)S(1)}, u32[]{:S(2)}, u32[]{:S(2)}) %collective-permute-start.4) | collective-permute-done | bytes 278560 | tf_op jit(solution)/shard_map/ppermute | solution.py:752
  42.7 5.2 collective-permute-start.7
  52.4 9.5 %collective-permute-start.10 = (bf16[1024,512]{1,0:T(8,128)(2,1)}, bf16[1024,512]{1,0:T(8,128)(2,1)}, u32[]{:S(2)}, u32[]{:S(2)}) collective-permute-start(bf16[1024,512]{1,0:T(8,128)(2,1)} %param.22), channel_id=1, source_target_pairs={{0,0},{1,1},{2,2},{3,3},{4,6},{5,7},{6,4},{7,5},{8,8},{9,9},{10,10... | collective-permute-start | bytes 3145736 | tf_op jit(solution)/shard_map/ppermute | solution.py:764
  64.7 6.8 %collective-permute-done.11.refs_1_ = bf16[2,96,512]{2,1,0:T(8,128)(2,1)S(1)} collective-permute-done((bf16[2,96,512]{2,1,0:T(8,128)(2,1)S(1)}, bf16[2,96,512]{2,1,0:T(8,128)(2,1)S(1)}, u32[]{:S(2)}, u32[]{:S(2)}) %collective-permute-start.11) | collective-permute-done | bytes 196640 | tf_op jit(solution)/shard_map/ppermute | solution.py:752
  74.5 6.0 %collective-permute-done.12.refs_2_ = bf16[2,96,512]{2,1,0:T(8,128)(2,1)S(1)} collective-permute-done((bf16[2,96,512]{2,1,0:T(8,128)(2,1)S(1)}, bf16[2,96,512]{2,1,0:T(8,128)(2,1)S(1)}, u32[]{:S(2)}, u32[]{:S(2)}) %collective-permute-start.12) | collective-permute-done | bytes 196640 | tf_op jit(solution)/shard_map/ppermute | solution.py:752
  86.2 9.3 %embed.1 = (bf16[7,512,512]{2,1,0:T(8,128)(2,1)}, f32[1024,512]{1,0:T(8,128)}, bf16[1024,512]{1,0:T(8,128)(2,1)}, bf16[1024,512]{1,0:T(8,128)(2,1)}, bf16[1024,5...) custom-call(s32[1]{0:T(128)} %bitcast.10.refs_0_.self_id, bf16[8,136,512]{2,1,0:T(8,128)(2,1)} %copy-done.1, ...), custom_call_target="tpu_custom_call" | custom-call | flops 3221225472 | bytes 12582912 | tf_op jit(solution)/shard_map/embed/pallas_call | solution.py:611
  101.1 18.6 %forward_layer.4 = (bf16[1024,512]{1,0:T(8,128)(2,1)}, f32[1024,512]{1,0:T(8,128)}, bf16[1024,512]{1,0:T(8,128)(2,1)}, bf16[4,1024,512]{2,1,0:T(8,128)(2,1)}, bf16[1024,512]{1,0:T(8,128)(2,1)}) custom-call(s32[4096]{0:T(1024)} %get-tuple-element.501.refs_0_, bf16[1024,512]{1,0:T(8,128)(2,1)} %get-tuple-element.266.refs_1_, ...), custom_call_target="tpu_custom_call" | custom-call | flops 4831838208 | bytes 25165824 | tf_op jit(solution)/shard_map/forward_layer/pallas_call | solution.py:186
  129.8 12.0 %collective-permute-done.17.refs_1_ = bf16[1024,512]{1,0:T(8,128)(2,1)} collective-permute-done((bf16[1024,512]{1,0:T(8,128)(2,1)}, bf16[1024,512]{1,0:T(8,128)(2,1)}, u32[]{:S(2)}, u32[]{:S(2)}) %collective-permute-start.17) | collective-permute-done | bytes 1048608 | tf_op jit(solution)/shard_map/ppermute | solution.py:769
  144.6 18.7 %forward_layer.5 = (bf16[1024,512]{1,0:T(8,128)(2,1)}, f32[1024,512]{1,0:T(8,128)}, bf16[1024,512]{1,0:T(8,128)(2,1)}, bf16[4,1024,512]{2,1,0:T(8,128)(2,1)}, bf16[1024,512]{1,0:T(8,128)(2,1)}) custom-call(s32[4096]{0:T(1024)} %get-tuple-element.502.refs_0_, bf16[1024,512]{1,0:T(8,128)(2,1)} %collective-permute-done.17.refs_1_, ...), custom_call_target="tpu_custom_call" | custom-call | flops 4831838208 | bytes 25165824 | tf_op jit(solution)/shard_map/forward_layer/pallas_call | solution.py:186
  163.4 4.6 collective-permute-start.23
  170.8 9.8 %collective-permute-done.22.refs_1_ = bf16[1024,512]{1,0:T(8,128)(2,1)S(1)} collective-permute-done((bf16[1024,512]{1,0:T(8,128)(2,1)}, bf16[1024,512]{1,0:T(8,128)(2,1)S(1)}, u32[]{:S(2)}, u32[]{:S(2)}) %collective-permute-start.22) | collective-permute-done | bytes 1048608 | tf_op jit(solution)/shard_map/ppermute | solution.py:769
  180.7 18.1 %forward_layer.6 = (bf16[1024,512]{1,0:T(8,128)(2,1)}, f32[1024,512]{1,0:T(8,128)}, bf16[1024,512]{1,0:T(8,128)(2,1)}, bf16[4,1024,512]{2,1,0:T(8,128)(2,1)}, bf16[1024,512]{1,0:T(8,128)(2,1)}) custom-call(s32[4096]{0:T(1024)} %get-tuple-element.502.refs_0_, bf16[1024,512]{1,0:T(8,128)(2,1)S(1)} %collective-permute-done.22.refs_1_, ...), custom_call_target="tpu_custom_call" | custom-call | flops 4831838208 | bytes 25165824 | tf_op jit(solution)/shard_map/forward_layer/pallas_call | solution.py:186
  198.7 4.5 collective-permute-start.25
  204.8 11.1 %collective-permute-done.24.refs_1_ = bf16[1024,512]{1,0:T(8,128)(2,1)S(1)} collective-permute-done((bf16[1024,512]{1,0:T(8,128)(2,1)}, bf16[1024,512]{1,0:T(8,128)(2,1)S(1)}, u32[]{:S(2)}, u32[]{:S(2)}) %collective-permute-start.24) | collective-permute-done | bytes 1048608 | tf_op jit(solution)/shard_map/ppermute | solution.py:769
  215.9 16.8 %forward_layer.7 = (bf16[1024,512]{1,0:T(8,128)(2,1)}, bf16[4,1024,512]{2,1,0:T(8,128)(2,1)}, bf16[1024,512]{1,0:T(8,128)(2,1)}) custom-call(s32[4096]{0:T(1024)} %get-tuple-element.503.refs_0_, bf16[1024,512]{1,0:T(8,128)(2,1)S(1)} %collective-permute-done.24.refs_1_, bf16[1024,512]{1,0:T(8,128)(2,1)} %get-tuple-element.285.refs_2_, ...), custom_call_target="tpu_custom_call" | custom-call | flops 4831838208 | bytes 25165824 | tf_op jit(solution)/shard_map/forward_layer/pallas_call | solution.py:186
  238.3 29.7 %backward_layer.4 = (bf16[1024,512]{1,0:T(8,128)(2,1)}, bf16[1024,512]{1,0:T(8,128)(2,1)}, bf16[1024,512]{1,0:T(8,128)(2,1)}, f32[2,512]{1,0:T(2,128)S(1)}, bf16...) custom-call(s32[4096]{0:T(1024)S(1)} %copy-done.10, ...), custom_call_target="tpu_custom_call" | custom-call | flops 4294967296 | bytes 25165824 | tf_op jit(solution)/shard_map/backward_layer/pallas_call | solution.py:374
  268.1 4.7 collective-permute-start.27
  273.4 10.8 %weight_layer.4 = (f32[1024,512]{1,0:T(8,128)}, f32[16,96,512]{2,1,0:T(8,128)S(1)}, bf16[16,96,512]{2,1,0:T(8,128)(2,1)S(1)}) custom-call(s32[1]{0:T(128)} %bitcast.10.refs_0_.self_id, f32[512,512]{1,0:T(8,128)S(1)} %pad.29.refs_1_, bf16[1024,512]{1,0:T(8,128)(2,1)} %get-tuple-element.286.refs_4_.refs_2_.latent_low, ...), custom_call_target="tpu_custom_call" | custom-call | flops 5368709120 | bytes 12582912 | tf_op jit(solution)/shard_map/weight_layer/pallas_call | solution.py:504
  285.5 5.3 collective-permute-start.28
  297.7 32.0 %backward_layer.5 = (bf16[1024,512]{1,0:T(8,128)(2,1)S(1)}, f32[1024,512]{1,0:T(8,128)S(1)}, bf16[1024,512]{1,0:T(8,128)(2,1)}, bf16[1024,512]{1,0:T(8,128)(2,1)...) custom-call(s32[4096]{0:T(1024)S(1)} %copy-done.4, ...), custom_call_target="tpu_custom_call" | custom-call | flops 4294967296 | bytes 25165824 | tf_op jit(solution)/shard_map/backward_layer/pallas_call | solution.py:374
  329.8 4.6 collective-permute-start.33
  334.4 11.1 %weight_layer.5 = (f32[1024,512]{1,0:T(8,128)}, f32[16,96,512]{2,1,0:T(8,128)S(1)}, bf16[16,96,512]{2,1,0:T(8,128)(2,1)S(1)}) custom-call(s32[1]{0:T(128)} %bitcast.10.refs_0_.self_id, bf16[1024,512]{1,0:T(8,128)(2,1)} %get-tuple-element.323.refs_1_, bf16[1024,512]{1,0:T(8,128)(2,1)S(1)} %get-tuple-element.324.refs_2_, ...), custom_call_target="tpu_custom_call" | custom-call | flops 5368709120 | bytes 12582912 | tf_op jit(solution)/shard_map/weight_layer/pallas_call | solution.py:504
  357.0 31.6 %backward_layer.6 = (bf16[1024,512]{1,0:T(8,128)(2,1)S(1)}, f32[1024,512]{1,0:T(8,128)S(1)}, bf16[1024,512]{1,0:T(8,128)(2,1)}, bf16[1024,512]{1,0:T(8,128)(2,1)...) custom-call(s32[4096]{0:T(1024)S(1)} %copy-done.4, ...), custom_call_target="tpu_custom_call" | custom-call | flops 4294967296 | bytes 25165824 | tf_op jit(solution)/shard_map/backward_layer/pallas_call | solution.py:374
  388.8 4.8 collective-permute-start.42
  393.6 11.4 %weight_layer.6 = (f32[1024,512]{1,0:T(8,128)}, f32[16,96,512]{2,1,0:T(8,128)S(1)}, bf16[16,96,512]{2,1,0:T(8,128)(2,1)S(1)}) custom-call(s32[1]{0:T(128)} %bitcast.10.refs_0_.self_id, bf16[1024,512]{1,0:T(8,128)(2,1)} %get-tuple-element.282.refs_4_.refs_5_.refs_3_.refs_1_, bf16[1024,512]{1,0:T(8,128)(2,1)S(1)} %get-tuple-element.369.refs_2_, ...), custom_call_target="tpu_custom_call" | custom-call | flops 5368709120 | bytes 12582912 | tf_op jit(solution)/shard_map/weight_layer/pallas_call | solution.py:504
  414.5 31.9 %backward_layer.7 = (bf16[1024,512]{1,0:T(8,128)(2,1)S(1)}, f32[1024,512]{1,0:T(8,128)}, bf16[1024,512]{1,0:T(8,128)(2,1)}, bf16[1024,512]{1,0:T(8,128)(2,1)}, b...) custom-call(s32[4096]{0:T(1024)S(1)} %copy-done.9, ...), custom_call_target="tpu_custom_call" | custom-call | flops 4294967296 | bytes 25165824 | tf_op jit(solution)/shard_map/backward_layer/pallas_call | solution.py:374
  446.6 4.6 collective-permute-start.51
  451.2 8.3 %weight_layer.7 = (f32[16,96,512]{2,1,0:T(8,128)S(1)}, bf16[16,96,512]{2,1,0:T(8,128)(2,1)S(1)}) custom-call(s32[1]{0:T(128)} %bitcast.10.refs_0_.self_id, bf16[1024,512]{1,0:T(8,128)(2,1)} %get-tuple-element.272.refs_4_.refs_6_.refs_3_.refs_1_, bf16[1024,512]{1,0:T(8,128)(2,1)S(1)} %get-tuple-element.414.refs_2_, ...), custom_call_target="tpu_custom_call" | custom-call | flops 5368709120 | bytes 12582912 | tf_op jit(solution)/shard_map/weight_layer/pallas_call | solution.py:504
  476.2 7.1 %tail_layer.1 = (f32[16,40,512]{2,1,0:T(8,128)S(1)}, bf16[16,40,512]{2,1,0:T(8,128)(2,1)S(1)}) custom-call(s32[1]{0:T(128)} %bitcast.10.refs_0_.self_id, f32[1]{0:T(128)} %bitcast.56.loss, bf16[1024,512]{1,0:T(8,128)(2,1)} %copy-done.24, bf16[1024,512]{1,0:T(8,128)(2,1)} %get-tuple-element.443.middle, bf16[1024,512]{1,0:T(8,128)(2,1)} %copy-done.25, ...), custom_call_target="tpu_custom_call" | custom-call | flops 1610612736 | bytes 12582912 | tf_op jit(solution)/shard_map/tail_layer/pallas_call | solution.py:686
  491.1 6.7 %collective-permute-done.58 = bf16[4,96,512]{2,1,0:T(8,128)(2,1)S(1)} collective-permute-done((bf16[4,96,512]{2,1,0:T(8,128)(2,1)S(1)}, bf16[4,96,512]{2,1,0:T(8,128)(2,1)S(1)}, u32[]{:S(2)}, u32[]{:S(2)}) %collective-permute-start.58) | collective-permute-done | bytes 393248 | tf_op jit(solution)/shard_map/ppermute | solution.py:752
  511.7 8.2 %collective-permute-done.64 = bf16[1,136,512]{2,1,0:T(8,128)(2,1)S(1)} collective-permute-done((bf16[1,136,512]{2,1,0:T(8,128)(2,1)S(1)}, bf16[1,136,512]{2,1,0:T(8,128)(2,1)S(1)}, u32[]{:S(2)}, u32[]{:S(2)}) %collective-permute-start.64) | collective-permute-done | bytes 139296 | tf_op jit(solution)/shard_map/ppermute | solution.py:752
  (311 shorter events, 129.9 us)
Async XLA Ops:
  7.2 173.4 %all-gather.2.cloned.1.call-start = ((), (), s32[]{:S(2)}) async-start(), calls=%async_computation | async-start | bytes 6488064 | tf_op jit(solution)/shard_map/all_gather | solution.py:879
  17.4 25.2 %collective-permute-start.6 = (bf16[1024,512]{1,0:T(8,128)(2,1)S(1)}, bf16[1024,512]{1,0:T(8,128)(2,1)S(1)}, u32[]{:S(2)}, u32[]{:S(2)}) collective-permute-start(bf16[1024,512]{1,0:T(8,128)(2,1)S(1)} %pad.26), channel_id=1, source_target_pairs={{0,0},{1,1},{2,2},{3,3},{4,6},{5,7},{6,4},{7,5},{8,8},{9,9},{10,10... | collective-permute-start | bytes 3145736 | tf_op jit(solution)/shard_map/ppermute | solution.py:764
  20.1 22.4 %collective-permute-start.4 = (bf16[2,136,512]{2,1,0:T(8,128)(2,1)S(1)}, bf16[2,136,512]{2,1,0:T(8,128)(2,1)S(1)}, u32[]{:S(2)}, u32[]{:S(2)}) collective-permute-start(bf16[2,136,512]{2,1,0:T(8,128)(2,1)S(1)} %pad_maximum_fusion.refs_0_), channel_id=1, source_target_pairs={{0,16},{1,17},{2,18},{3,19},{4,20},{5,21},{6,22},{7,23},{8,24},{9,... | collective-permute-start | bytes 835592 | tf_op jit(solution)/shard_map/ppermute | solution.py:752
  22.7 19.8 %collective-permute-start.5 = (bf16[2,136,512]{2,1,0:T(8,128)(2,1)S(1)}, bf16[2,136,512]{2,1,0:T(8,128)(2,1)S(1)}, u32[]{:S(2)}, u32[]{:S(2)}) collective-permute-start(bf16[2,136,512]{2,1,0:T(8,128)(2,1)S(1)} %pad_maximum_fusion.refs_0_), channel_id=1, source_target_pairs={{0,24},{1,25},{2,26},{3,27},{4,28},{5,29},{6,30},{7,31},{8,16},{9,... | collective-permute-start | bytes 835592 | tf_op jit(solution)/shard_map/ppermute | solution.py:752
  42.7 38.6 %collective-permute-start.7 = (bf16[8,136,512]{2,1,0:T(8,128)(2,1)S(1)}, bf16[8,136,512]{2,1,0:T(8,128)(2,1)}, u32[]{:S(2)}, u32[]{:S(2)}) collective-permute-start(bf16[8,136,512]{2,1,0:T(8,128)(2,1)S(1)} %join.2.refs_1_), channel_id=1, source_target_pairs={{0,4},{1,5},{2,6},{3,7},{4,0},{5,1},{6,2},{7,3},{8,12},{9,13},{10,... | collective-permute-start | bytes 3342344 | tf_op jit(solution)/shard_map/ppermute | solution.py:752
  47.9 32.6 %collective-permute-start.8 = (bf16[1024,512]{1,0:T(8,128)(2,1)S(1)}, bf16[1024,512]{1,0:T(8,128)(2,1)}, u32[]{:S(2)}, u32[]{:S(2)}) collective-permute-start(bf16[1024,512]{1,0:T(8,128)(2,1)S(1)} %collective-permute-done.6.refs_6_.inputs), channel_id=1, source_target_pairs={{0,1},{1,2},{2,3},{3,6},{6,7},{7,4},{4,5},{5,8},{8,9},{9,10},{10,1... | collective-permute-start | bytes 3145736 | tf_op jit(solution)/shard_map/ppermute | solution.py:769
  47.9 32.6 %collective-permute-start.9 = (bf16[1024,512]{1,0:T(8,128)(2,1)S(1)}, bf16[1024,512]{1,0:T(8,128)(2,1)}, u32[]{:S(2)}, u32[]{:S(2)}) collective-permute-start(bf16[1024,512]{1,0:T(8,128)(2,1)S(1)} %collective-permute-done.6.refs_6_.inputs), channel_id=1, source_target_pairs={{0,29},{1,0},{2,1},{3,2},{6,3},{7,6},{4,7},{5,4},{8,5},{9,8},{10,9... | collective-permute-start | bytes 3145736 | tf_op jit(solution)/shard_map/ppermute | solution.py:769
  52.4 28.2 %collective-permute-start.10 = (bf16[1024,512]{1,0:T(8,128)(2,1)}, bf16[1024,512]{1,0:T(8,128)(2,1)}, u32[]{:S(2)}, u32[]{:S(2)}) collective-permute-start(bf16[1024,512]{1,0:T(8,128)(2,1)} %param.22), channel_id=1, source_target_pairs={{0,0},{1,1},{2,2},{3,3},{4,6},{5,7},{6,4},{7,5},{8,8},{9,9},{10,10... | collective-permute-start | bytes 3145736 | tf_op jit(solution)/shard_map/ppermute | solution.py:764
  95.6 28.6 %collective-permute-start.19 = (bf16[8,96,512]{2,1,0:T(8,128)(2,1)S(1)}, bf16[8,96,512]{2,1,0:T(8,128)(2,1)S(1)}, u32[]{:S(2)}, u32[]{:S(2)}) collective-permute-start(bf16[8,96,512]{2,1,0:T(8,128)(2,1)S(1)} %join.3.refs_1_), channel_id=1, source_target_pairs={{0,4},{1,5},{2,6},{3,7},{4,0},{5,1},{6,2},{7,3},{8,12},{9,13},{10,... | collective-permute-start | bytes 2359304 | tf_op jit(solution)/shard_map/ppermute | solution.py:752
  119.7 22.1 %collective-permute-start.17 = (bf16[1024,512]{1,0:T(8,128)(2,1)}, bf16[1024,512]{1,0:T(8,128)(2,1)}, u32[]{:S(2)}, u32[]{:S(2)}) collective-permute-start(bf16[1024,512]{1,0:T(8,128)(2,1)} %get-tuple-element.271.refs_2_), channel_id=1, source_target_pairs={{0,1},{1,2},{2,3},{3,6},{6,7},{7,4},{4,5},{5,8},{8,9},{9,10},{10,1... | collective-permute-start | bytes 3145736 | tf_op jit(solution)/shard_map/ppermute | solution.py:769
  119.8 24.8 %collective-permute-start.18 = (bf16[1024,512]{1,0:T(8,128)(2,1)}, bf16[1024,512]{1,0:T(8,128)(2,1)}, u32[]{:S(2)}, u32[]{:S(2)}) collective-permute-start(bf16[1024,512]{1,0:T(8,128)(2,1)} %get-tuple-element.271.refs_2_), channel_id=1, source_target_pairs={{0,29},{1,0},{2,1},{3,2},{6,3},{7,6},{4,7},{5,4},{8,5},{9,8},{10,9... | collective-permute-start | bytes 3145736 | tf_op jit(solution)/shard_map/ppermute | solution.py:769
  163.3 17.3 %collective-permute-start.22 = (bf16[1024,512]{1,0:T(8,128)(2,1)}, bf16[1024,512]{1,0:T(8,128)(2,1)S(1)}, u32[]{:S(2)}, u32[]{:S(2)}) collective-permute-start(bf16[1024,512]{1,0:T(8,128)(2,1)} %get-tuple-element.281.refs_2_), channel_id=1, source_target_pairs={{0,1},{1,2},{2,3},{3,6},{6,7},{7,4},{4,5},{5,8},{8,9},{9,10},{10,1... | collective-permute-start | bytes 3145736 | tf_op jit(solution)/shard_map/ppermute | solution.py:769
  163.4 17.3 %collective-permute-start.23 = (bf16[1024,512]{1,0:T(8,128)(2,1)}, bf16[1024,512]{1,0:T(8,128)(2,1)S(1)}, u32[]{:S(2)}, u32[]{:S(2)}) collective-permute-start(bf16[1024,512]{1,0:T(8,128)(2,1)} %get-tuple-element.281.refs_2_), channel_id=1, source_target_pairs={{0,29},{1,0},{2,1},{3,2},{6,3},{7,6},{4,7},{5,4},{8,5},{9,8},{10,9... | collective-permute-start | bytes 3145736 | tf_op jit(solution)/shard_map/ppermute | solution.py:769
  168.8 35.3 %collective-permute-start.16 = (f32[1024,256]{0,1:T(8,128)S(1)}, f32[1024,256]{0,1:T(8,128)}, u32[]{:S(2)}, u32[]{:S(2)}) collective-permute-start(f32[1024,256]{0,1:T(8,128)S(1)} %copy-done.23), channel_id=1, source_target_pairs={{0,0},{1,1},{2,2},{3,3},{4,6},{5,7},{6,4},{7,5},{8,8},{9,9},{10,10... | collective-permute-start | bytes 3145736 | tf_op jit(solution)/shard_map/ppermute | solution.py:764
  268.1 17.2 %collective-permute-start.26 = (bf16[1024,512]{1,0:T(8,128)(2,1)}, bf16[1024,512]{1,0:T(8,128)(2,1)S(1)}, u32[]{:S(2)}, u32[]{:S(2)}) collective-permute-start(bf16[1024,512]{1,0:T(8,128)(2,1)} %get-tuple-element.291), channel_id=1, source_target_pairs={{0,1},{1,2},{2,3},{3,6},{6,7},{7,4},{4,5},{5,8},{8,9},{9,10},{10,1... | collective-permute-start | bytes 3145736 | tf_op jit(solution)/shard_map/ppermute | solution.py:769
  268.1 17.3 %collective-permute-start.27 = (bf16[1024,512]{1,0:T(8,128)(2,1)}, bf16[1024,512]{1,0:T(8,128)(2,1)S(1)}, u32[]{:S(2)}, u32[]{:S(2)}) collective-permute-start(bf16[1024,512]{1,0:T(8,128)(2,1)} %get-tuple-element.292), channel_id=1, source_target_pairs={{0,29},{1,0},{2,1},{3,2},{6,3},{7,6},{4,7},{5,4},{8,5},{9,8},{10,9... | collective-permute-start | bytes 3145736 | tf_op jit(solution)/shard_map/ppermute | solution.py:769
  294.1 35.6 %collective-permute-start.29 = (bf16[4,96,512]{2,1,0:T(8,128)(2,1)S(1)}, bf16[4,96,512]{2,1,0:T(8,128)(2,1)S(1)}, u32[]{:S(2)}, u32[]{:S(2)}) collective-permute-start(bf16[4,96,512]{2,1,0:T(8,128)(2,1)S(1)} %get-tuple-element.310), channel_id=1, source_target_pairs={{0,2},{1,3},{2,0},{3,1},{4,6},{5,7},{6,4},{7,5},{8,10},{9,11},{10,... | collective-permute-start | bytes 1179656 | tf_op jit(solution)/shard_map/ppermute | solution.py:752
  295.9 33.8 %collective-permute-start.30 = (bf16[4,96,512]{2,1,0:T(8,128)(2,1)S(1)}, bf16[4,96,512]{2,1,0:T(8,128)(2,1)S(1)}, u32[]{:S(2)}, u32[]{:S(2)}) collective-permute-start(bf16[4,96,512]{2,1,0:T(8,128)(2,1)S(1)} %get-tuple-element.311), channel_id=1, source_target_pairs={{0,4},{1,5},{2,6},{3,7},{4,0},{5,1},{6,2},{7,3},{8,12},{9,13},{10,... | collective-permute-start | bytes 1179656 | tf_op jit(solution)/shard_map/ppermute | solution.py:752
  297.6 32.1 %collective-permute-start.31 = (bf16[4,96,512]{2,1,0:T(8,128)(2,1)S(1)}, bf16[4,96,512]{2,1,0:T(8,128)(2,1)S(1)}, u32[]{:S(2)}, u32[]{:S(2)}) collective-permute-start(bf16[4,96,512]{2,1,0:T(8,128)(2,1)S(1)} %get-tuple-element.312), channel_id=1, source_target_pairs={{0,6},{1,7},{2,4},{3,5},{4,2},{5,3},{6,0},{7,1},{8,14},{9,15},{10,... | collective-permute-start | bytes 1179656 | tf_op jit(solution)/shard_map/ppermute | solution.py:752
  329.8 17.3 %collective-permute-start.33 = (bf16[1024,512]{1,0:T(8,128)(2,1)}, bf16[1024,512]{1,0:T(8,128)(2,1)S(1)}, u32[]{:S(2)}, u32[]{:S(2)}) collective-permute-start(bf16[1024,512]{1,0:T(8,128)(2,1)} %get-tuple-element.322), channel_id=1, source_target_pairs={{0,29},{1,0},{2,1},{3,2},{6,3},{7,6},{4,7},{5,4},{8,5},{9,8},{10,9... | collective-permute-start | bytes 3145736 | tf_op jit(solution)/shard_map/ppermute | solution.py:769
  350.0 38.6 %collective-permute-start.39 = (bf16[1,96,512]{2,1,0:T(8,128)(2,1)S(1)}, bf16[1,96,512]{2,1,0:T(8,128)(2,1)S(1)}, u32[]{:S(2)}, u32[]{:S(2)}) collective-permute-start(bf16[1,96,512]{2,1,0:T(8,128)(2,1)S(1)} %get-tuple-element.356), channel_id=1, source_target_pairs={{0,16},{1,17},{2,18},{3,19},{4,20},{5,21},{6,22},{7,23},{8,24},{9,... | collective-permute-start | bytes 294920 | tf_op jit(solution)/shard_map/ppermute | solution.py:752
  350.0 38.6 %collective-permute-start.40 = (bf16[1,96,512]{2,1,0:T(8,128)(2,1)S(1)}, bf16[1,96,512]{2,1,0:T(8,128)(2,1)S(1)}, u32[]{:S(2)}, u32[]{:S(2)}) collective-permute-start(bf16[1,96,512]{2,1,0:T(8,128)(2,1)S(1)} %get-tuple-element.357), channel_id=1, source_target_pairs={{0,24},{1,25},{2,26},{3,27},{4,28},{5,29},{6,30},{7,31},{8,16},{9,... | collective-permute-start | bytes 294920 | tf_op jit(solution)/shard_map/ppermute | solution.py:752
  352.7 36.0 %collective-permute-start.35 = (bf16[4,96,512]{2,1,0:T(8,128)(2,1)S(1)}, bf16[4,96,512]{2,1,0:T(8,128)(2,1)S(1)}, u32[]{:S(2)}, u32[]{:S(2)}) collective-permute-start(bf16[4,96,512]{2,1,0:T(8,128)(2,1)S(1)} %get-tuple-element.351), channel_id=1, source_target_pairs={{0,2},{1,3},{2,0},{3,1},{4,6},{5,7},{6,4},{7,5},{8,10},{9,11},{10,... | collective-permute-start | bytes 1179656 | tf_op jit(solution)/shard_map/ppermute | solution.py:752
  354.5 34.2 %collective-permute-start.36 = (bf16[4,96,512]{2,1,0:T(8,128)(2,1)S(1)}, bf16[4,96,512]{2,1,0:T(8,128)(2,1)S(1)}, u32[]{:S(2)}, u32[]{:S(2)}) collective-permute-start(bf16[4,96,512]{2,1,0:T(8,128)(2,1)S(1)} %get-tuple-element.352), channel_id=1, source_target_pairs={{0,4},{1,5},{2,6},{3,7},{4,0},{5,1},{6,2},{7,3},{8,12},{9,13},{10,... | collective-permute-start | bytes 1179656 | tf_op jit(solution)/shard_map/ppermute | solution.py:752
  355.6 33.2 %collective-permute-start.37 = (bf16[4,96,512]{2,1,0:T(8,128)(2,1)S(1)}, bf16[4,96,512]{2,1,0:T(8,128)(2,1)S(1)}, u32[]{:S(2)}, u32[]{:S(2)}) collective-permute-start(bf16[4,96,512]{2,1,0:T(8,128)(2,1)S(1)} %get-tuple-element.353), channel_id=1, source_target_pairs={{0,6},{1,7},{2,4},{3,5},{4,2},{5,3},{6,0},{7,1},{8,14},{9,15},{10,... | collective-permute-start | bytes 1179656 | tf_op jit(solution)/shard_map/ppermute | solution.py:752
  388.8 17.4 %collective-permute-start.42 = (bf16[1024,512]{1,0:T(8,128)(2,1)}, bf16[1024,512]{1,0:T(8,128)(2,1)S(1)}, u32[]{:S(2)}, u32[]{:S(2)}) collective-permute-start(bf16[1024,512]{1,0:T(8,128)(2,1)} %get-tuple-element.368), channel_id=1, source_target_pairs={{0,29},{1,0},{2,1},{3,2},{6,3},{7,6},{4,7},{5,4},{8,5},{9,8},{10,9... | collective-permute-start | bytes 3145736 | tf_op jit(solution)/shard_map/ppermute | solution.py:769
  406.2 40.2 %collective-permute-start.48 = (bf16[1,96,512]{2,1,0:T(8,128)(2,1)S(1)}, bf16[1,96,512]{2,1,0:T(8,128)(2,1)S(1)}, u32[]{:S(2)}, u32[]{:S(2)}) collective-permute-start(bf16[1,96,512]{2,1,0:T(8,128)(2,1)S(1)} %get-tuple-element.401), channel_id=1, source_target_pairs={{0,16},{1,17},{2,18},{3,19},{4,20},{5,21},{6,22},{7,23},{8,24},{9,... | collective-permute-start | bytes 294920 | tf_op jit(solution)/shard_map/ppermute | solution.py:752
  407.3 39.2 %collective-permute-start.49 = (bf16[1,96,512]{2,1,0:T(8,128)(2,1)S(1)}, bf16[1,96,512]{2,1,0:T(8,128)(2,1)S(1)}, u32[]{:S(2)}, u32[]{:S(2)}) collective-permute-start(bf16[1,96,512]{2,1,0:T(8,128)(2,1)S(1)} %get-tuple-element.402), channel_id=1, source_target_pairs={{0,24},{1,25},{2,26},{3,27},{4,28},{5,29},{6,30},{7,31},{8,16},{9,... | collective-permute-start | bytes 294920 | tf_op jit(solution)/shard_map/ppermute | solution.py:752
  411.0 35.6 %collective-permute-start.44 = (bf16[4,96,512]{2,1,0:T(8,128)(2,1)S(1)}, bf16[4,96,512]{2,1,0:T(8,128)(2,1)S(1)}, u32[]{:S(2)}, u32[]{:S(2)}) collective-permute-start(bf16[4,96,512]{2,1,0:T(8,128)(2,1)S(1)} %get-tuple-element.396), channel_id=1, source_target_pairs={{0,2},{1,3},{2,0},{3,1},{4,6},{5,7},{6,4},{7,5},{8,10},{9,11},{10,... | collective-permute-start | bytes 1179656 | tf_op jit(solution)/shard_map/ppermute | solution.py:752
  411.1 35.5 %collective-permute-start.45 = (bf16[4,96,512]{2,1,0:T(8,128)(2,1)S(1)}, bf16[4,96,512]{2,1,0:T(8,128)(2,1)S(1)}, u32[]{:S(2)}, u32[]{:S(2)}) collective-permute-start(bf16[4,96,512]{2,1,0:T(8,128)(2,1)S(1)} %get-tuple-element.397), channel_id=1, source_target_pairs={{0,4},{1,5},{2,6},{3,7},{4,0},{5,1},{6,2},{7,3},{8,12},{9,13},{10,... | collective-permute-start | bytes 1179656 | tf_op jit(solution)/shard_map/ppermute | solution.py:752
  412.9 33.7 %collective-permute-start.46 = (bf16[4,96,512]{2,1,0:T(8,128)(2,1)S(1)}, bf16[4,96,512]{2,1,0:T(8,128)(2,1)S(1)}, u32[]{:S(2)}, u32[]{:S(2)}) collective-permute-start(bf16[4,96,512]{2,1,0:T(8,128)(2,1)S(1)} %get-tuple-element.398), channel_id=1, source_target_pairs={{0,6},{1,7},{2,4},{3,5},{4,2},{5,3},{6,0},{7,1},{8,14},{9,15},{10,... | collective-permute-start | bytes 1179656 | tf_op jit(solution)/shard_map/ppermute | solution.py:752
  446.6 17.2 %collective-permute-start.51 = (bf16[1024,512]{1,0:T(8,128)(2,1)}, bf16[1024,512]{1,0:T(8,128)(2,1)S(1)}, u32[]{:S(2)}, u32[]{:S(2)}) collective-permute-start(bf16[1024,512]{1,0:T(8,128)(2,1)} %get-tuple-element.413), channel_id=1, source_target_pairs={{0,29},{1,0},{2,1},{3,2},{6,3},{7,6},{4,7},{5,4},{8,5},{9,8},{10,9... | collective-permute-start | bytes 3145736 | tf_op jit(solution)/shard_map/ppermute | solution.py:769
  (93 other events, 1034.5 us)
Sparse Core Ops, SparseCore 0:
  81.4 79.7 all-gather.1

commit v13 on v12

--- a/solution.py
+++ b/solution.py
@@ -957,7 +957,7 @@
     above, above_source = None, None
     layer_grads = [None] * layer_total
     gain_grads = [None] * layer_total
-    in_plane, in_slice = [], []
+    in_plane, in_slice, waiting = [], [], []
     for layer_id in reversed(range(layer_total)):
         source_low, stored, aggregate = stored_list[layer_id]
         sent_grad, grad_new, *slot_grads, grad_gain, grad_message, edge_hidden, b0, b1, b2, b3 = backward_layer(
@@ -968,8 +968,13 @@
             moved = len(in_plane)
             arrived, slot_grads = together(in_plane + in_slice, slot_grads)
             if in_slice:
-                layer_grads[layer_id + 2] = add_up(arrived[moved:]).reshape(6, share, width)
-            far = list(combine(device_count // 8, arrived[:moved]))
+                total = add_up(arrived[moved:]).reshape(-1, 6, share, width)
+                for index in range(total.shape[0]):
+                    layer_grads[layer_total - 1 - index] = total[index]
+            waiting.append(arrived[:moved])
+            if layer_id < layer_total - 2:
+                far = list(combine(device_count // 8, *waiting))
+                waiting = []
         from_before = shift(slot_grads[2], device_count, 1, direct)
         from_after = shift(slot_grads[0], device_count, -1, direct)
         back = [edge_hidden, grad_message, b0, b1, b2, b3]

time: 540 us -> 543 us (level)
  waiting for transfers between devices: 113 us -> 120 us
    ppermute x46 -> x43, waiting for transfers between devices: 70.7 us -> 76.8 us  [swap(): return lax.ppermute(cells, AXES, [(i, i ^ mask) for i in range(count)])]
    ppermute x46 -> x43, starting transfers between devices: 65.1 us -> 60.7 us  [swap(): return lax.ppermute(cells, AXES, [(i, i ^ mask) for i in range(count)])]
  transfers between devices with their start and end apart: 67 -> 64, of which waited for: 29 -> 32; matrix products, arithmetic and copies ran while one was open for 2% -> 2% of each run, Pallas kernels for 40% -> 40%
where the time goes in v13:
time: 543 us; the launch traced here: 533 us
  Pallas kernels  261 us (48%)
  waiting for transfers between devices  120 us (22%)
  starting transfers between devices  111 us (20%)
  between operations  17.3 us (3%)
  other arithmetic  9.86 us (2%)
  local copies, waits for them, and re-layouts  8 us (1%)
  matrix products  6.07 us (1%)
    pallas_call x4, Pallas kernels, backward_layer(): pl.pallas_call(functools.partial(backward_kernel, parts, mode), grid=(blo...  125 us
    ppermute x43, waiting for transfers between devices, swap(): return lax.ppermute(cells, AXES, [(i, i ^ mask) for i in range(count)])  76.8 us
    pallas_call x4, Pallas kernels, forward_layer(): pl.pallas_call(functools.partial(forward_kernel, parts, has_next), grid=(...  72.1 us
    ppermute x43, starting transfers between devices, swap(): return lax.ppermute(cells, AXES, [(i, i ^ mask) for i in range(count)])  60.7 us
    ppermute x16, waiting for transfers between devices, shift(): return lax.ppermute(cells, AXES, pairs)  43.5 us
    pallas_call x4, Pallas kernels, weight_layer(): pl.pallas_call(functools.partial(weight_kernel, above is not None, grad_n...  41.5 us
    ppermute x16, starting transfers between devices, shift(): return lax.ppermute(cells, AXES, pairs)  37 us
    ppermute x4, starting transfers between devices, bring(): lax.ppermute(cells, AXES, [(i, home((i + step) % count, direct)) for i in...  12.9 us
  transfers between devices with their start and end apart: 64, of which 32 were waited for; matrix products, arithmetic and copies ran while one was open for 2% of the time, Pallas kernels for 40%

profile of v13, /device:TPU:0, one launch (start us, length us, event | category | flops | bytes accessed | tf_op | source)
XLA Modules:
  0.0 533.5 jit_solution(4740071286427863636)
XLA Ops:
  22.8 8.5 %collective-permute-done.3.refs_1_ = bf16[2,136,512]{2,1,0:T(8,128)(2,1)S(1)} collective-permute-done((bf16[2,136,512]{2,1,0:T(8,128)(2,1)S(1)}, bf16[2,136,512]{2,1,0:T(8,128)(2,1)S(1)}, u32[]{:S(2)}, u32[]{:S(2)}) %collective-permute-start.3) | collective-permute-done | bytes 278560 | tf_op jit(solution)/shard_map/ppermute | solution.py:752
  31.3 11.3 %collective-permute-done.4.refs_2_ = bf16[2,136,512]{2,1,0:T(8,128)(2,1)S(1)} collective-permute-done((bf16[2,136,512]{2,1,0:T(8,128)(2,1)S(1)}, bf16[2,136,512]{2,1,0:T(8,128)(2,1)S(1)}, u32[]{:S(2)}, u32[]{:S(2)}) %collective-permute-start.4) | collective-permute-done | bytes 278560 | tf_op jit(solution)/shard_map/ppermute | solution.py:752
  42.7 5.2 collective-permute-start.7
  52.4 9.4 %collective-permute-start.10 = (bf16[1024,512]{1,0:T(8,128)(2,1)}, bf16[1024,512]{1,0:T(8,128)(2,1)}, u32[]{:S(2)}, u32[]{:S(2)}) collective-permute-start(bf16[1024,512]{1,0:T(8,128)(2,1)} %param.22), channel_id=1, source_target_pairs={{0,0},{1,1},{2,2},{3,3},{4,6},{5,7},{6,4},{7,5},{8,8},{9,9},{10,10... | collective-permute-start | bytes 3145736 | tf_op jit(solution)/shard_map/ppermute | solution.py:764
  64.7 6.9 %collective-permute-done.11.refs_1_ = bf16[2,96,512]{2,1,0:T(8,128)(2,1)S(1)} collective-permute-done((bf16[2,96,512]{2,1,0:T(8,128)(2,1)S(1)}, bf16[2,96,512]{2,1,0:T(8,128)(2,1)S(1)}, u32[]{:S(2)}, u32[]{:S(2)}) %collective-permute-start.11) | collective-permute-done | bytes 196640 | tf_op jit(solution)/shard_map/ppermute | solution.py:752
  74.5 5.9 %collective-permute-done.12.refs_2_ = bf16[2,96,512]{2,1,0:T(8,128)(2,1)S(1)} collective-permute-done((bf16[2,96,512]{2,1,0:T(8,128)(2,1)S(1)}, bf16[2,96,512]{2,1,0:T(8,128)(2,1)S(1)}, u32[]{:S(2)}, u32[]{:S(2)}) %collective-permute-start.12) | collective-permute-done | bytes 196640 | tf_op jit(solution)/shard_map/ppermute | solution.py:752
  86.2 9.3 %embed.1 = (bf16[7,512,512]{2,1,0:T(8,128)(2,1)}, f32[1024,512]{1,0:T(8,128)}, bf16[1024,512]{1,0:T(8,128)(2,1)}, bf16[1024,512]{1,0:T(8,128)(2,1)}, bf16[1024,5...) custom-call(s32[1]{0:T(128)} %bitcast.10.refs_0_.self_id, bf16[8,136,512]{2,1,0:T(8,128)(2,1)} %copy-done.1, ...), custom_call_target="tpu_custom_call" | custom-call | flops 3221225472 | bytes 12582912 | tf_op jit(solution)/shard_map/embed/pallas_call | solution.py:611
  101.1 18.5 %forward_layer.4 = (bf16[1024,512]{1,0:T(8,128)(2,1)}, f32[1024,512]{1,0:T(8,128)}, bf16[1024,512]{1,0:T(8,128)(2,1)}, bf16[4,1024,512]{2,1,0:T(8,128)(2,1)}, bf16[1024,512]{1,0:T(8,128)(2,1)}) custom-call(s32[4096]{0:T(1024)} %get-tuple-element.479.refs_0_, bf16[1024,512]{1,0:T(8,128)(2,1)} %get-tuple-element.254.refs_1_, ...), custom_call_target="tpu_custom_call" | custom-call | flops 4831838208 | bytes 25165824 | tf_op jit(solution)/shard_map/forward_layer/pallas_call | solution.py:186
  129.8 12.0 %collective-permute-done.17.refs_1_ = bf16[1024,512]{1,0:T(8,128)(2,1)} collective-permute-done((bf16[1024,512]{1,0:T(8,128)(2,1)}, bf16[1024,512]{1,0:T(8,128)(2,1)}, u32[]{:S(2)}, u32[]{:S(2)}) %collective-permute-start.17) | collective-permute-done | bytes 1048608 | tf_op jit(solution)/shard_map/ppermute | solution.py:769
  144.4 18.8 %forward_layer.5 = (bf16[1024,512]{1,0:T(8,128)(2,1)}, f32[1024,512]{1,0:T(8,128)}, bf16[1024,512]{1,0:T(8,128)(2,1)}, bf16[4,1024,512]{2,1,0:T(8,128)(2,1)}, bf16[1024,512]{1,0:T(8,128)(2,1)}) custom-call(s32[4096]{0:T(1024)} %get-tuple-element.480.refs_0_, bf16[1024,512]{1,0:T(8,128)(2,1)} %collective-permute-done.17.refs_1_, ...), custom_call_target="tpu_custom_call" | custom-call | flops 4831838208 | bytes 25165824 | tf_op jit(solution)/shard_map/forward_layer/pallas_call | solution.py:186
  163.3 4.6 collective-permute-start.23
  170.7 9.8 %collective-permute-done.22.refs_1_ = bf16[1024,512]{1,0:T(8,128)(2,1)S(1)} collective-permute-done((bf16[1024,512]{1,0:T(8,128)(2,1)}, bf16[1024,512]{1,0:T(8,128)(2,1)S(1)}, u32[]{:S(2)}, u32[]{:S(2)}) %collective-permute-start.22) | collective-permute-done | bytes 1048608 | tf_op jit(solution)/shard_map/ppermute | solution.py:769
  180.5 18.0 %forward_layer.6 = (bf16[1024,512]{1,0:T(8,128)(2,1)}, f32[1024,512]{1,0:T(8,128)}, bf16[1024,512]{1,0:T(8,128)(2,1)}, bf16[4,1024,512]{2,1,0:T(8,128)(2,1)}, bf16[1024,512]{1,0:T(8,128)(2,1)}) custom-call(s32[4096]{0:T(1024)} %get-tuple-element.480.refs_0_, bf16[1024,512]{1,0:T(8,128)(2,1)S(1)} %collective-permute-done.22.refs_1_, ...), custom_call_target="tpu_custom_call" | custom-call | flops 4831838208 | bytes 25165824 | tf_op jit(solution)/shard_map/forward_layer/pallas_call | solution.py:186
  204.6 11.1 %collective-permute-done.24.refs_1_ = bf16[1024,512]{1,0:T(8,128)(2,1)S(1)} collective-permute-done((bf16[1024,512]{1,0:T(8,128)(2,1)}, bf16[1024,512]{1,0:T(8,128)(2,1)S(1)}, u32[]{:S(2)}, u32[]{:S(2)}) %collective-permute-start.24) | collective-permute-done | bytes 1048608 | tf_op jit(solution)/shard_map/ppermute | solution.py:769
  215.7 16.8 %forward_layer.7 = (bf16[1024,512]{1,0:T(8,128)(2,1)}, bf16[4,1024,512]{2,1,0:T(8,128)(2,1)}, bf16[1024,512]{1,0:T(8,128)(2,1)}) custom-call(s32[4096]{0:T(1024)} %get-tuple-element.481.refs_0_, bf16[1024,512]{1,0:T(8,128)(2,1)S(1)} %collective-permute-done.24.refs_1_, bf16[1024,512]{1,0:T(8,128)(2,1)} %get-tuple-element.273.refs_2_, ...), custom_call_target="tpu_custom_call" | custom-call | flops 4831838208 | bytes 25165824 | tf_op jit(solution)/shard_map/forward_layer/pallas_call | solution.py:186
  238.1 29.8 %backward_layer.4 = (bf16[1024,512]{1,0:T(8,128)(2,1)}, bf16[1024,512]{1,0:T(8,128)(2,1)}, bf16[1024,512]{1,0:T(8,128)(2,1)}, f32[2,512]{1,0:T(2,128)S(1)}, bf16...) custom-call(s32[4096]{0:T(1024)S(1)} %copy-done.8, ...), custom_call_target="tpu_custom_call" | custom-call | flops 4294967296 | bytes 25165824 | tf_op jit(solution)/shard_map/backward_layer/pallas_call | solution.py:374
  267.9 4.7 collective-permute-start.27
  273.3 10.4 %weight_layer.4 = (f32[1024,512]{1,0:T(8,128)}, f32[16,96,512]{2,1,0:T(8,128)S(1)}, bf16[16,96,512]{2,1,0:T(8,128)(2,1)S(1)}) custom-call(s32[1]{0:T(128)} %bitcast.10.refs_0_.self_id, f32[512,512]{1,0:T(8,128)S(1)} %pad.29.refs_1_, bf16[1024,512]{1,0:T(8,128)(2,1)} %get-tuple-element.274.refs_4_.refs_2_.latent_low, ...), custom_call_target="tpu_custom_call" | custom-call | flops 5368709120 | bytes 12582912 | tf_op jit(solution)/shard_map/weight_layer/pallas_call | solution.py:504
  285.3 5.4 %collective-permute-start.28 = (bf16[16,96,512]{2,1,0:T(8,128)(2,1)S(1)}, bf16[16,96,512]{2,1,0:T(8,128)(2,1)S(1)}, u32[]{:S(2)}, u32[]{:S(2)}) collective-permute-start(bf16[16,96,512]{2,1,0:T(8,128)(2,1)S(1)} %get-tuple-element.292), channel_id=1, source_target_pairs={{0,1},{1,0},{2,3},{3,2},{4,5},{5,4},{6,7},{7,6},{8,9},{9,8},{10,11... | collective-permute-start | bytes 4718600 | tf_op jit(solution)/shard_map/ppermute | solution.py:752
  297.7 32.1 %backward_layer.5 = (bf16[1024,512]{1,0:T(8,128)(2,1)S(1)}, f32[1024,512]{1,0:T(8,128)S(1)}, bf16[1024,512]{1,0:T(8,128)(2,1)}, bf16[1024,512]{1,0:T(8,128)(2,1)...) custom-call(s32[4096]{0:T(1024)S(1)} %copy-done.6, ...), custom_call_target="tpu_custom_call" | custom-call | flops 4294967296 | bytes 25165824 | tf_op jit(solution)/shard_map/backward_layer/pallas_call | solution.py:374
  329.9 4.6 collective-permute-start.33
  334.5 11.4 %weight_layer.5 = (f32[1024,512]{1,0:T(8,128)}, f32[16,96,512]{2,1,0:T(8,128)S(1)}, bf16[16,96,512]{2,1,0:T(8,128)(2,1)S(1)}) custom-call(s32[1]{0:T(128)} %bitcast.10.refs_0_.self_id, bf16[1024,512]{1,0:T(8,128)(2,1)} %get-tuple-element.311.refs_1_, bf16[1024,512]{1,0:T(8,128)(2,1)S(1)} %get-tuple-element.312.refs_2_, ...), custom_call_target="tpu_custom_call" | custom-call | flops 5368709120 | bytes 12582912 | tf_op jit(solution)/shard_map/weight_layer/pallas_call | solution.py:504
  355.7 31.6 %backward_layer.6 = (bf16[1024,512]{1,0:T(8,128)(2,1)S(1)}, f32[1024,512]{1,0:T(8,128)S(1)}, bf16[1024,512]{1,0:T(8,128)(2,1)}, bf16[1024,512]{1,0:T(8,128)(2,1)...) custom-call(s32[4096]{0:T(1024)S(1)} %copy-done.6, ...), custom_call_target="tpu_custom_call" | custom-call | flops 4294967296 | bytes 25165824 | tf_op jit(solution)/shard_map/backward_layer/pallas_call | solution.py:374
  387.4 4.8 collective-permute-start.39
  392.2 11.4 %weight_layer.6 = (f32[1024,512]{1,0:T(8,128)}, f32[16,96,512]{2,1,0:T(8,128)S(1)}, bf16[16,96,512]{2,1,0:T(8,128)(2,1)S(1)}) custom-call(s32[1]{0:T(128)} %bitcast.10.refs_0_.self_id, bf16[1024,512]{1,0:T(8,128)(2,1)} %get-tuple-element.270.refs_4_.refs_5_.refs_3_.refs_1_, bf16[1024,512]{1,0:T(8,128)(2,1)S(1)} %get-tuple-element.345.refs_2_, ...), custom_call_target="tpu_custom_call" | custom-call | flops 5368709120 | bytes 12582912 | tf_op jit(solution)/shard_map/weight_layer/pallas_call | solution.py:504
  416.0 31.9 %backward_layer.7 = (bf16[1024,512]{1,0:T(8,128)(2,1)S(1)}, f32[1024,512]{1,0:T(8,128)}, bf16[1024,512]{1,0:T(8,128)(2,1)}, bf16[1024,512]{1,0:T(8,128)(2,1)}, b...) custom-call(s32[4096]{0:T(1024)S(1)} %copy-done.7, ...), custom_call_target="tpu_custom_call" | custom-call | flops 4294967296 | bytes 25165824 | tf_op jit(solution)/shard_map/backward_layer/pallas_call | solution.py:374
  448.1 4.6 collective-permute-start.48
  452.6 8.3 %weight_layer.7 = (f32[16,96,512]{2,1,0:T(8,128)S(1)}, bf16[16,96,512]{2,1,0:T(8,128)(2,1)S(1)}) custom-call(s32[1]{0:T(128)} %bitcast.10.refs_0_.self_id, bf16[1024,512]{1,0:T(8,128)(2,1)} %get-tuple-element.260.refs_4_.refs_6_.refs_3_.refs_1_, bf16[1024,512]{1,0:T(8,128)(2,1)S(1)} %get-tuple-element.394.refs_2_, ...), custom_call_target="tpu_custom_call" | custom-call | flops 5368709120 | bytes 12582912 | tf_op jit(solution)/shard_map/weight_layer/pallas_call | solution.py:504
  473.2 5.3 collective-permute-start.53
  478.5 7.1 %tail_layer.1 = (f32[16,40,512]{2,1,0:T(8,128)S(1)}, bf16[16,40,512]{2,1,0:T(8,128)(2,1)S(1)}) custom-call(s32[1]{0:T(128)} %bitcast.10.refs_0_.self_id, f32[1]{0:T(128)} %bitcast.56.loss, bf16[1024,512]{1,0:T(8,128)(2,1)} %copy-done.22, bf16[1024,512]{1,0:T(8,128)(2,1)} %get-tuple-element.423.middle, bf16[1024,512]{1,0:T(8,128)(2,1)} %copy-done.23, ...), custom_call_target="tpu_custom_call" | custom-call | flops 1610612736 | bytes 12582912 | tf_op jit(solution)/shard_map/tail_layer/pallas_call | solution.py:686
  493.4 6.9 %collective-permute-done.55 = bf16[4,96,512]{2,1,0:T(8,128)(2,1)S(1)} collective-permute-done((bf16[4,96,512]{2,1,0:T(8,128)(2,1)S(1)}, bf16[4,96,512]{2,1,0:T(8,128)(2,1)S(1)}, u32[]{:S(2)}, u32[]{:S(2)}) %collective-permute-start.55) | collective-permute-done | bytes 393248 | tf_op jit(solution)/shard_map/ppermute | solution.py:752
  514.2 8.2 %collective-permute-done.61 = bf16[1,136,512]{2,1,0:T(8,128)(2,1)S(1)} collective-permute-done((bf16[1,136,512]{2,1,0:T(8,128)(2,1)S(1)}, bf16[1,136,512]{2,1,0:T(8,128)(2,1)S(1)}, u32[]{:S(2)}, u32[]{:S(2)}) %collective-permute-start.61) | collective-permute-done | bytes 139296 | tf_op jit(solution)/shard_map/ppermute | solution.py:752
  (287 shorter events, 131.4 us)
Async XLA Ops:
  7.2 173.3 %all-gather.2.cloned.1.call-start = ((), (), s32[]{:S(2)}) async-start(), calls=%async_computation | async-start | bytes 6488064 | tf_op jit(solution)/shard_map/all_gather | solution.py:879
  17.4 25.2 %collective-permute-start.6 = (bf16[1024,512]{1,0:T(8,128)(2,1)S(1)}, bf16[1024,512]{1,0:T(8,128)(2,1)S(1)}, u32[]{:S(2)}, u32[]{:S(2)}) collective-permute-start(bf16[1024,512]{1,0:T(8,128)(2,1)S(1)} %pad.26), channel_id=1, source_target_pairs={{0,0},{1,1},{2,2},{3,3},{4,6},{5,7},{6,4},{7,5},{8,8},{9,9},{10,10... | collective-permute-start | bytes 3145736 | tf_op jit(solution)/shard_map/ppermute | solution.py:764
  20.1 22.4 %collective-permute-start.4 = (bf16[2,136,512]{2,1,0:T(8,128)(2,1)S(1)}, bf16[2,136,512]{2,1,0:T(8,128)(2,1)S(1)}, u32[]{:S(2)}, u32[]{:S(2)}) collective-permute-start(bf16[2,136,512]{2,1,0:T(8,128)(2,1)S(1)} %pad_maximum_fusion.refs_0_), channel_id=1, source_target_pairs={{0,16},{1,17},{2,18},{3,19},{4,20},{5,21},{6,22},{7,23},{8,24},{9,... | collective-permute-start | bytes 835592 | tf_op jit(solution)/shard_map/ppermute | solution.py:752
  22.7 19.8 %collective-permute-start.5 = (bf16[2,136,512]{2,1,0:T(8,128)(2,1)S(1)}, bf16[2,136,512]{2,1,0:T(8,128)(2,1)S(1)}, u32[]{:S(2)}, u32[]{:S(2)}) collective-permute-start(bf16[2,136,512]{2,1,0:T(8,128)(2,1)S(1)} %pad_maximum_fusion.refs_0_), channel_id=1, source_target_pairs={{0,24},{1,25},{2,26},{3,27},{4,28},{5,29},{6,30},{7,31},{8,16},{9,... | collective-permute-start | bytes 835592 | tf_op jit(solution)/shard_map/ppermute | solution.py:752
  42.7 38.6 %collective-permute-start.7 = (bf16[8,136,512]{2,1,0:T(8,128)(2,1)S(1)}, bf16[8,136,512]{2,1,0:T(8,128)(2,1)}, u32[]{:S(2)}, u32[]{:S(2)}) collective-permute-start(bf16[8,136,512]{2,1,0:T(8,128)(2,1)S(1)} %join.2.refs_1_), channel_id=1, source_target_pairs={{0,4},{1,5},{2,6},{3,7},{4,0},{5,1},{6,2},{7,3},{8,12},{9,13},{10,... | collective-permute-start | bytes 3342344 | tf_op jit(solution)/shard_map/ppermute | solution.py:752
  47.9 32.5 %collective-permute-start.8 = (bf16[1024,512]{1,0:T(8,128)(2,1)S(1)}, bf16[1024,512]{1,0:T(8,128)(2,1)}, u32[]{:S(2)}, u32[]{:S(2)}) collective-permute-start(bf16[1024,512]{1,0:T(8,128)(2,1)S(1)} %collective-permute-done.6.refs_6_.inputs), channel_id=1, source_target_pairs={{0,1},{1,2},{2,3},{3,6},{6,7},{7,4},{4,5},{5,8},{8,9},{9,10},{10,1... | collective-permute-start | bytes 3145736 | tf_op jit(solution)/shard_map/ppermute | solution.py:769
  47.9 32.5 %collective-permute-start.9 = (bf16[1024,512]{1,0:T(8,128)(2,1)S(1)}, bf16[1024,512]{1,0:T(8,128)(2,1)}, u32[]{:S(2)}, u32[]{:S(2)}) collective-permute-start(bf16[1024,512]{1,0:T(8,128)(2,1)S(1)} %collective-permute-done.6.refs_6_.inputs), channel_id=1, source_target_pairs={{0,29},{1,0},{2,1},{3,2},{6,3},{7,6},{4,7},{5,4},{8,5},{9,8},{10,9... | collective-permute-start | bytes 3145736 | tf_op jit(solution)/shard_map/ppermute | solution.py:769
  52.4 28.1 %collective-permute-start.10 = (bf16[1024,512]{1,0:T(8,128)(2,1)}, bf16[1024,512]{1,0:T(8,128)(2,1)}, u32[]{:S(2)}, u32[]{:S(2)}) collective-permute-start(bf16[1024,512]{1,0:T(8,128)(2,1)} %param.22), channel_id=1, source_target_pairs={{0,0},{1,1},{2,2},{3,3},{4,6},{5,7},{6,4},{7,5},{8,8},{9,9},{10,10... | collective-permute-start | bytes 3145736 | tf_op jit(solution)/shard_map/ppermute | solution.py:764
  95.6 28.6 %collective-permute-start.19 = (bf16[8,96,512]{2,1,0:T(8,128)(2,1)S(1)}, bf16[8,96,512]{2,1,0:T(8,128)(2,1)S(1)}, u32[]{:S(2)}, u32[]{:S(2)}) collective-permute-start(bf16[8,96,512]{2,1,0:T(8,128)(2,1)S(1)} %join.3.refs_1_), channel_id=1, source_target_pairs={{0,4},{1,5},{2,6},{3,7},{4,0},{5,1},{6,2},{7,3},{8,12},{9,13},{10,... | collective-permute-start | bytes 2359304 | tf_op jit(solution)/shard_map/ppermute | solution.py:752
  119.7 22.1 %collective-permute-start.17 = (bf16[1024,512]{1,0:T(8,128)(2,1)}, bf16[1024,512]{1,0:T(8,128)(2,1)}, u32[]{:S(2)}, u32[]{:S(2)}) collective-permute-start(bf16[1024,512]{1,0:T(8,128)(2,1)} %get-tuple-element.259.refs_2_), channel_id=1, source_target_pairs={{0,1},{1,2},{2,3},{3,6},{6,7},{7,4},{4,5},{5,8},{8,9},{9,10},{10,1... | collective-permute-start | bytes 3145736 | tf_op jit(solution)/shard_map/ppermute | solution.py:769
  119.7 24.7 %collective-permute-start.18 = (bf16[1024,512]{1,0:T(8,128)(2,1)}, bf16[1024,512]{1,0:T(8,128)(2,1)}, u32[]{:S(2)}, u32[]{:S(2)}) collective-permute-start(bf16[1024,512]{1,0:T(8,128)(2,1)} %get-tuple-element.259.refs_2_), channel_id=1, source_target_pairs={{0,29},{1,0},{2,1},{3,2},{6,3},{7,6},{4,7},{5,4},{8,5},{9,8},{10,9... | collective-permute-start | bytes 3145736 | tf_op jit(solution)/shard_map/ppermute | solution.py:769
  163.2 17.2 %collective-permute-start.22 = (bf16[1024,512]{1,0:T(8,128)(2,1)}, bf16[1024,512]{1,0:T(8,128)(2,1)S(1)}, u32[]{:S(2)}, u32[]{:S(2)}) collective-permute-start(bf16[1024,512]{1,0:T(8,128)(2,1)} %get-tuple-element.269.refs_2_), channel_id=1, source_target_pairs={{0,1},{1,2},{2,3},{3,6},{6,7},{7,4},{4,5},{5,8},{8,9},{9,10},{10,1... | collective-permute-start | bytes 3145736 | tf_op jit(solution)/shard_map/ppermute | solution.py:769
  163.3 17.2 %collective-permute-start.23 = (bf16[1024,512]{1,0:T(8,128)(2,1)}, bf16[1024,512]{1,0:T(8,128)(2,1)S(1)}, u32[]{:S(2)}, u32[]{:S(2)}) collective-permute-start(bf16[1024,512]{1,0:T(8,128)(2,1)} %get-tuple-element.269.refs_2_), channel_id=1, source_target_pairs={{0,29},{1,0},{2,1},{3,2},{6,3},{7,6},{4,7},{5,4},{8,5},{9,8},{10,9... | collective-permute-start | bytes 3145736 | tf_op jit(solution)/shard_map/ppermute | solution.py:769
  168.6 35.2 %collective-permute-start.16 = (f32[1024,256]{0,1:T(8,128)S(1)}, f32[1024,256]{0,1:T(8,128)}, u32[]{:S(2)}, u32[]{:S(2)}) collective-permute-start(f32[1024,256]{0,1:T(8,128)S(1)} %copy-done.21), channel_id=1, source_target_pairs={{0,0},{1,1},{2,2},{3,3},{4,6},{5,7},{6,4},{7,5},{8,8},{9,9},{10,10... | collective-permute-start | bytes 3145736 | tf_op jit(solution)/shard_map/ppermute | solution.py:764
  198.5 17.2 %collective-permute-start.24 = (bf16[1024,512]{1,0:T(8,128)(2,1)}, bf16[1024,512]{1,0:T(8,128)(2,1)S(1)}, u32[]{:S(2)}, u32[]{:S(2)}) collective-permute-start(bf16[1024,512]{1,0:T(8,128)(2,1)} %get-tuple-element.273.refs_2_), channel_id=1, source_target_pairs={{0,1},{1,2},{2,3},{3,6},{6,7},{7,4},{4,5},{5,8},{8,9},{9,10},{10,1... | collective-permute-start | bytes 3145736 | tf_op jit(solution)/shard_map/ppermute | solution.py:769
  267.9 17.2 %collective-permute-start.26 = (bf16[1024,512]{1,0:T(8,128)(2,1)}, bf16[1024,512]{1,0:T(8,128)(2,1)S(1)}, u32[]{:S(2)}, u32[]{:S(2)}) collective-permute-start(bf16[1024,512]{1,0:T(8,128)(2,1)} %get-tuple-element.279), channel_id=1, source_target_pairs={{0,1},{1,2},{2,3},{3,6},{6,7},{7,4},{4,5},{5,8},{8,9},{9,10},{10,1... | collective-permute-start | bytes 3145736 | tf_op jit(solution)/shard_map/ppermute | solution.py:769
  267.9 17.3 %collective-permute-start.27 = (bf16[1024,512]{1,0:T(8,128)(2,1)}, bf16[1024,512]{1,0:T(8,128)(2,1)S(1)}, u32[]{:S(2)}, u32[]{:S(2)}) collective-permute-start(bf16[1024,512]{1,0:T(8,128)(2,1)} %get-tuple-element.280), channel_id=1, source_target_pairs={{0,29},{1,0},{2,1},{3,2},{6,3},{7,6},{4,7},{5,4},{8,5},{9,8},{10,9... | collective-permute-start | bytes 3145736 | tf_op jit(solution)/shard_map/ppermute | solution.py:769
  294.1 35.7 %collective-permute-start.29 = (bf16[4,96,512]{2,1,0:T(8,128)(2,1)S(1)}, bf16[4,96,512]{2,1,0:T(8,128)(2,1)S(1)}, u32[]{:S(2)}, u32[]{:S(2)}) collective-permute-start(bf16[4,96,512]{2,1,0:T(8,128)(2,1)S(1)} %get-tuple-element.298), channel_id=1, source_target_pairs={{0,2},{1,3},{2,0},{3,1},{4,6},{5,7},{6,4},{7,5},{8,10},{9,11},{10,... | collective-permute-start | bytes 1179656 | tf_op jit(solution)/shard_map/ppermute | solution.py:752
  295.9 33.9 %collective-permute-start.30 = (bf16[4,96,512]{2,1,0:T(8,128)(2,1)S(1)}, bf16[4,96,512]{2,1,0:T(8,128)(2,1)S(1)}, u32[]{:S(2)}, u32[]{:S(2)}) collective-permute-start(bf16[4,96,512]{2,1,0:T(8,128)(2,1)S(1)} %get-tuple-element.299), channel_id=1, source_target_pairs={{0,4},{1,5},{2,6},{3,7},{4,0},{5,1},{6,2},{7,3},{8,12},{9,13},{10,... | collective-permute-start | bytes 1179656 | tf_op jit(solution)/shard_map/ppermute | solution.py:752
  297.5 32.3 %collective-permute-start.31 = (bf16[4,96,512]{2,1,0:T(8,128)(2,1)S(1)}, bf16[4,96,512]{2,1,0:T(8,128)(2,1)S(1)}, u32[]{:S(2)}, u32[]{:S(2)}) collective-permute-start(bf16[4,96,512]{2,1,0:T(8,128)(2,1)S(1)} %get-tuple-element.300), channel_id=1, source_target_pairs={{0,6},{1,7},{2,4},{3,5},{4,2},{5,3},{6,0},{7,1},{8,14},{9,15},{10,... | collective-permute-start | bytes 1179656 | tf_op jit(solution)/shard_map/ppermute | solution.py:752
  329.8 17.2 %collective-permute-start.32 = (bf16[1024,512]{1,0:T(8,128)(2,1)}, bf16[1024,512]{1,0:T(8,128)(2,1)S(1)}, u32[]{:S(2)}, u32[]{:S(2)}) collective-permute-start(bf16[1024,512]{1,0:T(8,128)(2,1)} %get-tuple-element.309), channel_id=1, source_target_pairs={{0,1},{1,2},{2,3},{3,6},{6,7},{7,4},{4,5},{5,8},{8,9},{9,10},{10,1... | collective-permute-start | bytes 3145736 | tf_op jit(solution)/shard_map/ppermute | solution.py:769
  329.9 17.3 %collective-permute-start.33 = (bf16[1024,512]{1,0:T(8,128)(2,1)}, bf16[1024,512]{1,0:T(8,128)(2,1)S(1)}, u32[]{:S(2)}, u32[]{:S(2)}) collective-permute-start(bf16[1024,512]{1,0:T(8,128)(2,1)} %get-tuple-element.310), channel_id=1, source_target_pairs={{0,29},{1,0},{2,1},{3,2},{6,3},{7,6},{4,7},{5,4},{8,5},{9,8},{10,9... | collective-permute-start | bytes 3145736 | tf_op jit(solution)/shard_map/ppermute | solution.py:769
  350.9 36.4 %collective-permute-start.35 = (bf16[4,96,512]{2,1,0:T(8,128)(2,1)S(1)}, bf16[4,96,512]{2,1,0:T(8,128)(2,1)S(1)}, u32[]{:S(2)}, u32[]{:S(2)}) collective-permute-start(bf16[4,96,512]{2,1,0:T(8,128)(2,1)S(1)} %get-tuple-element.331), channel_id=1, source_target_pairs={{0,2},{1,3},{2,0},{3,1},{4,6},{5,7},{6,4},{7,5},{8,10},{9,11},{10,... | collective-permute-start | bytes 1179656 | tf_op jit(solution)/shard_map/ppermute | solution.py:752
  351.4 35.9 %collective-permute-start.36 = (bf16[4,96,512]{2,1,0:T(8,128)(2,1)S(1)}, bf16[4,96,512]{2,1,0:T(8,128)(2,1)S(1)}, u32[]{:S(2)}, u32[]{:S(2)}) collective-permute-start(bf16[4,96,512]{2,1,0:T(8,128)(2,1)S(1)} %get-tuple-element.332), channel_id=1, source_target_pairs={{0,4},{1,5},{2,6},{3,7},{4,0},{5,1},{6,2},{7,3},{8,12},{9,13},{10,... | collective-permute-start | bytes 1179656 | tf_op jit(solution)/shard_map/ppermute | solution.py:752
  354.3 33.0 %collective-permute-start.37 = (bf16[4,96,512]{2,1,0:T(8,128)(2,1)S(1)}, bf16[4,96,512]{2,1,0:T(8,128)(2,1)S(1)}, u32[]{:S(2)}, u32[]{:S(2)}) collective-permute-start(bf16[4,96,512]{2,1,0:T(8,128)(2,1)S(1)} %get-tuple-element.333), channel_id=1, source_target_pairs={{0,6},{1,7},{2,4},{3,5},{4,2},{5,3},{6,0},{7,1},{8,14},{9,15},{10,... | collective-permute-start | bytes 1179656 | tf_op jit(solution)/shard_map/ppermute | solution.py:752
  387.4 17.4 %collective-permute-start.39 = (bf16[1024,512]{1,0:T(8,128)(2,1)}, bf16[1024,512]{1,0:T(8,128)(2,1)S(1)}, u32[]{:S(2)}, u32[]{:S(2)}) collective-permute-start(bf16[1024,512]{1,0:T(8,128)(2,1)} %get-tuple-element.344), channel_id=1, source_target_pairs={{0,29},{1,0},{2,1},{3,2},{6,3},{7,6},{4,7},{5,4},{8,5},{9,8},{10,9... | collective-permute-start | bytes 3145736 | tf_op jit(solution)/shard_map/ppermute | solution.py:769
  405.4 42.5 %collective-permute-start.45 = (bf16[1,192,512]{2,1,0:T(8,128)(2,1)S(1)}, bf16[1,192,512]{2,1,0:T(8,128)(2,1)S(1)}, u32[]{:S(2)}, u32[]{:S(2)}) collective-permute-start(bf16[1,192,512]{2,1,0:T(8,128)(2,1)S(1)} %get-tuple-element.381), channel_id=1, source_target_pairs={{0,16},{1,17},{2,18},{3,19},{4,20},{5,21},{6,22},{7,23},{8,24},{9,... | collective-permute-start | bytes 589832 | tf_op jit(solution)/shard_map/ppermute | solution.py:752
  405.5 42.5 %collective-permute-start.46 = (bf16[1,192,512]{2,1,0:T(8,128)(2,1)S(1)}, bf16[1,192,512]{2,1,0:T(8,128)(2,1)S(1)}, u32[]{:S(2)}, u32[]{:S(2)}) collective-permute-start(bf16[1,192,512]{2,1,0:T(8,128)(2,1)S(1)} %get-tuple-element.382), channel_id=1, source_target_pairs={{0,24},{1,25},{2,26},{3,27},{4,28},{5,29},{6,30},{7,31},{8,16},{9,... | collective-permute-start | bytes 589832 | tf_op jit(solution)/shard_map/ppermute | solution.py:752
  409.6 38.4 %collective-permute-start.41 = (bf16[4,96,512]{2,1,0:T(8,128)(2,1)S(1)}, bf16[4,96,512]{2,1,0:T(8,128)(2,1)S(1)}, u32[]{:S(2)}, u32[]{:S(2)}) collective-permute-start(bf16[4,96,512]{2,1,0:T(8,128)(2,1)S(1)} %get-tuple-element.376), channel_id=1, source_target_pairs={{0,2},{1,3},{2,0},{3,1},{4,6},{5,7},{6,4},{7,5},{8,10},{9,11},{10,... | collective-permute-start | bytes 1179656 | tf_op jit(solution)/shard_map/ppermute | solution.py:752
  409.6 38.3 %collective-permute-start.42 = (bf16[4,96,512]{2,1,0:T(8,128)(2,1)S(1)}, bf16[4,96,512]{2,1,0:T(8,128)(2,1)S(1)}, u32[]{:S(2)}, u32[]{:S(2)}) collective-permute-start(bf16[4,96,512]{2,1,0:T(8,128)(2,1)S(1)} %get-tuple-element.377), channel_id=1, source_target_pairs={{0,4},{1,5},{2,6},{3,7},{4,0},{5,1},{6,2},{7,3},{8,12},{9,13},{10,... | collective-permute-start | bytes 1179656 | tf_op jit(solution)/shard_map/ppermute | solution.py:752
  413.8 34.2 %collective-permute-start.43 = (bf16[4,96,512]{2,1,0:T(8,128)(2,1)S(1)}, bf16[4,96,512]{2,1,0:T(8,128)(2,1)S(1)}, u32[]{:S(2)}, u32[]{:S(2)}) collective-permute-start(bf16[4,96,512]{2,1,0:T(8,128)(2,1)S(1)} %get-tuple-element.378), channel_id=1, source_target_pairs={{0,6},{1,7},{2,4},{3,5},{4,2},{5,3},{6,0},{7,1},{8,14},{9,15},{10,... | collective-permute-start | bytes 1179656 | tf_op jit(solution)/shard_map/ppermute | solution.py:752
  448.1 17.2 %collective-permute-start.48 = (bf16[1024,512]{1,0:T(8,128)(2,1)}, bf16[1024,512]{1,0:T(8,128)(2,1)S(1)}, u32[]{:S(2)}, u32[]{:S(2)}) collective-permute-start(bf16[1024,512]{1,0:T(8,128)(2,1)} %get-tuple-element.393), channel_id=1, source_target_pairs={{0,29},{1,0},{2,1},{3,2},{6,3},{7,6},{4,7},{5,4},{8,5},{9,8},{10,9... | collective-permute-start | bytes 3145736 | tf_op jit(solution)/shard_map/ppermute | solution.py:769
  (82 other events, 894.1 us)
Sparse Core Ops, SparseCore 0:
  81.4 79.7 all-gather.1
